TPU v7x, 32 devices: a whole 2x2x4 slice. The times are simulated.
32 devices in a mesh: section: 2 (over y), row: 4 (over z), col: 4 (over x, core).
Axes of the slice: x: 2, y: 2, z: 4, core: 2. Of those that a mesh axis runs over, the one named last changes fastest.
Arguments:
- inputs: bfloat16 [2, 4096, 2048], P(None, ('row', 'col')), may hold values from -6 to 6
- cotangent: bfloat16 [2, 4096, 2048], P(None, ('row', 'col')), may hold values from -6 to 6
- qkv_weight: bfloat16 [2, 2048, 8, 768], P('section', 'row', 'col'), may hold values from -0.125 to 0.125
- qkv_bias: bfloat16 [2, 8, 768], P('section', 'col', 'row'), may hold values from -3 to 3
- out_weight: bfloat16 [2, 2048, 2048], P('section', 'col', 'row'), may hold values from -1 to 1
- fc_in_weight: bfloat16 [2, 2048, 8192], P('section', 'row', 'col'), may hold values from -0.125 to 0.125
- fc_in_bias: bfloat16 [2, 8192], P('section', ('col', 'row')), may hold values from -3 to 3
- fc_out_weight: bfloat16 [2, 8192, 2048], P('section', 'col', 'row'), may hold values from -0.0625 to 0.0625
- norm1_gain: bfloat16 [2, 2048], P('section', ('row', 'col')), may hold values from 0.099609375 to 1.8984375
- norm1_bias: bfloat16 [2, 2048], P('section', ('row', 'col')), may hold values from -2 to 2
- norm2_gain: bfloat16 [2, 2048], P('section', ('row', 'col')), may hold values from 0.099609375 to 1.8984375
- norm2_bias: bfloat16 [2, 2048], P('section', ('row', 'col')), may hold values from -2 to 2
- out_bias: bfloat16 [2, 2048], P('section', ('row', 'col')), may hold values from -3 to 3
- fc_out_bias: bfloat16 [2, 2048], P('section', ('row', 'col')), may hold values from -3 to 3
Outputs:
- layer_outputs: bfloat16 [2, 2, 4096, 2048], P('section', None, ('row', 'col'))
- input_gradients: bfloat16 [2, 2, 4096, 2048], P('section', None, ('row', 'col'))
- qkv_weight_grad: float32 [2, 2048, 8, 768], P('section', 'row', 'col')
- qkv_bias_grad: float32 [2, 8, 768], P('section', 'col', 'row')
- out_weight_grad: float32 [2, 2048, 2048], P('section', 'col', 'row')
- fc_in_weight_grad: float32 [2, 2048, 8192], P('section', 'row', 'col')
- fc_in_bias_grad: float32 [2, 8192], P('section', ('col', 'row'))
- fc_out_weight_grad: float32 [2, 8192, 2048], P('section', 'col', 'row')
- norm1_gain_grad: float32 [2, 2048], P('section', ('row', 'col'))
- norm1_bias_grad: float32 [2, 2048], P('section', ('row', 'col'))
- norm2_gain_grad: float32 [2, 2048], P('section', ('row', 'col'))
- norm2_bias_grad: float32 [2, 2048], P('section', ('row', 'col'))
- out_bias_grad: float32 [2, 2048], P('section', ('row', 'col'))
- fc_out_bias_grad: float32 [2, 2048], P('section', ('row', 'col'))
All inputs are finite; a program needn't handle non-finite values.
Results may differ from a plain program's by a relative error of at most 0.015.
Values may be sent and summed in bfloat16 or wider, within the bound.
No kernel may reach another device: no remote copies, remote signals or barrier semaphores. Data moves between devices by JAX's collectives and lax.ppermute only.
A program may use at most 384 MiB of HBM per device.

v0:
```python
import jax
import jax.numpy as jnp
from jax import lax
from jax.sharding import PartitionSpec as P

HD = 256
ROT = 64
SEQ_LEN = 1024


def from_behind(value, axis, steps):
    count = lax.axis_size(axis)
    initial, last = (max(0, -steps), min(count, count - steps))
    return lax.ppermute(value, axis, [(source, source + steps) for source in range(initial, last)])


def rotary_tables(length):
    positions = jnp.arange(length).astype(jnp.float32)
    inverse = 10000.0 ** (-jnp.arange(0, ROT, 2).astype(jnp.float32) / ROT)
    angles = positions[:, None] * inverse[None, :]
    angles = jnp.concatenate([angles, angles], axis=-1)
    return (jnp.cos(angles)[:, None, :], jnp.sin(angles)[:, None, :])


def rotate(values, cosines, sines):
    half_rot = ROT // 2
    turned = values[..., :ROT]
    first_half = turned[..., :half_rot]
    second_half = turned[..., half_rot:]
    swapped = jnp.concatenate([-second_half, first_half], axis=-1)
    return jnp.concatenate([turned * cosines + swapped * sines, values[..., ROT:]], axis=-1)


def rotate_back(grads, cosines, sines):

    def turn_values(values):
        return rotate(values, cosines, sines)

    unused, turn_pull = jax.vjp(turn_values, grads)
    return turn_pull(grads)[0]


def gelu_exact(values):
    return jax.nn.gelu(values, approximate=False)


def norm_rows(row_values):
    centred = row_values - jnp.mean(row_values, axis=-1, keepdims=True)
    inverse_std = lax.rsqrt(jnp.mean(centred * centred, axis=-1, keepdims=True) + 1e-05)
    return (centred * inverse_std, inverse_std)


def contract_rows(first_operand, second_operand):
    return lax.dot_general(
        first_operand, second_operand, (((0,), (0,)), ((), ())), preferred_element_type=jnp.float32
    )


def contract_cols(first_operand, second_operand):
    return lax.dot_general(
        first_operand, second_operand, (((1,), (1,)), ((), ())), preferred_element_type=jnp.float32
    )


def causal_block(row_start, block_rows, row_stop):
    query_pos = row_start + lax.broadcasted_iota(jnp.int32, (block_rows, row_stop), 0)
    key_pos = lax.broadcasted_iota(jnp.int32, (block_rows, row_stop), 1)
    return query_pos >= key_pos


def attention_forward(queries, keys_all, values_all):
    length = queries.shape[0]
    block_rows = min(512, length)
    score_scale = HD ** (-0.5)
    outputs_list = []
    sums_list = []
    for block_index in range(length // block_rows):
        row_start = block_index * block_rows
        row_stop = row_start + block_rows
        scores = (
            jnp.einsum(
                "qhd,khd->hqk",
                queries[row_start:row_stop],
                keys_all[:row_stop],
                preferred_element_type=jnp.float32,
            )
            * score_scale
        )
        scores = jnp.where(causal_block(row_start, block_rows, row_stop)[None], scores, -1e30)
        row_peak = jnp.max(scores, axis=-1, keepdims=True)
        exponents = jnp.exp(scores - row_peak)
        row_total = jnp.sum(exponents, axis=-1, keepdims=True)
        attention_probs = (exponents / row_total).astype(jnp.bfloat16)
        outputs_list.append(
            jnp.einsum(
                "hqk,khd->qhd",
                attention_probs,
                values_all[:row_stop],
                preferred_element_type=jnp.float32,
            )
        )
        sums_list.append((row_peak + jnp.log(row_total))[..., 0])
    attended = jnp.concatenate(outputs_list, axis=0).astype(jnp.bfloat16).reshape(length, -1)
    return (attended, jnp.concatenate(sums_list, axis=1))


def attention_backward(queries, keys_all, values_all, log_sums, grad_attended):
    length, heads_here = (queries.shape[0], queries.shape[1])
    block_rows = min(512, length)
    score_scale = HD ** (-0.5)
    grad_out = grad_attended.reshape(length, heads_here, HD)
    grad_queries_list = []
    grad_keys = jnp.zeros(queries.shape, jnp.float32)
    grad_values = jnp.zeros(queries.shape, jnp.float32)
    for block_index in range(length // block_rows):
        row_start = block_index * block_rows
        row_stop = row_start + block_rows
        scores = (
            jnp.einsum(
                "qhd,khd->hqk",
                queries[row_start:row_stop],
                keys_all[:row_stop],
                preferred_element_type=jnp.float32,
            )
            * score_scale
        )
        scores = jnp.where(causal_block(row_start, block_rows, row_stop)[None], scores, -1e30)
        attention_probs = jnp.exp(scores - log_sums[:, row_start:row_stop, None])
        low_probs = attention_probs.astype(jnp.bfloat16)
        grad_probs = jnp.einsum(
            "qhd,khd->hqk",
            grad_out[row_start:row_stop],
            values_all[:row_stop],
            preferred_element_type=jnp.float32,
        )
        centre_term = jnp.sum(attention_probs * grad_probs, axis=-1, keepdims=True)
        grad_scores = (attention_probs * (grad_probs - centre_term)).astype(jnp.bfloat16)
        grad_queries_list.append(
            jnp.einsum(
                "hqk,khd->qhd", grad_scores, keys_all[:row_stop], preferred_element_type=jnp.float32
            )
            * score_scale
        )
        grad_keys = grad_keys.at[:row_stop].add(
            jnp.einsum(
                "hqk,qhd->khd",
                grad_scores,
                queries[row_start:row_stop],
                preferred_element_type=jnp.float32,
            )
            * score_scale
        )
        grad_values = grad_values.at[:row_stop].add(
            jnp.einsum(
                "hqk,qhd->khd",
                low_probs,
                grad_out[row_start:row_stop],
                preferred_element_type=jnp.float32,
            )
        )
    return (jnp.concatenate(grad_queries_list, axis=0), grad_keys, grad_values)


def forward_turn(my_rows, weights, vectors, cosines, sines):
    qkv_w, qkv_b, out_w, fc_in_w, fc_in_b, fc_out_w = weights
    gain_one, bias_one, gain_two, bias_two, out_b, fc_out_b = vectors
    gathered = lax.all_gather(my_rows, "col", axis=0, tiled=True)
    scaled, inverse_std = norm_rows(gathered.astype(jnp.float32))
    normed_one = (scaled * gain_one + bias_one).astype(jnp.bfloat16)
    normed_two = (scaled * gain_two + bias_two).astype(jnp.bfloat16)
    length = gathered.shape[0]
    heads_here = qkv_w.shape[1]
    projected = jnp.dot(
        normed_one, qkv_w.reshape(qkv_w.shape[0], -1), preferred_element_type=jnp.float32
    ) + qkv_b.reshape(-1).astype(jnp.float32)
    projected = projected.reshape(length, heads_here, 3, HD)
    queries = rotate(projected[:, :, 0], cosines, sines).astype(jnp.bfloat16)
    keys_all = rotate(projected[:, :, 1], cosines, sines).astype(jnp.bfloat16)
    values_all = projected[:, :, 2].astype(jnp.bfloat16)
    attended, log_sums = attention_forward(queries, keys_all, values_all)
    inner_act = jnp.dot(normed_two, fc_in_w, preferred_element_type=jnp.float32) + fc_in_b.astype(
        jnp.float32
    )
    activated = gelu_exact(inner_act).astype(jnp.bfloat16)
    summed = lax.psum_scatter(
        jnp.dot(attended, out_w, preferred_element_type=jnp.float32)
        + jnp.dot(activated, fc_out_w, preferred_element_type=jnp.float32),
        "col",
        scatter_dimension=0,
        tiled=True,
    )
    output = (my_rows.astype(jnp.float32) + summed + out_b + fc_out_b).astype(jnp.bfloat16)
    kept_values = (
        gathered,
        normed_one,
        normed_two,
        queries,
        keys_all,
        values_all,
        attended,
        log_sums,
        inner_act,
    )
    return (output, kept_values)


def backward_turn(grad_rows, kept_values, weights, vectors, cosines, sines):
    (
        gathered,
        normed_one,
        normed_two,
        queries,
        keys_all,
        values_all,
        attended,
        log_sums,
        inner_act,
    ) = kept_values
    qkv_w, qkv_b, out_w, fc_in_w, fc_in_b, fc_out_w = weights
    gain_one, bias_one, gain_two, bias_two, out_b, fc_out_b = vectors
    grad_full = lax.all_gather(grad_rows, "col", axis=0, tiled=True)
    length = grad_full.shape[0]
    rows_here = grad_rows.shape[0]
    own_start = lax.axis_index("col") * rows_here
    activated = gelu_exact(inner_act).astype(jnp.bfloat16)
    out_w_grad = contract_rows(attended, grad_full)
    fc_out_w_grad = contract_rows(activated, grad_full)
    grad_attended = contract_cols(grad_full, out_w).astype(jnp.bfloat16)
    grad_activated = contract_cols(grad_full, fc_out_w)
    unused, gelu_pull = jax.vjp(gelu_exact, inner_act)
    grad_inner = gelu_pull(grad_activated)[0].astype(jnp.bfloat16)
    grad_queries, grad_keys, grad_values = attention_backward(
        queries, keys_all, values_all, log_sums, grad_attended
    )
    grad_q_pre = rotate_back(grad_queries, cosines, sines)
    grad_k_pre = rotate_back(grad_keys, cosines, sines)
    grad_projected = (
        jnp.stack([grad_q_pre, grad_k_pre, grad_values], axis=2)
        .astype(jnp.bfloat16)
        .reshape(length, -1)
    )
    qkv_flat = qkv_w.reshape(qkv_w.shape[0], -1)
    qkv_w_grad = contract_rows(normed_one, grad_projected).reshape(qkv_w.shape)
    qkv_b_grad = jnp.sum(grad_projected.astype(jnp.float32), axis=0).reshape(qkv_b.shape)
    fc_in_w_grad = contract_rows(normed_two, grad_inner)
    fc_in_b_grad = jnp.sum(grad_inner.astype(jnp.float32), axis=0)
    width = qkv_w.shape[0]
    scaled_full, inverse_full = norm_rows(gathered.astype(jnp.float32))
    scaled = lax.dynamic_slice_in_dim(scaled_full, own_start, rows_here, 0)
    inverse_std = lax.dynamic_slice_in_dim(inverse_full, own_start, rows_here, 0)
    dy_sum = jnp.sum(grad_rows.astype(jnp.float32), axis=0)
    both_grads = lax.psum_scatter(
        jnp.concatenate(
            [contract_cols(grad_projected, qkv_flat), contract_cols(grad_inner, fc_in_w)], axis=1
        ),
        "col",
        scatter_dimension=0,
        tiled=True,
    )
    grad_one = both_grads[:, :width]
    grad_two = both_grads[:, width:]
    combined = gain_one * grad_one + gain_two * grad_two
    vector_grads = (
        jnp.sum(grad_one * scaled, axis=0),
        jnp.sum(grad_one, axis=0),
        jnp.sum(grad_two * scaled, axis=0),
        jnp.sum(grad_two, axis=0),
        dy_sum,
    )
    grad_norm = inverse_std * (
        combined
        - jnp.mean(combined, axis=-1, keepdims=True)
        - scaled * jnp.mean(combined * scaled, axis=-1, keepdims=True)
    )
    grad_input = (grad_rows.astype(jnp.float32) + grad_norm).astype(jnp.bfloat16)
    matrix_grads = (qkv_w_grad, qkv_b_grad, out_w_grad, fc_in_w_grad, fc_in_b_grad, fc_out_w_grad)
    return (grad_input, matrix_grads, vector_grads)


def add_tuples(running, addend):
    if running is None:
        return addend
    return tuple((first_part + second_part for first_part, second_part in zip(running, addend)))


def local(
    inputs,
    cotangent,
    qkv_weight,
    qkv_bias,
    out_weight,
    fc_in_weight,
    fc_in_bias,
    fc_out_weight,
    norm1_gain,
    norm1_bias,
    norm2_gain,
    norm2_bias,
    out_bias,
    fc_out_bias,
):
    sections = lax.axis_size("section")
    section_index = lax.axis_index("section")
    micro_count = inputs.shape[0]
    tick_count = micro_count + sections - 1
    is_first = section_index == 0
    is_last = section_index == sections - 1
    cosines, sines = rotary_tables(SEQ_LEN)
    vectors = (
        lax.all_gather(norm1_gain[0], ("row", "col"), axis=0, tiled=True),
        lax.all_gather(norm1_bias[0], ("row", "col"), axis=0, tiled=True),
        lax.all_gather(norm2_gain[0], ("row", "col"), axis=0, tiled=True),
        lax.all_gather(norm2_bias[0], ("row", "col"), axis=0, tiled=True),
        lax.all_gather(out_bias[0], ("row", "col"), axis=0, tiled=True),
        lax.all_gather(fc_out_bias[0], ("row", "col"), axis=0, tiled=True),
    )
    vectors = tuple((member.astype(jnp.float32) for member in vectors))
    received = jnp.zeros_like(inputs[0])
    outputs_list = []
    kept_list = []
    for tick_index in range(tick_count):
        weights = (
            lax.all_gather(qkv_weight[0], "row", axis=0, tiled=True),
            lax.all_gather(qkv_bias[0], "row", axis=1, tiled=True),
            lax.all_gather(out_weight[0], "row", axis=1, tiled=True),
            lax.all_gather(fc_in_weight[0], "row", axis=0, tiled=True),
            lax.all_gather(fc_in_bias[0], "row", axis=0, tiled=True),
            lax.all_gather(fc_out_weight[0], "row", axis=1, tiled=True),
        )
        first_rows = inputs[min(tick_index, micro_count - 1)]
        my_rows = jnp.where(is_first, first_rows, received)
        output, kept_values = forward_turn(my_rows, weights, vectors, cosines, sines)
        outputs_list.append(output)
        kept_list.append(kept_values)
        if tick_index + 1 < tick_count:
            received = from_behind(output, "section", 1)
    layer_outputs = lax.dynamic_slice_in_dim(jnp.stack(outputs_list), section_index, micro_count, 0)
    stacked_kept = tuple((jnp.stack(members) for members in zip(*kept_list)))
    received_grad = jnp.zeros_like(inputs[0])
    grads_list = []
    matrix_total = None
    vector_total = None
    for tick_index in range(tick_count):
        weights = (
            lax.all_gather(qkv_weight[0], "row", axis=0, tiled=True),
            lax.all_gather(qkv_bias[0], "row", axis=1, tiled=True),
            lax.all_gather(out_weight[0], "row", axis=1, tiled=True),
            lax.all_gather(fc_in_weight[0], "row", axis=0, tiled=True),
            lax.all_gather(fc_in_bias[0], "row", axis=0, tiled=True),
            lax.all_gather(fc_out_weight[0], "row", axis=1, tiled=True),
        )
        if tick_index < micro_count:
            seed_grad = cotangent[tick_index]
        else:
            seed_grad = jnp.zeros_like(cotangent[0])
        grad_rows = jnp.where(is_last, seed_grad, received_grad)
        forward_index = jnp.clip(tick_index - sections + 1 + 2 * section_index, 0, tick_count - 1)
        kept_values = tuple(
            (
                lax.dynamic_index_in_dim(member, forward_index, 0, keepdims=False)
                for member in stacked_kept
            )
        )
        grad_input, matrix_grads, vector_grads = backward_turn(
            grad_rows, kept_values, weights, vectors, cosines, sines
        )
        grads_list.append(grad_input)
        if tick_index + 1 < tick_count:
            received_grad = from_behind(grad_input, "section", -1)
        matrix_part = (
            lax.psum_scatter(matrix_grads[0], "row", scatter_dimension=0, tiled=True),
            lax.psum_scatter(matrix_grads[1], "row", scatter_dimension=1, tiled=True),
            lax.psum_scatter(matrix_grads[2], "row", scatter_dimension=1, tiled=True),
            lax.psum_scatter(matrix_grads[3], "row", scatter_dimension=0, tiled=True),
            lax.psum_scatter(matrix_grads[4], "row", scatter_dimension=0, tiled=True),
            lax.psum_scatter(matrix_grads[5], "row", scatter_dimension=1, tiled=True),
        )
        vector_part = (
            lax.psum_scatter(vector_grads[0], ("row", "col"), scatter_dimension=0, tiled=True),
            lax.psum_scatter(vector_grads[1], ("row", "col"), scatter_dimension=0, tiled=True),
            lax.psum_scatter(vector_grads[2], ("row", "col"), scatter_dimension=0, tiled=True),
            lax.psum_scatter(vector_grads[3], ("row", "col"), scatter_dimension=0, tiled=True),
            lax.psum_scatter(vector_grads[4], ("row", "col"), scatter_dimension=0, tiled=True),
        )
        matrix_total = add_tuples(matrix_total, tuple(matrix_part))
        vector_total = add_tuples(vector_total, tuple(vector_part))
    input_gradients = lax.dynamic_slice_in_dim(
        jnp.stack(grads_list), sections - 1 - section_index, micro_count, 0
    )
    return (
        layer_outputs[None],
        input_gradients[None],
        matrix_total[0][None],
        matrix_total[1][None],
        matrix_total[2][None],
        matrix_total[3][None],
        matrix_total[4][None],
        matrix_total[5][None],
        vector_total[0][None],
        vector_total[1][None],
        vector_total[2][None],
        vector_total[3][None],
        vector_total[4][None],
        vector_total[4][None],
    )


def solution(mesh):
    return jax.shard_map(
        local,
        mesh=mesh,
        in_specs=(
            P(None, ("row", "col"), None),
            P(None, ("row", "col"), None),
            P("section", "row", "col", None),
            P("section", "col", "row"),
            P("section", "col", "row"),
            P("section", "row", "col"),
            P("section", ("col", "row")),
            P("section", "col", "row"),
            P("section", ("row", "col")),
            P("section", ("row", "col")),
            P("section", ("row", "col")),
            P("section", ("row", "col")),
            P("section", ("row", "col")),
            P("section", ("row", "col")),
        ),
        out_specs=(
            P("section", None, ("row", "col"), None),
            P("section", None, ("row", "col"), None),
            P("section", "row", "col", None),
            P("section", "col", "row"),
            P("section", "col", "row"),
            P("section", "row", "col"),
            P("section", ("col", "row")),
            P("section", "col", "row"),
            P("section", ("row", "col")),
            P("section", ("row", "col")),
            P("section", ("row", "col")),
            P("section", ("row", "col")),
            P("section", ("row", "col")),
            P("section", ("row", "col")),
        ),
        check_vma=False,
    )
```

profile of v0, /device:TPU:0, one launch (start us, length us, event | category | flops | bytes accessed | tf_op | source)
XLA Modules:
  0.0 2688.9 jit_solution(9472517517334116590)
XLA Ops:
  29.0 22.1 all-gather.2
  51.2 17.9 all-gather.1
  69.2 19.3 all-gather.7
  88.5 19.9 all-gather.6
  132.7 31.9 %all-gather.35.cloned.1.call-done = bf16[1,2048,2,768]{3,2,0,1:T(2,128)(2,1)} async-done(((bf16[1,512,2,768]{3,2,0,1:T(2,128)(2,1)}), bf16[1,2048,2,768]{3,2,0,1:T(2,128)(2,1)}) %all-gather.35.cloned.1.call-update) | async-done | bytes 6291472 | tf_op jit(solution)/shard_map/all_gather | solution.py:323
  220.2 139.7 %all-gather.39.cloned.1.call-done = bf16[1,2048,2048]{2,1,0:T(8,128)(2,1)} async-done(((bf16[1,512,2048]{2,1,0:T(8,128)(2,1)}), bf16[1,2048,2048]{2,1,0:T(8,128)(2,1)}) %all-gather.39.cloned.1.call-update) | async-done | bytes 8388624 | tf_op jit(solution)/shard_map/all_gather | solution.py:326
  374.9 134.3 %all-gather.41.cloned.1.call-done = bf16[1,2048,2048]{2,1,0:T(8,128)(2,1)} async-done(((bf16[1,2048,512]{2,1,0:T(8,128)(2,1)}), bf16[1,2048,2048]{2,1,0:T(8,128)(2,1)}) %all-gather.41.cloned.1.call-update) | async-done | bytes 8388624 | tf_op jit(solution)/shard_map/all_gather | solution.py:328
  509.2 32.0 %fusion.154 = f32[1024,2048]{1,0:T(8,128)} fusion(f32[1024,2048]{1,0:T(8,128)} %fusion.332, bf16[1,2048,2048]{2,1,0:T(8,128)(2,1)} %all-gather.41.cloned.1.call-done, f32[1024,2048]{1,0:T(8,128)} %fusion.89, f32[2048]{0:T(1024)S(1)} %bitcast.925), kind=kOutput, calls=%fused_computation.236 | convolution fusion | flops 8730443776 | bytes 33562624 | tf_op jit(solution)/shard_map/dot_general | solution.py:187
  541.9 18.7 all-gather.12
  578.3 32.8 %reduce-scatter.14.cloned.1.call-done = f32[256,2048]{1,0:T(8,128)} async-done(((f32[1024,2048]{1,0:T(8,128)}), f32[256,2048]{1,0:T(8,128)}) %reduce-scatter.14.cloned.1.call-update) | async-done | bytes 2097168 | tf_op jit(solution)/shard_map/reduce_scatter | solution.py:185
  617.6 22.2 collective-permute-done
  641.3 35.2 %all-gather.25.cloned.1.call-done = bf16[1024,2048]{1,0:T(8,128)(2,1)} async-done(((bf16[256,2048]{1,0:T(8,128)(2,1)}), bf16[1024,2048]{1,0:T(8,128)(2,1)}) %all-gather.25.cloned.1.call-update) | async-done | bytes 4194320 | tf_op jit(solution)/shard_map/all_gather | solution.py:167
  738.9 31.1 %fusion.157 = f32[1024,2048]{1,0:T(8,128)} fusion(f32[1024,2048]{1,0:T(8,128)S(1)} %fusion.330, bf16[1,2048,2048]{2,1,0:T(8,128)(2,1)} %all-gather.41.cloned.1.call-done, f32[1024,2048]{1,0:T(8,128)S(1)} %fusion.87, f32[2048]{0:T(1024)S(1)} %bitcast.926), kind=kOutput, calls=%fused_computation.237 | convolution fusion | flops 8730443776 | bytes 33562624 | tf_op jit(solution)/shard_map/dot_general | solution.py:187
  773.5 68.1 %reduce-scatter.16.cloned.1.call-done = f32[256,2048]{1,0:T(8,128)} async-done(((f32[1024,2048]{1,0:T(8,128)}), f32[256,2048]{1,0:T(8,128)}) %reduce-scatter.16.cloned.1.call-update) | async-done | bytes 2097168 | tf_op jit(solution)/shard_map/reduce_scatter | solution.py:185
  848.0 22.2 collective-permute-done.1
  996.3 18.5 add_bitcast_fusion.2
  1024.8 35.7 %fusion.41 = (f32[1024,2048]{1,0:T(8,128)}, f32[1024,2048]{1,0:T(8,128)}) fusion(f32[3,1024,2048]{2,1,0:T(8,128)S(1)} %pad_maximum_fusion, s32[]{:T(128)S(6)} %min.11, s32[]{:T(128)S(6)} %min.10), kind=kLoop, calls=%fused_computation.69 | loop fusion | flops 260046848 | bytes 33554440 | tf_op jit(solution)/shard_map/jvp()/erfc | solution.py:44
  1087.0 20.6 convert_reduce_fusion.8
  1151.8 99.9 %reduce-scatter.20.cloned.1.call-done = f32[256,4096]{1,0:T(8,128)} async-done(((f32[1024,4096]{1,0:T(8,128)}), f32[256,4096]{1,0:T(8,128)}) %reduce-scatter.20.cloned.1.call-update) | async-done | bytes 4194320 | tf_op jit(solution)/shard_map/reduce_scatter | solution.py:252
  1261.2 25.3 collective-permute-done.2
  1292.8 29.4 %all-gather.29.cloned.1.call-done = bf16[1024,2048]{1,0:T(8,128)(2,1)} async-done(((bf16[256,2048]{1,0:T(8,128)(2,1)}), bf16[1024,2048]{1,0:T(8,128)(2,1)}) %all-gather.29.cloned.1.call-update) | async-done | bytes 4194320 | tf_op jit(solution)/shard_map/all_gather | solution.py:221
  1360.6 20.9 convert_reduce_fusion.7
  1405.5 120.1 %reduce-scatter.22.cloned.1.call-done = f32[256,4096]{1,0:T(8,128)} async-done(((f32[1024,4096]{1,0:T(8,128)}), f32[256,4096]{1,0:T(8,128)}) %reduce-scatter.22.cloned.1.call-update) | async-done | bytes 4194320 | tf_op jit(solution)/shard_map/reduce_scatter | solution.py:252
  1561.8 32.1 %fusion.160 = f32[1024,2048]{1,0:T(8,128)} fusion(f32[1024,2048]{1,0:T(8,128)} %fusion.328, bf16[1,2048,2048]{2,1,0:T(8,128)(2,1)} %all-gather.41.cloned.1.call-done, f32[1024,2048]{1,0:T(8,128)} %fusion.85, f32[2048]{0:T(1024)S(1)} %bitcast.928), kind=kOutput, calls=%fused_computation.238 | convolution fusion | flops 8730443776 | bytes 33562624 | tf_op jit(solution)/shard_map/dot_general | solution.py:187
  1667.8 18.2 add_add_fusion.2
  1686.1 32.1 %convert_reduce_fusion.6 = (f32[2048]{0:T(1024)}, bf16[1024,2048]{1,0:T(8,128)(2,1)S(1)}) fusion(bf16[1024,2048]{1,0:T(8,128)(2,1)} %all-gather.31.cloned.1.call-done, bf16[1,2048,2048]{2,1,0:T(8,128)(2,1)} %all-gather.41.cloned.1.call-done, f32[3,1024,2048]{2,1,0:T(8,128)} %copy-done, s32[]{:T(128)S(6)} %min.12), kind=kOutput, calls=%fused_computation.137 | convolution fusion | flops 8745121792 | bytes 25174020 | tf_op jit(solution)/shard_map/dot_general | solution.py:60
  1789.8 23.4 add_add_fusion.1
  1847.7 33.7 %add_add_fusion = f32[2048,2048]{1,0:T(8,128)} fusion(f32[2048,2048]{1,0:T(8,128)} %fusion.166, f32[2048,2048]{1,0:T(8,128)} %fusion.168, bf16[1024,2048]{1,0:T(8,128)(2,1)S(1)} %copy-done.208, f32[3,1024,2048]{2,1,0:T(8,128)} %copy-done, s32[]{:T(128)S(6)} %min.12), kind=kOutput, calls=%fused_computation.4 | convolution fusion | flops 8734638080 | bytes 62914564 | tf_op jit(solution)/shard_map/dot_general | solution.py:54
  1910.8 122.4 %reduce-scatter.24.cloned.1.call-done = f32[256,4096]{1,0:T(8,128)} async-done(((f32[1024,4096]{1,0:T(8,128)}), f32[256,4096]{1,0:T(8,128)}) %reduce-scatter.24.cloned.1.call-update) | async-done | bytes 4194320 | tf_op jit(solution)/shard_map/reduce_scatter | solution.py:252
  2037.5 63.9 %all-reduce.36 = (f32[2048]{0:T(1024)S(1)}, f32[2048]{0:T(1024)S(1)}, f32[2048]{0:T(1024)S(1)}, f32[2048]{0:T(1024)S(1)}, f32[2048]{0:T(1024)S(1)}) all-reduce(f32[2048]{0:T(1024)S(1)} %add_add_fusion.8, f32[2048]{0:T(1024)S(1)} %add_add_fusion.7, ...), channel_id=50, replica_groups=mesh['section'=2,'row'=4,'col'=4] {'row','col'}, use_global_device_ids=true, to_apply=%region_67.68.clone | all-reduce | flops 10240 | bytes 81920
  2113.5 283.7 %reduce-scatter.30.cloned.1.call-done = f32[512,2048]{1,0:T(8,128)} async-done(((f32[2048,2048]{1,0:T(8,128)}), f32[512,2048]{1,0:T(8,128)}) %reduce-scatter.30.cloned.1.call-update) | async-done | bytes 4194320 | tf_op jit(solution)/shard_map/reduce_scatter | solution.py:374
  2397.2 284.0 %reduce-scatter.32.cloned.1.call-done = f32[2048,512]{1,0:T(8,128)} async-done(((f32[2048,2048]{1,0:T(8,128)}), f32[2048,512]{1,0:T(8,128)}) %reduce-scatter.32.cloned.1.call-update) | async-done | bytes 4194320 | tf_op jit(solution)/shard_map/reduce_scatter | solution.py:376
  (785 shorter events, 758.1 us)
Async XLA Ops:
  7.2 120.6 %all-gather.33.cloned.1.call-start = ((), (), s32[]{:S(2)}) async-start(), calls=%async_computation.21 | async-start | bytes 5242880 | tf_op jit(solution)/shard_map/all_gather | solution.py:167
  9.6 155.0 %all-gather.35.cloned.1.call-start = ((), (), s32[]{:S(2)}) async-start(), calls=%async_computation.22 | async-start | bytes 7864320 | tf_op jit(solution)/shard_map/all_gather | solution.py:323
  10.3 201.7 %all-gather.37.cloned.1.call-start = ((), (), s32[]{:S(2)}) async-start(), calls=%async_computation.23 | async-start | bytes 2621440 | tf_op jit(solution)/shard_map/all_gather | solution.py:325
  11.1 348.9 %all-gather.39.cloned.1.call-start = ((), (), s32[]{:S(2)}) async-start(), calls=%async_computation.24 | async-start | bytes 10485760 | tf_op jit(solution)/shard_map/all_gather | solution.py:326
  11.7 497.5 %all-gather.41.cloned.1.call-start = ((), (), s32[]{:S(2)}) async-start(), calls=%async_computation.25 | async-start | bytes 10485760 | tf_op jit(solution)/shard_map/all_gather | solution.py:328
  12.2 598.8 %reduce-scatter.14.cloned.1.call-start = ((), (), s32[]{:S(2)}) async-start(), calls=%async_computation.11 | async-start | bytes 10485760 | tf_op jit(solution)/shard_map/reduce_scatter | solution.py:185
  88.4 271.5 %copy-start.157 = (f32[1,2048]{1,0:T(1,128)}, f32[1,2048]{1,0:T(1,128)S(1)}, u32[]{:S(2)}) copy-start(f32[1,2048]{1,0:T(1,128)S(1)} %convert_element_type.510) | copy-start | bytes 24580
  108.4 251.6 %copy-start.118 = (f32[1,2048]{1,0:T(1,128)}, f32[1,2048]{1,0:T(1,128)S(1)}, u32[]{:S(2)}) copy-start(f32[1,2048]{1,0:T(1,128)S(1)} %convert_element_type.509) | copy-start | bytes 24580
  124.3 871.9 %copy-start.161 = (f32[1,2048]{1,0:T(1,128)}, f32[1,2048]{1,0:T(1,128)S(1)}, u32[]{:S(2)}) copy-start(f32[1,2048]{1,0:T(1,128)S(1)} %convert_element_type.511) | copy-start | bytes 24580
  131.4 228.5 %copy-start.134 = (f32[1024]{0:T(1024)}, f32[1024]{0:T(1024)S(1)}, u32[]{:S(2)}) copy-start(f32[1024]{0:T(1024)S(1)} %broadcast_multiply_fusion.9) | copy-start | bytes 12292
  132.7 227.3 %copy-start.183 = (f32[1024]{0:T(1024)}, f32[1024]{0:T(1024)S(1)}, u32[]{:S(2)}) copy-start(f32[1024]{0:T(1024)S(1)} %add_rsqrt_fusion.5) | copy-start | bytes 12292
  541.3 135.2 %all-gather.25.cloned.1.call-start = ((), (), s32[]{:S(2)}) async-start(), calls=%async_computation.12 | async-start | bytes 5242880 | tf_op jit(solution)/shard_map/all_gather | solution.py:167
  614.0 25.7 collective-permute-start
  640.9 200.7 %reduce-scatter.16.cloned.1.call-start = ((), (), s32[]{:S(2)}) async-start(), calls=%async_computation.13 | async-start | bytes 10485760 | tf_op jit(solution)/shard_map/reduce_scatter | solution.py:185
  770.0 107.6 %all-gather.43.cloned.1.call-start = ((), (), s32[]{:S(2)}) async-start(), calls=%async_computation.26 | async-start | bytes 5242880 | tf_op jit(solution)/shard_map/all_gather | solution.py:221
  773.5 140.1 %all-gather.27.cloned.1.call-start = ((), (), s32[]{:S(2)}) async-start(), calls=%async_computation.14 | async-start | bytes 5242880 | tf_op jit(solution)/shard_map/all_gather | solution.py:167
  844.5 25.6 collective-permute-start.1
  871.3 380.4 %reduce-scatter.20.cloned.1.call-start = ((), (), s32[]{:S(2)}) async-start(), calls=%async_computation.16 | async-start | bytes 20971520 | tf_op jit(solution)/shard_map/reduce_scatter | solution.py:252
  1126.5 195.8 %all-gather.29.cloned.1.call-start = ((), (), s32[]{:S(2)}) async-start(), calls=%async_computation.17 | async-start | bytes 5242880 | tf_op jit(solution)/shard_map/all_gather | solution.py:221
  1259.8 26.8 collective-permute-start.2
  1288.5 237.1 %reduce-scatter.22.cloned.1.call-start = ((), (), s32[]{:S(2)}) async-start(), calls=%async_computation.18 | async-start | bytes 20971520 | tf_op jit(solution)/shard_map/reduce_scatter | solution.py:252
  1400.4 242.3 %all-gather.31.cloned.1.call-start = ((), (), s32[]{:S(2)}) async-start(), calls=%async_computation.19 | async-start | bytes 5242880 | tf_op jit(solution)/shard_map/all_gather | solution.py:221
  1532.8 26.6 collective-permute-start.3
  1561.3 323.4 %reduce-scatter.18.cloned.1.call-start = ((), (), s32[]{:S(2)}) async-start(), calls=%async_computation.15 | async-start | bytes 10485760 | tf_op jit(solution)/shard_map/reduce_scatter | solution.py:185
  1594.0 308.6 %reduce-scatter.34.cloned.1.call-start = ((), (), s32[]{:S(2)}) async-start(), calls=%async_computation.31 | async-start | bytes 491520
  1667.8 236.9 %reduce-scatter.26.cloned.1.call-start = ((), (), s32[]{:S(2)}) async-start(), calls=%async_computation.27 | async-start | bytes 15728640 | tf_op jit(solution)/shard_map/reduce_scatter | solution.py:371
  1686.1 347.1 %reduce-scatter.24.cloned.1.call-start = ((), (), s32[]{:S(2)}) async-start(), calls=%async_computation.20 | async-start | bytes 20971520 | tf_op jit(solution)/shard_map/reduce_scatter | solution.py:252
  1746.3 367.1 %reduce-scatter.28.cloned.1.call-start = ((), (), s32[]{:S(2)}) async-start(), calls=%async_computation.28 | async-start | bytes 5242880 | tf_op jit(solution)/shard_map/reduce_scatter | solution.py:373
  1758.7 638.5 %reduce-scatter.30.cloned.1.call-start = ((), (), s32[]{:S(2)}) async-start(), calls=%async_computation.29 | async-start | bytes 20971520 | tf_op jit(solution)/shard_map/reduce_scatter | solution.py:374
  1813.2 868.1 %reduce-scatter.32.cloned.1.call-start = ((), (), s32[]{:S(2)}) async-start(), calls=%async_computation.30 | async-start | bytes 20971520 | tf_op jit(solution)/shard_map/reduce_scatter | solution.py:376
  1904.7 199.2 %copy-start.49 = (bf16[256,2048]{1,0:T(8,128)(2,1)S(1)}, bf16[256,2048]{1,0:T(8,128)(2,1)}, u32[]{:S(2)}) copy-start(bf16[256,2048]{1,0:T(8,128)(2,1)} %get-tuple-element.319) | copy-start | bytes 3145732
  2101.5 580.2 %copy-start.213 = (f32[1,128]{1,0:T(1,128)}, f32[1,128]{1,0:T(1,128)S(1)}, u32[]{:S(2)}) copy-start(f32[1,128]{1,0:T(1,128)S(1)} %dynamic-slice_bitcast_fusion.33) | copy-start | bytes 1540
  (222 other events, 4978.6 us)
Sparse Core Ops, SparseCore 0:
  10.2 37.2 all-gather.32
  49.0 115.4 all-gather.34
  166.1 43.9 all-gather.36
  211.5 148.4 all-gather.38
  361.4 147.7 all-gather.40
  541.4 69.6 reduce-scatter.13
  641.0 35.4 all-gather.24
  770.2 71.3 reduce-scatter.15
  843.2 34.4 all-gather.42
  879.1 34.4 all-gather.26
  1126.6 125.0 reduce-scatter.19
  1288.7 33.5 all-gather.28
  1400.5 125.0 reduce-scatter.21
  1561.4 33.5 all-gather.30
  1597.4 71.4 reduce-scatter.17
  1671.0 20.7 reduce-scatter.33
  1694.0 210.6 reduce-scatter.25
  1907.1 126.0 reduce-scatter.23
  2036.1 77.3 reduce-scatter.27
  2116.2 280.9 reduce-scatter.29
  2400.1 281.0 reduce-scatter.31
where the time goes:
time: 2700 us; the launch traced here: 2690 us
  waiting for transfers between devices  1500 us (56%)
  matrix products  560 us (21%)
  other arithmetic  240 us (9%)
  blocking collectives  224 us (8%)
  local copies, waits for them, and re-layouts  134 us (5%)
    reduce_scatter x3, waiting for transfers between devices, backward_turn(): lax.psum_scatter(jnp.concatenate([contract_cols(grad_projected, qkv_flat)...  342 us
    reduce_scatter x1, waiting for transfers between devices, local(): lax.psum_scatter(matrix_grads[5], 'row', scatter_dimension=1, tiled=True)  284 us
    reduce_scatter x1, waiting for transfers between devices, local(): lax.psum_scatter(matrix_grads[3], 'row', scatter_dimension=0, tiled=True)  284 us
    dot_general x12, matrix products, contract_rows(): lax.dot_general(first_operand, second_operand, (((0,), (0,)), ((), ())),...  167 us
    dot_general x12, matrix products, contract_cols(): lax.dot_general(first_operand, second_operand, (((1,), (1,)), ((), ())),...  161 us
    all_gather x1, waiting for transfers between devices, local(): lax.all_gather(fc_in_weight[0], 'row', axis=0, tiled=True)  140 us
    all_gather x1, waiting for transfers between devices, local(): lax.all_gather(fc_out_weight[0], 'row', axis=1, tiled=True)  134 us
    reduce_scatter x3, waiting for transfers between devices, forward_turn(): lax.psum_scatter(jnp.dot(attended, out_w, preferred_element_type=jnp.floa...  101 us
  transfers between devices with their start and end apart: 25, of which 20 were waited for; matrix products, arithmetic and copies ran while one was open for 18% of the time, Pallas kernels for 0%

commit v1 on v0

--- a/solution.py
+++ b/solution.py
@@ -1,6 +1,8 @@
 import jax
 import jax.numpy as jnp
 from jax import lax
+from jax.experimental import pallas as pl
+from jax.experimental.pallas import tpu as pltpu
 from jax.sharding import PartitionSpec as P
 
 HD = 256
@@ -283,7 +285,7 @@
     return tuple((first_part + second_part for first_part, second_part in zip(running, addend)))
 
 
-def local(
+def relay_local(
     inputs,
     cotangent,
     qkv_weight,
@@ -405,9 +407,478 @@
     )
 
 
+F32 = jnp.float32
+BF16 = jnp.bfloat16
+LANES = 128
+
+
+def swap(value, axis, bit):
+    count = lax.axis_size(axis)
+    return lax.ppermute(value, axis, [(source, source ^ bit) for source in range(count)])
+
+
+def sum_over(value, axis):
+    bit = 1
+    while bit < lax.axis_size(axis):
+        value = value + swap(value, axis, bit)
+        bit *= 2
+    return value
+
+
+def place(part, axis, index, length):
+    shape = list(part.shape)
+    shape[axis] = length
+    start = index * part.shape[axis]
+    return lax.dynamic_update_slice_in_dim(jnp.zeros(shape, part.dtype), part, start, axis)
+
+
+def take(value, axis, index, size):
+    return lax.dynamic_slice_in_dim(value, index * size, size, axis)
+
+
+def gather_rows(block):
+    half = block.shape[0] // 2
+    beside = swap(block, "col", 2)
+    across = swap(block, "section", 1)
+    corner = jnp.concatenate(
+        [swap(beside[:half], "section", 1), swap(across[half:], "col", 2)], axis=0
+    )
+    near = jnp.concatenate([block, beside], axis=0)
+    far = jnp.concatenate([across, corner], axis=0)
+    return jnp.concatenate([near, swap(near, "col", 1), far, swap(far, "col", 1)], axis=0), across
+
+
+def scatter_rows(partial):
+    rows, width = partial.shape
+    block = rows // 8
+    half = block // 2
+    parts = partial.reshape(2, 2, 2 * block, width)
+    sums = []
+    for micro in range(2):
+        arrived = swap(parts[micro, 1], "col", 1)
+        sums.append((parts[micro, 0].astype(F32) + arrived.astype(F32)).astype(BF16))
+    near, far = sums
+    first = swap(
+        jnp.concatenate([far[:half], far[block : block + half]], axis=0), "section", 1
+    ).astype(F32)
+    second = swap(
+        jnp.concatenate([near[block + half :], far[block + half :]], axis=0), "col", 2
+    ).astype(F32)
+    top_keep = near[:half].astype(F32) + first[:half]
+    top_send = (near[block : block + half].astype(F32) + first[half:]).astype(BF16)
+    low_keep = near[half:block].astype(F32) + second[:half]
+    low_send = (far[half:block].astype(F32) + second[half:]).astype(BF16)
+    top = top_keep + swap(top_send, "col", 2).astype(F32)
+    low = low_keep + swap(low_send, "section", 1).astype(F32)
+    return jnp.concatenate([top, low], axis=0)
+
+
+def turn(values, cosines, sines):
+    lead = values[:, :LANES]
+    lane = lax.broadcasted_iota(jnp.int32, lead.shape, 1)
+    ahead = pltpu.roll(lead, LANES - ROT // 2, 1)
+    behind = pltpu.roll(lead, ROT // 2, 1)
+    lead = lead * cosines + jnp.where(lane < ROT // 2, ahead, behind) * sines
+    return jnp.concatenate([lead, values[:, LANES:]], axis=1)
+
+
+def mm(first_operand, second_operand):
+    return jnp.dot(first_operand, second_operand, preferred_element_type=F32)
+
+
+def project_kernel(x_ref, w_ref, e_ref, cos_ref, sin_ref, q_ref, k_ref, v_ref):
+    projected = mm(x_ref[...], w_ref[...]) + e_ref[...]
+    cosines, sines = cos_ref[...], sin_ref[...]
+    q_ref[...] = (turn(projected[:, :HD], cosines, sines) * HD ** (-0.5)).astype(BF16)
+    k_ref[...] = turn(projected[:, HD : 2 * HD], cosines, sines).astype(BF16)
+    v_ref[...] = projected[:, 2 * HD :].astype(BF16)
+
+
+def inner_kernel(x_ref, w_ref, e_ref, act_ref, slope_ref):
+    inner = mm(x_ref[...], w_ref[...]) + e_ref[...]
+    below = 0.5 + 0.5 * lax.erf(inner * 0.7071067811865476)
+    act_ref[...] = (inner * below).astype(BF16)
+    density = jnp.exp(-0.5 * inner * inner) * 0.3989422804014327
+    slope_ref[...] = (below + inner * density).astype(BF16)
+
+
+def two_kernel(a_ref, b_ref, c_ref, d_ref, out_ref):
+    out_ref[...] = (mm(a_ref[...], b_ref[...]) + mm(c_ref[...], d_ref[...])).astype(BF16)
+
+
+def two_turned_kernel(a_ref, b_ref, c_ref, d_ref, out_ref):
+    out_ref[...] = (
+        contract_cols(a_ref[...], b_ref[...]) + contract_cols(c_ref[...], d_ref[...])
+    ).astype(BF16)
+
+
+def attend_kernel(q_ref, k_ref, v_ref, row_ref, col_ref, out_ref, log_ref):
+    scores = contract_cols(q_ref[...], k_ref[...])
+    scores = jnp.where(row_ref[...] >= col_ref[...], scores, -1e30)
+    peak = jnp.max(scores, axis=1, keepdims=True)
+    exponents = jnp.exp(scores - peak)
+    total = jnp.sum(exponents, axis=1, keepdims=True)
+    out_ref[...] = mm((exponents / total).astype(BF16), v_ref[...]).astype(BF16)
+    log_ref[...] = peak + jnp.log(total)
+
+
+def attend_back_kernel(
+    q_ref, k_ref, v_ref, row_ref, col_ref, log_ref, do_ref, cos_ref, sin_ref, out_ref, dk_ref, dv_ref
+):
+    step = pl.program_id(1)
+    block = q_ref.shape[0]
+
+    @pl.when(step == 0)
+    def _():
+        dk_ref[...] = jnp.zeros_like(dk_ref)
+        dv_ref[...] = jnp.zeros_like(dv_ref)
+
+    queries, keys_all, grads = (q_ref[...], k_ref[...], do_ref[...])
+    scores = contract_cols(queries, keys_all)
+    scores = jnp.where(row_ref[...] >= col_ref[...], scores, -1e30)
+    probs = jnp.exp(scores - log_ref[...])
+    grad_probs = contract_cols(grads, v_ref[...])
+    centre = jnp.sum(probs * grad_probs, axis=1, keepdims=True)
+    grad_scores = (probs * (grad_probs - centre)).astype(BF16)
+    rows = pl.ds(pl.multiple_of(step * block, block), block)
+    cosines, sines = cos_ref[rows, :], sin_ref[rows, :]
+    grad_queries = mm(grad_scores, keys_all) * HD ** (-0.5)
+    out_ref[rows, :HD] = turn(grad_queries, cosines, -sines).astype(BF16)
+    dk_ref[...] += contract_rows(grad_scores, queries)
+    dv_ref[...] += contract_rows(probs.astype(BF16), grads)
+
+    @pl.when(step == pl.num_programs(1) - 1)
+    def _():
+        out_ref[:, HD : 2 * HD] = turn(dk_ref[...], cos_ref[...], -sin_ref[...]).astype(BF16)
+        out_ref[:, 2 * HD :] = dv_ref[...].astype(BF16)
+
+
+ROW_BLOCK = 256
+
+
+def by_rows(width, block=ROW_BLOCK):
+    return pl.BlockSpec((block, width), lambda i: (i, 0))
+
+
+def whole(shape):
+    return pl.BlockSpec(shape, lambda *unused: (0,) * len(shape))
+
+
+def cost(flops, *arrays):
+    return pl.CostEstimate(
+        flops=flops,
+        transcendentals=0,
+        bytes_accessed=sum(array.size * array.dtype.itemsize for array in arrays),
+    )
+
+
+def project(x, w, e, tables):
+    rows, width = x.shape
+    per_micro = tables[0].shape[0] // ROW_BLOCK
+    table = pl.BlockSpec((ROW_BLOCK, LANES), lambda i: (i % per_micro, 0))
+    out = jax.ShapeDtypeStruct((rows, HD), BF16)
+    return pl.pallas_call(
+        project_kernel,
+        grid=(rows // ROW_BLOCK,),
+        in_specs=[by_rows(width), whole(w.shape), whole(e.shape), table, table],
+        out_specs=[by_rows(HD)] * 3,
+        out_shape=[out] * 3,
+        cost_estimate=cost(2 * rows * w.size, x, w, out, out, out),
+        name="project",
+    )(x, w, e, *tables)
+
+
+def inner_layer(x, w, e):
+    rows, width = x.shape
+    out = jax.ShapeDtypeStruct((rows, w.shape[1]), BF16)
+    return pl.pallas_call(
+        inner_kernel,
+        grid=(rows // ROW_BLOCK,),
+        in_specs=[by_rows(width), whole(w.shape), whole(e.shape)],
+        out_specs=[by_rows(w.shape[1])] * 2,
+        out_shape=[out] * 2,
+        cost_estimate=cost(2 * rows * w.size, x, w, out, out),
+        name="inner",
+    )(x, w, e)
+
+
+def two_products(kernel, a, b, c, d, width, name):
+    rows = a.shape[0]
+    out = jax.ShapeDtypeStruct((rows, width), BF16)
+    return pl.pallas_call(
+        kernel,
+        grid=(rows // ROW_BLOCK,),
+        in_specs=[by_rows(a.shape[1]), whole(b.shape), by_rows(c.shape[1]), whole(d.shape)],
+        out_specs=by_rows(width),
+        out_shape=out,
+        cost_estimate=cost(2 * rows * (b.size + d.size), a, b, c, d, out),
+        name=name,
+    )(a, b, c, d)
+
+
+def attend(queries, keys_all, values_all, places):
+    rows = queries.shape[0]
+    length = places.shape[0]
+    steps = length // ROW_BLOCK
+    row = pl.BlockSpec((ROW_BLOCK, HD), lambda m, i: (m * steps + i, 0))
+    every = pl.BlockSpec((length, HD), lambda m, i: (m, 0))
+    out = jax.ShapeDtypeStruct((rows, HD), BF16)
+    return pl.pallas_call(
+        attend_kernel,
+        grid=(rows // length, steps),
+        in_specs=[
+            row,
+            every,
+            every,
+            pl.BlockSpec((ROW_BLOCK, 1), lambda m, i: (i, 0)),
+            pl.BlockSpec((1, length), lambda m, i: (0, 0)),
+        ],
+        out_specs=[row, pl.BlockSpec((ROW_BLOCK, 1), lambda m, i: (m * steps + i, 0))],
+        out_shape=[out, jax.ShapeDtypeStruct((rows, 1), F32)],
+        cost_estimate=cost(4 * rows * length * HD, queries, keys_all, values_all, out),
+        name="attend",
+    )(queries, keys_all, values_all, places[:, None], places[None, :])
+
+
+def attend_back(queries, keys_all, values_all, places, log_sums, grads, tables):
+    rows = queries.shape[0]
+    length = places.shape[0]
+    steps = length // ROW_BLOCK
+    row = pl.BlockSpec((ROW_BLOCK, HD), lambda m, i: (m * steps + i, 0))
+    every = pl.BlockSpec((length, HD), lambda m, i: (m, 0))
+    out = jax.ShapeDtypeStruct((rows, 3 * HD), BF16)
+    return pl.pallas_call(
+        attend_back_kernel,
+        grid=(rows // length, steps),
+        in_specs=[
+            row,
+            every,
+            every,
+            pl.BlockSpec((ROW_BLOCK, 1), lambda m, i: (i, 0)),
+            pl.BlockSpec((1, length), lambda m, i: (0, 0)),
+            pl.BlockSpec((ROW_BLOCK, 1), lambda m, i: (m * steps + i, 0)),
+            row,
+            whole(tables[0].shape),
+            whole(tables[1].shape),
+        ],
+        out_specs=pl.BlockSpec((length, 3 * HD), lambda m, i: (m, 0)),
+        out_shape=out,
+        scratch_shapes=[pltpu.VMEM((length, HD), F32), pltpu.VMEM((length, HD), F32)],
+        cost_estimate=cost(10 * rows * length * HD, queries, keys_all, values_all, grads, out),
+        name="attend_back",
+    )(queries, keys_all, values_all, places[:, None], places[None, :], log_sums, grads, *tables)
+
+
+def local(
+    inputs,
+    cotangent,
+    qkv_weight,
+    qkv_bias,
+    out_weight,
+    fc_in_weight,
+    fc_in_bias,
+    fc_out_weight,
+    norm1_gain,
+    norm1_bias,
+    norm2_gain,
+    norm2_bias,
+    out_bias,
+    fc_out_bias,
+):
+    s, r, c = (lax.axis_index("section"), lax.axis_index("row"), lax.axis_index("col"))
+    rows_axis, cols_axis = (lax.axis_size("row"), lax.axis_size("col"))
+    low = s == 0
+    qkv_w, out_w, fc_in_w, fc_out_w = (
+        qkv_weight[0], out_weight[0], fc_in_weight[0], fc_out_weight[0],
+    )
+    deep, heads_here = qkv_w.shape[0], qkv_w.shape[1]
+    per = heads_here // 2 * 3 * HD
+    inner_here = fc_in_w.shape[1]
+    model = inputs.shape[2]
+
+    def both_layers(own_first, own_second):
+        return (jnp.where(low, own_first, own_second), jnp.where(low, own_second, own_first))
+
+    def trade(value, axis):
+        size = value.shape[axis] // 2
+        kept = take(value, axis, s, size)
+        return both_layers(kept, swap(take(value, axis, 1 - s, size), "section", 1))
+
+    def gathered(shard, axis):
+        return lax.all_gather(shard, "row", axis=axis, tiled=True)
+
+    held = jnp.stack(
+        [
+            norm1_gain[0].astype(F32),
+            norm1_bias[0].astype(F32),
+            norm2_gain[0].astype(F32),
+            norm2_bias[0].astype(F32),
+            out_bias[0].astype(F32) + fc_out_bias[0].astype(F32),
+        ]
+    )
+    held = sum_over(place(held, 1, c, deep), "col")
+    gain_one, shift_one, gain_two, shift_two, end_bias = (held[i] for i in range(5))
+
+    out_pair = trade(out_w, 0)
+    fc_out_pair = trade(fc_out_w, 0)
+    qkv_flat = qkv_w.reshape(deep, -1)
+    qkv_pair = trade((qkv_flat.astype(F32) * gain_one[:, None]).astype(BF16), 1)
+    fc_in_pair = trade((fc_in_w.astype(F32) * gain_two[:, None]).astype(BF16), 1)
+
+    own_qkv = mm(shift_one.astype(BF16)[None], qkv_flat)[0]
+    own_fc = mm(shift_two.astype(BF16)[None], fc_in_w)[0]
+    own_qkv = own_qkv + place(qkv_bias[0].astype(F32), 1, r, 3 * HD).reshape(-1)
+    own_fc = own_fc + place(fc_in_bias[0].astype(F32), 0, r, inner_here)
+    biases = sum_over(
+        jnp.concatenate([own_qkv, own_fc, place(end_bias, 0, r, model)]), "row"
+    )
+    biases = both_layers(biases, swap(biases, "section", 1))
+    qkv_e, fc_e, end_e = ([], [], [])
+    for member in biases:
+        qkv_e.append(take(member[: 2 * per], 0, s, per)[None])
+        fc_e.append(take(member[2 * per : 2 * per + inner_here], 0, s, inner_here // 2)[None])
+        end_e.append(member[2 * per + inner_here :])
+
+    block_rows = inputs.shape[1]
+    masks = jnp.array([0, 2, 1, 3], jnp.int32)
+    places = ((c ^ masks)[:, None] * block_rows + jnp.arange(block_rows)[None]).reshape(-1)
+    half_rot = ROT // 2
+    inverse = 10000.0 ** (-jnp.arange(0, ROT, 2).astype(F32) / ROT)
+    angles = places.astype(F32)[:, None] * inverse[None]
+    ones = jnp.ones((places.shape[0], LANES - ROT), F32)
+    cosines, sines = (jnp.cos(angles), jnp.sin(angles))
+    tables = (
+        jnp.concatenate([cosines, cosines, ones], axis=1),
+        jnp.concatenate([-sines, sines, 0.0 * ones], axis=1),
+    )
+
+    hidden = lax.dynamic_index_in_dim(inputs, s, 0, keepdims=False)
+    seed = lax.dynamic_index_in_dim(cotangent, s, 0, keepdims=False)
+
+    hidden_list, kept_list, ends = ([], [], [])
+    for layer in range(2):
+        hidden_list.append(hidden)
+        scaled, unused = norm_rows(hidden.astype(F32))
+        x, unused = gather_rows(scaled.astype(BF16))
+        w_out = gathered(out_pair[layer], 1)
+        w_fc_out = gathered(fc_out_pair[layer], 1)
+        w_qkv = gathered(qkv_pair[layer], 0)
+        w_fc_in = gathered(fc_in_pair[layer], 0)
+        queries, keys_all, values_all = project(x, w_qkv, qkv_e[layer], tables)
+        attended, log_sums = attend(queries, keys_all, values_all, places)
+        activated, slopes = inner_layer(x, w_fc_in, fc_e[layer])
+        partial = two_products(
+            two_kernel, attended, w_out, activated, w_fc_out, model, "outer"
+        )
+        summed = scatter_rows(partial)
+        hidden = (hidden.astype(F32) + summed + end_e[layer]).astype(BF16)
+        ends.append(hidden)
+        kept_list.append(
+            (x, queries, keys_all, values_all, attended, log_sums, activated, slopes,
+             w_qkv, w_out, w_fc_in, w_fc_out)
+        )
+
+    def reduced(value, axis):
+        return lax.psum_scatter(value, "row", scatter_dimension=axis, tiled=True)
+
+    grads = seed
+    grads_out, matrix_list, small_list = ([None, None], [None, None], [None, None])
+    for layer in (1, 0):
+        (x, queries, keys_all, values_all, attended, log_sums, activated, slopes,
+         w_qkv, w_out, w_fc_in, w_fc_out) = kept_list[layer]
+        dy, across = gather_rows(grads)
+        if layer == 0:
+            grads_out[1] = jnp.where(low, grads, across), jnp.where(low, across, grads)
+        dy_sum = jnp.sum(grads.astype(F32), axis=0)
+        out_part = reduced(contract_rows(attended, dy).astype(BF16), 1)
+        fc_out_part = reduced(contract_rows(activated, dy).astype(BF16), 1)
+        grad_attended = contract_cols(dy, w_out).astype(BF16)
+        grad_inner = (contract_cols(dy, w_fc_out) * slopes.astype(F32)).astype(BF16)
+        grad_projected = attend_back(
+            queries, keys_all, values_all, places, log_sums, grad_attended, tables
+        )
+        fc_in_part = reduced(contract_rows(x, grad_inner).astype(BF16), 0)
+        qkv_part = reduced(contract_rows(x, grad_projected).astype(BF16), 0)
+        partial = two_products(
+            two_turned_kernel, grad_projected, w_qkv, grad_inner, w_fc_in, model, "inward"
+        )
+        combined = scatter_rows(partial)
+        scaled, inverse_std = norm_rows(hidden_list[layer].astype(F32))
+        grad_norm = inverse_std * (
+            combined
+            - jnp.mean(combined, axis=-1, keepdims=True)
+            - scaled * jnp.mean(combined * scaled, axis=-1, keepdims=True)
+        )
+        grads = (grads.astype(F32) + grad_norm).astype(BF16)
+        small = jnp.concatenate(
+            [
+                jnp.sum(grad_projected.astype(F32), axis=0),
+                jnp.sum(grad_inner.astype(F32), axis=0),
+                sum_over(sum_over(dy_sum, "section"), "col"),
+            ]
+        )
+        matrix_list[layer] = (qkv_part, out_part, fc_in_part, fc_out_part)
+        small_list[layer] = sum_over(small, "row")
+
+    def to_owner(first, second):
+        upper = lax.ppermute(first, "section", [(1, 0)])
+        lower = lax.ppermute(second, "section", [(0, 1)])
+        return (jnp.where(low, first, lower), jnp.where(low, upper, second))
+
+    smalls = to_owner(*small_list)
+    qkv_b_grad = jnp.concatenate([member[:per] for member in smalls])
+    fc_in_b_grad = jnp.concatenate([member[per : per + inner_here // 2] for member in smalls])
+    end_grad = jnp.where(low, small_list[0], small_list[1])[per + inner_here // 2 :]
+    qkv_g, out_g, fc_in_g, fc_out_g = (
+        to_owner(*members) for members in zip(*matrix_list)
+    )
+    qkv_g = jnp.concatenate(qkv_g, axis=1).astype(F32)
+    fc_in_g = jnp.concatenate(fc_in_g, axis=1).astype(F32)
+    qkv_w_grad = gain_one[:, None] * qkv_g + shift_one[:, None] * qkv_b_grad[None]
+    fc_in_w_grad = gain_two[:, None] * fc_in_g + shift_two[:, None] * fc_in_b_grad[None]
+    qkv_full, fc_full = (qkv_flat.astype(F32), fc_in_w.astype(F32))
+    norms = jnp.stack(
+        [
+            jnp.sum(qkv_full * qkv_g, axis=1),
+            jnp.sum(qkv_full * qkv_b_grad[None], axis=1),
+            jnp.sum(fc_full * fc_in_g, axis=1),
+            jnp.sum(fc_full * fc_in_b_grad[None], axis=1),
+        ]
+    )
+    norms = take(sum_over(norms, "col"), 1, c, deep // cols_axis)
+    end_grad = take(end_grad, 0, r * cols_axis + c, deep // cols_axis)
+    last = lax.ppermute(ends[1], "section", [(0, 1)])
+    middle = swap(ends[0], "section", 1)
+    layer_outputs = jnp.stack([jnp.where(low, ends[0], last), jnp.where(low, middle, ends[1])])
+    first = lax.ppermute(grads, "section", [(1, 0)])
+    input_gradients = jnp.stack(
+        [jnp.where(low, grads, grads_out[1][0]), jnp.where(low, first, grads_out[1][1])]
+    )
+    return (
+        layer_outputs[None],
+        input_gradients[None],
+        qkv_w_grad.reshape(qkv_w.shape)[None],
+        take(qkv_b_grad.reshape(heads_here, -1), 1, r, 3 * HD // rows_axis)[None],
+        jnp.concatenate(out_g, axis=0).astype(F32)[None],
+        fc_in_w_grad[None],
+        take(fc_in_b_grad, 0, r, inner_here // rows_axis)[None],
+        jnp.concatenate(fc_out_g, axis=0).astype(F32)[None],
+        norms[0][None],
+        norms[1][None],
+        norms[2][None],
+        norms[3][None],
+        end_grad[None],
+        end_grad[None],
+    )
+
+
 def solution(mesh):
+    sizes = mesh.shape
+    paired = sizes["section"] == 2 and sizes["col"] == 4
+    rows_even = sizes["row"] & (sizes["row"] - 1) == 0
+    body = local if paired and rows_even else relay_local
     return jax.shard_map(
-        local,
+        body,
         mesh=mesh,
         in_specs=(
             P(None, ("row", "col"), None),

time: 2700 us -> 1170 us (0.43)
  waiting for transfers between devices: 1500 us -> 530 us
  matrix products: 560 us -> 124 us
  blocking collectives: 224 us -> 0 us
  Pallas kernels: 0 us -> 184 us
  other arithmetic: 240 us -> 114 us
  starting transfers between devices: 12 us -> 93.6 us
  local copies, waits for them, and re-layouts: 134 us -> 92.7 us
    reduce_scatter x10 -> x8, waiting for transfers between devices: 1020 us -> 39.4 us  [reduced(): return lax.psum_scatter(value, 'row', scatter_dimension=axis, tiled=True)]
    ppermute x4 -> x82, waiting for transfers between devices: 86 us -> 371 us  [the longest x70 311 us: swap(): lax.ppermute(value, axis, [(source, source ^ bit) for source in range(cou...]
    all_gather x10 -> x8, waiting for transfers between devices: 394 us -> 119 us  [gathered(): return lax.all_gather(shard, 'row', axis=axis, tiled=True)]
    dot_general x54 -> x2, matrix products: 232 us -> 2.29 us  [mm(): return jnp.dot(first_operand, second_operand, preferred_element_type=F32)]
    pallas_call x0 -> x12, Pallas kernels: none -> 184 us  [the longest x4 75.1 us: two_products(): pl.pallas_call(kernel, grid=(rows // ROW_BLOCK,), in_specs=[by_rows(a.sha...]
    all_gather x8 -> x0, blocking collectives: 148 us -> none  [the longest x1 22.1 us: local(): lax.all_gather(norm1_bias[0], ('row', 'col'), axis=0, tiled=True)]
    dot_general x12 -> x4, matrix products: 161 us -> 41.7 us  [contract_cols(): lax.dot_general(first_operand, second_operand, (((1,), (1,)), ((), ())),...]
    another operation x26 -> x5, other arithmetic: 113 us -> 6.42 us  [the longest x2 3.52 us: local(): jnp.stack([jnp.where(low, grads, grads_out[1][0]), jnp.where(low, first,...]
  transfers between devices with their start and end apart: 25 -> 98, of which waited for: 20 -> 46; matrix products, arithmetic and copies ran while one was open for 18% -> 25% of each run, Pallas kernels for 0% -> 14%
where the time goes in v1:
time: 1170 us; the launch traced here: 1160 us
  waiting for transfers between devices  530 us (45%)
  Pallas kernels  184 us (16%)
  matrix products  124 us (11%)
  other arithmetic  114 us (10%)
  starting transfers between devices  93.6 us (8%)
  local copies, waits for them, and re-layouts  92.7 us (8%)
  between operations  16 us (1%)
    ppermute x70, waiting for transfers between devices, swap(): lax.ppermute(value, axis, [(source, source ^ bit) for source in range(cou...  311 us
    all_gather x8, waiting for transfers between devices, gathered(): return lax.all_gather(shard, 'row', axis=axis, tiled=True)  119 us
    dot_general x8, matrix products, contract_rows(): lax.dot_general(first_operand, second_operand, (((0,), (0,)), ((), ())),...  80.4 us
    pallas_call x4, Pallas kernels, two_products(): pl.pallas_call(kernel, grid=(rows // ROW_BLOCK,), in_specs=[by_rows(a.sha...  75.1 us
    ppermute x5, waiting for transfers between devices, to_owner(): upper = lax.ppermute(first, 'section', [(1, 0)])  60.1 us
    ppermute x70, starting transfers between devices, swap(): lax.ppermute(value, axis, [(source, source ^ bit) for source in range(cou...  51.6 us
    unnamed x187, local copies, waits for them, and re-layouts  50.1 us
    dot_general x4, matrix products, contract_cols(): lax.dot_general(first_operand, second_operand, (((1,), (1,)), ((), ())),...  41.7 us
  transfers between devices with their start and end apart: 98, of which 46 were waited for; matrix products, arithmetic and copies ran while one was open for 25% of the time, Pallas kernels for 14%

profile of v1, /device:TPU:0, one launch (start us, length us, event | category | flops | bytes accessed | tf_op | source)
XLA Modules:
  0.0 1155.3 jit_solution(1782771891793966703)
XLA Ops:
  18.7 17.5 %collective-permute-done.8 = bf16[512,768]{1,0:T(8,128)(2,1)} collective-permute-done((bf16[512,768]{1,0:T(8,128)(2,1)S(1)}, bf16[512,768]{1,0:T(8,128)(2,1)}, u32[]{:S(2)}, u32[]{:S(2)}) %collective-permute-start.8) | collective-permute-done | bytes 786464 | tf_op jit(solution)/shard_map/ppermute | solution.py:417
  42.6 22.6 %collective-permute-done.13 = bf16[512,1024]{1,0:T(8,128)(2,1)S(1)} collective-permute-done((bf16[512,1024]{1,0:T(8,128)(2,1)S(1)}, bf16[512,1024]{1,0:T(8,128)(2,1)S(1)}, u32[]{:S(2)}, u32[]{:S(2)}) %collective-permute-start.13) | collective-permute-done | bytes 1048608 | tf_op jit(solution)/shard_map/ppermute | solution.py:417
  77.1 21.6 %collective-permute-done.14 = bf16[1024,512]{1,0:T(8,128)(2,1)S(1)} collective-permute-done((bf16[1024,512]{1,0:T(8,128)(2,1)S(1)}, bf16[1024,512]{1,0:T(8,128)(2,1)S(1)}, u32[]{:S(2)}, u32[]{:S(2)}) %collective-permute-start.14) | collective-permute-done | bytes 1048608 | tf_op jit(solution)/shard_map/ppermute | solution.py:417
  106.0 18.9 %collective-permute-done.2 = bf16[256,2048]{1,0:T(8,128)(2,1)S(1)} collective-permute-done((bf16[256,2048]{1,0:T(8,128)(2,1)}, bf16[256,2048]{1,0:T(8,128)(2,1)S(1)}, u32[]{:S(2)}, u32[]{:S(2)}) %collective-permute-start.2) | collective-permute-done | bytes 1048608 | tf_op jit(solution)/shard_map/ppermute | solution.py:417
  168.9 12.7 %project.2 = (bf16[2048,256]{1,0:T(8,128)(2,1)}, bf16[2048,256]{1,0:T(8,128)(2,1)}, bf16[2048,256]{1,0:T(8,128)(2,1)}) custom-call(bf16[2048,2048]{1,0:T(8,128)(2,1)} %constant_dynamic-update-slice_fusion.x_ref, bf16[2048,768]{1,0:T(8,128)(2,1)} %all-gather.9.cloned.1.call-done.w_ref.b_ref, f32[1,768]{1,0:T(1,128)} %broadcast_in_dim.26.e_ref, ...), custom_call_target="tpu_custom_call" | custom-call | flops 6442450944 | bytes 14680064 | tf_op jit(solution)/shard_map/project/pallas_call | solution.py:580
  192.4 16.9 %inner.2 = (bf16[2048,1024]{1,0:T(8,128)(2,1)}, bf16[2048,1024]{1,0:T(8,128)(2,1)}) custom-call(bf16[2048,2048]{1,0:T(8,128)(2,1)} %constant_dynamic-update-slice_fusion.x_ref, bf16[2048,1024]{1,0:T(8,128)(2,1)} %all-gather.13.cloned.1.call-done.w_ref.d_ref, f32[1,1024]{1,0:T(1,128)} %bitcast.247), custom_call_target="tpu_custom_call" | custom-call | flops 8589934592 | bytes 20971520 | tf_op jit(solution)/shard_map/inner/pallas_call | solution.py:594
  214.1 81.7 %all-gather.15.cloned.1.call-done.d_ref = bf16[1024,2048]{1,0:T(8,128)(2,1)} async-done(((bf16[1024,512]{1,0:T(8,128)(2,1)}), bf16[1024,2048]{1,0:T(8,128)(2,1)}) %all-gather.15.cloned.1.call-update) | async-done | bytes 4194320 | tf_op jit(solution)/shard_map/all_gather | solution.py:708
  295.8 16.0 %outer.2 = bf16[2048,2048]{1,0:T(8,128)(2,1)} custom-call(bf16[2048,256]{1,0:T(8,128)(2,1)} %get-tuple-element.31.a_ref, bf16[256,2048]{1,0:T(8,128)(2,1)} %all-gather.11.cloned.1.call-done.b_ref, bf16[2048,1024]{1,0:T(8,128)(2,1)} %get-tuple-element.32.c_ref, bf16[1024,2048]{1,0:T(8,128)(2,1)} %all-gather.15.cloned.1.call-done.d_ref), custom_call_target="tpu_custom_call" | custom-call | flops 10737418240 | bytes 18874368 | tf_op jit(solution)/shard_map/outer/pallas_call | solution.py:608
  335.7 20.7 %collective-permute-done.19 = bf16[256,2048]{1,0:T(8,128)(2,1)S(1)} collective-permute-done((bf16[256,2048]{1,0:T(8,128)(2,1)S(1)}, bf16[256,2048]{1,0:T(8,128)(2,1)S(1)}, u32[]{:S(2)}, u32[]{:S(2)}) %collective-permute-start.19) | collective-permute-done | bytes 1048608 | tf_op jit(solution)/shard_map/ppermute | solution.py:417
  360.2 20.3 %collective-permute-done.37 = bf16[256,2048]{1,0:T(8,128)(2,1)S(1)} collective-permute-done((bf16[256,2048]{1,0:T(8,128)(2,1)S(1)}, bf16[256,2048]{1,0:T(8,128)(2,1)S(1)}, u32[]{:S(2)}, u32[]{:S(2)}) %collective-permute-start.37) | collective-permute-done | bytes 1048608 | tf_op jit(solution)/shard_map/ppermute | solution.py:417
  462.1 12.7 %project.3 = (bf16[2048,256]{1,0:T(8,128)(2,1)}, bf16[2048,256]{1,0:T(8,128)(2,1)}, bf16[2048,256]{1,0:T(8,128)(2,1)}) custom-call(bf16[2048,2048]{1,0:T(8,128)(2,1)} %constant_dynamic-update-slice_fusion.7.x_ref, bf16[2048,768]{1,0:T(8,128)(2,1)} %all-gather.17.cloned.1.call-done.w_ref.b_ref, f32[1,768]{1,0:T(1,128)} %broadcast_in_dim.29.e_ref, ...), custom_call_target="tpu_custom_call" | custom-call | flops 6442450944 | bytes 14680064 | tf_op jit(solution)/shard_map/project/pallas_call | solution.py:580
  485.8 14.2 %attend_back.2.a_ref = bf16[2048,768]{1,0:T(8,128)(2,1)} custom-call(bf16[2048,256]{1,0:T(8,128)(2,1)} %get-tuple-element.33.q_ref, bf16[2048,256]{1,0:T(8,128)(2,1)} %get-tuple-element.34.k_ref, bf16[2048,256]{1,0:T(8,128)(2,1)} %get-tuple-element.35.v_ref, s32[1024,1]{1,0:T(8,128)} %bitcast.219, s32[1,1024]{1,0:T(1,128)} %bitcast.239, ...), custom_call_target="tpu_custom_call" | custom-call | flops 5368709120 | bytes 7340032 | tf_op jit(solution)/shard_map/attend_back/pallas_call | solution.py:650
  499.9 16.8 %inner.3 = (bf16[2048,1024]{1,0:T(8,128)(2,1)}, bf16[2048,1024]{1,0:T(8,128)(2,1)}) custom-call(bf16[2048,2048]{1,0:T(8,128)(2,1)} %constant_dynamic-update-slice_fusion.7.x_ref, bf16[2048,1024]{1,0:T(8,128)(2,1)} %all-gather.21.cloned.1.call-done.w_ref.d_ref, f32[1,1024]{1,0:T(1,128)} %bitcast.246), custom_call_target="tpu_custom_call" | custom-call | flops 8589934592 | bytes 20971520 | tf_op jit(solution)/shard_map/inner/pallas_call | solution.py:594
  516.8 33.0 %all-gather.23.cloned.1.call-done.d_ref = bf16[1024,2048]{1,0:T(8,128)(2,1)} async-done(((bf16[1024,512]{1,0:T(8,128)(2,1)}), bf16[1024,2048]{1,0:T(8,128)(2,1)}) %all-gather.23.cloned.1.call-update) | async-done | bytes 4194320 | tf_op jit(solution)/shard_map/all_gather | solution.py:708
  549.8 16.2 %convert_reduce_fusion = (f32[1024]{0:T(1024)}, bf16[2048,1024]{1,0:T(8,128)(2,1)}) fusion(bf16[2048,1024]{1,0:T(8,128)(2,1)} %get-tuple-element.39, bf16[2048,2048]{1,0:T(8,128)(2,1)} %constant_dynamic-update-slice_fusion.14, bf16[1024,2048]{1,0:T(8,128)(2,1)} %all-gather.23.cloned.1.call-done.d_ref), kind=kOutput, calls=%fused_computation | convolution fusion | flops 8600419328 | bytes 20975616 | tf_op jit(solution)/shard_map/dot_general | solution.py:62
  566.0 21.5 %inward.2 = bf16[2048,2048]{1,0:T(8,128)(2,1)} custom-call(bf16[2048,768]{1,0:T(8,128)(2,1)} %attend_back.2.a_ref, bf16[2048,768]{1,0:T(8,128)(2,1)} %all-gather.17.cloned.1.call-done.w_ref.b_ref, bf16[2048,1024]{1,0:T(8,128)(2,1)} %get-tuple-element.132.c_ref, bf16[2048,1024]{1,0:T(8,128)(2,1)} %all-gather.21.cloned.1.call-done.w_ref.d_ref), custom_call_target="tpu_custom_call" | custom-call | flops 15032385536 | bytes 23068672 | tf_op jit(solution)/shard_map/inward/pallas_call | solution.py:608
  609.5 17.8 %collective-permute-done.45 = bf16[256,2048]{1,0:T(8,128)(2,1)} collective-permute-done((bf16[256,2048]{1,0:T(8,128)(2,1)S(1)}, bf16[256,2048]{1,0:T(8,128)(2,1)}, u32[]{:S(2)}, u32[]{:S(2)}) %collective-permute-start.45) | collective-permute-done | bytes 1048608 | tf_op jit(solution)/shard_map/ppermute | solution.py:417
  657.0 20.7 %collective-permute-done.47 = bf16[256,2048]{1,0:T(8,128)(2,1)S(1)} collective-permute-done((bf16[256,2048]{1,0:T(8,128)(2,1)S(1)}, bf16[256,2048]{1,0:T(8,128)(2,1)S(1)}, u32[]{:S(2)}, u32[]{:S(2)}) %collective-permute-start.47) | collective-permute-done | bytes 1048608 | tf_op jit(solution)/shard_map/ppermute | solution.py:417
  680.4 12.1 %collective-permute-done.51 = bf16[128,2048]{1,0:T(8,128)(2,1)S(1)} collective-permute-done((bf16[128,2048]{1,0:T(8,128)(2,1)S(1)}, bf16[128,2048]{1,0:T(8,128)(2,1)S(1)}, u32[]{:S(2)}, u32[]{:S(2)}) %collective-permute-start.51) | collective-permute-done | bytes 524320 | tf_op jit(solution)/shard_map/ppermute | solution.py:417
  705.4 14.1 %convolution_convert_fusion = bf16[1024,2048]{1,0:T(8,128)(2,1)} fusion(bf16[2048,1024]{1,0:T(8,128)(2,1)} %get-tuple-element.37.c_ref, bf16[2048,2048]{1,0:T(8,128)(2,1)} %constant_dynamic-update-slice_fusion.14), kind=kOutput, calls=%fused_computation.31 | convolution fusion | flops 8592031744 | bytes 16777216 | tf_op jit(solution)/shard_map/dot_general | solution.py:56
  719.8 14.0 %convolution_convert_fusion.2 = bf16[2048,1024]{1,0:T(8,128)(2,1)} fusion(bf16[2048,2048]{1,0:T(8,128)(2,1)} %constant_dynamic-update-slice_fusion.7.x_ref, bf16[2048,1024]{1,0:T(8,128)(2,1)} %get-tuple-element.132.c_ref), kind=kOutput, calls=%fused_computation.33 | convolution fusion | flops 8592031744 | bytes 16777216 | tf_op jit(solution)/shard_map/dot_general | solution.py:56
  733.9 16.1 %outer.3 = bf16[2048,2048]{1,0:T(8,128)(2,1)} custom-call(bf16[2048,256]{1,0:T(8,128)(2,1)} %get-tuple-element.36.a_ref, bf16[256,2048]{1,0:T(8,128)(2,1)} %all-gather.19.cloned.1.call-done.b_ref, bf16[2048,1024]{1,0:T(8,128)(2,1)} %get-tuple-element.37.c_ref, bf16[1024,2048]{1,0:T(8,128)(2,1)} %all-gather.23.cloned.1.call-done.d_ref), custom_call_target="tpu_custom_call" | custom-call | flops 10737418240 | bytes 18874368 | tf_op jit(solution)/shard_map/outer/pallas_call | solution.py:608
  762.3 14.2 %attend_back.3.a_ref = bf16[2048,768]{1,0:T(8,128)(2,1)} custom-call(bf16[2048,256]{1,0:T(8,128)(2,1)} %get-tuple-element.28.q_ref, bf16[2048,256]{1,0:T(8,128)(2,1)} %get-tuple-element.29.k_ref, bf16[2048,256]{1,0:T(8,128)(2,1)} %get-tuple-element.30.v_ref, s32[1024,1]{1,0:T(8,128)} %bitcast.220, s32[1,1024]{1,0:T(1,128)} %bitcast.240, ...), custom_call_target="tpu_custom_call" | custom-call | flops 5368709120 | bytes 7340032 | tf_op jit(solution)/shard_map/attend_back/pallas_call | solution.py:650
  823.9 23.2 %collective-permute-done.67 = f32[2048]{0:T(1024)S(1)} collective-permute-done((f32[2048]{0:T(1024)S(1)}, f32[2048]{0:T(1024)S(1)}, u32[]{:S(2)}, u32[]{:S(2)}) %collective-permute-start.67) | collective-permute-done | bytes 8224 | tf_op jit(solution)/shard_map/ppermute | solution.py:417
  898.6 21.4 %inward.3 = bf16[2048,2048]{1,0:T(8,128)(2,1)} custom-call(bf16[2048,768]{1,0:T(8,128)(2,1)} %attend_back.3.a_ref, bf16[2048,768]{1,0:T(8,128)(2,1)} %all-gather.9.cloned.1.call-done.w_ref.b_ref, bf16[2048,1024]{1,0:T(8,128)(2,1)} %copy-done.75, bf16[2048,1024]{1,0:T(8,128)(2,1)} %all-gather.13.cloned.1.call-done.w_ref.d_ref), custom_call_target="tpu_custom_call" | custom-call | flops 15032385536 | bytes 23068672 | tf_op jit(solution)/shard_map/inward/pallas_call | solution.py:608
  926.6 13.0 %convolution_convert_fusion.1 = bf16[1024,2048]{1,0:T(8,128)(2,1)} fusion(bf16[2048,1024]{1,0:T(8,128)(2,1)S(1)} %copy-done.73, bf16[2048,2048]{1,0:T(8,128)(2,1)} %copy-done.2), kind=kOutput, calls=%fused_computation.32 | convolution fusion | flops 8592031744 | bytes 16777216 | tf_op jit(solution)/shard_map/dot_general | solution.py:56
  959.7 13.5 %collective-permute-done.57 = bf16[256,2048]{1,0:T(8,128)(2,1)} collective-permute-done((bf16[256,2048]{1,0:T(8,128)(2,1)}, bf16[256,2048]{1,0:T(8,128)(2,1)}, u32[]{:S(2)}, u32[]{:S(2)}) %collective-permute-start.57) | collective-permute-done | bytes 1048608 | tf_op jit(solution)/shard_map/ppermute | solution.py:417
  989.4 12.4 %collective-permute-done.58 = bf16[128,2048]{1,0:T(8,128)(2,1)S(1)} collective-permute-done((bf16[128,2048]{1,0:T(8,128)(2,1)S(1)}, bf16[128,2048]{1,0:T(8,128)(2,1)S(1)}, u32[]{:S(2)}, u32[]{:S(2)}) %collective-permute-start.58) | collective-permute-done | bytes 524320 | tf_op jit(solution)/shard_map/ppermute | solution.py:417
  1020.5 18.1 %collective-permute-done.75 = bf16[256,512]{1,0:T(8,128)(2,1)} collective-permute-done((bf16[256,512]{1,0:T(8,128)(2,1)}, bf16[256,512]{1,0:T(8,128)(2,1)}, u32[]{:S(2)}, u32[]{:S(2)}) %collective-permute-start.75) | collective-permute-done | bytes 262176 | tf_op jit(solution)/shard_map/ppermute | solution.py:824
  1045.0 16.0 %collective-permute-done.61 = bf16[512,768]{1,0:T(8,128)(2,1)S(1)} collective-permute-done((bf16[512,768]{1,0:T(8,128)(2,1)}, bf16[512,768]{1,0:T(8,128)(2,1)S(1)}, u32[]{:S(2)}, u32[]{:S(2)}) %collective-permute-start.61) | collective-permute-done | bytes 786464 | tf_op jit(solution)/shard_map/ppermute | solution.py:824
  1077.2 39.4 %reduce-scatter.21.cloned.1.call-done = bf16[1024,512]{1,0:T(8,128)(2,1)} async-done(((bf16[1024,2048]{1,0:T(8,128)(2,1)}), bf16[1024,512]{1,0:T(8,128)(2,1)}) %reduce-scatter.21.cloned.1.call-update) | async-done | bytes 1048592 | tf_op jit(solution)/shard_map/reduce_scatter | solution.py:782
  1125.7 17.5 %collective-permute-done.79 = bf16[1024,512]{1,0:T(8,128)(2,1)S(1)} collective-permute-done((bf16[1024,512]{1,0:T(8,128)(2,1)}, bf16[1024,512]{1,0:T(8,128)(2,1)S(1)}, u32[]{:S(2)}, u32[]{:S(2)}) %collective-permute-start.79) | collective-permute-done | bytes 1048608 | tf_op jit(solution)/shard_map/ppermute | solution.py:824
  (579 shorter events, 492.2 us)
Async XLA Ops:
  7.2 161.7 %all-gather.9.cloned.1.call-start = ((), (), s32[]{:S(2)}) async-start(), calls=%async_computation.8 | async-start | bytes 3932160 | tf_op jit(solution)/shard_map/all_gather | solution.py:708
  39.1 153.4 %all-gather.13.cloned.1.call-start = ((), (), s32[]{:S(2)}) async-start(), calls=%async_computation.10 | async-start | bytes 5242880 | tf_op jit(solution)/shard_map/all_gather | solution.py:708
  68.3 145.8 %all-gather.11.cloned.1.call-start = ((), (), s32[]{:S(2)}) async-start(), calls=%async_computation.9 | async-start | bytes 1310720 | tf_op jit(solution)/shard_map/all_gather | solution.py:708
  75.9 219.9 %all-gather.15.cloned.1.call-start = ((), (), s32[]{:S(2)}) async-start(), calls=%async_computation.11 | async-start | bytes 5242880 | tf_op jit(solution)/shard_map/all_gather | solution.py:708
  100.4 343.1 %all-gather.19.cloned.1.call-start = ((), (), s32[]{:S(2)}) async-start(), calls=%async_computation.13 | async-start | bytes 1310720 | tf_op jit(solution)/shard_map/all_gather | solution.py:708
  134.6 327.4 %all-gather.17.cloned.1.call-start = ((), (), s32[]{:S(2)}) async-start(), calls=%async_computation.12 | async-start | bytes 3932160 | tf_op jit(solution)/shard_map/all_gather | solution.py:708
  155.0 345.0 %all-gather.21.cloned.1.call-start = ((), (), s32[]{:S(2)}) async-start(), calls=%async_computation.14 | async-start | bytes 5242880 | tf_op jit(solution)/shard_map/all_gather | solution.py:708
  317.2 232.6 %all-gather.23.cloned.1.call-start = ((), (), s32[]{:S(2)}) async-start(), calls=%async_computation.15 | async-start | bytes 5242880 | tf_op jit(solution)/shard_map/all_gather | solution.py:708
  334.3 46.2 %collective-permute-start.37 = (bf16[256,2048]{1,0:T(8,128)(2,1)S(1)}, bf16[256,2048]{1,0:T(8,128)(2,1)S(1)}, u32[]{:S(2)}, u32[]{:S(2)}) collective-permute-start(bf16[256,2048]{1,0:T(8,128)(2,1)S(1)} %get-tuple-element.53), channel_id=1, source_target_pairs={{0,16},{16,0},{1,17},{17,1},{2,18},{18,2},{3,19},{19,3},{4,20},{20... | collective-permute-start | bytes 3145736 | tf_op jit(solution)/shard_map/ppermute | solution.py:417
  334.9 46.3 %collective-permute-start.35 = (bf16[256,2048]{1,0:T(8,128)(2,1)S(1)}, bf16[256,2048]{1,0:T(8,128)(2,1)S(1)}, u32[]{:S(2)}, u32[]{:S(2)}) collective-permute-start(bf16[256,2048]{1,0:T(8,128)(2,1)S(1)} %get-tuple-element.53), channel_id=1, source_target_pairs={{0,2},{1,3},{2,0},{3,1},{4,6},{5,7},{6,4},{7,5},{8,10},{9,11},{10,... | collective-permute-start | bytes 3145736 | tf_op jit(solution)/shard_map/ppermute | solution.py:417
  356.7 35.0 %collective-permute-start.20 = (bf16[128,2048]{1,0:T(8,128)(2,1)S(1)}, bf16[128,2048]{1,0:T(8,128)(2,1)S(1)}, u32[]{:S(2)}, u32[]{:S(2)}) collective-permute-start(bf16[128,2048]{1,0:T(8,128)(2,1)S(1)} %fusion.55), channel_id=1, source_target_pairs={{0,16},{16,0},{1,17},{17,1},{2,18},{18,2},{3,19},{19,3},{4,20},{20... | collective-permute-start | bytes 1572872 | tf_op jit(solution)/shard_map/ppermute | solution.py:417
  384.3 35.1 %collective-permute-start.36 = (bf16[512,2048]{1,0:T(8,128)(2,1)}, bf16[512,2048]{1,0:T(8,128)(2,1)}, u32[]{:S(2)}, u32[]{:S(2)}) collective-permute-start(bf16[512,2048]{1,0:T(8,128)(2,1)} %pad_maximum_fusion.4), channel_id=1, source_target_pairs={{0,1},{1,0},{2,3},{3,2},{4,5},{5,4},{6,7},{7,6},{8,9},{9,8},{10,11... | collective-permute-start | bytes 6291464 | tf_op jit(solution)/shard_map/ppermute | solution.py:417
  404.5 35.8 %collective-permute-start.40 = (bf16[512,2048]{1,0:T(8,128)(2,1)}, bf16[512,2048]{1,0:T(8,128)(2,1)}, u32[]{:S(2)}, u32[]{:S(2)}) collective-permute-start(bf16[512,2048]{1,0:T(8,128)(2,1)} %pad_maximum_fusion.5), channel_id=1, source_target_pairs={{0,1},{1,0},{2,3},{3,2},{4,5},{5,4},{6,7},{7,6},{8,9},{9,8},{10,11... | collective-permute-start | bytes 6291464 | tf_op jit(solution)/shard_map/ppermute | solution.py:417
  407.5 469.5 %reduce-scatter.15.cloned.1.call-start = ((), (), s32[]{:S(2)}) async-start(), calls=%async_computation.19 | async-start | bytes 1310720 | tf_op jit(solution)/shard_map/reduce_scatter | solution.py:782
  609.4 342.9 %reduce-scatter.11.cloned.1.call-start = ((), (), s32[]{:S(2)}) async-start(), calls=%async_computation.17 | async-start | bytes 3932160 | tf_op jit(solution)/shard_map/reduce_scatter | solution.py:782
  649.0 359.0 %reduce-scatter.13.cloned.1.call-start = ((), (), s32[]{:S(2)}) async-start(), calls=%async_computation.18 | async-start | bytes 1310720 | tf_op jit(solution)/shard_map/reduce_scatter | solution.py:782
  705.4 304.6 %reduce-scatter.23.cloned.1.call-start = ((), (), s32[]{:S(2)}) async-start(), calls=%async_computation.23 | async-start | bytes 5242880 | tf_op jit(solution)/shard_map/reduce_scatter | solution.py:782
  719.6 297.6 %reduce-scatter.19.cloned.1.call-start = ((), (), s32[]{:S(2)}) async-start(), calls=%async_computation.21 | async-start | bytes 5242880 | tf_op jit(solution)/shard_map/reduce_scatter | solution.py:782
  733.8 306.8 %reduce-scatter.9.cloned.1.call-start = ((), (), s32[]{:S(2)}) async-start(), calls=%async_computation.16 | async-start | bytes 3932160 | tf_op jit(solution)/shard_map/reduce_scatter | solution.py:782
  788.1 278.9 %reduce-scatter.17.cloned.1.call-start = ((), (), s32[]{:S(2)}) async-start(), calls=%async_computation.20 | async-start | bytes 5242880 | tf_op jit(solution)/shard_map/reduce_scatter | solution.py:782
  795.8 56.8 %collective-permute-start.31 = (bf16[256,2048]{1,0:T(8,128)(2,1)S(1)}, bf16[256,2048]{1,0:T(8,128)(2,1)}, u32[]{:S(2)}, u32[]{:S(2)}) collective-permute-start(bf16[256,2048]{1,0:T(8,128)(2,1)S(1)} %pad_maximum_fusion.13), channel_id=1, source_target_pairs={{0,2},{1,3},{2,0},{3,1},{4,6},{5,7},{6,4},{7,5},{8,10},{9,11},{10,... | collective-permute-start | bytes 3145736 | tf_op jit(solution)/shard_map/ppermute | solution.py:417
  821.6 294.9 %reduce-scatter.21.cloned.1.call-start = ((), (), s32[]{:S(2)}) async-start(), calls=%async_computation.22 | async-start | bytes 5242880 | tf_op jit(solution)/shard_map/reduce_scatter | solution.py:782
  821.8 35.6 %collective-permute-start.29 = (bf16[256,2048]{1,0:T(8,128)(2,1)S(1)}, bf16[256,2048]{1,0:T(8,128)(2,1)S(1)}, u32[]{:S(2)}, u32[]{:S(2)}) collective-permute-start(bf16[256,2048]{1,0:T(8,128)(2,1)S(1)} %pad_maximum_fusion.12), channel_id=1, source_target_pairs={{0,16},{16,0},{1,17},{17,1},{2,18},{18,2},{3,19},{19,3},{4,20},{20... | collective-permute-start | bytes 3145736 | tf_op jit(solution)/shard_map/ppermute | solution.py:417
  851.9 42.4 %collective-permute-start.34 = (bf16[256,2048]{1,0:T(8,128)(2,1)S(1)}, bf16[256,2048]{1,0:T(8,128)(2,1)}, u32[]{:S(2)}, u32[]{:S(2)}) collective-permute-start(bf16[256,2048]{1,0:T(8,128)(2,1)S(1)} %get-tuple-element.63), channel_id=1, source_target_pairs={{0,16},{16,0},{1,17},{17,1},{2,18},{18,2},{3,19},{19,3},{4,20},{20... | collective-permute-start | bytes 3145736 | tf_op jit(solution)/shard_map/ppermute | solution.py:417
  856.1 35.3 %collective-permute-start.32 = (bf16[128,2048]{1,0:T(8,128)(2,1)}, bf16[128,2048]{1,0:T(8,128)(2,1)}, u32[]{:S(2)}, u32[]{:S(2)}) collective-permute-start(bf16[128,2048]{1,0:T(8,128)(2,1)} %fusion.51), channel_id=1, source_target_pairs={{0,16},{16,0},{1,17},{17,1},{2,18},{18,2},{3,19},{19,3},{4,20},{20... | collective-permute-start | bytes 1572872 | tf_op jit(solution)/shard_map/ppermute | solution.py:417
  875.7 102.9 %collective-permute-start.72 = (f32[3840]{0:T(1024)S(1)}, f32[3840]{0:T(1024)S(1)}, u32[]{:S(2)}, u32[]{:S(2)}) collective-permute-start(f32[3840]{0:T(1024)S(1)} %add.397), channel_id=1, source_target_pairs={{0,16},{1,17},{2,18},{3,19},{4,20},{5,21},{6,22},{7,23},{8,24},{9,... | collective-permute-start | bytes 46088 | tf_op jit(solution)/shard_map/ppermute | solution.py:825
  887.8 129.4 %collective-permute-start.74 = (bf16[256,512]{1,0:T(8,128)(2,1)}, bf16[256,512]{1,0:T(8,128)(2,1)}, u32[]{:S(2)}, u32[]{:S(2)}) collective-permute-start(bf16[256,512]{1,0:T(8,128)(2,1)} %reduce-scatter.15.cloned.1.call-done), channel_id=1, source_target_pairs={{0,16},{1,17},{2,18},{3,19},{4,20},{5,21},{6,22},{7,23},{8,24},{9,... | collective-permute-start | bytes 786440 | tf_op jit(solution)/shard_map/ppermute | solution.py:825
  955.1 89.7 %collective-permute-start.60 = (bf16[512,768]{1,0:T(8,128)(2,1)}, bf16[512,768]{1,0:T(8,128)(2,1)}, u32[]{:S(2)}, u32[]{:S(2)}) collective-permute-start(bf16[512,768]{1,0:T(8,128)(2,1)} %reduce-scatter.11.cloned.1.call-done), channel_id=1, source_target_pairs={{0,16},{1,17},{2,18},{3,19},{4,20},{5,21},{6,22},{7,23},{8,24},{9,... | collective-permute-start | bytes 2359304 | tf_op jit(solution)/shard_map/ppermute | solution.py:825
  1006.0 35.9 %collective-permute-start.59 = (bf16[256,2048]{1,0:T(8,128)(2,1)}, bf16[256,2048]{1,0:T(8,128)(2,1)}, u32[]{:S(2)}, u32[]{:S(2)}) collective-permute-start(bf16[256,2048]{1,0:T(8,128)(2,1)} %get-tuple-element.57), channel_id=1, source_target_pairs={{16,0},{17,1},{18,2},{19,3},{20,4},{21,5},{22,6},{23,7},{24,8},{25... | collective-permute-start | bytes 3145736 | tf_op jit(solution)/shard_map/ppermute | solution.py:853
  1010.0 107.8 %collective-permute-start.78 = (bf16[1024,512]{1,0:T(8,128)(2,1)}, bf16[1024,512]{1,0:T(8,128)(2,1)}, u32[]{:S(2)}, u32[]{:S(2)}) collective-permute-start(bf16[1024,512]{1,0:T(8,128)(2,1)} %reduce-scatter.23.cloned.1.call-done), channel_id=1, source_target_pairs={{0,16},{1,17},{2,18},{3,19},{4,20},{5,21},{6,22},{7,23},{8,24},{9,... | collective-permute-start | bytes 3145736 | tf_op jit(solution)/shard_map/ppermute | solution.py:825
  1017.2 102.0 %collective-permute-start.76 = (bf16[512,1024]{1,0:T(8,128)(2,1)}, bf16[512,1024]{1,0:T(8,128)(2,1)}, u32[]{:S(2)}, u32[]{:S(2)}) collective-permute-start(bf16[512,1024]{1,0:T(8,128)(2,1)} %reduce-scatter.19.cloned.1.call-done), channel_id=1, source_target_pairs={{0,16},{1,17},{2,18},{3,19},{4,20},{5,21},{6,22},{7,23},{8,24},{9,... | collective-permute-start | bytes 3145736 | tf_op jit(solution)/shard_map/ppermute | solution.py:825
  1067.0 52.3 %collective-permute-start.77 = (bf16[512,1024]{1,0:T(8,128)(2,1)}, bf16[512,1024]{1,0:T(8,128)(2,1)}, u32[]{:S(2)}, u32[]{:S(2)}) collective-permute-start(bf16[512,1024]{1,0:T(8,128)(2,1)} %reduce-scatter.17.cloned.1.call-done), channel_id=1, source_target_pairs={{16,0},{17,1},{18,2},{19,3},{20,4},{21,5},{22,6},{23,7},{24,8},{25... | collective-permute-start | bytes 3145736 | tf_op jit(solution)/shard_map/ppermute | solution.py:824
  (147 other events, 1980.8 us)
Sparse Core Ops, SparseCore 0:
  39.2 64.1 all-gather.8
  105.6 80.3 all-gather.12
  187.6 26.4 all-gather.10
  215.5 80.2 all-gather.14
  297.2 26.4 all-gather.18
  325.1 62.8 all-gather.16
  389.5 79.3 all-gather.20
  470.5 79.2 all-gather.22
  609.5 23.9 reduce-scatter.14
  649.1 57.3 reduce-scatter.10
  708.8 27.1 reduce-scatter.12
  738.2 75.2 reduce-scatter.22
  815.8 78.0 reduce-scatter.18
  896.0 61.1 reduce-scatter.8
  959.4 77.0 reduce-scatter.16
  1039.2 77.2 reduce-scatter.20

commit v2 on v1

v2 whole, which is shorter than its diff:
```python
import math

import jax
import jax.numpy as jnp
from jax import lax
from jax.experimental import pallas as pl
from jax.experimental.pallas import tpu as pltpu
from jax.sharding import PartitionSpec as P


SECTION, ROW, COL = ("section", "row", "col")
HD = 256
ROT = 64
SEQ_LEN = 1024


def from_behind(value, axis, steps):
    count = lax.axis_size(axis)
    initial, last = (max(0, -steps), min(count, count - steps))
    return lax.ppermute(value, axis, [(source, source + steps) for source in range(initial, last)])


def rotary_tables(length):
    positions = jnp.arange(length).astype(jnp.float32)
    inverse = 10000.0 ** (-jnp.arange(0, ROT, 2).astype(jnp.float32) / ROT)
    angles = positions[:, None] * inverse[None, :]
    angles = jnp.concatenate([angles, angles], axis=-1)
    return (jnp.cos(angles)[:, None, :], jnp.sin(angles)[:, None, :])


def rotate(values, cosines, sines):
    half_rot = ROT // 2
    turned = values[..., :ROT]
    first_half = turned[..., :half_rot]
    second_half = turned[..., half_rot:]
    swapped = jnp.concatenate([-second_half, first_half], axis=-1)
    return jnp.concatenate([turned * cosines + swapped * sines, values[..., ROT:]], axis=-1)


def rotate_back(grads, cosines, sines):

    def turn_values(values):
        return rotate(values, cosines, sines)

    _, turn_pull = jax.vjp(turn_values, grads)
    return turn_pull(grads)[0]


def gelu_exact(values):
    return jax.nn.gelu(values, approximate=False)


def norm_rows(row_values):
    centred = row_values - jnp.mean(row_values, axis=-1, keepdims=True)
    inverse_std = lax.rsqrt(jnp.mean(centred * centred, axis=-1, keepdims=True) + 1e-05)
    return (centred * inverse_std, inverse_std)


def contract_rows(first_operand, second_operand):
    return lax.dot_general(
        first_operand, second_operand, (((0,), (0,)), ((), ())), preferred_element_type=jnp.float32
    )


def contract_cols(first_operand, second_operand):
    return lax.dot_general(
        first_operand, second_operand, (((1,), (1,)), ((), ())), preferred_element_type=jnp.float32
    )


def causal_block(row_start, block_rows, row_stop):
    query_pos = row_start + lax.broadcasted_iota(jnp.int32, (block_rows, row_stop), 0)
    key_pos = lax.broadcasted_iota(jnp.int32, (block_rows, row_stop), 1)
    return query_pos >= key_pos


def attention_forward(queries, keys_all, values_all):
    length = queries.shape[0]
    block_rows = min(512, length)
    score_scale = HD ** (-0.5)
    outputs_list = []
    sums_list = []
    for block_index in range(length // block_rows):
        row_start = block_index * block_rows
        row_stop = row_start + block_rows
        scores = (
            jnp.einsum(
                "qhd,khd->hqk",
                queries[row_start:row_stop],
                keys_all[:row_stop],
                preferred_element_type=jnp.float32,
            )
            * score_scale
        )
        scores = jnp.where(causal_block(row_start, block_rows, row_stop)[None], scores, -1e30)
        row_peak = jnp.max(scores, axis=-1, keepdims=True)
        exponents = jnp.exp(scores - row_peak)
        row_total = jnp.sum(exponents, axis=-1, keepdims=True)
        attention_probs = (exponents / row_total).astype(jnp.bfloat16)
        outputs_list.append(
            jnp.einsum(
                "hqk,khd->qhd",
                attention_probs,
                values_all[:row_stop],
                preferred_element_type=jnp.float32,
            )
        )
        sums_list.append((row_peak + jnp.log(row_total))[..., 0])
    attended = jnp.concatenate(outputs_list, axis=0).astype(jnp.bfloat16).reshape(length, -1)
    return (attended, jnp.concatenate(sums_list, axis=1))


def attention_backward(queries, keys_all, values_all, log_sums, grad_attended):
    length, heads_here = (queries.shape[0], queries.shape[1])
    block_rows = min(512, length)
    score_scale = HD ** (-0.5)
    grad_out = grad_attended.reshape(length, heads_here, HD)
    grad_queries_list = []
    grad_keys = jnp.zeros(queries.shape, jnp.float32)
    grad_values = jnp.zeros(queries.shape, jnp.float32)
    for block_index in range(length // block_rows):
        row_start = block_index * block_rows
        row_stop = row_start + block_rows
        scores = (
            jnp.einsum(
                "qhd,khd->hqk",
                queries[row_start:row_stop],
                keys_all[:row_stop],
                preferred_element_type=jnp.float32,
            )
            * score_scale
        )
        scores = jnp.where(causal_block(row_start, block_rows, row_stop)[None], scores, -1e30)
        attention_probs = jnp.exp(scores - log_sums[:, row_start:row_stop, None])
        low_probs = attention_probs.astype(jnp.bfloat16)
        grad_probs = jnp.einsum(
            "qhd,khd->hqk",
            grad_out[row_start:row_stop],
            values_all[:row_stop],
            preferred_element_type=jnp.float32,
        )
        centre_term = jnp.sum(attention_probs * grad_probs, axis=-1, keepdims=True)
        grad_scores = (attention_probs * (grad_probs - centre_term)).astype(jnp.bfloat16)
        grad_queries_list.append(
            jnp.einsum(
                "hqk,khd->qhd", grad_scores, keys_all[:row_stop], preferred_element_type=jnp.float32
            )
            * score_scale
        )
        grad_keys = grad_keys.at[:row_stop].add(
            jnp.einsum(
                "hqk,qhd->khd",
                grad_scores,
                queries[row_start:row_stop],
                preferred_element_type=jnp.float32,
            )
            * score_scale
        )
        grad_values = grad_values.at[:row_stop].add(
            jnp.einsum(
                "hqk,qhd->khd",
                low_probs,
                grad_out[row_start:row_stop],
                preferred_element_type=jnp.float32,
            )
        )
    return (jnp.concatenate(grad_queries_list, axis=0), grad_keys, grad_values)


def forward_turn(my_rows, weights, vectors, cosines, sines):
    qkv_w, qkv_b, out_w, fc_in_w, fc_in_b, fc_out_w = weights
    gain_one, bias_one, gain_two, bias_two, out_b, fc_out_b = vectors
    gathered = lax.all_gather(my_rows, COL, axis=0, tiled=True)
    scaled, _ = norm_rows(gathered.astype(jnp.float32))
    normed_one = (scaled * gain_one + bias_one).astype(jnp.bfloat16)
    normed_two = (scaled * gain_two + bias_two).astype(jnp.bfloat16)
    length = gathered.shape[0]
    heads_here = qkv_w.shape[1]
    projected = jnp.dot(
        normed_one, qkv_w.reshape(qkv_w.shape[0], -1), preferred_element_type=jnp.float32
    ) + qkv_b.reshape(-1).astype(jnp.float32)
    projected = projected.reshape(length, heads_here, 3, HD)
    queries = rotate(projected[:, :, 0], cosines, sines).astype(jnp.bfloat16)
    keys_all = rotate(projected[:, :, 1], cosines, sines).astype(jnp.bfloat16)
    values_all = projected[:, :, 2].astype(jnp.bfloat16)
    attended, log_sums = attention_forward(queries, keys_all, values_all)
    inner_act = jnp.dot(normed_two, fc_in_w, preferred_element_type=jnp.float32) + fc_in_b.astype(
        jnp.float32
    )
    activated = gelu_exact(inner_act).astype(jnp.bfloat16)
    summed = lax.psum_scatter(
        jnp.dot(attended, out_w, preferred_element_type=jnp.float32)
        + jnp.dot(activated, fc_out_w, preferred_element_type=jnp.float32),
        COL,
        scatter_dimension=0,
        tiled=True,
    )
    output = (my_rows.astype(jnp.float32) + summed + out_b + fc_out_b).astype(jnp.bfloat16)
    kept_values = (
        gathered,
        normed_one,
        normed_two,
        queries,
        keys_all,
        values_all,
        attended,
        log_sums,
        inner_act,
    )
    return (output, kept_values)


def backward_turn(grad_rows, kept_values, weights, vectors, cosines, sines):
    (
        gathered,
        normed_one,
        normed_two,
        queries,
        keys_all,
        values_all,
        attended,
        log_sums,
        inner_act,
    ) = kept_values
    qkv_w, qkv_b, out_w, fc_in_w, _, fc_out_w = weights
    gain_one, _, gain_two, _, _, _ = vectors
    grad_full = lax.all_gather(grad_rows, COL, axis=0, tiled=True)
    length = grad_full.shape[0]
    rows_here = grad_rows.shape[0]
    own_start = lax.axis_index(COL) * rows_here
    activated = gelu_exact(inner_act).astype(jnp.bfloat16)
    out_w_grad = contract_rows(attended, grad_full)
    fc_out_w_grad = contract_rows(activated, grad_full)
    grad_attended = contract_cols(grad_full, out_w).astype(jnp.bfloat16)
    grad_activated = contract_cols(grad_full, fc_out_w)
    _, gelu_pull = jax.vjp(gelu_exact, inner_act)
    grad_inner = gelu_pull(grad_activated)[0].astype(jnp.bfloat16)
    grad_queries, grad_keys, grad_values = attention_backward(
        queries, keys_all, values_all, log_sums, grad_attended
    )
    grad_q_pre = rotate_back(grad_queries, cosines, sines)
    grad_k_pre = rotate_back(grad_keys, cosines, sines)
    grad_projected = (
        jnp.stack([grad_q_pre, grad_k_pre, grad_values], axis=2)
        .astype(jnp.bfloat16)
        .reshape(length, -1)
    )
    qkv_flat = qkv_w.reshape(qkv_w.shape[0], -1)
    qkv_w_grad = contract_rows(normed_one, grad_projected).reshape(qkv_w.shape)
    qkv_b_grad = jnp.sum(grad_projected.astype(jnp.float32), axis=0).reshape(qkv_b.shape)
    fc_in_w_grad = contract_rows(normed_two, grad_inner)
    fc_in_b_grad = jnp.sum(grad_inner.astype(jnp.float32), axis=0)
    width = qkv_w.shape[0]
    scaled_full, inverse_full = norm_rows(gathered.astype(jnp.float32))
    scaled = lax.dynamic_slice_in_dim(scaled_full, own_start, rows_here, 0)
    inverse_std = lax.dynamic_slice_in_dim(inverse_full, own_start, rows_here, 0)
    dy_sum = jnp.sum(grad_rows.astype(jnp.float32), axis=0)
    both_grads = lax.psum_scatter(
        jnp.concatenate(
            [contract_cols(grad_projected, qkv_flat), contract_cols(grad_inner, fc_in_w)], axis=1
        ),
        COL,
        scatter_dimension=0,
        tiled=True,
    )
    grad_one = both_grads[:, :width]
    grad_two = both_grads[:, width:]
    combined = gain_one * grad_one + gain_two * grad_two
    vector_grads = (
        jnp.sum(grad_one * scaled, axis=0),
        jnp.sum(grad_one, axis=0),
        jnp.sum(grad_two * scaled, axis=0),
        jnp.sum(grad_two, axis=0),
        dy_sum,
    )
    grad_norm = inverse_std * (
        combined
        - jnp.mean(combined, axis=-1, keepdims=True)
        - scaled * jnp.mean(combined * scaled, axis=-1, keepdims=True)
    )
    grad_input = (grad_rows.astype(jnp.float32) + grad_norm).astype(jnp.bfloat16)
    matrix_grads = (qkv_w_grad, qkv_b_grad, out_w_grad, fc_in_w_grad, fc_in_b_grad, fc_out_w_grad)
    return (grad_input, matrix_grads, vector_grads)


def add_tuples(running, addend):
    if running is None:
        return addend
    return tuple((first_part + second_part for first_part, second_part in zip(running, addend)))


def relay_local(
    inputs,
    cotangent,
    qkv_weight,
    qkv_bias,
    out_weight,
    fc_in_weight,
    fc_in_bias,
    fc_out_weight,
    norm1_gain,
    norm1_bias,
    norm2_gain,
    norm2_bias,
    out_bias,
    fc_out_bias,
):
    sections = lax.axis_size(SECTION)
    section_index = lax.axis_index(SECTION)
    micro_count = inputs.shape[0]
    tick_count = micro_count + sections - 1
    is_first = section_index == 0
    is_last = section_index == sections - 1
    cosines, sines = rotary_tables(SEQ_LEN)
    vectors = (
        lax.all_gather(norm1_gain[0], (ROW, COL), axis=0, tiled=True),
        lax.all_gather(norm1_bias[0], (ROW, COL), axis=0, tiled=True),
        lax.all_gather(norm2_gain[0], (ROW, COL), axis=0, tiled=True),
        lax.all_gather(norm2_bias[0], (ROW, COL), axis=0, tiled=True),
        lax.all_gather(out_bias[0], (ROW, COL), axis=0, tiled=True),
        lax.all_gather(fc_out_bias[0], (ROW, COL), axis=0, tiled=True),
    )
    vectors = tuple((member.astype(jnp.float32) for member in vectors))
    received = jnp.zeros_like(inputs[0])
    outputs_list = []
    kept_list = []
    for tick_index in range(tick_count):
        weights = (
            lax.all_gather(qkv_weight[0], ROW, axis=0, tiled=True),
            lax.all_gather(qkv_bias[0], ROW, axis=1, tiled=True),
            lax.all_gather(out_weight[0], ROW, axis=1, tiled=True),
            lax.all_gather(fc_in_weight[0], ROW, axis=0, tiled=True),
            lax.all_gather(fc_in_bias[0], ROW, axis=0, tiled=True),
            lax.all_gather(fc_out_weight[0], ROW, axis=1, tiled=True),
        )
        first_rows = inputs[min(tick_index, micro_count - 1)]
        my_rows = jnp.where(is_first, first_rows, received)
        output, kept_values = forward_turn(my_rows, weights, vectors, cosines, sines)
        outputs_list.append(output)
        kept_list.append(kept_values)
        if tick_index + 1 < tick_count:
            received = from_behind(output, SECTION, 1)
    layer_outputs = lax.dynamic_slice_in_dim(jnp.stack(outputs_list), section_index, micro_count, 0)
    stacked_kept = tuple((jnp.stack(members) for members in zip(*kept_list)))
    received_grad = jnp.zeros_like(inputs[0])
    grads_list = []
    matrix_total = None
    vector_total = None
    for tick_index in range(tick_count):
        weights = (
            lax.all_gather(qkv_weight[0], ROW, axis=0, tiled=True),
            lax.all_gather(qkv_bias[0], ROW, axis=1, tiled=True),
            lax.all_gather(out_weight[0], ROW, axis=1, tiled=True),
            lax.all_gather(fc_in_weight[0], ROW, axis=0, tiled=True),
            lax.all_gather(fc_in_bias[0], ROW, axis=0, tiled=True),
            lax.all_gather(fc_out_weight[0], ROW, axis=1, tiled=True),
        )
        if tick_index < micro_count:
            seed_grad = cotangent[tick_index]
        else:
            seed_grad = jnp.zeros_like(cotangent[0])
        grad_rows = jnp.where(is_last, seed_grad, received_grad)
        forward_index = jnp.clip(tick_index - sections + 1 + 2 * section_index, 0, tick_count - 1)
        kept_values = tuple(
            (
                lax.dynamic_index_in_dim(member, forward_index, 0, keepdims=False)
                for member in stacked_kept
            )
        )
        grad_input, matrix_grads, vector_grads = backward_turn(
            grad_rows, kept_values, weights, vectors, cosines, sines
        )
        grads_list.append(grad_input)
        if tick_index + 1 < tick_count:
            received_grad = from_behind(grad_input, SECTION, -1)
        matrix_part = (
            lax.psum_scatter(matrix_grads[0], ROW, scatter_dimension=0, tiled=True),
            lax.psum_scatter(matrix_grads[1], ROW, scatter_dimension=1, tiled=True),
            lax.psum_scatter(matrix_grads[2], ROW, scatter_dimension=1, tiled=True),
            lax.psum_scatter(matrix_grads[3], ROW, scatter_dimension=0, tiled=True),
            lax.psum_scatter(matrix_grads[4], ROW, scatter_dimension=0, tiled=True),
            lax.psum_scatter(matrix_grads[5], ROW, scatter_dimension=1, tiled=True),
        )
        vector_part = (
            lax.psum_scatter(vector_grads[0], (ROW, COL), scatter_dimension=0, tiled=True),
            lax.psum_scatter(vector_grads[1], (ROW, COL), scatter_dimension=0, tiled=True),
            lax.psum_scatter(vector_grads[2], (ROW, COL), scatter_dimension=0, tiled=True),
            lax.psum_scatter(vector_grads[3], (ROW, COL), scatter_dimension=0, tiled=True),
            lax.psum_scatter(vector_grads[4], (ROW, COL), scatter_dimension=0, tiled=True),
        )
        matrix_total = add_tuples(matrix_total, tuple(matrix_part))
        vector_total = add_tuples(vector_total, tuple(vector_part))
    input_gradients = lax.dynamic_slice_in_dim(
        jnp.stack(grads_list), sections - 1 - section_index, micro_count, 0
    )
    return (
        layer_outputs[None],
        input_gradients[None],
        matrix_total[0][None],
        matrix_total[1][None],
        matrix_total[2][None],
        matrix_total[3][None],
        matrix_total[4][None],
        matrix_total[5][None],
        vector_total[0][None],
        vector_total[1][None],
        vector_total[2][None],
        vector_total[3][None],
        vector_total[4][None],
        vector_total[4][None],
    )


F32 = jnp.float32
BF16 = jnp.bfloat16
LANES = 128


def swap(value, axis, bit):
    count = lax.axis_size(axis)
    return lax.ppermute(value, axis, [(source, source ^ bit) for source in range(count)])


def sum_over(value, axis):
    bit = 1
    while bit < lax.axis_size(axis):
        value = value + swap(value, axis, bit)
        bit *= 2
    return value


def place(part, axis, index, length):
    shape = list(part.shape)
    shape[axis] = length
    start = index * part.shape[axis]
    return lax.dynamic_update_slice_in_dim(jnp.zeros(shape, part.dtype), part, start, axis)


def take(value, axis, index, size):
    return lax.dynamic_slice_in_dim(value, index * size, size, axis)


def after(value, *others):
    return lax.optimization_barrier((value, *others))[0]


def gather_rows(block):
    half = block.shape[0] // 2
    across = swap(block, SECTION, 1)
    beside = swap(block, COL, 2)
    corner = jnp.concatenate(
        [swap(beside[:half], SECTION, 1), swap(across[half:], COL, 2)], axis=0
    )
    near = jnp.concatenate([block, beside], axis=0)
    far = jnp.concatenate([across, corner], axis=0)
    return jnp.concatenate([near, swap(near, COL, 1), far, swap(far, COL, 1)], axis=0), across


def pair_sum(keep_ref, came_ref, start, size):
    rows = pl.ds(start, size)
    return keep_ref[rows, :].astype(F32) + came_ref[rows, :].astype(F32)


def first_sum_kernel(keep_ref, came_ref, across_ref, beside_ref):
    block = keep_ref.shape[0] // 4
    half = block // 2
    for ref, starts in (
        (across_ref, (2 * block, 3 * block)),
        (beside_ref, (block + half, 3 * block + half)),
    ):
        for place, start in enumerate(starts):
            ref[place * half : (place + 1) * half, :] = pair_sum(
                keep_ref, came_ref, start, half
            ).astype(BF16)


def second_sum_kernel(keep_ref, came_ref, across_ref, beside_ref, top_ref, low_ref, kept_ref):
    block = keep_ref.shape[0] // 4
    half = block // 2
    kept_ref[:half, :] = pair_sum(keep_ref, came_ref, 0, half) + across_ref[:half, :].astype(F32)
    kept_ref[half:, :] = (
        pair_sum(keep_ref, came_ref, half, half) + beside_ref[:half, :].astype(F32)
    )
    top = pair_sum(keep_ref, came_ref, block, half) + across_ref[half:, :].astype(F32)
    top_ref[...] = top.astype(BF16)
    low = pair_sum(keep_ref, came_ref, 2 * block + half, half) + beside_ref[half:, :].astype(F32)
    low_ref[...] = low.astype(BF16)


def column_call(kernel, width, ins, outs):
    tile = 512

    def spec(shape):
        lead = shape[:-1]
        return pl.BlockSpec(lead + (tile,), lambda i: (0,) * len(lead) + (i,))

    return pl.pallas_call(
        kernel,
        grid=(width // tile,),
        in_specs=[spec(member.shape) for member in ins],
        out_specs=[spec(member.shape) for member in outs],
        out_shape=outs,
        cost_estimate=cost(0, *ins, *outs),
    )(*ins)


def scatter_rows(product):
    sent = product(1)
    came = swap(sent, COL, 1)
    keep = product(0)
    rows, width = keep.shape
    block = rows // 4
    half = block // 2
    whole_block = jax.ShapeDtypeStruct((block, width), BF16)
    half_block = jax.ShapeDtypeStruct((half, width), BF16)
    across, beside = column_call(first_sum_kernel, width, [keep, came], [whole_block, whole_block])
    across = swap(across, SECTION, 1)
    beside = swap(beside, COL, 2)
    top, low, keep = column_call(
        second_sum_kernel,
        width,
        [keep, came, across, beside],
        [half_block, half_block, jax.ShapeDtypeStruct((block, width), F32)],
    )
    arrived = jnp.concatenate([swap(top, COL, 2), swap(low, SECTION, 1)], axis=0)
    return keep + arrived.astype(F32)


def turn(values, cosines, sines):
    lead = values[:, :LANES]
    lane = lax.broadcasted_iota(jnp.int32, lead.shape, 1)
    ahead = pltpu.roll(lead, LANES - ROT // 2, 1)
    behind = pltpu.roll(lead, ROT // 2, 1)
    lead = lead * cosines + jnp.where(lane < ROT // 2, ahead, behind) * sines
    return jnp.concatenate([lead, values[:, LANES:]], axis=1)


def mm(first_operand, second_operand):
    return jnp.dot(first_operand, second_operand, preferred_element_type=F32)


def project_kernel(x_ref, wq_ref, wk_ref, wv_ref, e_ref, cos_ref, sin_ref, q_ref, k_ref, v_ref):
    x, cosines, sines = (x_ref[...], cos_ref[...], sin_ref[...])
    queries = mm(x, wq_ref[...]) + e_ref[:, :HD]
    q_ref[...] = (turn(queries, cosines, sines) * HD ** (-0.5)).astype(BF16)
    keys_here = mm(x, wk_ref[...]) + e_ref[:, HD : 2 * HD]
    k_ref[...] = turn(keys_here, cosines, sines).astype(BF16)
    v_ref[...] = (mm(x, wv_ref[...]) + e_ref[:, 2 * HD :]).astype(BF16)


def inner_kernel(x_ref, w_ref, e_ref, held_ref, act_ref, slope_ref):
    inner = mm(x_ref[...], w_ref[...]) + e_ref[...]
    below = 0.5 + 0.5 * lax.erf(inner * 0.7071067811865476)
    act_ref[...] = (inner * below).astype(BF16)
    density = jnp.exp(-0.5 * inner * inner) * 0.3989422804014327
    slope_ref[...] = (below + inner * density).astype(BF16)


def outer_kernel(act_ref, w_ref, wo_ref, out_ref):
    inner = w_ref.shape[0]
    total = mm(act_ref[:, :inner], w_ref[...]) + mm(act_ref[:, inner:], wo_ref[...])
    out_ref[...] = total.astype(BF16)


def outer_back_kernel(dy_ref, w_ref, wo_ref, slope_ref, dz_ref, do_ref, sum_ref):
    dy = dy_ref[...]
    dz = (contract_cols(dy, w_ref[...]) * slope_ref[...].astype(F32)).astype(BF16)
    dz_ref[...] = dz
    do_ref[...] = contract_cols(dy, wo_ref[...]).astype(BF16)

    @pl.when(pl.program_id(0) == 0)
    def _():
        sum_ref[...] = jnp.zeros_like(sum_ref)

    sum_ref[...] += jnp.sum(dz.astype(F32), axis=0, keepdims=True)


def inward_kernel(dz_ref, wf_ref, wq_ref, wk_ref, wv_ref, out_ref):
    start = wf_ref.shape[1]
    total = contract_cols(dz_ref[:, :start], wf_ref[...])
    for w_ref in (wq_ref, wk_ref, wv_ref):
        total += contract_cols(dz_ref[:, start : start + HD], w_ref[...])
        start += HD
    out_ref[...] = total.astype(BF16)


def attend_kernel(q_ref, k_ref, v_ref, row_ref, col_ref, out_ref, log_ref):
    scores = contract_cols(q_ref[...], k_ref[...])
    scores = jnp.where(row_ref[...] >= col_ref[...], scores, -1e30)
    peak = jnp.max(scores, axis=1, keepdims=True)
    exponents = jnp.exp(scores - peak)
    total = jnp.sum(exponents, axis=1, keepdims=True)
    out_ref[...] = mm((exponents / total).astype(BF16), v_ref[...]).astype(BF16)
    log_ref[...] = peak + jnp.log(total)


def attend_back_kernel(
    q_ref, k_ref, v_ref, row_ref, col_ref, log_ref, do_ref, cos_ref, sin_ref, held_ref,
    all_ref, sum_ref, out_ref, dk_ref, dv_ref, sem,
):
    step = pl.program_id(1)
    block = q_ref.shape[0]

    @pl.when(step == 0)
    def _():
        dk_ref[...] = jnp.zeros_like(dk_ref)
        dv_ref[...] = jnp.zeros_like(dv_ref)

    @pl.when((step == 0) & (pl.program_id(0) == 0))
    def _():
        sum_ref[...] = jnp.zeros_like(sum_ref)

    def column_sum(values):
        return jnp.sum(values.astype(F32), axis=0, keepdims=True)

    queries, keys_all, grads = (q_ref[...], k_ref[...], do_ref[...])
    scores = contract_cols(queries, keys_all)
    scores = jnp.where(row_ref[...] >= col_ref[...], scores, -1e30)
    probs = jnp.exp(scores - log_ref[...])
    grad_probs = contract_cols(grads, v_ref[...])
    centre = jnp.sum(probs * grad_probs, axis=1, keepdims=True)
    grad_scores = (probs * (grad_probs - centre)).astype(BF16)
    rows = pl.ds(pl.multiple_of(step * block, block), block)
    cosines, sines = cos_ref[rows, :], sin_ref[rows, :]
    grad_queries = mm(grad_scores, keys_all) * HD ** (-0.5)
    grad_queries = turn(grad_queries, cosines, -sines).astype(BF16)
    out_ref[rows, :HD] = grad_queries
    sum_ref[:, :HD] += column_sum(grad_queries)
    dk_ref[...] += contract_rows(grad_scores, queries)
    dv_ref[...] += contract_rows(probs.astype(BF16), grads)

    @pl.when(step == pl.num_programs(1) - 1)
    def _():
        grad_keys = turn(dk_ref[...], cos_ref[...], -sin_ref[...]).astype(BF16)
        grad_values = dv_ref[...].astype(BF16)
        out_ref[:, HD : 2 * HD] = grad_keys
        out_ref[:, 2 * HD :] = grad_values
        sum_ref[:, HD : 2 * HD] += column_sum(grad_keys)
        sum_ref[:, 2 * HD :] += column_sum(grad_values)
        length, width = out_ref.shape
        micro = pl.ds(pl.multiple_of(pl.program_id(0) * length, length), length)
        copy = pltpu.make_async_copy(
            out_ref, all_ref.at[micro, pl.ds(all_ref.shape[1] - width, width)], sem
        )
        copy.start()
        copy.wait()


ROW_BLOCK = 256


def by_rows(width, block=ROW_BLOCK):
    return pl.BlockSpec((block, width), lambda i: (i, 0))


def whole(shape):
    return pl.BlockSpec(shape, lambda *unused: (0,) * len(shape))


def panel(width, place):
    return lambda deep: pl.BlockSpec((deep, width), lambda *unused: (0, place))


def cost(flops, *arrays):
    return pl.CostEstimate(
        flops=flops,
        transcendentals=0,
        bytes_accessed=sum(math.prod(array.shape) * array.dtype.itemsize for array in arrays),
    )


def heads_panels(array, inner):
    return [panel(HD, inner // HD + part)(array.shape[0]) for part in range(3)]


def project(x, w, inner, e, tables):
    rows, width = x.shape
    per_micro = tables[0].shape[0] // ROW_BLOCK
    table = pl.BlockSpec((ROW_BLOCK, LANES), lambda i: (i % per_micro, 0))
    out = jax.ShapeDtypeStruct((rows, HD), BF16)
    return pl.pallas_call(
        project_kernel,
        grid=(rows // ROW_BLOCK,),
        in_specs=[by_rows(width), *heads_panels(w, inner), whole(e.shape), table, table],
        out_specs=[by_rows(HD)] * 3,
        out_shape=[out] * 3,
        cost_estimate=cost(6 * rows * width * HD, x, out, out, out),
        name="project",
    )(x, w, w, w, e, *tables)


def inner_layer(x, w, e, held):
    rows, width = x.shape
    inner = e.shape[1]
    slope = jax.ShapeDtypeStruct((rows, inner), BF16)
    return pl.pallas_call(
        inner_kernel,
        grid=(rows // ROW_BLOCK,),
        in_specs=[
            by_rows(width),
            panel(inner, 0)(width),
            whole(e.shape),
            pl.BlockSpec(memory_space=pl.ANY),
        ],
        out_specs=[by_rows(inner)] * 2,
        out_shape=[jax.ShapeDtypeStruct(held.shape, BF16), slope],
        input_output_aliases={3: 0},
        cost_estimate=cost(2 * rows * width * inner, x, slope, slope),
        name="inner",
    )(x, w, e, held)


def split_rows(width, other):
    return pl.BlockSpec((ROW_BLOCK, width), lambda i: (i // 2 * 4 + 2 * other + i % 2, 0))


def outer_panels(pair, inner):
    (w, first), (wo, second) = pair
    return [
        pl.BlockSpec((inner, w.shape[1]), lambda *unused: (first // inner, 0)),
        pl.BlockSpec((HD, wo.shape[1]), lambda *unused: (second // HD, 0)),
    ]


def outer(act, pair, other):
    rows, width = (act.shape[0] // 2, pair[0][0].shape[1])
    out = jax.ShapeDtypeStruct((rows, width), BF16)
    return pl.pallas_call(
        outer_kernel,
        grid=(rows // ROW_BLOCK,),
        in_specs=[split_rows(act.shape[1], other), *outer_panels(pair, act.shape[1] - HD)],
        out_specs=by_rows(width),
        out_shape=out,
        cost_estimate=cost(2 * rows * width * act.shape[1], act, out),
        name="outer",
    )(act, pair[0][0], pair[1][0])


def inward(dz, w_in, w_qkv, offset, other):
    rows, width = (dz.shape[0] // 2, w_in.shape[0])
    out = jax.ShapeDtypeStruct((rows, width), BF16)
    return pl.pallas_call(
        inward_kernel,
        grid=(rows // ROW_BLOCK,),
        in_specs=[
            split_rows(dz.shape[1], other),
            panel(dz.shape[1] - 3 * HD, 0)(width),
            *heads_panels(w_qkv, offset),
        ],
        out_specs=by_rows(width),
        out_shape=out,
        cost_estimate=cost(2 * rows * width * dz.shape[1], dz, out),
        name="inward",
    )(dz, w_in, w_qkv, w_qkv, w_qkv)


def outer_back(dy, pair, slopes):
    rows, width = dy.shape
    inner = slopes.shape[1]
    dz = jax.ShapeDtypeStruct((rows, inner + 3 * HD), BF16)
    return pl.pallas_call(
        outer_back_kernel,
        grid=(rows // ROW_BLOCK,),
        in_specs=[by_rows(width), *outer_panels(pair, inner), by_rows(inner)],
        out_specs=[by_rows(inner), by_rows(HD), whole((1, inner))],
        out_shape=[
            dz,
            jax.ShapeDtypeStruct((rows, HD), BF16),
            jax.ShapeDtypeStruct((1, inner), F32),
        ],
        cost_estimate=cost(2 * rows * width * (inner + HD), dy, slopes, slopes),
        name="outer_back",
    )(dy, pair[0][0], pair[1][0], slopes)


def attend(queries, keys_all, values_all, places, inner):
    rows = queries.shape[0]
    length = places.shape[0]
    steps = length // ROW_BLOCK
    row = pl.BlockSpec((ROW_BLOCK, HD), lambda m, i: (m * steps + i, 0))
    every = pl.BlockSpec((length, HD), lambda m, i: (m, 0))
    return pl.pallas_call(
        attend_kernel,
        grid=(rows // length, steps),
        in_specs=[
            row,
            every,
            every,
            pl.BlockSpec((ROW_BLOCK, 1), lambda m, i: (i, 0)),
            pl.BlockSpec((1, length), lambda m, i: (0, 0)),
        ],
        out_specs=[
            pl.BlockSpec((ROW_BLOCK, HD), lambda m, i: (m * steps + i, inner // HD)),
            pl.BlockSpec((ROW_BLOCK, 1), lambda m, i: (m * steps + i, 0)),
        ],
        out_shape=[
            jax.ShapeDtypeStruct((rows, inner + HD), BF16),
            jax.ShapeDtypeStruct((rows, 1), F32),
        ],
        cost_estimate=cost(4 * rows * length * HD, queries, keys_all, values_all, queries),
        name="attend",
    )(queries, keys_all, values_all, places[:, None], places[None, :])


def attend_back(queries, keys_all, values_all, places, log_sums, grads, tables, held):
    rows = queries.shape[0]
    length = places.shape[0]
    steps = length // ROW_BLOCK
    row = pl.BlockSpec((ROW_BLOCK, HD), lambda m, i: (m * steps + i, 0))
    every = pl.BlockSpec((length, HD), lambda m, i: (m, 0))
    anywhere = pl.BlockSpec(memory_space=pl.ANY)
    return pl.pallas_call(
        attend_back_kernel,
        grid=(rows // length, steps),
        in_specs=[
            row,
            every,
            every,
            pl.BlockSpec((ROW_BLOCK, 1), lambda m, i: (i, 0)),
            pl.BlockSpec((1, length), lambda m, i: (0, 0)),
            pl.BlockSpec((ROW_BLOCK, 1), lambda m, i: (m * steps + i, 0)),
            row,
            whole(tables[0].shape),
            whole(tables[1].shape),
            anywhere,
        ],
        out_specs=[anywhere, whole((1, 3 * HD))],
        out_shape=[
            jax.ShapeDtypeStruct(held.shape, BF16),
            jax.ShapeDtypeStruct((1, 3 * HD), F32),
        ],
        scratch_shapes=[
            pltpu.VMEM((length, 3 * HD), BF16),
            pltpu.VMEM((length, HD), F32),
            pltpu.VMEM((length, HD), F32),
            pltpu.SemaphoreType.DMA,
        ],
        input_output_aliases={9: 0},
        cost_estimate=cost(10 * rows * length * HD, queries, keys_all, values_all, grads),
        name="attend_back",
    )(
        queries, keys_all, values_all, places[:, None], places[None, :], log_sums, grads, *tables,
        held,
    )


def local(
    inputs,
    cotangent,
    qkv_weight,
    qkv_bias,
    out_weight,
    fc_in_weight,
    fc_in_bias,
    fc_out_weight,
    norm1_gain,
    norm1_bias,
    norm2_gain,
    norm2_bias,
    out_bias,
    fc_out_bias,
):
    s, r, c = (lax.axis_index(SECTION), lax.axis_index(ROW), lax.axis_index(COL))
    rows_axis, cols_axis = (lax.axis_size(ROW), lax.axis_size(COL))
    low = s == 0
    qkv_w, out_w, fc_in_w, fc_out_w = (
        qkv_weight[0], out_weight[0], fc_in_weight[0], fc_out_weight[0],
    )
    deep, heads_here = qkv_w.shape[0], qkv_w.shape[1]
    per = 3 * HD
    inner = fc_in_w.shape[1] // 2
    model = inputs.shape[2]

    def both_layers(own_first, own_second):
        return (jnp.where(low, own_first, own_second), jnp.where(low, own_second, own_first))

    def trade(value, axis, *others):
        size = value.shape[axis] // 2
        kept = take(value, axis, s, size)
        came = swap(after(take(value, axis, 1 - s, size), *others), SECTION, 1)
        return kept, came

    def gathered(shard, axis):
        return lax.all_gather(shard, ROW, axis=axis, tiled=True)

    held = jnp.stack(
        [
            norm1_gain[0].astype(F32),
            norm1_bias[0].astype(F32),
            norm2_gain[0].astype(F32),
            norm2_bias[0].astype(F32),
            out_bias[0].astype(F32) + fc_out_bias[0].astype(F32),
        ]
    )
    held_both = jnp.stack([held, swap(held, SECTION, 1)])
    out_half = trade(out_w, 0, held_both)
    qkv_half = trade(qkv_w, 1, out_half[1])
    qkv_half = tuple(member.reshape(deep, per) for member in qkv_half)
    fc_in_half = trade(fc_in_w, 1, qkv_half[1])
    fc_out_half = trade(fc_out_w, 0, fc_in_half[1])
    held_both = sum_over(place(held_both, 2, c, deep), COL)
    held = held_both[0]
    gain_one, shift_one, gain_two, shift_two, end_bias = (held[i] for i in range(5))
    gains = both_layers(held, held_both[1])

    def scaled_pair(half, row):
        return tuple(
            (part.astype(F32) * gain[row][:, None]).astype(BF16)
            for part, gain in zip(both_layers(*half), gains)
        )

    out_pair = both_layers(*out_half)
    qkv_pair = scaled_pair(qkv_half, 0)
    fc_in_pair = scaled_pair(fc_in_half, 2)
    fc_out_pair = both_layers(*fc_out_half)
    w_out0 = gathered(out_pair[0], 1)
    w_qkv0 = gathered(qkv_pair[0], 0)
    w_fc_in0 = gathered(fc_in_pair[0], 0)
    w_fc_out0 = gathered(fc_out_pair[0], 1)
    w_ins1 = gathered(jnp.concatenate([fc_in_pair[1], qkv_pair[1]], axis=1), 0)
    w_outs1 = gathered(jnp.concatenate([fc_out_pair[1], out_pair[1]], axis=0), 1)
    w_ins = ((w_fc_in0, w_qkv0, 0), (w_ins1, w_ins1, inner))
    w_outs = (((w_fc_out0, 0), (w_out0, 0)), ((w_outs1, 0), (w_outs1, inner)))
    qkv_flat = qkv_w.reshape(deep, -1)

    own_qkv = mm(shift_one.astype(BF16)[None], qkv_flat)[0]
    own_fc = mm(shift_two.astype(BF16)[None], fc_in_w)[0]
    own_qkv = own_qkv + place(qkv_bias[0].astype(F32), 1, r, per).reshape(-1)
    own_fc = own_fc + place(fc_in_bias[0].astype(F32), 0, r, 2 * inner)
    biases = sum_over(
        jnp.concatenate([own_qkv, own_fc, place(end_bias, 0, r, model)]), ROW
    )
    biases = both_layers(biases, swap(biases, SECTION, 1))
    qkv_e, fc_e, end_e = ([], [], [])
    for member in biases:
        qkv_e.append(take(member[: 2 * per], 0, s, per)[None])
        fc_e.append(take(member[2 * per : 2 * per + 2 * inner], 0, s, inner)[None])
        end_e.append(member[2 * per + 2 * inner :])

    block_rows = inputs.shape[1]
    masks = jnp.array([0, 2, 1, 3], jnp.int32)
    places = ((c ^ masks)[:, None] * block_rows + jnp.arange(block_rows)[None]).reshape(-1)
    inverse = 10000.0 ** (-jnp.arange(0, ROT, 2).astype(F32) / ROT)
    angles = places.astype(F32)[:, None] * inverse[None]
    ones = jnp.ones((places.shape[0], LANES - ROT), F32)
    cosines, sines = (jnp.cos(angles), jnp.sin(angles))
    tables = (
        jnp.concatenate([cosines, cosines, ones], axis=1),
        jnp.concatenate([-sines, sines, 0.0 * ones], axis=1),
    )

    hidden = lax.dynamic_index_in_dim(inputs, s, 0, keepdims=False)
    seed = lax.dynamic_index_in_dim(cotangent, s, 0, keepdims=False)
    hidden = after(hidden, fc_out_half[1])

    hidden_list, kept_list, ends = ([], [], [])
    seed_rows = None
    for layer in range(2):
        hidden_list.append(hidden)
        scaled, unused = norm_rows(hidden.astype(F32))
        x, unused = gather_rows(scaled.astype(BF16))
        if layer == 0:
            seed_rows, unused = gather_rows(after(seed, x))
            x = after(x, seed_rows)
        w_fc_in, w_qkv, offset = w_ins[layer]
        queries, keys_all, values_all = project(x, w_qkv, offset, qkv_e[layer], tables)
        attended, log_sums = attend(queries, keys_all, values_all, places, inner)
        act, slopes = inner_layer(x, w_fc_in, fc_e[layer], attended)
        kept = (x, queries, keys_all, values_all, log_sums, slopes, act)
        if layer == 1:
            outs_grad1 = contract_rows(act, seed_rows).astype(BF16)
            seed_rows = after(seed_rows, outs_grad1)
        kept_list.append(kept)
        if layer == 0:
            summed = scatter_rows(lambda other: outer(act, w_outs[0], other))
            hidden = (hidden.astype(F32) + summed + end_e[layer]).astype(BF16)
            ends.append(hidden)
            middle = swap(hidden, SECTION, 1)

    def reduced(value, axis):
        return lax.psum_scatter(value, ROW, scatter_dimension=axis, tiled=True)

    outs_part1 = reduced(outs_grad1, 1)
    grads = seed
    ins_list, small_list = ([None, None], [None, None])
    for layer in (1, 0):
        x, queries, keys_all, values_all, log_sums, slopes, act = kept_list[layer]
        w_fc_in, w_qkv, offset = w_ins[layer]
        if layer == 1:
            dy = seed_rows
        else:
            dy, across = gather_rows(grads)
            middle_grads = (jnp.where(low, grads, across), jnp.where(low, across, grads))
        dy_sum = jnp.sum(grads.astype(F32), axis=0)
        dz, grad_attended, inner_sum = outer_back(dy, w_outs[layer], slopes)
        dz, heads_sum = attend_back(
            queries, keys_all, values_all, places, log_sums, grad_attended, tables, dz
        )
        combined = scatter_rows(lambda other: inward(dz, w_fc_in, w_qkv, offset, other))
        ins_grad = contract_rows(x, dz).astype(BF16)
        ins_list[layer] = reduced(ins_grad, 0)
        scaled, inverse_std = norm_rows(hidden_list[layer].astype(F32))
        grad_norm = inverse_std * (
            combined
            - jnp.mean(combined, axis=-1, keepdims=True)
            - scaled * jnp.mean(combined * scaled, axis=-1, keepdims=True)
        )
        grads = (grads.astype(F32) + grad_norm).astype(BF16)
        small_list[layer] = (heads_sum[0], inner_sum[0], dy_sum)
        if layer == 0:
            fc_out_part0 = reduced(contract_rows(act[:, :inner], dy).astype(BF16), 1)
            out_part0 = reduced(contract_rows(act[:, inner:], dy).astype(BF16), 1)
    act = after(kept_list[1][-1], small_list[0][0])
    summed = scatter_rows(lambda other: outer(act, w_outs[1], other))
    ends.append((hidden_list[1].astype(F32) + summed + end_e[1]).astype(BF16))

    def to_owner(first, second, upper, lower):
        return (jnp.where(low, first, lower), jnp.where(low, upper, second))

    def to_first(value):
        return lax.ppermute(value, SECTION, [(1, 0)])

    def to_second(value):
        return lax.ppermute(value, SECTION, [(0, 1)])

    ends_sum = jnp.concatenate([member[2] for member in small_list])
    ends_sum = sum_over(sum_over(ends_sum, SECTION), COL)
    small = sum_over(
        jnp.concatenate([*small_list[0][:2], *small_list[1][:2], ends_sum]), ROW
    )
    sums = small[: 2 * (per + inner)]
    smalls = to_owner(
        *jnp.split(sums, 2), *jnp.split(swap(sums, SECTION, 1), 2)
    )
    end_grad = jnp.where(low, *jnp.split(small[2 * (per + inner) :], 2))
    qkv_b_grad = jnp.concatenate([member[:per] for member in smalls])
    fc_in_b_grad = jnp.concatenate([member[per:] for member in smalls])
    outs_lower = to_second(outs_part1)
    ins_lower = to_second(ins_list[1])
    ins_upper = to_first(ins_list[0])
    ins_g = to_owner(*ins_list, ins_upper, ins_lower)
    qkv_g = jnp.concatenate([member[:, inner:] for member in ins_g], axis=1).astype(F32)
    fc_in_g = jnp.concatenate([member[:, :inner] for member in ins_g], axis=1).astype(F32)
    qkv_w_grad = gain_one[:, None] * qkv_g + shift_one[:, None] * qkv_b_grad[None]
    fc_in_w_grad = gain_two[:, None] * fc_in_g + shift_two[:, None] * fc_in_b_grad[None]
    qkv_full, fc_full = (qkv_flat.astype(F32), fc_in_w.astype(F32))
    norms = jnp.stack(
        [
            jnp.sum(qkv_full * qkv_g, axis=1),
            jnp.sum(qkv_full * qkv_b_grad[None], axis=1),
            jnp.sum(fc_full * fc_in_g, axis=1),
            jnp.sum(fc_full * fc_in_b_grad[None], axis=1),
        ]
    )
    norms = take(sum_over(norms, COL), 1, c, deep // cols_axis)
    end_grad = take(end_grad, 0, r * cols_axis + c, deep // cols_axis)
    fc_out_upper = to_first(after(fc_out_part0, ins_upper))
    fc_out_w_grad = jnp.concatenate(
        [
            jnp.where(low, fc_out_part0, outs_lower[:inner]),
            jnp.where(low, fc_out_upper, outs_part1[:inner]),
        ],
        axis=0,
    ).astype(F32)[None]
    qkv_w_grad = qkv_w_grad.reshape(qkv_w.shape)[None]
    fc_in_w_grad = fc_in_w_grad[None]
    out_part0, fc_out_w_grad, norms = lax.optimization_barrier(
        (out_part0, fc_out_w_grad, norms)
    )
    out_upper = to_first(out_part0)
    out_w_grad = jnp.concatenate(
        [
            jnp.where(low, out_part0, outs_lower[inner:]),
            jnp.where(low, out_upper, outs_part1[inner:]),
        ],
        axis=0,
    ).astype(F32)
    last = to_second(ends[1])
    layer_outputs = jnp.stack([jnp.where(low, ends[0], last), jnp.where(low, middle, ends[1])])
    first = to_first(grads)
    input_gradients = jnp.stack(
        [jnp.where(low, grads, middle_grads[0]), jnp.where(low, first, middle_grads[1])]
    )
    return (
        layer_outputs[None],
        input_gradients[None],
        qkv_w_grad,
        take(qkv_b_grad.reshape(heads_here, -1), 1, r, per // rows_axis)[None],
        out_w_grad[None],
        fc_in_w_grad,
        take(fc_in_b_grad, 0, r, 2 * inner // rows_axis)[None],
        fc_out_w_grad,
        norms[0][None],
        norms[1][None],
        norms[2][None],
        norms[3][None],
        end_grad[None],
        end_grad[None],
    )


def all_of_it(*arrays):
    return local(*arrays)


def solution(mesh):
    sizes = mesh.shape
    paired = sizes[SECTION] == 2 and sizes[COL] == 4
    rows_even = sizes[ROW] & (sizes[ROW] - 1) == 0
    body = all_of_it if paired and rows_even else relay_local
    step = jax.shard_map(
        body,
        mesh=mesh,
        in_specs=(
            P(None, (ROW, COL), None),
            P(None, (ROW, COL), None),
            P(SECTION, ROW, COL, None),
            P(SECTION, COL, ROW),
            P(SECTION, COL, ROW),
            P(SECTION, ROW, COL),
            P(SECTION, (COL, ROW)),
            P(SECTION, COL, ROW),
            P(SECTION, (ROW, COL)),
            P(SECTION, (ROW, COL)),
            P(SECTION, (ROW, COL)),
            P(SECTION, (ROW, COL)),
            P(SECTION, (ROW, COL)),
            P(SECTION, (ROW, COL)),
        ),
        out_specs=(
            P(SECTION, None, (ROW, COL), None),
            P(SECTION, None, (ROW, COL), None),
            P(SECTION, ROW, COL, None),
            P(SECTION, COL, ROW),
            P(SECTION, COL, ROW),
            P(SECTION, ROW, COL),
            P(SECTION, (COL, ROW)),
            P(SECTION, COL, ROW),
            P(SECTION, (ROW, COL)),
            P(SECTION, (ROW, COL)),
            P(SECTION, (ROW, COL)),
            P(SECTION, (ROW, COL)),
            P(SECTION, (ROW, COL)),
            P(SECTION, (ROW, COL)),
        ),
        check_vma=False,
    )
    if body is relay_local:
        return step
    return step
```

time: 1170 us -> 1080 us (0.923)
  Pallas kernels: 184 us -> 285 us
  waiting for transfers between devices: 530 us -> 446 us
  matrix products: 124 us -> 84.2 us
  other arithmetic: 114 us -> 83 us
  starting transfers between devices: 93.6 us -> 75.9 us
    pallas_call x4 -> x18, Pallas kernels: 75.1 us -> 172 us  [the longest x4 51.8 us: inward(): pl.pallas_call(inward_kernel, grid=(rows // ROW_BLOCK,), in_specs=[split_...]
    dot_general x4 -> x0, matrix products: 41.7 us -> none  [contract_cols(): lax.dot_general(first_operand, second_operand, (((1,), (1,)), ((), ())),...]
    all_gather x8 -> x6, waiting for transfers between devices: 119 us -> 79.2 us  [gathered(): return lax.all_gather(shard, ROW, axis=axis, tiled=True)]
    reduce_scatter x8 -> x5, waiting for transfers between devices: 39.4 us -> 2.25 us  [reduced(): return lax.psum_scatter(value, ROW, scatter_dimension=axis, tiled=True)]
    convert_element_type x27 -> x7, other arithmetic: 41.3 us -> 12.1 us  [the longest x2 6.28 us: scaled_pair(): (part.astype(F32) * gain[row][:, None]).astype(BF16)]
    ppermute x70 -> x63, waiting for transfers between devices: 311 us -> 293 us  [swap(): lax.ppermute(value, axis, [(source, source ^ bit) for source in range(cou...]
    squeeze x4 -> x1, local copies, waits for them, and re-layouts: 17.7 us -> 0.07 us  [local(): hidden = lax.dynamic_index_in_dim(inputs, s, 0, keepdims=False)]
    ppermute x12 -> x7, starting transfers between devices: 29.2 us -> 14.9 us  [the longest x3 9.77 us: to_second(): return lax.ppermute(value, SECTION, [(0, 1)])]
  transfers between devices with their start and end apart: 98 -> 81, of which waited for: 46 -> 42; matrix products, arithmetic and copies ran while one was open for 25% -> 20% of each run, Pallas kernels for 14% -> 24%
where the time goes in v2:
time: 1080 us; the launch traced here: 1070 us
  waiting for transfers between devices  446 us (41%)
  Pallas kernels  285 us (26%)
  matrix products  84.2 us (8%)
  other arithmetic  83 us (8%)
  local copies, waits for them, and re-layouts  81.7 us (8%)
  starting transfers between devices  75.9 us (7%)
  between operations  15.2 us (1%)
    ppermute x63, waiting for transfers between devices, swap(): lax.ppermute(value, axis, [(source, source ^ bit) for source in range(cou...  293 us
    dot_general x5, matrix products, contract_rows(): lax.dot_general(first_operand, second_operand, (((0,), (0,)), ((), ())),...  80.5 us
    all_gather x6, waiting for transfers between devices, gathered(): return lax.all_gather(shard, ROW, axis=axis, tiled=True)  79.2 us
    ppermute x63, starting transfers between devices, swap(): lax.ppermute(value, axis, [(source, source ^ bit) for source in range(cou...  60.4 us
    pallas_call x4, Pallas kernels, inward(): pl.pallas_call(inward_kernel, grid=(rows // ROW_BLOCK,), in_specs=[split_...  51.8 us
    pallas_call x8, Pallas kernels, column_call(): pl.pallas_call(kernel, grid=(width // tile,), in_specs=[spec(member.shape...  44.6 us
    unnamed x148, local copies, waits for them, and re-layouts  43.6 us
    ppermute x4, waiting for transfers between devices, to_first(): return lax.ppermute(value, SECTION, [(1, 0)])  40.4 us
  transfers between devices with their start and end apart: 81, of which 42 were waited for; matrix products, arithmetic and copies ran while one was open for 20% of the time, Pallas kernels for 24%

profile of v2, /device:TPU:0, one launch (start us, length us, event | category | flops | bytes accessed | tf_op | source)
XLA Modules:
  0.0 1071.6 jit_solution(15186833306242026801)
XLA Ops:
  21.7 17.1 %collective-permute-done = f32[5,128]{1,0:T(8,128)S(1)} collective-permute-done((f32[5,128]{1,0:T(8,128)S(1)}, f32[5,128]{1,0:T(8,128)S(1)}, u32[]{:S(2)}, u32[]{:S(2)}) %collective-permute-start) | collective-permute-done | bytes 2592 | tf_op jit(solution)/shard_map/ppermute | solution.py:421
  48.7 23.9 %collective-permute-done.3 = bf16[512,1024]{1,0:T(8,128)(2,1)} collective-permute-done((bf16[512,1024]{1,0:T(8,128)(2,1)S(1)}, bf16[512,1024]{1,0:T(8,128)(2,1)}, u32[]{:S(2)}, u32[]{:S(2)}) %collective-permute-start.3) | collective-permute-done | bytes 1048608 | tf_op jit(solution)/shard_map/ppermute | solution.py:421
  78.7 23.1 %collective-permute-done.4 = bf16[1024,512]{1,0:T(8,128)(2,1)} collective-permute-done((bf16[1024,512]{1,0:T(8,128)(2,1)}, bf16[1024,512]{1,0:T(8,128)(2,1)}, u32[]{:S(2)}, u32[]{:S(2)}) %collective-permute-start.4) | collective-permute-done | bytes 1048608 | tf_op jit(solution)/shard_map/ppermute | solution.py:421
  107.2 19.6 %collective-permute-done.5 = bf16[256,2048]{1,0:T(8,128)(2,1)S(1)} collective-permute-done((bf16[256,2048]{1,0:T(8,128)(2,1)}, bf16[256,2048]{1,0:T(8,128)(2,1)S(1)}, u32[]{:S(2)}, u32[]{:S(2)}) %collective-permute-start.5) | collective-permute-done | bytes 1048608 | tf_op jit(solution)/shard_map/ppermute | solution.py:421
  172.0 14.1 %collective-permute-done.11 = bf16[256,2048]{1,0:T(8,128)(2,1)} collective-permute-done((bf16[256,2048]{1,0:T(8,128)(2,1)}, bf16[256,2048]{1,0:T(8,128)(2,1)}, u32[]{:S(2)}, u32[]{:S(2)}) %collective-permute-start.11) | collective-permute-done | bytes 1048608 | tf_op jit(solution)/shard_map/ppermute | solution.py:421
  228.2 13.4 %project.2 = (bf16[2048,256]{1,0:T(8,128)(2,1)}, bf16[2048,256]{1,0:T(8,128)(2,1)}, bf16[2048,256]{1,0:T(8,128)(2,1)}) custom-call(bf16[2048,2048]{1,0:T(8,128)(2,1)} %constant_dynamic-update-slice_fusion.x_ref, bf16[2048,768]{1,0:T(8,128)(2,1)} %all-gather.9.cloned.1.call-done.wq_ref.wk_ref.wv_ref, ...), custom_call_target="tpu_custom_call" | custom-call | flops 6442450944 | bytes 11534336 | tf_op jit(solution)/shard_map/project/pallas_call | solution.py:681
  252.4 16.8 %inner.2 = (bf16[2048,1280]{1,0:T(8,128)(2,1)}, bf16[2048,1024]{1,0:T(8,128)(2,1)}) custom-call(bf16[2048,2048]{1,0:T(8,128)(2,1)} %constant_dynamic-update-slice_fusion.x_ref, bf16[2048,1024]{1,0:T(8,128)(2,1)} %all-gather.7.cloned.1.call-done.w_ref.wf_ref, f32[1,1024]{1,0:T(1,128)} %bitcast.160, ...), custom_call_target="tpu_custom_call", output_to_operand_aliasing={{0}: (3, {})} | custom-call | flops 8589934592 | bytes 16777216 | tf_op jit(solution)/shard_map/inner/pallas_call | solution.py:696
  269.2 34.1 %all-gather.11.cloned.1.call-done.w_ref = bf16[1024,2048]{1,0:T(8,128)(2,1)} async-done(((bf16[1024,512]{1,0:T(8,128)(2,1)}), bf16[1024,2048]{1,0:T(8,128)(2,1)}) %all-gather.11.cloned.1.call-update) | async-done | bytes 4194320 | tf_op jit(solution)/shard_map/all_gather | solution.py:884
  331.6 22.8 %collective-permute-done.23.across_ref = bf16[256,2048]{1,0:T(8,128)(2,1)S(1)} collective-permute-done((bf16[256,2048]{1,0:T(8,128)(2,1)}, bf16[256,2048]{1,0:T(8,128)(2,1)S(1)}, u32[]{:S(2)}, u32[]{:S(2)}) %collective-permute-start.23) | collective-permute-done | bytes 1048608 | tf_op jit(solution)/shard_map/ppermute | solution.py:421
  385.1 20.4 %collective-permute-done.27 = bf16[256,2048]{1,0:T(8,128)(2,1)S(1)} collective-permute-done((bf16[256,2048]{1,0:T(8,128)(2,1)}, bf16[256,2048]{1,0:T(8,128)(2,1)S(1)}, u32[]{:S(2)}, u32[]{:S(2)}) %collective-permute-start.27) | collective-permute-done | bytes 1048608 | tf_op jit(solution)/shard_map/ppermute | solution.py:421
  409.4 12.0 %collective-permute-done.30 = bf16[128,2048]{1,0:T(8,128)(2,1)S(1)} collective-permute-done((bf16[128,2048]{1,0:T(8,128)(2,1)S(1)}, bf16[128,2048]{1,0:T(8,128)(2,1)S(1)}, u32[]{:S(2)}, u32[]{:S(2)}) %collective-permute-start.30) | collective-permute-done | bytes 524320 | tf_op jit(solution)/shard_map/ppermute | solution.py:421
  436.2 13.0 %project.3 = (bf16[2048,256]{1,0:T(8,128)(2,1)}, bf16[2048,256]{1,0:T(8,128)(2,1)}, bf16[2048,256]{1,0:T(8,128)(2,1)}) custom-call(bf16[2048,2048]{1,0:T(8,128)(2,1)} %constant_dynamic-update-slice_fusion.14.x_ref, bf16[2048,1792]{1,0:T(8,128)(2,1)} %all-gather.15.cloned.1.call-done.wq_ref.wk_ref.wv_ref.w_ref.wf_ref, ...), custom_call_target="tpu_custom_call" | custom-call | flops 6442450944 | bytes 11534336 | tf_op jit(solution)/shard_map/project/pallas_call | solution.py:681
  460.1 16.7 %inner.3 = (bf16[2048,1280]{1,0:T(8,128)(2,1)}, bf16[2048,1024]{1,0:T(8,128)(2,1)}) custom-call(bf16[2048,2048]{1,0:T(8,128)(2,1)} %constant_dynamic-update-slice_fusion.14.x_ref, bf16[2048,1792]{1,0:T(8,128)(2,1)} %all-gather.15.cloned.1.call-done.wq_ref.wk_ref.wv_ref.w_ref.wf_ref, f32[1,1024]{1,0:T(1,128)} %bitcast.161, ...), custom_call_target="tpu_custom_call", output_to_operand_aliasing={{0}: (3, {})} | custom-call | flops 8589934592 | bytes 16777216 | tf_op jit(solution)/shard_map/inner/pallas_call | solution.py:696
  476.9 16.7 %convolution_convert_fusion.2 = bf16[1280,2048]{1,0:T(8,128)(2,1)} fusion(bf16[2048,1280]{1,0:T(8,128)(2,1)} %get-tuple-element.109.act_ref, bf16[2048,2048]{1,0:T(8,128)(2,1)} %constant_dynamic-update-slice_fusion.7.dy_ref), kind=kOutput, calls=%fused_computation.2 | convolution fusion | flops 10740039680 | bytes 18874368 | tf_op jit(solution)/shard_map/dot_general | solution.py:60
  493.5 41.0 %all-gather.17.cloned.1.call-done.w_ref.wo_ref = bf16[1280,2048]{1,0:T(8,128)(2,1)} async-done(((bf16[1280,512]{1,0:T(8,128)(2,1)}), bf16[1280,2048]{1,0:T(8,128)(2,1)}) %all-gather.17.cloned.1.call-update) | async-done | bytes 5242896 | tf_op jit(solution)/shard_map/all_gather | solution.py:884
  534.5 17.1 %outer_back.2 = (bf16[2048,1792]{1,0:T(8,128)(2,1)}, bf16[2048,256]{1,0:T(8,128)(2,1)}, f32[1,1024]{1,0:T(1,128)}) custom-call(bf16[2048,2048]{1,0:T(8,128)(2,1)} %constant_dynamic-update-slice_fusion.7.dy_ref, bf16[1280,2048]{1,0:T(8,128)(2,1)} %all-gather.17.cloned.1.call-done.w_ref.wo_ref, bf16[1280,2048]{1,0:T(8,128)(2,1)} %all-gather.17.cloned.1.call-done.w_ref.wo_ref, ...), custom_call_target="tpu_custom_call" | custom-call | flops 10737418240 | bytes 16777216 | tf_op jit(solution)/shard_map/outer_back/pallas_call | solution.py:761
  551.5 15.9 %attend_back.2 = (bf16[2048,1792]{1,0:T(8,128)(2,1)}, f32[1,768]{1,0:T(1,128)}) custom-call(bf16[2048,256]{1,0:T(8,128)(2,1)} %get-tuple-element.88.q_ref, bf16[2048,256]{1,0:T(8,128)(2,1)} %get-tuple-element.89.k_ref, bf16[2048,256]{1,0:T(8,128)(2,1)} %get-tuple-element.90.v_ref, s32[1024,1]{1,0:T(8,128)} %bitcast.127, ...), custom_call_target="tpu_custom_call", output_to_operand_aliasing={{0}: (9, {})} | custom-call | flops 5368709120 | bytes 4194304 | tf_op jit(solution)/shard_map/attend_back/pallas_call | solution.py:812
  567.4 21.5 %convolution_convert_fusion = bf16[2048,1792]{1,0:T(8,128)(2,1)} fusion(bf16[2048,2048]{1,0:T(8,128)(2,1)} %constant_dynamic-update-slice_fusion.14.x_ref, bf16[2048,1792]{1,0:T(8,128)(2,1)} %get-tuple-element.99.dz_ref), kind=kOutput, calls=%fused_computation | convolution fusion | flops 15036055552 | bytes 23068672 | tf_op jit(solution)/shard_map/dot_general | solution.py:60
  589.0 12.9 %inward.5 = bf16[1024,2048]{1,0:T(8,128)(2,1)} custom-call(bf16[2048,1792]{1,0:T(8,128)(2,1)} %get-tuple-element.99.dz_ref, bf16[2048,1792]{1,0:T(8,128)(2,1)} %all-gather.15.cloned.1.call-done.wq_ref.wk_ref.wv_ref.w_ref.wf_ref, bf16[2048,1792]{1,0:T(8,128)(2,1)} %all-gather.15.cloned.1.call-done.wq_ref.wk_ref.wv_ref.w_ref.wf_ref, ...), custom_call_target="tpu_custom_call" | custom-call | flops 7516192768 | bytes 11534336 | tf_op jit(solution)/shard_map/inward/pallas_call | solution.py:742
  601.9 12.9 %inward.4.keep_ref = bf16[1024,2048]{1,0:T(8,128)(2,1)} custom-call(bf16[2048,1792]{1,0:T(8,128)(2,1)} %get-tuple-element.99.dz_ref, bf16[2048,1792]{1,0:T(8,128)(2,1)} %all-gather.15.cloned.1.call-done.wq_ref.wk_ref.wv_ref.w_ref.wf_ref, bf16[2048,1792]{1,0:T(8,128)(2,1)} %all-gather.15.cloned.1.call-done.wq_ref.wk_ref.wv_ref.w_ref.wf_ref, ...), custom_call_target="tpu_custom_call" | custom-call | flops 7516192768 | bytes 11534336 | tf_op jit(solution)/shard_map/inward/pallas_call | solution.py:742
  623.0 22.7 %collective-permute-done.34.across_ref = bf16[256,2048]{1,0:T(8,128)(2,1)S(1)} collective-permute-done((bf16[256,2048]{1,0:T(8,128)(2,1)}, bf16[256,2048]{1,0:T(8,128)(2,1)S(1)}, u32[]{:S(2)}, u32[]{:S(2)}) %collective-permute-start.34) | collective-permute-done | bytes 1048608 | tf_op jit(solution)/shard_map/ppermute | solution.py:421
  675.3 21.5 %collective-permute-done.38 = bf16[256,2048]{1,0:T(8,128)(2,1)S(1)} collective-permute-done((bf16[256,2048]{1,0:T(8,128)(2,1)S(1)}, bf16[256,2048]{1,0:T(8,128)(2,1)S(1)}, u32[]{:S(2)}, u32[]{:S(2)}) %collective-permute-start.38) | collective-permute-done | bytes 1048608 | tf_op jit(solution)/shard_map/ppermute | solution.py:421
  699.6 11.9 %collective-permute-done.41 = bf16[128,2048]{1,0:T(8,128)(2,1)S(1)} collective-permute-done((bf16[128,2048]{1,0:T(8,128)(2,1)S(1)}, bf16[128,2048]{1,0:T(8,128)(2,1)S(1)}, u32[]{:S(2)}, u32[]{:S(2)}) %collective-permute-start.41) | collective-permute-done | bytes 524320 | tf_op jit(solution)/shard_map/ppermute | solution.py:421
  721.6 18.4 %outer_back.3 = (bf16[2048,1792]{1,0:T(8,128)(2,1)}, bf16[2048,256]{1,0:T(8,128)(2,1)}, f32[1,1024]{1,0:T(1,128)}) custom-call(bf16[2048,2048]{1,0:T(8,128)(2,1)} %constant_dynamic-update-slice_fusion.21.dy_ref, bf16[1024,2048]{1,0:T(8,128)(2,1)} %all-gather.11.cloned.1.call-done.w_ref, bf16[256,2048]{1,0:T(8,128)(2,1)} %all-gather.13.cloned.1.call-done.wo_ref, ...), custom_call_target="tpu_custom_call" | custom-call | flops 10737418240 | bytes 16777216 | tf_op jit(solution)/shard_map/outer_back/pallas_call | solution.py:761
  740.0 15.8 %attend_back.3 = (bf16[2048,1792]{1,0:T(8,128)(2,1)}, f32[1,768]{1,0:T(1,128)}) custom-call(bf16[2048,256]{1,0:T(8,128)(2,1)} %get-tuple-element.78.q_ref, bf16[2048,256]{1,0:T(8,128)(2,1)} %get-tuple-element.79.k_ref, bf16[2048,256]{1,0:T(8,128)(2,1)} %get-tuple-element.80.v_ref, s32[1024,1]{1,0:T(8,128)} %bitcast.128, ...), custom_call_target="tpu_custom_call", output_to_operand_aliasing={{0}: (9, {})} | custom-call | flops 5368709120 | bytes 4194304 | tf_op jit(solution)/shard_map/attend_back/pallas_call | solution.py:812
  755.8 21.2 %convolution_convert_fusion.1 = bf16[2048,1792]{1,0:T(8,128)(2,1)} fusion(bf16[2048,2048]{1,0:T(8,128)(2,1)} %constant_dynamic-update-slice_fusion.x_ref, bf16[2048,1792]{1,0:T(8,128)(2,1)} %get-tuple-element.115.dz_ref), kind=kOutput, calls=%fused_computation.1 | convolution fusion | flops 15036055552 | bytes 23068672 | tf_op jit(solution)/shard_map/dot_general | solution.py:60
  777.1 14.1 %fusion.4 = bf16[1024,2048]{1,0:T(8,128)(2,1)} fusion(bf16[2048,2048]{1,0:T(8,128)(2,1)} %constant_dynamic-update-slice_fusion.21.dy_ref, bf16[2048,1280]{1,0:T(8,128)(2,1)} %get-tuple-element.82.act_ref), kind=kOutput, calls=%fused_computation.12 | convolution fusion | flops 8592031744 | bytes 16777216 | tf_op jit(solution)/shard_map/dot_general | solution.py:60
  791.2 13.1 %inward.7 = bf16[1024,2048]{1,0:T(8,128)(2,1)} custom-call(bf16[2048,1792]{1,0:T(8,128)(2,1)} %get-tuple-element.115.dz_ref, bf16[2048,1024]{1,0:T(8,128)(2,1)} %all-gather.7.cloned.1.call-done.w_ref.wf_ref, bf16[2048,768]{1,0:T(8,128)(2,1)} %all-gather.9.cloned.1.call-done.wq_ref.wk_ref.wv_ref, ...), custom_call_target="tpu_custom_call" | custom-call | flops 7516192768 | bytes 11534336 | tf_op jit(solution)/shard_map/inward/pallas_call | solution.py:742
  822.4 13.0 %inward.6.keep_ref = bf16[1024,2048]{1,0:T(8,128)(2,1)} custom-call(bf16[2048,1792]{1,0:T(8,128)(2,1)} %get-tuple-element.115.dz_ref, bf16[2048,1024]{1,0:T(8,128)(2,1)} %all-gather.7.cloned.1.call-done.w_ref.wf_ref, bf16[2048,768]{1,0:T(8,128)(2,1)} %all-gather.9.cloned.1.call-done.wq_ref.wk_ref.wv_ref, ...), custom_call_target="tpu_custom_call" | custom-call | flops 7516192768 | bytes 11534336 | tf_op jit(solution)/shard_map/inward/pallas_call | solution.py:742
  910.7 12.6 %collective-permute-done.64 = f32[3584]{0:T(1024)S(1)} collective-permute-done((f32[3584]{0:T(1024)S(1)}, f32[3584]{0:T(1024)S(1)}, u32[]{:S(2)}, u32[]{:S(2)}) %collective-permute-start.64) | collective-permute-done | bytes 14368 | tf_op jit(solution)/shard_map/ppermute | solution.py:421
  963.0 31.7 %collective-permute-done.49 = bf16[256,2048]{1,0:T(8,128)(2,1)} collective-permute-done((bf16[256,2048]{1,0:T(8,128)(2,1)}, bf16[256,2048]{1,0:T(8,128)(2,1)}, u32[]{:S(2)}, u32[]{:S(2)}) %collective-permute-start.49) | collective-permute-done | bytes 1048608 | tf_op jit(solution)/shard_map/ppermute | solution.py:1024
  1030.5 19.5 %collective-permute-done.66 = bf16[1024,512]{1,0:T(8,128)(2,1)S(1)} collective-permute-done((bf16[1024,512]{1,0:T(8,128)(2,1)}, bf16[1024,512]{1,0:T(8,128)(2,1)S(1)}, u32[]{:S(2)}, u32[]{:S(2)}) %collective-permute-start.66) | collective-permute-done | bytes 1048608 | tf_op jit(solution)/shard_map/ppermute | solution.py:1021
  (462 shorter events, 456.1 us)
Async XLA Ops:
  7.2 221.0 %all-gather.9.cloned.1.call-start = ((), (), s32[]{:S(2)}) async-start(), calls=%async_computation.6 | async-start | bytes 3932160 | tf_op jit(solution)/shard_map/all_gather | solution.py:884
  47.0 205.4 %all-gather.7.cloned.1.call-start = ((), (), s32[]{:S(2)}) async-start(), calls=%async_computation.5 | async-start | bytes 5242880 | tf_op jit(solution)/shard_map/all_gather | solution.py:884
  76.0 193.2 %all-gather.13.cloned.1.call-start = ((), (), s32[]{:S(2)}) async-start(), calls=%async_computation.8 | async-start | bytes 1310720 | tf_op jit(solution)/shard_map/all_gather | solution.py:884
  106.6 196.7 %all-gather.11.cloned.1.call-start = ((), (), s32[]{:S(2)}) async-start(), calls=%async_computation.7 | async-start | bytes 5242880 | tf_op jit(solution)/shard_map/all_gather | solution.py:884
  136.4 299.8 %all-gather.15.cloned.1.call-start = ((), (), s32[]{:S(2)}) async-start(), calls=%async_computation.9 | async-start | bytes 9175040 | tf_op jit(solution)/shard_map/all_gather | solution.py:884
  162.0 27.7 %collective-permute-start.13 = (bf16[256,2048]{1,0:T(8,128)(2,1)}, bf16[256,2048]{1,0:T(8,128)(2,1)}, u32[]{:S(2)}, u32[]{:S(2)}) collective-permute-start(bf16[256,2048]{1,0:T(8,128)(2,1)} %get-tuple-element.76), channel_id=1, source_target_pairs={{0,16},{16,0},{1,17},{17,1},{2,18},{18,2},{3,19},{19,3},{4,20},{20... | collective-permute-start | bytes 3145736 | tf_op jit(solution)/shard_map/ppermute | solution.py:421
  170.2 28.1 %collective-permute-start.19 = (f32[5632]{0:T(1024)S(1)}, f32[5632]{0:T(1024)S(1)}, u32[]{:S(2)}, u32[]{:S(2)}) collective-permute-start(f32[5632]{0:T(1024)S(1)} %pad_maximum_fusion.10), channel_id=1, source_target_pairs={{0,4},{4,0},{8,12},{12,8},{1,5},{5,1},{9,13},{13,9},{2,6},{6,2},{1... | collective-permute-start | bytes 67592 | tf_op jit(solution)/shard_map/ppermute | solution.py:421
  210.9 323.6 %all-gather.17.cloned.1.call-start = ((), (), s32[]{:S(2)}) async-start(), calls=%async_computation.10 | async-start | bytes 6553600 | tf_op jit(solution)/shard_map/all_gather | solution.py:884
  382.2 26.5 %collective-permute-start.29 = (bf16[256,2048]{1,0:T(8,128)(2,1)}, bf16[256,2048]{1,0:T(8,128)(2,1)S(1)}, u32[]{:S(2)}, u32[]{:S(2)}) collective-permute-start(bf16[256,2048]{1,0:T(8,128)(2,1)} %get-tuple-element.145), channel_id=1, source_target_pairs={{0,16},{16,0},{1,17},{17,1},{2,18},{18,2},{3,19},{19,3},{4,20},{20... | collective-permute-start | bytes 3145736 | tf_op jit(solution)/shard_map/ppermute | solution.py:421
  384.9 539.2 %reduce-scatter.8.cloned.1.call-start = ((), (), s32[]{:S(2)}) async-start(), calls=%async_computation.12 | async-start | bytes 9175040 | tf_op jit(solution)/shard_map/reduce_scatter | solution.py:981
  588.9 354.1 %reduce-scatter.14.cloned.1.call-start = ((), (), s32[]{:S(2)}) async-start(), calls=%async_computation.15 | async-start | bytes 6553600 | tf_op jit(solution)/shard_map/reduce_scatter | solution.py:981
  656.6 302.1 %reduce-scatter.6.cloned.1.call-start = ((), (), s32[]{:S(2)}) async-start(), calls=%async_computation.11 | async-start | bytes 9175040 | tf_op jit(solution)/shard_map/reduce_scatter | solution.py:981
  777.0 246.3 %reduce-scatter.12.cloned.1.call-start = ((), (), s32[]{:S(2)}) async-start(), calls=%async_computation.14 | async-start | bytes 5242880 | tf_op jit(solution)/shard_map/reduce_scatter | solution.py:981
  791.2 262.2 %reduce-scatter.10.cloned.1.call-start = ((), (), s32[]{:S(2)}) async-start(), calls=%async_computation.13 | async-start | bytes 1310720 | tf_op jit(solution)/shard_map/reduce_scatter | solution.py:981
  804.3 31.1 %collective-permute-start.51 = (bf16[1024,2048]{1,0:T(8,128)(2,1)}, bf16[1024,2048]{1,0:T(8,128)(2,1)}, u32[]{:S(2)}, u32[]{:S(2)}) collective-permute-start(bf16[1024,2048]{1,0:T(8,128)(2,1)} %inward.7), channel_id=1, source_target_pairs={{0,1},{1,0},{2,3},{3,2},{4,5},{5,4},{6,7},{7,6},{8,9},{9,8},{10,11... | collective-permute-start | bytes 12582920 | tf_op jit(solution)/shard_map/ppermute | solution.py:421
  814.9 40.4 %collective-permute-start.44 = (bf16[1024,2048]{1,0:T(8,128)(2,1)}, bf16[1024,2048]{1,0:T(8,128)(2,1)}, u32[]{:S(2)}, u32[]{:S(2)}) collective-permute-start(bf16[1024,2048]{1,0:T(8,128)(2,1)} %outer.7), channel_id=1, source_target_pairs={{0,1},{1,0},{2,3},{3,2},{4,5},{5,4},{6,7},{7,6},{8,9},{9,8},{10,11... | collective-permute-start | bytes 12582920 | tf_op jit(solution)/shard_map/ppermute | solution.py:421
  841.3 26.3 %collective-permute-start.53 = (bf16[256,2048]{1,0:T(8,128)(2,1)}, bf16[256,2048]{1,0:T(8,128)(2,1)}, u32[]{:S(2)}, u32[]{:S(2)}) collective-permute-start(bf16[256,2048]{1,0:T(8,128)(2,1)} %get-tuple-element.117), channel_id=1, source_target_pairs={{0,2},{1,3},{2,0},{3,1},{4,6},{5,7},{6,4},{7,5},{8,10},{9,11},{10,... | collective-permute-start | bytes 3145736 | tf_op jit(solution)/shard_map/ppermute | solution.py:421
  853.0 31.0 %collective-permute-start.63 = (f32[7680]{0:T(1024)S(1)}, f32[7680]{0:T(1024)S(1)}, u32[]{:S(2)}, u32[]{:S(2)}) collective-permute-start(f32[7680]{0:T(1024)S(1)} %add.259), channel_id=1, source_target_pairs={{0,8},{4,12},{8,0},{12,4},{1,9},{5,13},{9,1},{13,5},{2,10},{6,14},... | collective-permute-start | bytes 92168 | tf_op jit(solution)/shard_map/ppermute | solution.py:421
  860.4 29.0 %collective-permute-start.45 = (bf16[256,2048]{1,0:T(8,128)(2,1)}, bf16[256,2048]{1,0:T(8,128)(2,1)}, u32[]{:S(2)}, u32[]{:S(2)}) collective-permute-start(bf16[256,2048]{1,0:T(8,128)(2,1)} %get-tuple-element.110), channel_id=1, source_target_pairs={{0,16},{16,0},{1,17},{17,1},{2,18},{18,2},{3,19},{19,3},{4,20},{20... | collective-permute-start | bytes 3145736 | tf_op jit(solution)/shard_map/ppermute | solution.py:421
  861.9 28.2 %collective-permute-start.46 = (bf16[256,2048]{1,0:T(8,128)(2,1)}, bf16[256,2048]{1,0:T(8,128)(2,1)}, u32[]{:S(2)}, u32[]{:S(2)}) collective-permute-start(bf16[256,2048]{1,0:T(8,128)(2,1)} %get-tuple-element.111), channel_id=1, source_target_pairs={{0,2},{1,3},{2,0},{3,1},{4,6},{5,7},{6,4},{7,5},{8,10},{9,11},{10,... | collective-permute-start | bytes 3145736 | tf_op jit(solution)/shard_map/ppermute | solution.py:421
  873.8 27.6 %collective-permute-start.54 = (bf16[128,2048]{1,0:T(8,128)(2,1)}, bf16[128,2048]{1,0:T(8,128)(2,1)}, u32[]{:S(2)}, u32[]{:S(2)}) collective-permute-start(bf16[128,2048]{1,0:T(8,128)(2,1)} %get-tuple-element.119), channel_id=1, source_target_pairs={{0,2},{1,3},{2,0},{3,1},{4,6},{5,7},{6,4},{7,5},{8,10},{9,11},{10,... | collective-permute-start | bytes 1572872 | tf_op jit(solution)/shard_map/ppermute | solution.py:421
  875.7 26.9 %collective-permute-start.55 = (bf16[128,2048]{1,0:T(8,128)(2,1)}, bf16[128,2048]{1,0:T(8,128)(2,1)}, u32[]{:S(2)}, u32[]{:S(2)}) collective-permute-start(bf16[128,2048]{1,0:T(8,128)(2,1)} %get-tuple-element.120), channel_id=1, source_target_pairs={{0,16},{16,0},{1,17},{17,1},{2,18},{18,2},{3,19},{19,3},{4,20},{20... | collective-permute-start | bytes 1572872 | tf_op jit(solution)/shard_map/ppermute | solution.py:421
  884.0 44.2 %collective-permute-start.50 = (bf16[256,2048]{1,0:T(8,128)(2,1)S(1)}, bf16[256,2048]{1,0:T(8,128)(2,1)}, u32[]{:S(2)}, u32[]{:S(2)}) collective-permute-start(bf16[256,2048]{1,0:T(8,128)(2,1)S(1)} %get-tuple-element.147), channel_id=1, source_target_pairs={{0,16},{16,0},{1,17},{17,1},{2,18},{18,2},{3,19},{19,3},{4,20},{20... | collective-permute-start | bytes 3145736 | tf_op jit(solution)/shard_map/ppermute | solution.py:421
  889.4 34.0 %collective-permute-start.64 = (f32[3584]{0:T(1024)S(1)}, f32[3584]{0:T(1024)S(1)}, u32[]{:S(2)}, u32[]{:S(2)}) collective-permute-start(f32[3584]{0:T(1024)S(1)} %slice.221), channel_id=1, source_target_pairs={{0,16},{16,0},{1,17},{17,1},{2,18},{18,2},{3,19},{19,3},{4,20},{20... | collective-permute-start | bytes 43016 | tf_op jit(solution)/shard_map/ppermute | solution.py:421
  896.1 32.1 %collective-permute-start.47 = (bf16[128,2048]{1,0:T(8,128)(2,1)}, bf16[128,2048]{1,0:T(8,128)(2,1)}, u32[]{:S(2)}, u32[]{:S(2)}) collective-permute-start(bf16[128,2048]{1,0:T(8,128)(2,1)} %get-tuple-element.113), channel_id=1, source_target_pairs={{0,2},{1,3},{2,0},{3,1},{4,6},{5,7},{6,4},{7,5},{8,10},{9,11},{10,... | collective-permute-start | bytes 1572872 | tf_op jit(solution)/shard_map/ppermute | solution.py:421
  901.3 33.3 %collective-permute-start.48 = (bf16[128,2048]{1,0:T(8,128)(2,1)}, bf16[128,2048]{1,0:T(8,128)(2,1)}, u32[]{:S(2)}, u32[]{:S(2)}) collective-permute-start(bf16[128,2048]{1,0:T(8,128)(2,1)} %get-tuple-element.114), channel_id=1, source_target_pairs={{0,16},{16,0},{1,17},{17,1},{2,18},{18,2},{3,19},{19,3},{4,20},{20... | collective-permute-start | bytes 1572872 | tf_op jit(solution)/shard_map/ppermute | solution.py:421
  909.4 46.9 %collective-permute-start.56 = (bf16[256,2048]{1,0:T(8,128)(2,1)}, bf16[256,2048]{1,0:T(8,128)(2,1)}, u32[]{:S(2)}, u32[]{:S(2)}) collective-permute-start(bf16[256,2048]{1,0:T(8,128)(2,1)} %get-tuple-element.141), channel_id=1, source_target_pairs={{16,0},{17,1},{18,2},{19,3},{20,4},{21,5},{22,6},{23,7},{24,8},{25... | collective-permute-start | bytes 3145736 | tf_op jit(solution)/shard_map/ppermute | solution.py:1021
  924.1 72.3 %collective-permute-start.57 = (bf16[512,1792]{1,0:T(8,128)(2,1)}, bf16[512,1792]{1,0:T(8,128)(2,1)}, u32[]{:S(2)}, u32[]{:S(2)}) collective-permute-start(bf16[512,1792]{1,0:T(8,128)(2,1)} %reduce-scatter.8.cloned.1.call-done), channel_id=1, source_target_pairs={{0,16},{1,17},{2,18},{3,19},{4,20},{5,21},{6,22},{7,23},{8,24},{9,... | collective-permute-start | bytes 5505032 | tf_op jit(solution)/shard_map/ppermute | solution.py:1024
  939.0 55.7 %collective-permute-start.49 = (bf16[256,2048]{1,0:T(8,128)(2,1)}, bf16[256,2048]{1,0:T(8,128)(2,1)}, u32[]{:S(2)}, u32[]{:S(2)}) collective-permute-start(bf16[256,2048]{1,0:T(8,128)(2,1)} %get-tuple-element.143), channel_id=1, source_target_pairs={{0,16},{1,17},{2,18},{3,19},{4,20},{5,21},{6,22},{7,23},{8,24},{9,... | collective-permute-start | bytes 3145736 | tf_op jit(solution)/shard_map/ppermute | solution.py:1024
  943.0 81.6 %collective-permute-start.65 = (bf16[1280,512]{1,0:T(8,128)(2,1)}, bf16[1280,512]{1,0:T(8,128)(2,1)}, u32[]{:S(2)}, u32[]{:S(2)}) collective-permute-start(bf16[1280,512]{1,0:T(8,128)(2,1)} %reduce-scatter.14.cloned.1.call-done), channel_id=1, source_target_pairs={{0,16},{1,17},{2,18},{3,19},{4,20},{5,21},{6,22},{7,23},{8,24},{9,... | collective-permute-start | bytes 3932168 | tf_op jit(solution)/shard_map/ppermute | solution.py:1024
  958.7 43.3 %collective-permute-start.58 = (bf16[512,1792]{1,0:T(8,128)(2,1)}, bf16[512,1792]{1,0:T(8,128)(2,1)S(1)}, u32[]{:S(2)}, u32[]{:S(2)}) collective-permute-start(bf16[512,1792]{1,0:T(8,128)(2,1)} %reduce-scatter.6.cloned.1.call-done), channel_id=1, source_target_pairs={{16,0},{17,1},{18,2},{19,3},{20,4},{21,5},{22,6},{23,7},{24,8},{25... | collective-permute-start | bytes 5505032 | tf_op jit(solution)/shard_map/ppermute | solution.py:1021
  1023.3 26.7 %collective-permute-start.66 = (bf16[1024,512]{1,0:T(8,128)(2,1)}, bf16[1024,512]{1,0:T(8,128)(2,1)S(1)}, u32[]{:S(2)}, u32[]{:S(2)}) collective-permute-start(bf16[1024,512]{1,0:T(8,128)(2,1)} %reduce-scatter.12.cloned.1.call-done), channel_id=1, source_target_pairs={{16,0},{17,1},{18,2},{19,3},{20,4},{21,5},{22,6},{23,7},{24,8},{25... | collective-permute-start | bytes 3145736 | tf_op jit(solution)/shard_map/ppermute | solution.py:1021
  (108 other events, 1716.3 us)
Sparse Core Ops, SparseCore 0:
  47.1 63.7 all-gather.8
  113.1 79.3 all-gather.6
  194.0 27.0 all-gather.12
  223.1 80.1 all-gather.10
  305.2 130.9 all-gather.14
  438.2 96.2 all-gather.16
  589.1 126.1 reduce-scatter.7
  717.5 94.3 reduce-scatter.13
  814.2 129.6 reduce-scatter.5
  946.0 77.2 reduce-scatter.11
  1025.6 27.7 reduce-scatter.9

commit v3 on v2

--- a/solution.py
+++ b/solution.py
@@ -448,12 +448,11 @@
     half = block.shape[0] // 2
     across = swap(block, SECTION, 1)
     beside = swap(block, COL, 2)
-    corner = jnp.concatenate(
-        [swap(beside[:half], SECTION, 1), swap(across[half:], COL, 2)], axis=0
-    )
+    corner = jnp.concatenate([swap(beside[:half], SECTION, 1), swap(across[half:], COL, 2)], axis=0)
     near = jnp.concatenate([block, beside], axis=0)
     far = jnp.concatenate([across, corner], axis=0)
-    return jnp.concatenate([near, swap(near, COL, 1), far, swap(far, COL, 1)], axis=0), across
+    near_other, far_other = (swap(near, COL, 1), swap(far, COL, 1))
+    return jnp.concatenate([near, near_other, far, far_other], axis=0), across
 
 
 def pair_sum(keep_ref, came_ref, start, size):
@@ -562,7 +561,7 @@
     out_ref[...] = total.astype(BF16)
 
 
-def outer_back_kernel(dy_ref, w_ref, wo_ref, slope_ref, dz_ref, do_ref, sum_ref):
+def outer_back_kernel(dy_ref, w_ref, wo_ref, slope_ref, dz_ref, do_ref, sum_ref, dy_sum_ref):
     dy = dy_ref[...]
     dz = (contract_cols(dy, w_ref[...]) * slope_ref[...].astype(F32)).astype(BF16)
     dz_ref[...] = dz
@@ -571,8 +570,10 @@
     @pl.when(pl.program_id(0) == 0)
     def _():
         sum_ref[...] = jnp.zeros_like(sum_ref)
+        dy_sum_ref[...] = jnp.zeros_like(dy_sum_ref)
 
     sum_ref[...] += jnp.sum(dz.astype(F32), axis=0, keepdims=True)
+    dy_sum_ref[...] += jnp.sum(dy.astype(F32), axis=0, keepdims=True)
 
 
 def inward_kernel(dz_ref, wf_ref, wq_ref, wk_ref, wv_ref, out_ref):
@@ -762,11 +763,12 @@
         outer_back_kernel,
         grid=(rows // ROW_BLOCK,),
         in_specs=[by_rows(width), *outer_panels(pair, inner), by_rows(inner)],
-        out_specs=[by_rows(inner), by_rows(HD), whole((1, inner))],
+        out_specs=[by_rows(inner), by_rows(HD), whole((1, inner)), whole((1, width))],
         out_shape=[
             dz,
             jax.ShapeDtypeStruct((rows, HD), BF16),
             jax.ShapeDtypeStruct((1, inner), F32),
+            jax.ShapeDtypeStruct((1, width), F32),
         ],
         cost_estimate=cost(2 * rows * width * (inner + HD), dy, slopes, slopes),
         name="outer_back",
@@ -893,11 +895,12 @@
         ]
     )
     held_both = jnp.stack([held, swap(held, SECTION, 1)])
-    out_half = trade(out_w, 0, held_both)
-    qkv_half = trade(qkv_w, 1, out_half[1])
-    qkv_half = tuple(member.reshape(deep, per) for member in qkv_half)
+    qkv_flat = qkv_w.reshape(deep, -1)
+    qkv_half = trade(qkv_flat, 1, held_both)
     fc_in_half = trade(fc_in_w, 1, qkv_half[1])
-    fc_out_half = trade(fc_out_w, 0, fc_in_half[1])
+    outs_kept = jnp.concatenate([take(fc_out_w, 0, s, inner), take(out_w, 0, s, HD)], axis=0)
+    outs_sent = jnp.concatenate([take(fc_out_w, 0, 1 - s, inner), take(out_w, 0, 1 - s, HD)], axis=0)
+    outs_came = swap(after(outs_sent, fc_in_half[1]), SECTION, 1)
     held_both = sum_over(place(held_both, 2, c, deep), COL)
     held = held_both[0]
     gain_one, shift_one, gain_two, shift_two, end_bias = (held[i] for i in range(5))
@@ -909,19 +912,16 @@
             for part, gain in zip(both_layers(*half), gains)
         )
 
-    out_pair = both_layers(*out_half)
     qkv_pair = scaled_pair(qkv_half, 0)
     fc_in_pair = scaled_pair(fc_in_half, 2)
-    fc_out_pair = both_layers(*fc_out_half)
-    w_out0 = gathered(out_pair[0], 1)
+    outs_pair = both_layers(outs_kept, outs_came)
     w_qkv0 = gathered(qkv_pair[0], 0)
     w_fc_in0 = gathered(fc_in_pair[0], 0)
-    w_fc_out0 = gathered(fc_out_pair[0], 1)
+    w_outs0 = gathered(outs_pair[0], 1)
     w_ins1 = gathered(jnp.concatenate([fc_in_pair[1], qkv_pair[1]], axis=1), 0)
-    w_outs1 = gathered(jnp.concatenate([fc_out_pair[1], out_pair[1]], axis=0), 1)
+    w_outs1 = gathered(outs_pair[1], 1)
     w_ins = ((w_fc_in0, w_qkv0, 0), (w_ins1, w_ins1, inner))
-    w_outs = (((w_fc_out0, 0), (w_out0, 0)), ((w_outs1, 0), (w_outs1, inner)))
-    qkv_flat = qkv_w.reshape(deep, -1)
+    w_outs = tuple(((member, 0), (member, inner)) for member in (w_outs0, w_outs1))
 
     own_qkv = mm(shift_one.astype(BF16)[None], qkv_flat)[0]
     own_fc = mm(shift_two.astype(BF16)[None], fc_in_w)[0]
@@ -951,7 +951,7 @@
 
     hidden = lax.dynamic_index_in_dim(inputs, s, 0, keepdims=False)
     seed = lax.dynamic_index_in_dim(cotangent, s, 0, keepdims=False)
-    hidden = after(hidden, fc_out_half[1])
+    hidden = after(hidden, outs_came)
 
     hidden_list, kept_list, ends = ([], [], [])
     seed_rows = None
@@ -991,8 +991,7 @@
         else:
             dy, across = gather_rows(grads)
             middle_grads = (jnp.where(low, grads, across), jnp.where(low, across, grads))
-        dy_sum = jnp.sum(grads.astype(F32), axis=0)
-        dz, grad_attended, inner_sum = outer_back(dy, w_outs[layer], slopes)
+        dz, grad_attended, inner_sum, dy_sum = outer_back(dy, w_outs[layer], slopes)
         dz, heads_sum = attend_back(
             queries, keys_all, values_all, places, log_sums, grad_attended, tables, dz
         )
@@ -1006,12 +1005,13 @@
             - scaled * jnp.mean(combined * scaled, axis=-1, keepdims=True)
         )
         grads = (grads.astype(F32) + grad_norm).astype(BF16)
-        small_list[layer] = (heads_sum[0], inner_sum[0], dy_sum)
+        small_list[layer] = (heads_sum[0], inner_sum[0], dy_sum[0])
         if layer == 0:
             fc_out_part0 = reduced(contract_rows(act[:, :inner], dy).astype(BF16), 1)
             out_part0 = reduced(contract_rows(act[:, inner:], dy).astype(BF16), 1)
-    act = after(kept_list[1][-1], small_list[0][0])
+    act = kept_list[1][-1]
     summed = scatter_rows(lambda other: outer(act, w_outs[1], other))
+    summed = after(summed, small_list[0][0])
     ends.append((hidden_list[1].astype(F32) + summed + end_e[1]).astype(BF16))
 
     def to_owner(first, second, upper, lower):
@@ -1023,15 +1023,14 @@
     def to_second(value):
         return lax.ppermute(value, SECTION, [(0, 1)])
 
-    ends_sum = jnp.concatenate([member[2] for member in small_list])
-    ends_sum = sum_over(sum_over(ends_sum, SECTION), COL)
     small = sum_over(
-        jnp.concatenate([*small_list[0][:2], *small_list[1][:2], ends_sum]), ROW
+        jnp.concatenate(
+            [*small_list[0][:2], *small_list[1][:2], small_list[0][2], small_list[1][2]]
+        ),
+        ROW,
     )
     sums = small[: 2 * (per + inner)]
-    smalls = to_owner(
-        *jnp.split(sums, 2), *jnp.split(swap(sums, SECTION, 1), 2)
-    )
+    smalls = to_owner(*jnp.split(sums, 2), *jnp.split(swap(sums, SECTION, 1), 2))
     end_grad = jnp.where(low, *jnp.split(small[2 * (per + inner) :], 2))
     qkv_b_grad = jnp.concatenate([member[:per] for member in smalls])
     fc_in_b_grad = jnp.concatenate([member[per:] for member in smalls])

time: 1080 us -> 1090 us (level)
  waiting for transfers between devices: 446 us -> 464 us
  local copies, waits for them, and re-layouts: 81.7 us -> 67.6 us
    ppermute x63 -> x59, waiting for transfers between devices: 293 us -> 326 us  [swap(): lax.ppermute(value, axis, [(source, source ^ bit) for source in range(cou...]
    ppermute x3, waiting for transfers between devices: 31.7 us -> 17.1 us  [to_second(): return lax.ppermute(value, SECTION, [(0, 1)])]
    all_gather x6 -> x5, waiting for transfers between devices: 79.2 us -> 70.4 us  [gathered(): return lax.all_gather(shard, ROW, axis=axis, tiled=True)]
    unnamed x148 -> x149, local copies, waits for them, and re-layouts: 43.6 us -> 37.3 us
    ppermute x63 -> x59, starting transfers between devices: 60.4 us -> 59.8 us  [swap(): lax.ppermute(value, axis, [(source, source ^ bit) for source in range(cou...]
  transfers between devices with their start and end apart: 81 -> 76, of which waited for: 42 -> 39; matrix products, arithmetic and copies ran while one was open for 20% -> 18% of each run, Pallas kernels for 24% -> 23%
where the time goes in v3:
time: 1090 us; the launch traced here: 1080 us
  waiting for transfers between devices  464 us (43%)
  Pallas kernels  286 us (26%)
  matrix products  82.7 us (8%)
  other arithmetic  80.2 us (7%)
  starting transfers between devices  78.9 us (7%)
  local copies, waits for them, and re-layouts  67.6 us (6%)
  between operations  15.9 us (1%)
    ppermute x59, waiting for transfers between devices, swap(): lax.ppermute(value, axis, [(source, source ^ bit) for source in range(cou...  326 us
    dot_general x5, matrix products, contract_rows(): lax.dot_general(first_operand, second_operand, (((0,), (0,)), ((), ())),...  80.6 us
    all_gather x5, waiting for transfers between devices, gathered(): return lax.all_gather(shard, ROW, axis=axis, tiled=True)  70.4 us
    ppermute x59, starting transfers between devices, swap(): lax.ppermute(value, axis, [(source, source ^ bit) for source in range(cou...  59.8 us
    pallas_call x4, Pallas kernels, inward(): pl.pallas_call(inward_kernel, grid=(rows // ROW_BLOCK,), in_specs=[split_...  51.8 us
    ppermute x4, waiting for transfers between devices, to_first(): return lax.ppermute(value, SECTION, [(1, 0)])  50.7 us
    pallas_call x8, Pallas kernels, column_call(): pl.pallas_call(kernel, grid=(width // tile,), in_specs=[spec(member.shape...  44.6 us
    pallas_call x4, Pallas kernels, outer(): pl.pallas_call(outer_kernel, grid=(rows // ROW_BLOCK,), in_specs=[split_r...  40 us
  transfers between devices with their start and end apart: 76, of which 39 were waited for; matrix products, arithmetic and copies ran while one was open for 18% of the time, Pallas kernels for 23%

profile of v3, /device:TPU:0, one launch (start us, length us, event | category | flops | bytes accessed | tf_op | source)
XLA Modules:
  0.0 1075.4 jit_solution(4578287452465851602)
XLA Ops:
  14.7 17.5 %collective-permute-done = f32[5,128]{1,0:T(8,128)S(1)} collective-permute-done((f32[5,128]{1,0:T(8,128)S(1)}, f32[5,128]{1,0:T(8,128)S(1)}, u32[]{:S(2)}, u32[]{:S(2)}) %collective-permute-start) | collective-permute-done | bytes 2592 | tf_op jit(solution)/shard_map/ppermute | solution.py:421
  43.6 22.4 %collective-permute-done.2 = bf16[512,1024]{1,0:T(8,128)(2,1)} collective-permute-done((bf16[512,1024]{1,0:T(8,128)(2,1)S(1)}, bf16[512,1024]{1,0:T(8,128)(2,1)}, u32[]{:S(2)}, u32[]{:S(2)}) %collective-permute-start.2) | collective-permute-done | bytes 1048608 | tf_op jit(solution)/shard_map/ppermute | solution.py:421
  75.2 27.4 %collective-permute-done.3 = bf16[1280,512]{1,0:T(8,128)(2,1)} collective-permute-done((bf16[1280,512]{1,0:T(8,128)(2,1)}, bf16[1280,512]{1,0:T(8,128)(2,1)}, u32[]{:S(2)}, u32[]{:S(2)}) %collective-permute-start.3) | collective-permute-done | bytes 1310752 | tf_op jit(solution)/shard_map/ppermute | solution.py:421
  111.6 15.9 %collective-permute-done.4 = bf16[256,2048]{1,0:T(8,128)(2,1)S(1)} collective-permute-done((bf16[256,2048]{1,0:T(8,128)(2,1)}, bf16[256,2048]{1,0:T(8,128)(2,1)S(1)}, u32[]{:S(2)}, u32[]{:S(2)}) %collective-permute-start.4) | collective-permute-done | bytes 1048608 | tf_op jit(solution)/shard_map/ppermute | solution.py:421
  160.3 18.4 %collective-permute-done.10 = bf16[256,2048]{1,0:T(8,128)(2,1)} collective-permute-done((bf16[256,2048]{1,0:T(8,128)(2,1)}, bf16[256,2048]{1,0:T(8,128)(2,1)}, u32[]{:S(2)}, u32[]{:S(2)}) %collective-permute-start.10) | collective-permute-done | bytes 1048608 | tf_op jit(solution)/shard_map/ppermute | solution.py:421
  219.8 12.8 %project.2 = (bf16[2048,256]{1,0:T(8,128)(2,1)}, bf16[2048,256]{1,0:T(8,128)(2,1)}, bf16[2048,256]{1,0:T(8,128)(2,1)}) custom-call(bf16[2048,2048]{1,0:T(8,128)(2,1)} %copy-done.32, bf16[2048,768]{1,0:T(8,128)(2,1)} %all-gather.8.cloned.1.call-done.wq_ref.wk_ref.wv_ref, bf16[2048,768]{1,0:T(8,128)(2,1)} %all-gather.8.cloned.1.call-done.wq_ref.wk_ref.wv_ref, ...), custom_call_target="tpu_custom_call" | custom-call | flops 6442450944 | bytes 11534336 | tf_op jit(solution)/shard_map/project/pallas_call | solution.py:682
  243.4 16.8 %inner.2 = (bf16[2048,1280]{1,0:T(8,128)(2,1)}, bf16[2048,1024]{1,0:T(8,128)(2,1)}) custom-call(bf16[2048,2048]{1,0:T(8,128)(2,1)} %copy-done.32, bf16[2048,1024]{1,0:T(8,128)(2,1)} %all-gather.6.cloned.1.call-done.w_ref.wf_ref, f32[1,1024]{1,0:T(1,128)} %bitcast.153, bf16[2048,1280]{1,0:T(8,128)(2,1)} %get-tuple-element.81.held_ref), custom_call_target="tpu_custom_call", output_to_operand_aliasing={{0}: (3, {})} | custom-call | flops 8589934592 | bytes 16777216 | tf_op jit(solution)/shard_map/inner/pallas_call | solution.py:697
  260.2 26.1 %all-gather.10.cloned.1.call-done.w_ref.wo_ref = bf16[1280,2048]{1,0:T(8,128)(2,1)} async-done(((bf16[1280,512]{1,0:T(8,128)(2,1)}), bf16[1280,2048]{1,0:T(8,128)(2,1)}) %all-gather.10.cloned.1.call-update) | async-done | bytes 5242896 | tf_op jit(solution)/shard_map/all_gather | solution.py:886
  314.6 22.8 %collective-permute-done.22.across_ref = bf16[256,2048]{1,0:T(8,128)(2,1)S(1)} collective-permute-done((bf16[256,2048]{1,0:T(8,128)(2,1)}, bf16[256,2048]{1,0:T(8,128)(2,1)S(1)}, u32[]{:S(2)}, u32[]{:S(2)}) %collective-permute-start.22) | collective-permute-done | bytes 1048608 | tf_op jit(solution)/shard_map/ppermute | solution.py:421
  366.7 21.6 %collective-permute-done.26 = bf16[256,2048]{1,0:T(8,128)(2,1)S(1)} collective-permute-done((bf16[256,2048]{1,0:T(8,128)(2,1)}, bf16[256,2048]{1,0:T(8,128)(2,1)S(1)}, u32[]{:S(2)}, u32[]{:S(2)}) %collective-permute-start.26) | collective-permute-done | bytes 1048608 | tf_op jit(solution)/shard_map/ppermute | solution.py:421
  419.2 13.3 %project.3 = (bf16[2048,256]{1,0:T(8,128)(2,1)}, bf16[2048,256]{1,0:T(8,128)(2,1)}, bf16[2048,256]{1,0:T(8,128)(2,1)}) custom-call(bf16[2048,2048]{1,0:T(8,128)(2,1)} %constant_dynamic-update-slice_fusion.14.x_ref, bf16[2048,1792]{1,0:T(8,128)(2,1)} %all-gather.12.cloned.1.call-done.wq_ref.wk_ref.wv_ref.w_ref.wf_ref, ...), custom_call_target="tpu_custom_call" | custom-call | flops 6442450944 | bytes 11534336 | tf_op jit(solution)/shard_map/project/pallas_call | solution.py:682
  443.3 16.7 %inner.3 = (bf16[2048,1280]{1,0:T(8,128)(2,1)}, bf16[2048,1024]{1,0:T(8,128)(2,1)}) custom-call(bf16[2048,2048]{1,0:T(8,128)(2,1)} %constant_dynamic-update-slice_fusion.14.x_ref, bf16[2048,1792]{1,0:T(8,128)(2,1)} %all-gather.12.cloned.1.call-done.wq_ref.wk_ref.wv_ref.w_ref.wf_ref, f32[1,1024]{1,0:T(1,128)} %bitcast.154, ...), custom_call_target="tpu_custom_call", output_to_operand_aliasing={{0}: (3, {})} | custom-call | flops 8589934592 | bytes 16777216 | tf_op jit(solution)/shard_map/inner/pallas_call | solution.py:697
  460.0 16.6 %convolution_convert_fusion.2 = bf16[1280,2048]{1,0:T(8,128)(2,1)} fusion(bf16[2048,1280]{1,0:T(8,128)(2,1)} %get-tuple-element.92.act_ref, bf16[2048,2048]{1,0:T(8,128)(2,1)} %constant_dynamic-update-slice_fusion.7.dy_ref), kind=kOutput, calls=%fused_computation.2 | convolution fusion | flops 10740039680 | bytes 18874368 | tf_op jit(solution)/shard_map/dot_general | solution.py:60
  476.6 40.2 %all-gather.14.cloned.1.call-done.w_ref.wo_ref = bf16[1280,2048]{1,0:T(8,128)(2,1)} async-done(((bf16[1280,512]{1,0:T(8,128)(2,1)}), bf16[1280,2048]{1,0:T(8,128)(2,1)}) %all-gather.14.cloned.1.call-update) | async-done | bytes 5242896 | tf_op jit(solution)/shard_map/all_gather | solution.py:886
  516.8 18.2 %outer_back.2 = (bf16[2048,1792]{1,0:T(8,128)(2,1)}, bf16[2048,256]{1,0:T(8,128)(2,1)}, f32[1,1024]{1,0:T(1,128)}, f32[1,2048]{1,0:T(1,128)}) custom-call(bf16[2048,2048]{1,0:T(8,128)(2,1)} %constant_dynamic-update-slice_fusion.7.dy_ref, bf16[1280,2048]{1,0:T(8,128)(2,1)} %all-gather.14.cloned.1.call-done.w_ref.wo_ref, ...), custom_call_target="tpu_custom_call" | custom-call | flops 10737418240 | bytes 16777216 | tf_op jit(solution)/shard_map/outer_back/pallas_call | solution.py:762
  535.0 15.9 %attend_back.2 = (bf16[2048,1792]{1,0:T(8,128)(2,1)}, f32[1,768]{1,0:T(1,128)}) custom-call(bf16[2048,256]{1,0:T(8,128)(2,1)} %get-tuple-element.88.q_ref, bf16[2048,256]{1,0:T(8,128)(2,1)} %get-tuple-element.89.k_ref, bf16[2048,256]{1,0:T(8,128)(2,1)} %get-tuple-element.90.v_ref, s32[1024,1]{1,0:T(8,128)} %bitcast.118, ...), custom_call_target="tpu_custom_call", output_to_operand_aliasing={{0}: (9, {})} | custom-call | flops 5368709120 | bytes 4194304 | tf_op jit(solution)/shard_map/attend_back/pallas_call | solution.py:814
  551.0 21.7 %convolution_convert_fusion = bf16[2048,1792]{1,0:T(8,128)(2,1)} fusion(bf16[2048,2048]{1,0:T(8,128)(2,1)} %constant_dynamic-update-slice_fusion.14.x_ref, bf16[2048,1792]{1,0:T(8,128)(2,1)} %get-tuple-element.104.dz_ref), kind=kOutput, calls=%fused_computation | convolution fusion | flops 15036055552 | bytes 23068672 | tf_op jit(solution)/shard_map/dot_general | solution.py:60
  572.7 12.9 %inward.5 = bf16[1024,2048]{1,0:T(8,128)(2,1)} custom-call(bf16[2048,1792]{1,0:T(8,128)(2,1)} %get-tuple-element.104.dz_ref, bf16[2048,1792]{1,0:T(8,128)(2,1)} %all-gather.12.cloned.1.call-done.wq_ref.wk_ref.wv_ref.w_ref.wf_ref, bf16[2048,1792]{1,0:T(8,128)(2,1)} %all-gather.12.cloned.1.call-done.wq_ref.wk_ref.wv_ref.w_ref.wf_ref, ...), custom_call_target="tpu_custom_call" | custom-call | flops 7516192768 | bytes 11534336 | tf_op jit(solution)/shard_map/inward/pallas_call | solution.py:743
  585.6 12.9 %inward.4.keep_ref = bf16[1024,2048]{1,0:T(8,128)(2,1)} custom-call(bf16[2048,1792]{1,0:T(8,128)(2,1)} %get-tuple-element.104.dz_ref, bf16[2048,1792]{1,0:T(8,128)(2,1)} %all-gather.12.cloned.1.call-done.wq_ref.wk_ref.wv_ref.w_ref.wf_ref, bf16[2048,1792]{1,0:T(8,128)(2,1)} %all-gather.12.cloned.1.call-done.wq_ref.wk_ref.wv_ref.w_ref.wf_ref, ...), custom_call_target="tpu_custom_call" | custom-call | flops 7516192768 | bytes 11534336 | tf_op jit(solution)/shard_map/inward/pallas_call | solution.py:743
  606.6 22.8 %collective-permute-done.38.across_ref = bf16[256,2048]{1,0:T(8,128)(2,1)S(1)} collective-permute-done((bf16[256,2048]{1,0:T(8,128)(2,1)}, bf16[256,2048]{1,0:T(8,128)(2,1)S(1)}, u32[]{:S(2)}, u32[]{:S(2)}) %collective-permute-start.38) | collective-permute-done | bytes 1048608 | tf_op jit(solution)/shard_map/ppermute | solution.py:421
  658.9 21.5 %collective-permute-done.42 = bf16[256,2048]{1,0:T(8,128)(2,1)S(1)} collective-permute-done((bf16[256,2048]{1,0:T(8,128)(2,1)S(1)}, bf16[256,2048]{1,0:T(8,128)(2,1)S(1)}, u32[]{:S(2)}, u32[]{:S(2)}) %collective-permute-start.42) | collective-permute-done | bytes 1048608 | tf_op jit(solution)/shard_map/ppermute | solution.py:421
  704.1 18.3 %outer_back.3 = (bf16[2048,1792]{1,0:T(8,128)(2,1)}, bf16[2048,256]{1,0:T(8,128)(2,1)}, f32[1,1024]{1,0:T(1,128)}, f32[1,2048]{1,0:T(1,128)}) custom-call(bf16[2048,2048]{1,0:T(8,128)(2,1)} %constant_dynamic-update-slice_fusion.21.dy_ref, bf16[1280,2048]{1,0:T(8,128)(2,1)} %all-gather.10.cloned.1.call-done.w_ref.wo_ref, ...), custom_call_target="tpu_custom_call" | custom-call | flops 10737418240 | bytes 16777216 | tf_op jit(solution)/shard_map/outer_back/pallas_call | solution.py:762
  722.4 15.9 %attend_back.3 = (bf16[2048,1792]{1,0:T(8,128)(2,1)}, f32[1,768]{1,0:T(1,128)}) custom-call(bf16[2048,256]{1,0:T(8,128)(2,1)} %get-tuple-element.78.q_ref, bf16[2048,256]{1,0:T(8,128)(2,1)} %get-tuple-element.79.k_ref, bf16[2048,256]{1,0:T(8,128)(2,1)} %get-tuple-element.80.v_ref, s32[1024,1]{1,0:T(8,128)} %bitcast.119, ...), custom_call_target="tpu_custom_call", output_to_operand_aliasing={{0}: (9, {})} | custom-call | flops 5368709120 | bytes 4194304 | tf_op jit(solution)/shard_map/attend_back/pallas_call | solution.py:814
  738.3 21.2 %convolution_convert_fusion.1 = bf16[2048,1792]{1,0:T(8,128)(2,1)} fusion(bf16[2048,2048]{1,0:T(8,128)(2,1)} %copy-done.32, bf16[2048,1792]{1,0:T(8,128)(2,1)} %get-tuple-element.115.dz_ref), kind=kOutput, calls=%fused_computation.1 | convolution fusion | flops 15036055552 | bytes 23068672 | tf_op jit(solution)/shard_map/dot_general | solution.py:60
  769.9 14.0 %fusion.4 = bf16[1024,2048]{1,0:T(8,128)(2,1)} fusion(bf16[2048,2048]{1,0:T(8,128)(2,1)} %constant_dynamic-update-slice_fusion.21.dy_ref, bf16[2048,1280]{1,0:T(8,128)(2,1)} %get-tuple-element.82.act_ref), kind=kOutput, calls=%fused_computation.12 | convolution fusion | flops 8592031744 | bytes 16777216 | tf_op jit(solution)/shard_map/dot_general | solution.py:60
  784.0 13.1 %inward.7 = bf16[1024,2048]{1,0:T(8,128)(2,1)} custom-call(bf16[2048,1792]{1,0:T(8,128)(2,1)} %get-tuple-element.115.dz_ref, bf16[2048,1024]{1,0:T(8,128)(2,1)} %all-gather.6.cloned.1.call-done.w_ref.wf_ref, bf16[2048,768]{1,0:T(8,128)(2,1)} %all-gather.8.cloned.1.call-done.wq_ref.wk_ref.wv_ref, ...), custom_call_target="tpu_custom_call" | custom-call | flops 7516192768 | bytes 11534336 | tf_op jit(solution)/shard_map/inward/pallas_call | solution.py:743
  813.7 24.2 %collective-permute-done.33.across_ref = bf16[256,2048]{1,0:T(8,128)(2,1)S(1)} collective-permute-done((bf16[256,2048]{1,0:T(8,128)(2,1)}, bf16[256,2048]{1,0:T(8,128)(2,1)S(1)}, u32[]{:S(2)}, u32[]{:S(2)}) %collective-permute-start.33) | collective-permute-done | bytes 1048608 | tf_op jit(solution)/shard_map/ppermute | solution.py:421
  864.7 12.9 %inward.6.keep_ref = bf16[1024,2048]{1,0:T(8,128)(2,1)} custom-call(bf16[2048,1792]{1,0:T(8,128)(2,1)} %get-tuple-element.115.dz_ref, bf16[2048,1024]{1,0:T(8,128)(2,1)} %all-gather.6.cloned.1.call-done.w_ref.wf_ref, bf16[2048,768]{1,0:T(8,128)(2,1)} %all-gather.8.cloned.1.call-done.wq_ref.wk_ref.wv_ref, ...), custom_call_target="tpu_custom_call" | custom-call | flops 7516192768 | bytes 11534336 | tf_op jit(solution)/shard_map/inward/pallas_call | solution.py:743
  917.6 19.4 %collective-permute-done.60 = f32[3584]{0:T(1024)S(1)} collective-permute-done((f32[3584]{0:T(1024)S(1)}, f32[3584]{0:T(1024)S(1)}, u32[]{:S(2)}, u32[]{:S(2)}) %collective-permute-start.60) | collective-permute-done | bytes 14368 | tf_op jit(solution)/shard_map/ppermute | solution.py:421
  975.1 17.1 %collective-permute-done.56 = bf16[512,1792]{1,0:T(8,128)(2,1)} collective-permute-done((bf16[512,1792]{1,0:T(8,128)(2,1)}, bf16[512,1792]{1,0:T(8,128)(2,1)}, u32[]{:S(2)}, u32[]{:S(2)}) %collective-permute-start.56) | collective-permute-done | bytes 1835040 | tf_op jit(solution)/shard_map/ppermute | solution.py:1024
  994.0 12.6 %collective-permute-done.57 = bf16[512,1792]{1,0:T(8,128)(2,1)S(1)} collective-permute-done((bf16[512,1792]{1,0:T(8,128)(2,1)}, bf16[512,1792]{1,0:T(8,128)(2,1)S(1)}, u32[]{:S(2)}, u32[]{:S(2)}) %collective-permute-start.57) | collective-permute-done | bytes 1835040 | tf_op jit(solution)/shard_map/ppermute | solution.py:1021
  1033.7 20.3 %collective-permute-done.62 = bf16[1024,512]{1,0:T(8,128)(2,1)S(1)} collective-permute-done((bf16[1024,512]{1,0:T(8,128)(2,1)}, bf16[1024,512]{1,0:T(8,128)(2,1)S(1)}, u32[]{:S(2)}, u32[]{:S(2)}) %collective-permute-start.62) | collective-permute-done | bytes 1048608 | tf_op jit(solution)/shard_map/ppermute | solution.py:1021
  (449 shorter events, 456.3 us)
Async XLA Ops:
  7.2 212.6 %all-gather.8.cloned.1.call-start = ((), (), s32[]{:S(2)}) async-start(), calls=%async_computation.6 | async-start | bytes 3932160 | tf_op jit(solution)/shard_map/all_gather | solution.py:886
  11.4 26.0 %collective-permute-start.1 = (bf16[512,768]{1,0:T(8,128)(2,1)S(1)}, bf16[512,768]{1,0:T(8,128)(2,1)}, u32[]{:S(2)}, u32[]{:S(2)}) collective-permute-start(bf16[512,768]{1,0:T(8,128)(2,1)S(1)} %constant_dynamic-slice_fusion.3), channel_id=1, source_target_pairs={{0,16},{16,0},{1,17},{17,1},{2,18},{18,2},{3,19},{19,3},{4,20},{20... | collective-permute-start | bytes 2359304 | tf_op jit(solution)/shard_map/ppermute | solution.py:421
  40.4 203.0 %all-gather.6.cloned.1.call-start = ((), (), s32[]{:S(2)}) async-start(), calls=%async_computation.5 | async-start | bytes 5242880 | tf_op jit(solution)/shard_map/all_gather | solution.py:886
  69.5 216.8 %all-gather.10.cloned.1.call-start = ((), (), s32[]{:S(2)}) async-start(), calls=%async_computation.7 | async-start | bytes 6553600 | tf_op jit(solution)/shard_map/all_gather | solution.py:886
  73.4 29.2 %collective-permute-start.3 = (bf16[1280,512]{1,0:T(8,128)(2,1)}, bf16[1280,512]{1,0:T(8,128)(2,1)}, u32[]{:S(2)}, u32[]{:S(2)}) collective-permute-start(bf16[1280,512]{1,0:T(8,128)(2,1)} %pad_maximum_fusion.9), channel_id=1, source_target_pairs={{0,16},{16,0},{1,17},{17,1},{2,18},{18,2},{3,19},{19,3},{4,20},{20... | collective-permute-start | bytes 3932168 | tf_op jit(solution)/shard_map/ppermute | solution.py:421
  110.0 309.2 %all-gather.12.cloned.1.call-start = ((), (), s32[]{:S(2)}) async-start(), calls=%async_computation.8 | async-start | bytes 9175040 | tf_op jit(solution)/shard_map/all_gather | solution.py:886
  153.2 25.5 %collective-permute-start.10 = (bf16[256,2048]{1,0:T(8,128)(2,1)}, bf16[256,2048]{1,0:T(8,128)(2,1)}, u32[]{:S(2)}, u32[]{:S(2)}) collective-permute-start(bf16[256,2048]{1,0:T(8,128)(2,1)} %dynamic-slice_bitcast_fusion.1), channel_id=1, source_target_pairs={{0,2},{1,3},{2,0},{3,1},{4,6},{5,7},{6,4},{7,5},{8,10},{9,11},{10,... | collective-permute-start | bytes 3145736 | tf_op jit(solution)/shard_map/ppermute | solution.py:421
  154.7 26.2 %collective-permute-start.12 = (bf16[256,2048]{1,0:T(8,128)(2,1)}, bf16[256,2048]{1,0:T(8,128)(2,1)}, u32[]{:S(2)}, u32[]{:S(2)}) collective-permute-start(bf16[256,2048]{1,0:T(8,128)(2,1)} %dynamic-slice_bitcast_fusion.1), channel_id=1, source_target_pairs={{0,16},{16,0},{1,17},{17,1},{2,18},{18,2},{3,19},{19,3},{4,20},{20... | collective-permute-start | bytes 3145736 | tf_op jit(solution)/shard_map/ppermute | solution.py:421
  158.6 31.1 %collective-permute-start.18 = (f32[5632]{0:T(1024)S(1)}, f32[5632]{0:T(1024)S(1)}, u32[]{:S(2)}, u32[]{:S(2)}) collective-permute-start(f32[5632]{0:T(1024)S(1)} %pad_maximum_fusion.11), channel_id=1, source_target_pairs={{0,4},{4,0},{8,12},{12,8},{1,5},{5,1},{9,13},{13,9},{2,6},{6,2},{1... | collective-permute-start | bytes 67592 | tf_op jit(solution)/shard_map/ppermute | solution.py:421
  202.3 314.5 %all-gather.14.cloned.1.call-start = ((), (), s32[]{:S(2)}) async-start(), calls=%async_computation.9 | async-start | bytes 6553600 | tf_op jit(solution)/shard_map/all_gather | solution.py:886
  311.7 25.7 %collective-permute-start.22 = (bf16[256,2048]{1,0:T(8,128)(2,1)}, bf16[256,2048]{1,0:T(8,128)(2,1)S(1)}, u32[]{:S(2)}, u32[]{:S(2)}) collective-permute-start(bf16[256,2048]{1,0:T(8,128)(2,1)} %get-tuple-element.83), channel_id=1, source_target_pairs={{0,16},{16,0},{1,17},{17,1},{2,18},{18,2},{3,19},{19,3},{4,20},{20... | collective-permute-start | bytes 3145736 | tf_op jit(solution)/shard_map/ppermute | solution.py:421
  313.2 25.5 %collective-permute-start.23 = (bf16[256,2048]{1,0:T(8,128)(2,1)}, bf16[256,2048]{1,0:T(8,128)(2,1)S(1)}, u32[]{:S(2)}, u32[]{:S(2)}) collective-permute-start(bf16[256,2048]{1,0:T(8,128)(2,1)} %get-tuple-element.84), channel_id=1, source_target_pairs={{0,2},{1,3},{2,0},{3,1},{4,6},{5,7},{6,4},{7,5},{8,10},{9,11},{10,... | collective-permute-start | bytes 3145736 | tf_op jit(solution)/shard_map/ppermute | solution.py:421
  365.2 26.5 %collective-permute-start.28 = (bf16[256,2048]{1,0:T(8,128)(2,1)}, bf16[256,2048]{1,0:T(8,128)(2,1)S(1)}, u32[]{:S(2)}, u32[]{:S(2)}) collective-permute-start(bf16[256,2048]{1,0:T(8,128)(2,1)} %get-tuple-element.145), channel_id=1, source_target_pairs={{0,16},{16,0},{1,17},{17,1},{2,18},{18,2},{3,19},{19,3},{4,20},{20... | collective-permute-start | bytes 3145736 | tf_op jit(solution)/shard_map/ppermute | solution.py:421
  366.7 579.3 %reduce-scatter.8.cloned.1.call-start = ((), (), s32[]{:S(2)}) async-start(), calls=%async_computation.11 | async-start | bytes 9175040 | tf_op jit(solution)/shard_map/reduce_scatter | solution.py:981
  572.6 380.8 %reduce-scatter.14.cloned.1.call-start = ((), (), s32[]{:S(2)}) async-start(), calls=%async_computation.14 | async-start | bytes 6553600 | tf_op jit(solution)/shard_map/reduce_scatter | solution.py:981
  603.7 25.7 %collective-permute-start.38 = (bf16[256,2048]{1,0:T(8,128)(2,1)}, bf16[256,2048]{1,0:T(8,128)(2,1)S(1)}, u32[]{:S(2)}, u32[]{:S(2)}) collective-permute-start(bf16[256,2048]{1,0:T(8,128)(2,1)} %get-tuple-element.105), channel_id=1, source_target_pairs={{0,16},{16,0},{1,17},{17,1},{2,18},{18,2},{3,19},{19,3},{4,20},{20... | collective-permute-start | bytes 3145736 | tf_op jit(solution)/shard_map/ppermute | solution.py:421
  605.2 25.4 %collective-permute-start.39 = (bf16[256,2048]{1,0:T(8,128)(2,1)}, bf16[256,2048]{1,0:T(8,128)(2,1)S(1)}, u32[]{:S(2)}, u32[]{:S(2)}) collective-permute-start(bf16[256,2048]{1,0:T(8,128)(2,1)} %get-tuple-element.106), channel_id=1, source_target_pairs={{0,2},{1,3},{2,0},{3,1},{4,6},{5,7},{6,4},{7,5},{8,10},{9,11},{10,... | collective-permute-start | bytes 3145736 | tf_op jit(solution)/shard_map/ppermute | solution.py:421
  640.3 316.5 %reduce-scatter.6.cloned.1.call-start = ((), (), s32[]{:S(2)}) async-start(), calls=%async_computation.10 | async-start | bytes 9175040 | tf_op jit(solution)/shard_map/reduce_scatter | solution.py:981
  759.5 266.9 %reduce-scatter.12.cloned.1.call-start = ((), (), s32[]{:S(2)}) async-start(), calls=%async_computation.13 | async-start | bytes 5242880 | tf_op jit(solution)/shard_map/reduce_scatter | solution.py:981
  769.4 37.6 %collective-permute-start.32 = (bf16[1024,2048]{1,0:T(8,128)(2,1)}, bf16[1024,2048]{1,0:T(8,128)(2,1)}, u32[]{:S(2)}, u32[]{:S(2)}) collective-permute-start(bf16[1024,2048]{1,0:T(8,128)(2,1)} %outer.7), channel_id=1, source_target_pairs={{0,1},{1,0},{2,3},{3,2},{4,5},{5,4},{6,7},{7,6},{8,9},{9,8},{10,11... | collective-permute-start | bytes 12582920 | tf_op jit(solution)/shard_map/ppermute | solution.py:421
  784.0 272.8 %reduce-scatter.10.cloned.1.call-start = ((), (), s32[]{:S(2)}) async-start(), calls=%async_computation.12 | async-start | bytes 1310720 | tf_op jit(solution)/shard_map/reduce_scatter | solution.py:981
  797.1 80.4 %collective-permute-start.50 = (bf16[1024,2048]{1,0:T(8,128)(2,1)}, bf16[1024,2048]{1,0:T(8,128)(2,1)}, u32[]{:S(2)}, u32[]{:S(2)}) collective-permute-start(bf16[1024,2048]{1,0:T(8,128)(2,1)} %inward.7), channel_id=1, source_target_pairs={{0,1},{1,0},{2,3},{3,2},{4,5},{5,4},{6,7},{7,6},{8,9},{9,8},{10,11... | collective-permute-start | bytes 12582920 | tf_op jit(solution)/shard_map/ppermute | solution.py:421
  812.1 25.8 %collective-permute-start.33 = (bf16[256,2048]{1,0:T(8,128)(2,1)}, bf16[256,2048]{1,0:T(8,128)(2,1)S(1)}, u32[]{:S(2)}, u32[]{:S(2)}) collective-permute-start(bf16[256,2048]{1,0:T(8,128)(2,1)} %get-tuple-element.93), channel_id=1, source_target_pairs={{0,16},{16,0},{1,17},{17,1},{2,18},{18,2},{3,19},{19,3},{4,20},{20... | collective-permute-start | bytes 3145736 | tf_op jit(solution)/shard_map/ppermute | solution.py:421
  812.7 25.5 %collective-permute-start.34 = (bf16[256,2048]{1,0:T(8,128)(2,1)}, bf16[256,2048]{1,0:T(8,128)(2,1)}, u32[]{:S(2)}, u32[]{:S(2)}) collective-permute-start(bf16[256,2048]{1,0:T(8,128)(2,1)} %get-tuple-element.94), channel_id=1, source_target_pairs={{0,2},{1,3},{2,0},{3,1},{4,6},{5,7},{6,4},{7,5},{8,10},{9,11},{10,... | collective-permute-start | bytes 3145736 | tf_op jit(solution)/shard_map/ppermute | solution.py:421
  846.4 48.2 %collective-permute-start.49 = (bf16[256,2048]{1,0:T(8,128)(2,1)S(1)}, bf16[256,2048]{1,0:T(8,128)(2,1)S(1)}, u32[]{:S(2)}, u32[]{:S(2)}) collective-permute-start(bf16[256,2048]{1,0:T(8,128)(2,1)S(1)} %get-tuple-element.147), channel_id=1, source_target_pairs={{0,16},{16,0},{1,17},{17,1},{2,18},{18,2},{3,19},{19,3},{4,20},{20... | collective-permute-start | bytes 3145736 | tf_op jit(solution)/shard_map/ppermute | solution.py:421
  864.2 28.0 %collective-permute-start.58 = (f32[7680]{0:T(1024)S(1)}, f32[7680]{0:T(1024)S(1)}, u32[]{:S(2)}, u32[]{:S(2)}) collective-permute-start(f32[7680]{0:T(1024)S(1)} %constant_dynamic-update-slice_fusion.29), channel_id=1, source_target_pairs={{0,4},{4,0},{8,12},{12,8},{1,5},{5,1},{9,13},{13,9},{2,6},{6,2},{1... | collective-permute-start | bytes 92168 | tf_op jit(solution)/shard_map/ppermute | solution.py:421
  898.1 57.7 %collective-permute-start.48 = (bf16[256,2048]{1,0:T(8,128)(2,1)}, bf16[256,2048]{1,0:T(8,128)(2,1)}, u32[]{:S(2)}, u32[]{:S(2)}) collective-permute-start(bf16[256,2048]{1,0:T(8,128)(2,1)} %get-tuple-element.141), channel_id=1, source_target_pairs={{0,16},{1,17},{2,18},{3,19},{4,20},{5,21},{6,22},{7,23},{8,24},{9,... | collective-permute-start | bytes 3145736 | tf_op jit(solution)/shard_map/ppermute | solution.py:1024
  943.9 28.4 %collective-permute-start.55 = (bf16[256,2048]{1,0:T(8,128)(2,1)}, bf16[256,2048]{1,0:T(8,128)(2,1)}, u32[]{:S(2)}, u32[]{:S(2)}) collective-permute-start(bf16[256,2048]{1,0:T(8,128)(2,1)} %get-tuple-element.139), channel_id=1, source_target_pairs={{16,0},{17,1},{18,2},{19,3},{20,4},{21,5},{22,6},{23,7},{24,8},{25... | collective-permute-start | bytes 3145736 | tf_op jit(solution)/shard_map/ppermute | solution.py:1021
  946.0 46.2 %collective-permute-start.56 = (bf16[512,1792]{1,0:T(8,128)(2,1)}, bf16[512,1792]{1,0:T(8,128)(2,1)}, u32[]{:S(2)}, u32[]{:S(2)}) collective-permute-start(bf16[512,1792]{1,0:T(8,128)(2,1)} %reduce-scatter.8.cloned.1.call-done), channel_id=1, source_target_pairs={{0,16},{1,17},{2,18},{3,19},{4,20},{5,21},{6,22},{7,23},{8,24},{9,... | collective-permute-start | bytes 5505032 | tf_op jit(solution)/shard_map/ppermute | solution.py:1024
  953.4 74.4 %collective-permute-start.61 = (bf16[1280,512]{1,0:T(8,128)(2,1)}, bf16[1280,512]{1,0:T(8,128)(2,1)}, u32[]{:S(2)}, u32[]{:S(2)}) collective-permute-start(bf16[1280,512]{1,0:T(8,128)(2,1)} %reduce-scatter.14.cloned.1.call-done), channel_id=1, source_target_pairs={{0,16},{1,17},{2,18},{3,19},{4,20},{5,21},{6,22},{7,23},{8,24},{9,... | collective-permute-start | bytes 3932168 | tf_op jit(solution)/shard_map/ppermute | solution.py:1024
  956.8 49.7 %collective-permute-start.57 = (bf16[512,1792]{1,0:T(8,128)(2,1)}, bf16[512,1792]{1,0:T(8,128)(2,1)S(1)}, u32[]{:S(2)}, u32[]{:S(2)}) collective-permute-start(bf16[512,1792]{1,0:T(8,128)(2,1)} %reduce-scatter.6.cloned.1.call-done), channel_id=1, source_target_pairs={{16,0},{17,1},{18,2},{19,3},{20,4},{21,5},{22,6},{23,7},{24,8},{25... | collective-permute-start | bytes 5505032 | tf_op jit(solution)/shard_map/ppermute | solution.py:1021
  1026.3 27.6 %collective-permute-start.62 = (bf16[1024,512]{1,0:T(8,128)(2,1)}, bf16[1024,512]{1,0:T(8,128)(2,1)S(1)}, u32[]{:S(2)}, u32[]{:S(2)}) collective-permute-start(bf16[1024,512]{1,0:T(8,128)(2,1)} %reduce-scatter.12.cloned.1.call-done), channel_id=1, source_target_pairs={{16,0},{17,1},{18,2},{19,3},{20,4},{21,5},{22,6},{23,7},{24,8},{25... | collective-permute-start | bytes 3145736 | tf_op jit(solution)/shard_map/ppermute | solution.py:1021
  (104 other events, 1670.5 us)
Sparse Core Ops, SparseCore 0:
  40.5 64.8 all-gather.7
  107.6 79.3 all-gather.5
  189.2 97.0 all-gather.9
  288.3 130.8 all-gather.11
  420.6 96.2 all-gather.13
  572.8 126.1 reduce-scatter.7
  701.2 94.3 reduce-scatter.13
  797.9 129.6 reduce-scatter.5
  929.9 77.2 reduce-scatter.11
  1009.3 27.8 reduce-scatter.9

commit v4 on v3

--- a/solution.py
+++ b/solution.py
@@ -448,11 +448,28 @@
     half = block.shape[0] // 2
     across = swap(block, SECTION, 1)
     beside = swap(block, COL, 2)
+    across, beside = lax.optimization_barrier((across, beside))
     corner = jnp.concatenate([swap(beside[:half], SECTION, 1), swap(across[half:], COL, 2)], axis=0)
     near = jnp.concatenate([block, beside], axis=0)
     far = jnp.concatenate([across, corner], axis=0)
     near_other, far_other = (swap(near, COL, 1), swap(far, COL, 1))
     return jnp.concatenate([near, near_other, far, far_other], axis=0), across
+
+
+def gather_pieces(shard):
+    def send(value, pairs):
+        return lax.ppermute(value, ROW, pairs)
+
+    opposite = swap(shard, ROW, 2)
+    behind = send(shard, [(0, 1), (1, 2), (2, 3)])
+    ahead = send(shard, [(3, 2), (2, 1), (1, 0)])
+    last = send(opposite, [(2, 3), (1, 0)])
+    return shard, ahead, opposite, behind, last
+
+
+def in_turn(pieces, row):
+    shard, ahead, opposite, behind, last = pieces
+    return (shard, jnp.where(row == 3, last, ahead), opposite, jnp.where(row == 0, last, behind))
 
 
 def pair_sum(keep_ref, came_ref, start, size):
@@ -555,17 +572,31 @@
     slope_ref[...] = (below + inner * density).astype(BF16)
 
 
-def outer_kernel(act_ref, w_ref, wo_ref, out_ref):
-    inner = w_ref.shape[0]
-    total = mm(act_ref[:, :inner], w_ref[...]) + mm(act_ref[:, inner:], wo_ref[...])
-    out_ref[...] = total.astype(BF16)
-
-
-def outer_back_kernel(dy_ref, w_ref, wo_ref, slope_ref, dz_ref, do_ref, sum_ref, dy_sum_ref):
+def piece_columns(row_ref, w_refs):
+    width = w_refs[0].shape[1]
+    for step, w_ref in enumerate(w_refs):
+        place = lax.rem(row_ref[0] + step, len(w_refs))
+        yield w_ref, pl.ds(pl.multiple_of(place * width, width), width)
+
+
+def outer_kernel(row_ref, act_ref, w0_ref, w1_ref, w2_ref, w3_ref, out_ref):
+    act = act_ref[...]
+    for w_ref, columns in piece_columns(row_ref, (w0_ref, w1_ref, w2_ref, w3_ref)):
+        out_ref[:, columns] = mm(act, w_ref[...]).astype(BF16)
+
+
+def outer_back_kernel(
+    row_ref, dy_ref, w0_ref, w1_ref, w2_ref, w3_ref, slope_ref, dz_ref, do_ref, sum_ref, dy_sum_ref
+):
+    inner = slope_ref.shape[1]
+    total = None
+    for w_ref, columns in piece_columns(row_ref, (w0_ref, w1_ref, w2_ref, w3_ref)):
+        part = contract_cols(dy_ref[:, columns], w_ref[...])
+        total = part if total is None else total + part
     dy = dy_ref[...]
-    dz = (contract_cols(dy, w_ref[...]) * slope_ref[...].astype(F32)).astype(BF16)
+    dz = (total[:, :inner] * slope_ref[...].astype(F32)).astype(BF16)
     dz_ref[...] = dz
-    do_ref[...] = contract_cols(dy, wo_ref[...]).astype(BF16)
+    do_ref[...] = total[:, inner:].astype(BF16)
 
     @pl.when(pl.program_id(0) == 0)
     def _():
@@ -715,26 +746,22 @@
     return pl.BlockSpec((ROW_BLOCK, width), lambda i: (i // 2 * 4 + 2 * other + i % 2, 0))
 
 
-def outer_panels(pair, inner):
-    (w, first), (wo, second) = pair
-    return [
-        pl.BlockSpec((inner, w.shape[1]), lambda *unused: (first // inner, 0)),
-        pl.BlockSpec((HD, wo.shape[1]), lambda *unused: (second // HD, 0)),
-    ]
-
-
-def outer(act, pair, other):
-    rows, width = (act.shape[0] // 2, pair[0][0].shape[1])
+def outer(act, pieces, row, other):
+    rows, width = (act.shape[0] // 2, len(pieces) * pieces[0].shape[1])
     out = jax.ShapeDtypeStruct((rows, width), BF16)
     return pl.pallas_call(
         outer_kernel,
         grid=(rows // ROW_BLOCK,),
-        in_specs=[split_rows(act.shape[1], other), *outer_panels(pair, act.shape[1] - HD)],
+        in_specs=[
+            pl.BlockSpec(memory_space=pltpu.SMEM),
+            split_rows(act.shape[1], other),
+            *(whole(piece.shape) for piece in pieces),
+        ],
         out_specs=by_rows(width),
         out_shape=out,
         cost_estimate=cost(2 * rows * width * act.shape[1], act, out),
         name="outer",
-    )(act, pair[0][0], pair[1][0])
+    )(row, act, *pieces)
 
 
 def inward(dz, w_in, w_qkv, offset, other):
@@ -755,14 +782,19 @@
     )(dz, w_in, w_qkv, w_qkv, w_qkv)
 
 
-def outer_back(dy, pair, slopes):
+def outer_back(dy, pieces, row, slopes):
     rows, width = dy.shape
     inner = slopes.shape[1]
     dz = jax.ShapeDtypeStruct((rows, inner + 3 * HD), BF16)
     return pl.pallas_call(
         outer_back_kernel,
         grid=(rows // ROW_BLOCK,),
-        in_specs=[by_rows(width), *outer_panels(pair, inner), by_rows(inner)],
+        in_specs=[
+            pl.BlockSpec(memory_space=pltpu.SMEM),
+            by_rows(width),
+            *(whole(piece.shape) for piece in pieces),
+            by_rows(inner),
+        ],
         out_specs=[by_rows(inner), by_rows(HD), whole((1, inner)), whole((1, width))],
         out_shape=[
             dz,
@@ -772,7 +804,7 @@
         ],
         cost_estimate=cost(2 * rows * width * (inner + HD), dy, slopes, slopes),
         name="outer_back",
-    )(dy, pair[0][0], pair[1][0], slopes)
+    )(row, dy, *pieces, slopes)
 
 
 def attend(queries, keys_all, values_all, places, inner):
@@ -917,11 +949,10 @@
     outs_pair = both_layers(outs_kept, outs_came)
     w_qkv0 = gathered(qkv_pair[0], 0)
     w_fc_in0 = gathered(fc_in_pair[0], 0)
-    w_outs0 = gathered(outs_pair[0], 1)
     w_ins1 = gathered(jnp.concatenate([fc_in_pair[1], qkv_pair[1]], axis=1), 0)
-    w_outs1 = gathered(outs_pair[1], 1)
     w_ins = ((w_fc_in0, w_qkv0, 0), (w_ins1, w_ins1, inner))
-    w_outs = tuple(((member, 0), (member, inner)) for member in (w_outs0, w_outs1))
+    w_outs = [gather_pieces(outs_pair[layer]) for layer in range(2)]
+    row = r.astype(jnp.int32)[None]
 
     own_qkv = mm(shift_one.astype(BF16)[None], qkv_flat)[0]
     own_fc = mm(shift_two.astype(BF16)[None], fc_in_w)[0]
@@ -961,18 +992,22 @@
         x, unused = gather_rows(scaled.astype(BF16))
         if layer == 0:
             seed_rows, unused = gather_rows(after(seed, x))
-            x = after(x, seed_rows)
         w_fc_in, w_qkv, offset = w_ins[layer]
         queries, keys_all, values_all = project(x, w_qkv, offset, qkv_e[layer], tables)
         attended, log_sums = attend(queries, keys_all, values_all, places, inner)
         act, slopes = inner_layer(x, w_fc_in, fc_e[layer], attended)
+        if layer == 0:
+            *pieces, act, unused = lax.optimization_barrier((*w_outs[0][1:], act, seed_rows))
+            w_outs[0] = in_turn((w_outs[0][0], *pieces), r)
         kept = (x, queries, keys_all, values_all, log_sums, slopes, act)
         if layer == 1:
             outs_grad1 = contract_rows(act, seed_rows).astype(BF16)
             seed_rows = after(seed_rows, outs_grad1)
+            *pieces, unused = lax.optimization_barrier((*w_outs[1][1:], outs_grad1))
+            w_outs[1] = in_turn((w_outs[1][0], *pieces), r)
         kept_list.append(kept)
         if layer == 0:
-            summed = scatter_rows(lambda other: outer(act, w_outs[0], other))
+            summed = scatter_rows(lambda other: outer(act, w_outs[0], row, other))
             hidden = (hidden.astype(F32) + summed + end_e[layer]).astype(BF16)
             ends.append(hidden)
             middle = swap(hidden, SECTION, 1)
@@ -991,7 +1026,7 @@
         else:
             dy, across = gather_rows(grads)
             middle_grads = (jnp.where(low, grads, across), jnp.where(low, across, grads))
-        dz, grad_attended, inner_sum, dy_sum = outer_back(dy, w_outs[layer], slopes)
+        dz, grad_attended, inner_sum, dy_sum = outer_back(dy, w_outs[layer], row, slopes)
         dz, heads_sum = attend_back(
             queries, keys_all, values_all, places, log_sums, grad_attended, tables, dz
         )
@@ -1010,7 +1045,7 @@
             fc_out_part0 = reduced(contract_rows(act[:, :inner], dy).astype(BF16), 1)
             out_part0 = reduced(contract_rows(act[:, inner:], dy).astype(BF16), 1)
     act = kept_list[1][-1]
-    summed = scatter_rows(lambda other: outer(act, w_outs[1], other))
+    summed = scatter_rows(lambda other: outer(act, w_outs[1], row, other))
     summed = after(summed, small_list[0][0])
     ends.append((hidden_list[1].astype(F32) + summed + end_e[1]).astype(BF16))
 
@@ -1030,7 +1065,8 @@
         ROW,
     )
     sums = small[: 2 * (per + inner)]
-    smalls = to_owner(*jnp.split(sums, 2), *jnp.split(swap(sums, SECTION, 1), 2))
+    sums_other = swap(sums, SECTION, 1)
+    smalls = to_owner(*jnp.split(sums, 2), *jnp.split(sums_other, 2))
     end_grad = jnp.where(low, *jnp.split(small[2 * (per + inner) :], 2))
     qkv_b_grad = jnp.concatenate([member[:per] for member in smalls])
     fc_in_b_grad = jnp.concatenate([member[per:] for member in smalls])
@@ -1042,15 +1078,22 @@
     fc_in_g = jnp.concatenate([member[:, :inner] for member in ins_g], axis=1).astype(F32)
     qkv_w_grad = gain_one[:, None] * qkv_g + shift_one[:, None] * qkv_b_grad[None]
     fc_in_w_grad = gain_two[:, None] * fc_in_g + shift_two[:, None] * fc_in_b_grad[None]
-    qkv_full, fc_full = (qkv_flat.astype(F32), fc_in_w.astype(F32))
-    norms = jnp.stack(
-        [
-            jnp.sum(qkv_full * qkv_g, axis=1),
-            jnp.sum(qkv_full * qkv_b_grad[None], axis=1),
-            jnp.sum(fc_full * fc_in_g, axis=1),
-            jnp.sum(fc_full * fc_in_b_grad[None], axis=1),
-        ]
-    )
+    norm_parts = []
+    for layer, (w_q, w_f) in enumerate(zip(both_layers(*qkv_half), both_layers(*fc_in_half))):
+        w_q, w_f = (w_q.astype(F32), w_f.astype(F32))
+        heads, hidden_sum = jnp.split(sums[layer * (per + inner) :][: per + inner], [per])
+        part = ins_list[layer].astype(F32)
+        norm_parts.append(
+            jnp.stack(
+                [
+                    jnp.sum(w_q * part[:, inner:], axis=1),
+                    jnp.sum(w_q * heads[None], axis=1),
+                    jnp.sum(w_f * part[:, :inner], axis=1),
+                    jnp.sum(w_f * hidden_sum[None], axis=1),
+                ]
+            )
+        )
+    norms = jnp.where(low, *norm_parts) + swap(jnp.where(low, *norm_parts[::-1]), SECTION, 1)
     norms = take(sum_over(norms, COL), 1, c, deep // cols_axis)
     end_grad = take(end_grad, 0, r * cols_axis + c, deep // cols_axis)
     fc_out_upper = to_first(after(fc_out_part0, ins_upper))
@@ -1105,8 +1148,7 @@
 def solution(mesh):
     sizes = mesh.shape
     paired = sizes[SECTION] == 2 and sizes[COL] == 4
-    rows_even = sizes[ROW] & (sizes[ROW] - 1) == 0
-    body = all_of_it if paired and rows_even else relay_local
+    body = all_of_it if paired and sizes[ROW] == 4 else relay_local
     step = jax.shard_map(
         body,
         mesh=mesh,

time: 1090 us -> 1250 us (1.15)
  waiting for transfers between devices: 464 us -> 604 us
    ppermute x59 -> x62, waiting for transfers between devices: 326 us -> 453 us  [swap(): lax.ppermute(value, axis, [(source, source ^ bit) for source in range(cou...]
    ppermute x0 -> x6, waiting for transfers between devices: none -> 57.8 us  [send(): return lax.ppermute(value, ROW, pairs)]
    all_gather x5 -> x3, waiting for transfers between devices: 70.4 us -> 29.1 us  [gathered(): return lax.all_gather(shard, ROW, axis=axis, tiled=True)]
    ppermute x4, waiting for transfers between devices: 50.7 us -> 22.7 us  [to_first(): return lax.ppermute(value, SECTION, [(1, 0)])]
    ppermute x3, waiting for transfers between devices: 17.1 us -> 41.3 us  [to_second(): return lax.ppermute(value, SECTION, [(0, 1)])]
    unnamed x149 -> x151, local copies, waits for them, and re-layouts: 37.3 us -> 41.9 us
    ppermute x59 -> x62, starting transfers between devices: 59.8 us -> 57.7 us  [swap(): lax.ppermute(value, axis, [(source, source ^ bit) for source in range(cou...]
  transfers between devices with their start and end apart: 76 -> 83, of which waited for: 39 -> 45; matrix products, arithmetic and copies ran while one was open for 18% -> 17% of each run, Pallas kernels for 23% -> 19%
where the time goes in v4:
time: 1250 us; the launch traced here: 1240 us
  waiting for transfers between devices  604 us (48%)
  Pallas kernels  287 us (23%)
  other arithmetic  91.4 us (7%)
  starting transfers between devices  88.9 us (7%)
  matrix products  81.5 us (7%)
  local copies, waits for them, and re-layouts  74.5 us (6%)
  between operations  15.4 us (1%)
    ppermute x62, waiting for transfers between devices, swap(): lax.ppermute(value, axis, [(source, source ^ bit) for source in range(cou...  453 us
    dot_general x5, matrix products, contract_rows(): lax.dot_general(first_operand, second_operand, (((0,), (0,)), ((), ())),...  80.8 us
    ppermute x6, waiting for transfers between devices, send(): return lax.ppermute(value, ROW, pairs)  57.8 us
    ppermute x62, starting transfers between devices, swap(): lax.ppermute(value, axis, [(source, source ^ bit) for source in range(cou...  57.7 us
    pallas_call x4, Pallas kernels, inward(): pl.pallas_call(inward_kernel, grid=(rows // ROW_BLOCK,), in_specs=[split_...  52.3 us
    pallas_call x8, Pallas kernels, column_call(): pl.pallas_call(kernel, grid=(width // tile,), in_specs=[spec(member.shape...  44.4 us
    unnamed x151, local copies, waits for them, and re-layouts  41.9 us
    ppermute x3, waiting for transfers between devices, to_second(): return lax.ppermute(value, SECTION, [(0, 1)])  41.3 us
  transfers between devices with their start and end apart: 83, of which 45 were waited for; matrix products, arithmetic and copies ran while one was open for 17% of the time, Pallas kernels for 19%

profile of v4, /device:TPU:0, one launch (start us, length us, event | category | flops | bytes accessed | tf_op | source)
XLA Modules:
  0.0 1243.1 jit_solution(4498325691575860219)
XLA Ops:
  22.0 14.0 %collective-permute-done.1 = bf16[512,768]{1,0:T(8,128)(2,1)} collective-permute-done((bf16[512,768]{1,0:T(8,128)(2,1)}, bf16[512,768]{1,0:T(8,128)(2,1)}, u32[]{:S(2)}, u32[]{:S(2)}) %collective-permute-start.1) | collective-permute-done | bytes 786464 | tf_op jit(solution)/shard_map/ppermute | solution.py:421
  44.7 15.2 %collective-permute-done.2 = bf16[512,1024]{1,0:T(8,128)(2,1)} collective-permute-done((bf16[512,1024]{1,0:T(8,128)(2,1)S(1)}, bf16[512,1024]{1,0:T(8,128)(2,1)}, u32[]{:S(2)}, u32[]{:S(2)}) %collective-permute-start.2) | collective-permute-done | bytes 1048608 | tf_op jit(solution)/shard_map/ppermute | solution.py:421
  60.7 28.1 %collective-permute-done.3 = bf16[1280,512]{1,0:T(8,128)(2,1)} collective-permute-done((bf16[1280,512]{1,0:T(8,128)(2,1)}, bf16[1280,512]{1,0:T(8,128)(2,1)}, u32[]{:S(2)}, u32[]{:S(2)}) %collective-permute-start.3) | collective-permute-done | bytes 1310752 | tf_op jit(solution)/shard_map/ppermute | solution.py:421
  172.7 15.5 %collective-permute-done.19 = bf16[256,2048]{1,0:T(8,128)(2,1)S(1)} collective-permute-done((bf16[256,2048]{1,0:T(8,128)(2,1)S(1)}, bf16[256,2048]{1,0:T(8,128)(2,1)S(1)}, u32[]{:S(2)}, u32[]{:S(2)}) %collective-permute-start.19) | collective-permute-done | bytes 1048608 | tf_op jit(solution)/shard_map/ppermute | solution.py:421
  194.8 12.7 %project.2 = (bf16[2048,256]{1,0:T(8,128)(2,1)}, bf16[2048,256]{1,0:T(8,128)(2,1)}, bf16[2048,256]{1,0:T(8,128)(2,1)}) custom-call(bf16[2048,2048]{1,0:T(8,128)(2,1)} %constant_dynamic-update-slice_fusion.x_ref, bf16[2048,768]{1,0:T(8,128)(2,1)} %all-gather.6.cloned.1.call-done.wq_ref.wk_ref.wv_ref, ...), custom_call_target="tpu_custom_call" | custom-call | flops 6442450944 | bytes 11534336 | tf_op jit(solution)/shard_map/project/pallas_call | solution.py:713
  207.5 35.8 %collective-permute-done.5.w2_ref = bf16[1280,512]{1,0:T(8,128)(2,1)} collective-permute-done((bf16[1280,512]{1,0:T(8,128)(2,1)}, bf16[1280,512]{1,0:T(8,128)(2,1)}, u32[]{:S(2)}, u32[]{:S(2)}) %collective-permute-start.5) | collective-permute-done | bytes 1310752 | tf_op jit(solution)/shard_map/ppermute | solution.py:421
  262.1 16.7 %inner.2 = (bf16[2048,1280]{1,0:T(8,128)(2,1)}, bf16[2048,1024]{1,0:T(8,128)(2,1)}) custom-call(bf16[2048,2048]{1,0:T(8,128)(2,1)} %constant_dynamic-update-slice_fusion.x_ref, bf16[2048,1024]{1,0:T(8,128)(2,1)} %all-gather.4.cloned.1.call-done.w_ref.wf_ref, f32[1,1024]{1,0:T(1,128)} %bitcast.170, ...), custom_call_target="tpu_custom_call", output_to_operand_aliasing={{0}: (3, {})} | custom-call | flops 8589934592 | bytes 16777216 | tf_op jit(solution)/shard_map/inner/pallas_call | solution.py:728
  323.5 22.5 %collective-permute-done.26.across_ref = bf16[256,2048]{1,0:T(8,128)(2,1)S(1)} collective-permute-done((bf16[256,2048]{1,0:T(8,128)(2,1)}, bf16[256,2048]{1,0:T(8,128)(2,1)S(1)}, u32[]{:S(2)}, u32[]{:S(2)}) %collective-permute-start.26) | collective-permute-done | bytes 1048608 | tf_op jit(solution)/shard_map/ppermute | solution.py:421
  374.4 21.2 %collective-permute-done.30 = bf16[256,2048]{1,0:T(8,128)(2,1)S(1)} collective-permute-done((bf16[256,2048]{1,0:T(8,128)(2,1)S(1)}, bf16[256,2048]{1,0:T(8,128)(2,1)S(1)}, u32[]{:S(2)}, u32[]{:S(2)}) %collective-permute-start.30) | collective-permute-done | bytes 1048608 | tf_op jit(solution)/shard_map/ppermute | solution.py:421
  398.6 13.0 %collective-permute-done.33 = bf16[128,2048]{1,0:T(8,128)(2,1)S(1)} collective-permute-done((bf16[128,2048]{1,0:T(8,128)(2,1)S(1)}, bf16[128,2048]{1,0:T(8,128)(2,1)S(1)}, u32[]{:S(2)}, u32[]{:S(2)}) %collective-permute-start.33) | collective-permute-done | bytes 524320 | tf_op jit(solution)/shard_map/ppermute | solution.py:421
  421.2 29.1 %all-gather.8.cloned.1.call-done.wq_ref.wk_ref.wv_ref.w_ref.wf_ref = bf16[2048,1792]{1,0:T(8,128)(2,1)} async-done(((bf16[512,1792]{1,0:T(8,128)(2,1)}), bf16[2048,1792]{1,0:T(8,128)(2,1)}) %all-gather.8.cloned.1.call-update) | async-done | bytes 7340048 | tf_op jit(solution)/shard_map/all_gather | solution.py:918
  473.9 16.7 %inner.3 = (bf16[2048,1280]{1,0:T(8,128)(2,1)}, bf16[2048,1024]{1,0:T(8,128)(2,1)}) custom-call(bf16[2048,2048]{1,0:T(8,128)(2,1)} %constant_dynamic-update-slice_fusion.14.x_ref, bf16[2048,1792]{1,0:T(8,128)(2,1)} %all-gather.8.cloned.1.call-done.wq_ref.wk_ref.wv_ref.w_ref.wf_ref, f32[1,1024]{1,0:T(1,128)} %bitcast.171, ...), custom_call_target="tpu_custom_call", output_to_operand_aliasing={{0}: (3, {})} | custom-call | flops 8589934592 | bytes 16777216 | tf_op jit(solution)/shard_map/inner/pallas_call | solution.py:728
  490.6 17.0 %convolution_convert_fusion.2 = bf16[1280,2048]{1,0:T(8,128)(2,1)} fusion(bf16[2048,1280]{1,0:T(8,128)(2,1)} %get-tuple-element.118.act_ref, bf16[2048,2048]{1,0:T(8,128)(2,1)} %constant_dynamic-update-slice_fusion.7.dy_ref), kind=kOutput, calls=%fused_computation.2 | convolution fusion | flops 10740039680 | bytes 18874368 | tf_op jit(solution)/shard_map/dot_general | solution.py:60
  515.4 107.3 %collective-permute-done.37.w2_ref = bf16[1280,512]{1,0:T(8,128)(2,1)S(1)} collective-permute-done((bf16[1280,512]{1,0:T(8,128)(2,1)S(1)}, bf16[1280,512]{1,0:T(8,128)(2,1)S(1)}, u32[]{:S(2)}, u32[]{:S(2)}) %collective-permute-start.37) | collective-permute-done | bytes 1310752 | tf_op jit(solution)/shard_map/ppermute | solution.py:421
  634.1 47.8 %collective-permute-done.39 = bf16[1280,512]{1,0:T(8,128)(2,1)S(1)} collective-permute-done((bf16[1280,512]{1,0:T(8,128)(2,1)S(1)}, bf16[1280,512]{1,0:T(8,128)(2,1)S(1)}, u32[]{:S(2)}, u32[]{:S(2)}) %collective-permute-start.39) | collective-permute-done | bytes 1310752 | tf_op jit(solution)/shard_map/ppermute | solution.py:461
  683.6 18.8 %outer_back.2 = (bf16[2048,1792]{1,0:T(8,128)(2,1)}, bf16[2048,256]{1,0:T(8,128)(2,1)}, f32[1,1024]{1,0:T(1,128)}, f32[1,2048]{1,0:T(1,128)}) custom-call(s32[1]{0:T(128)} %bitcast.6.row_ref, bf16[2048,2048]{1,0:T(8,128)(2,1)} %constant_dynamic-update-slice_fusion.7.dy_ref, bf16[1280,512]{1,0:T(8,128)(2,1)} %get-tuple-element.196.w0_ref, ...), custom_call_target="tpu_custom_call" | custom-call | flops 10737418240 | bytes 16777216 | tf_op jit(solution)/shard_map/outer_back/pallas_call | solution.py:789
  702.4 15.9 %attend_back.2 = (bf16[2048,1792]{1,0:T(8,128)(2,1)}, f32[1,768]{1,0:T(1,128)}) custom-call(bf16[2048,256]{1,0:T(8,128)(2,1)} %get-tuple-element.114.q_ref, bf16[2048,256]{1,0:T(8,128)(2,1)} %get-tuple-element.115.k_ref, bf16[2048,256]{1,0:T(8,128)(2,1)} %get-tuple-element.116.v_ref, s32[1024,1]{1,0:T(8,128)} %bitcast.119, ...), custom_call_target="tpu_custom_call", output_to_operand_aliasing={{0}: (9, {})} | custom-call | flops 5368709120 | bytes 4194304 | tf_op jit(solution)/shard_map/attend_back/pallas_call | solution.py:846
  718.3 12.9 %inward.5 = bf16[1024,2048]{1,0:T(8,128)(2,1)} custom-call(bf16[2048,1792]{1,0:T(8,128)(2,1)} %get-tuple-element.134.dz_ref, bf16[2048,1792]{1,0:T(8,128)(2,1)} %all-gather.8.cloned.1.call-done.wq_ref.wk_ref.wv_ref.w_ref.wf_ref, bf16[2048,1792]{1,0:T(8,128)(2,1)} %all-gather.8.cloned.1.call-done.wq_ref.wk_ref.wv_ref.w_ref.wf_ref, ...), custom_call_target="tpu_custom_call" | custom-call | flops 7516192768 | bytes 11534336 | tf_op jit(solution)/shard_map/inward/pallas_call | solution.py:770
  731.2 21.2 %convolution_convert_fusion = bf16[2048,1792]{1,0:T(8,128)(2,1)} fusion(bf16[2048,2048]{1,0:T(8,128)(2,1)} %constant_dynamic-update-slice_fusion.14.x_ref, bf16[2048,1792]{1,0:T(8,128)(2,1)} %get-tuple-element.134.dz_ref), kind=kOutput, calls=%fused_computation | convolution fusion | flops 15036055552 | bytes 23068672 | tf_op jit(solution)/shard_map/dot_general | solution.py:60
  752.4 13.0 %inward.4.keep_ref = bf16[1024,2048]{1,0:T(8,128)(2,1)} custom-call(bf16[2048,1792]{1,0:T(8,128)(2,1)} %get-tuple-element.134.dz_ref, bf16[2048,1792]{1,0:T(8,128)(2,1)} %all-gather.8.cloned.1.call-done.wq_ref.wk_ref.wv_ref.w_ref.wf_ref, bf16[2048,1792]{1,0:T(8,128)(2,1)} %all-gather.8.cloned.1.call-done.wq_ref.wk_ref.wv_ref.w_ref.wf_ref, ...), custom_call_target="tpu_custom_call" | custom-call | flops 7516192768 | bytes 11534336 | tf_op jit(solution)/shard_map/inward/pallas_call | solution.py:770
  773.6 22.8 %collective-permute-done.46.across_ref = bf16[256,2048]{1,0:T(8,128)(2,1)S(1)} collective-permute-done((bf16[256,2048]{1,0:T(8,128)(2,1)}, bf16[256,2048]{1,0:T(8,128)(2,1)S(1)}, u32[]{:S(2)}, u32[]{:S(2)}) %collective-permute-start.46) | collective-permute-done | bytes 1048608 | tf_op jit(solution)/shard_map/ppermute | solution.py:421
  826.2 21.6 %collective-permute-done.50 = bf16[256,2048]{1,0:T(8,128)(2,1)S(1)} collective-permute-done((bf16[256,2048]{1,0:T(8,128)(2,1)S(1)}, bf16[256,2048]{1,0:T(8,128)(2,1)S(1)}, u32[]{:S(2)}, u32[]{:S(2)}) %collective-permute-start.50) | collective-permute-done | bytes 1048608 | tf_op jit(solution)/shard_map/ppermute | solution.py:421
  850.7 13.2 %collective-permute-done.53 = bf16[128,2048]{1,0:T(8,128)(2,1)S(1)} collective-permute-done((bf16[128,2048]{1,0:T(8,128)(2,1)S(1)}, bf16[128,2048]{1,0:T(8,128)(2,1)S(1)}, u32[]{:S(2)}, u32[]{:S(2)}) %collective-permute-start.53) | collective-permute-done | bytes 524320 | tf_op jit(solution)/shard_map/ppermute | solution.py:421
  871.4 18.8 %outer_back.3 = (bf16[2048,1792]{1,0:T(8,128)(2,1)}, bf16[2048,256]{1,0:T(8,128)(2,1)}, f32[1,1024]{1,0:T(1,128)}, f32[1,2048]{1,0:T(1,128)}) custom-call(s32[1]{0:T(128)} %bitcast.6.row_ref, bf16[2048,2048]{1,0:T(8,128)(2,1)} %constant_dynamic-update-slice_fusion.21.dy_ref, bf16[1280,512]{1,0:T(8,128)(2,1)} %get-tuple-element.197.w0_ref, ...), custom_call_target="tpu_custom_call" | custom-call | flops 10737418240 | bytes 16777216 | tf_op jit(solution)/shard_map/outer_back/pallas_call | solution.py:789
  890.1 15.9 %attend_back.3 = (bf16[2048,1792]{1,0:T(8,128)(2,1)}, f32[1,768]{1,0:T(1,128)}) custom-call(bf16[2048,256]{1,0:T(8,128)(2,1)} %get-tuple-element.94.q_ref, bf16[2048,256]{1,0:T(8,128)(2,1)} %get-tuple-element.95.k_ref, bf16[2048,256]{1,0:T(8,128)(2,1)} %get-tuple-element.96.v_ref, s32[1024,1]{1,0:T(8,128)} %bitcast.120, ...), custom_call_target="tpu_custom_call", output_to_operand_aliasing={{0}: (9, {})} | custom-call | flops 5368709120 | bytes 4194304 | tf_op jit(solution)/shard_map/attend_back/pallas_call | solution.py:846
  906.1 21.4 %convolution_convert_fusion.1 = bf16[2048,1792]{1,0:T(8,128)(2,1)} fusion(bf16[2048,2048]{1,0:T(8,128)(2,1)} %constant_dynamic-update-slice_fusion.x_ref, bf16[2048,1792]{1,0:T(8,128)(2,1)} %get-tuple-element.147.dz_ref), kind=kOutput, calls=%fused_computation.1 | convolution fusion | flops 15036055552 | bytes 23068672 | tf_op jit(solution)/shard_map/dot_general | solution.py:60
  938.0 14.0 %fusion.2 = bf16[1024,2048]{1,0:T(8,128)(2,1)} fusion(bf16[2048,2048]{1,0:T(8,128)(2,1)} %constant_dynamic-update-slice_fusion.21.dy_ref, bf16[2048,1280]{1,0:T(8,128)(2,1)} %get-tuple-element.102.act_ref), kind=kOutput, calls=%fused_computation.6 | convolution fusion | flops 8592031744 | bytes 16777216 | tf_op jit(solution)/shard_map/dot_general | solution.py:60
  952.1 13.3 %inward.7 = bf16[1024,2048]{1,0:T(8,128)(2,1)} custom-call(bf16[2048,1792]{1,0:T(8,128)(2,1)} %get-tuple-element.147.dz_ref, bf16[2048,1024]{1,0:T(8,128)(2,1)} %all-gather.4.cloned.1.call-done.w_ref.wf_ref, bf16[2048,768]{1,0:T(8,128)(2,1)} %all-gather.6.cloned.1.call-done.wq_ref.wk_ref.wv_ref, ...), custom_call_target="tpu_custom_call" | custom-call | flops 7516192768 | bytes 11534336 | tf_op jit(solution)/shard_map/inward/pallas_call | solution.py:770
  982.9 23.3 %collective-permute-done.41.across_ref = bf16[256,2048]{1,0:T(8,128)(2,1)S(1)} collective-permute-done((bf16[256,2048]{1,0:T(8,128)(2,1)}, bf16[256,2048]{1,0:T(8,128)(2,1)S(1)}, u32[]{:S(2)}, u32[]{:S(2)}) %collective-permute-start.41) | collective-permute-done | bytes 1048608 | tf_op jit(solution)/shard_map/ppermute | solution.py:421
  1033.2 13.0 %inward.6.keep_ref = bf16[1024,2048]{1,0:T(8,128)(2,1)} custom-call(bf16[2048,1792]{1,0:T(8,128)(2,1)} %get-tuple-element.147.dz_ref, bf16[2048,1024]{1,0:T(8,128)(2,1)} %all-gather.4.cloned.1.call-done.w_ref.wf_ref, bf16[2048,768]{1,0:T(8,128)(2,1)} %all-gather.6.cloned.1.call-done.wq_ref.wk_ref.wv_ref, ...), custom_call_target="tpu_custom_call" | custom-call | flops 7516192768 | bytes 11534336 | tf_op jit(solution)/shard_map/inward/pallas_call | solution.py:770
  1086.2 20.0 %collective-permute-done.68 = f32[3584]{0:T(1024)S(1)} collective-permute-done((f32[3584]{0:T(1024)S(1)}, f32[3584]{0:T(1024)S(1)}, u32[]{:S(2)}, u32[]{:S(2)}) %collective-permute-start.68) | collective-permute-done | bytes 14368 | tf_op jit(solution)/shard_map/ppermute | solution.py:421
  1152.5 32.7 %collective-permute-done.64 = bf16[512,1792]{1,0:T(8,128)(2,1)} collective-permute-done((bf16[512,1792]{1,0:T(8,128)(2,1)}, bf16[512,1792]{1,0:T(8,128)(2,1)}, u32[]{:S(2)}, u32[]{:S(2)}) %collective-permute-start.64) | collective-permute-done | bytes 1835040 | tf_op jit(solution)/shard_map/ppermute | solution.py:1059
  (470 shorter events, 503.0 us)
Async XLA Ops:
  7.2 187.6 %all-gather.6.cloned.1.call-start = ((), (), s32[]{:S(2)}) async-start(), calls=%async_computation.6 | async-start | bytes 3932160 | tf_op jit(solution)/shard_map/all_gather | solution.py:918
  39.8 222.3 %all-gather.4.cloned.1.call-start = ((), (), s32[]{:S(2)}) async-start(), calls=%async_computation.5 | async-start | bytes 5242880 | tf_op jit(solution)/shard_map/all_gather | solution.py:918
  59.9 28.8 %collective-permute-start.3 = (bf16[1280,512]{1,0:T(8,128)(2,1)}, bf16[1280,512]{1,0:T(8,128)(2,1)}, u32[]{:S(2)}, u32[]{:S(2)}) collective-permute-start(bf16[1280,512]{1,0:T(8,128)(2,1)} %pad_maximum_fusion.9), channel_id=1, source_target_pairs={{0,16},{16,0},{1,17},{17,1},{2,18},{18,2},{3,19},{19,3},{4,20},{20... | collective-permute-start | bytes 3932168 | tf_op jit(solution)/shard_map/ppermute | solution.py:421
  101.4 348.9 %all-gather.8.cloned.1.call-start = ((), (), s32[]{:S(2)}) async-start(), calls=%async_computation.7 | async-start | bytes 9175040 | tf_op jit(solution)/shard_map/all_gather | solution.py:918
  117.6 35.5 %collective-permute-start.10 = (bf16[512,2048]{1,0:T(8,128)(2,1)}, bf16[512,2048]{1,0:T(8,128)(2,1)}, u32[]{:S(2)}, u32[]{:S(2)}) collective-permute-start(bf16[512,2048]{1,0:T(8,128)(2,1)} %pad_maximum_fusion), channel_id=1, source_target_pairs={{0,1},{1,0},{2,3},{3,2},{4,5},{5,4},{6,7},{7,6},{8,9},{9,8},{10,11... | collective-permute-start | bytes 6291464 | tf_op jit(solution)/shard_map/ppermute | solution.py:421
  169.7 73.6 %collective-permute-start.5 = (bf16[1280,512]{1,0:T(8,128)(2,1)}, bf16[1280,512]{1,0:T(8,128)(2,1)}, u32[]{:S(2)}, u32[]{:S(2)}) collective-permute-start(bf16[1280,512]{1,0:T(8,128)(2,1)} %get-tuple-element.197.w0_ref), channel_id=1, source_target_pairs={{0,8},{4,12},{8,0},{12,4},{1,9},{5,13},{9,1},{13,5},{2,10},{6,14},... | collective-permute-start | bytes 3932168 | tf_op jit(solution)/shard_map/ppermute | solution.py:421
  170.3 119.8 %collective-permute-start.4 = (bf16[1280,512]{1,0:T(8,128)(2,1)}, bf16[1280,512]{1,0:T(8,128)(2,1)}, u32[]{:S(2)}, u32[]{:S(2)}) collective-permute-start(bf16[1280,512]{1,0:T(8,128)(2,1)} %get-tuple-element.197.w0_ref), channel_id=1, source_target_pairs={{12,8},{8,4},{4,0},{13,9},{9,5},{5,1},{14,10},{10,6},{6,2},{15,11}... | collective-permute-start | bytes 3932168 | tf_op jit(solution)/shard_map/ppermute | solution.py:461
  190.2 55.5 %collective-permute-start.22 = (bf16[128,2048]{1,0:T(8,128)(2,1)}, bf16[128,2048]{1,0:T(8,128)(2,1)}, u32[]{:S(2)}, u32[]{:S(2)}) collective-permute-start(bf16[128,2048]{1,0:T(8,128)(2,1)} %slice.180), channel_id=1, source_target_pairs={{0,16},{16,0},{1,17},{17,1},{2,18},{18,2},{3,19},{19,3},{4,20},{20... | collective-permute-start | bytes 1572872 | tf_op jit(solution)/shard_map/ppermute | solution.py:421
  191.7 55.4 %collective-permute-start.23 = (bf16[128,2048]{1,0:T(8,128)(2,1)}, bf16[128,2048]{1,0:T(8,128)(2,1)}, u32[]{:S(2)}, u32[]{:S(2)}) collective-permute-start(bf16[128,2048]{1,0:T(8,128)(2,1)} %slice.181), channel_id=1, source_target_pairs={{0,2},{1,3},{2,0},{3,1},{4,6},{5,7},{6,4},{7,5},{8,10},{9,11},{10,... | collective-permute-start | bytes 1572872 | tf_op jit(solution)/shard_map/ppermute | solution.py:421
  194.8 84.0 %collective-permute-start.21 = (bf16[512,2048]{1,0:T(8,128)(2,1)}, bf16[512,2048]{1,0:T(8,128)(2,1)}, u32[]{:S(2)}, u32[]{:S(2)}) collective-permute-start(bf16[512,2048]{1,0:T(8,128)(2,1)} %pad_maximum_fusion.2), channel_id=1, source_target_pairs={{0,1},{1,0},{2,3},{3,2},{4,5},{5,4},{6,7},{7,6},{8,9},{9,8},{10,11... | collective-permute-start | bytes 6291464 | tf_op jit(solution)/shard_map/ppermute | solution.py:421
  243.3 46.8 %collective-permute-start.6 = (bf16[1280,512]{1,0:T(8,128)(2,1)}, bf16[1280,512]{1,0:T(8,128)(2,1)}, u32[]{:S(2)}, u32[]{:S(2)}) collective-permute-start(bf16[1280,512]{1,0:T(8,128)(2,1)} %get-tuple-element.197.w0_ref), channel_id=1, source_target_pairs={{0,4},{4,8},{8,12},{1,5},{5,9},{9,13},{2,6},{6,10},{10,14},{3,7},{... | collective-permute-start | bytes 3932168 | tf_op jit(solution)/shard_map/ppermute | solution.py:461
  245.7 44.4 %collective-permute-start.7 = (bf16[1280,512]{1,0:T(8,128)(2,1)}, bf16[1280,512]{1,0:T(8,128)(2,1)}, u32[]{:S(2)}, u32[]{:S(2)}) collective-permute-start(bf16[1280,512]{1,0:T(8,128)(2,1)} %collective-permute-done.5.w2_ref), channel_id=1, source_target_pairs={{8,12},{4,0},{9,13},{5,1},{10,14},{6,2},{11,15},{7,3},{24,28},{20,... | collective-permute-start | bytes 3932168 | tf_op jit(solution)/shard_map/ppermute | solution.py:461
  249.9 36.9 %collective-permute-start.24 = (bf16[512,2048]{1,0:T(8,128)(2,1)}, bf16[512,2048]{1,0:T(8,128)(2,1)}, u32[]{:S(2)}, u32[]{:S(2)}) collective-permute-start(bf16[512,2048]{1,0:T(8,128)(2,1)} %pad_maximum_fusion.3), channel_id=1, source_target_pairs={{0,1},{1,0},{2,3},{3,2},{4,5},{5,4},{6,7},{7,6},{8,9},{9,8},{10,11... | collective-permute-start | bytes 6291464 | tf_op jit(solution)/shard_map/ppermute | solution.py:421
  305.4 810.4 %reduce-scatter.14.cloned.1.call-start = ((), (), s32[]{:S(2)}) async-start(), calls=%async_computation.12 | async-start | bytes 6553600 | tf_op jit(solution)/shard_map/reduce_scatter | solution.py:1016
  507.6 614.8 %reduce-scatter.8.cloned.1.call-start = ((), (), s32[]{:S(2)}) async-start(), calls=%async_computation.9 | async-start | bytes 9175040 | tf_op jit(solution)/shard_map/reduce_scatter | solution.py:1016
  508.9 113.8 %collective-permute-start.37 = (bf16[1280,512]{1,0:T(8,128)(2,1)S(1)}, bf16[1280,512]{1,0:T(8,128)(2,1)S(1)}, u32[]{:S(2)}, u32[]{:S(2)}) collective-permute-start(bf16[1280,512]{1,0:T(8,128)(2,1)S(1)} %copy-done.33), channel_id=1, source_target_pairs={{0,8},{4,12},{8,0},{12,4},{1,9},{5,13},{9,1},{13,5},{2,10},{6,14},... | collective-permute-start | bytes 3932168 | tf_op jit(solution)/shard_map/ppermute | solution.py:421
  509.5 124.5 %collective-permute-start.36 = (bf16[1280,512]{1,0:T(8,128)(2,1)S(1)}, bf16[1280,512]{1,0:T(8,128)(2,1)S(1)}, u32[]{:S(2)}, u32[]{:S(2)}) collective-permute-start(bf16[1280,512]{1,0:T(8,128)(2,1)S(1)} %copy-done.33), channel_id=1, source_target_pairs={{12,8},{8,4},{4,0},{13,9},{9,5},{5,1},{14,10},{10,6},{6,2},{15,11}... | collective-permute-start | bytes 3932168 | tf_op jit(solution)/shard_map/ppermute | solution.py:461
  510.8 123.3 %collective-permute-start.38 = (bf16[1280,512]{1,0:T(8,128)(2,1)S(1)}, bf16[1280,512]{1,0:T(8,128)(2,1)S(1)}, u32[]{:S(2)}, u32[]{:S(2)}) collective-permute-start(bf16[1280,512]{1,0:T(8,128)(2,1)S(1)} %copy-done.33), channel_id=1, source_target_pairs={{0,4},{4,8},{8,12},{1,5},{5,9},{9,13},{2,6},{6,10},{10,14},{3,7},{... | collective-permute-start | bytes 3932168 | tf_op jit(solution)/shard_map/ppermute | solution.py:461
  622.7 59.1 %collective-permute-start.39 = (bf16[1280,512]{1,0:T(8,128)(2,1)S(1)}, bf16[1280,512]{1,0:T(8,128)(2,1)S(1)}, u32[]{:S(2)}, u32[]{:S(2)}) collective-permute-start(bf16[1280,512]{1,0:T(8,128)(2,1)S(1)} %collective-permute-done.37.w2_ref), channel_id=1, source_target_pairs={{8,12},{4,0},{9,13},{5,1},{10,14},{6,2},{11,15},{7,3},{24,28},{20,... | collective-permute-start | bytes 3932168 | tf_op jit(solution)/shard_map/ppermute | solution.py:461
  731.2 34.3 %collective-permute-start.45 = (bf16[1024,2048]{1,0:T(8,128)(2,1)}, bf16[1024,2048]{1,0:T(8,128)(2,1)}, u32[]{:S(2)}, u32[]{:S(2)}) collective-permute-start(bf16[1024,2048]{1,0:T(8,128)(2,1)} %inward.5), channel_id=1, source_target_pairs={{0,1},{1,0},{2,3},{3,2},{4,5},{5,4},{6,7},{7,6},{8,9},{9,8},{10,11... | collective-permute-start | bytes 12582920 | tf_op jit(solution)/shard_map/ppermute | solution.py:421
  752.4 385.8 %reduce-scatter.6.cloned.1.call-start = ((), (), s32[]{:S(2)}) async-start(), calls=%async_computation.8 | async-start | bytes 9175040 | tf_op jit(solution)/shard_map/reduce_scatter | solution.py:1016
  770.6 25.8 %collective-permute-start.46 = (bf16[256,2048]{1,0:T(8,128)(2,1)}, bf16[256,2048]{1,0:T(8,128)(2,1)S(1)}, u32[]{:S(2)}, u32[]{:S(2)}) collective-permute-start(bf16[256,2048]{1,0:T(8,128)(2,1)} %get-tuple-element.135), channel_id=1, source_target_pairs={{0,16},{16,0},{1,17},{17,1},{2,18},{18,2},{3,19},{19,3},{4,20},{20... | collective-permute-start | bytes 3145736 | tf_op jit(solution)/shard_map/ppermute | solution.py:421
  927.5 223.3 %reduce-scatter.12.cloned.1.call-start = ((), (), s32[]{:S(2)}) async-start(), calls=%async_computation.11 | async-start | bytes 5242880 | tf_op jit(solution)/shard_map/reduce_scatter | solution.py:1016
  937.5 38.0 %collective-permute-start.40 = (bf16[1024,2048]{1,0:T(8,128)(2,1)}, bf16[1024,2048]{1,0:T(8,128)(2,1)}, u32[]{:S(2)}, u32[]{:S(2)}) collective-permute-start(bf16[1024,2048]{1,0:T(8,128)(2,1)} %outer.7), channel_id=1, source_target_pairs={{0,1},{1,0},{2,3},{3,2},{4,5},{5,4},{6,7},{7,6},{8,9},{9,8},{10,11... | collective-permute-start | bytes 12582920 | tf_op jit(solution)/shard_map/ppermute | solution.py:421
  952.0 273.0 %reduce-scatter.10.cloned.1.call-start = ((), (), s32[]{:S(2)}) async-start(), calls=%async_computation.10 | async-start | bytes 1310720 | tf_op jit(solution)/shard_map/reduce_scatter | solution.py:1016
  965.4 80.8 %collective-permute-start.58 = (bf16[1024,2048]{1,0:T(8,128)(2,1)}, bf16[1024,2048]{1,0:T(8,128)(2,1)}, u32[]{:S(2)}, u32[]{:S(2)}) collective-permute-start(bf16[1024,2048]{1,0:T(8,128)(2,1)} %inward.7), channel_id=1, source_target_pairs={{0,1},{1,0},{2,3},{3,2},{4,5},{5,4},{6,7},{7,6},{8,9},{9,8},{10,11... | collective-permute-start | bytes 12582920 | tf_op jit(solution)/shard_map/ppermute | solution.py:421
  1015.4 48.4 %collective-permute-start.57 = (bf16[256,2048]{1,0:T(8,128)(2,1)S(1)}, bf16[256,2048]{1,0:T(8,128)(2,1)S(1)}, u32[]{:S(2)}, u32[]{:S(2)}) collective-permute-start(bf16[256,2048]{1,0:T(8,128)(2,1)S(1)} %get-tuple-element.187), channel_id=1, source_target_pairs={{0,16},{16,0},{1,17},{17,1},{2,18},{18,2},{3,19},{19,3},{4,20},{20... | collective-permute-start | bytes 3145736 | tf_op jit(solution)/shard_map/ppermute | solution.py:421
  1033.1 27.9 %collective-permute-start.66 = (f32[7680]{0:T(1024)S(1)}, f32[7680]{0:T(1024)S(1)}, u32[]{:S(2)}, u32[]{:S(2)}) collective-permute-start(f32[7680]{0:T(1024)S(1)} %constant_dynamic-update-slice_fusion.29), channel_id=1, source_target_pairs={{0,4},{4,0},{8,12},{12,8},{1,5},{5,1},{9,13},{13,9},{2,6},{6,2},{1... | collective-permute-start | bytes 92168 | tf_op jit(solution)/shard_map/ppermute | solution.py:421
  1067.7 57.4 %collective-permute-start.56 = (bf16[256,2048]{1,0:T(8,128)(2,1)}, bf16[256,2048]{1,0:T(8,128)(2,1)}, u32[]{:S(2)}, u32[]{:S(2)}) collective-permute-start(bf16[256,2048]{1,0:T(8,128)(2,1)} %get-tuple-element.177), channel_id=1, source_target_pairs={{0,16},{1,17},{2,18},{3,19},{4,20},{5,21},{6,22},{7,23},{8,24},{9,... | collective-permute-start | bytes 3145736 | tf_op jit(solution)/shard_map/ppermute | solution.py:1059
  1115.8 35.0 %collective-permute-start.69 = (bf16[1280,512]{1,0:T(8,128)(2,1)}, bf16[1280,512]{1,0:T(8,128)(2,1)}, u32[]{:S(2)}, u32[]{:S(2)}) collective-permute-start(bf16[1280,512]{1,0:T(8,128)(2,1)} %reduce-scatter.14.cloned.1.call-done), channel_id=1, source_target_pairs={{0,16},{1,17},{2,18},{3,19},{4,20},{5,21},{6,22},{7,23},{8,24},{9,... | collective-permute-start | bytes 3932168 | tf_op jit(solution)/shard_map/ppermute | solution.py:1059
  1122.4 62.8 %collective-permute-start.64 = (bf16[512,1792]{1,0:T(8,128)(2,1)}, bf16[512,1792]{1,0:T(8,128)(2,1)}, u32[]{:S(2)}, u32[]{:S(2)}) collective-permute-start(bf16[512,1792]{1,0:T(8,128)(2,1)} %reduce-scatter.8.cloned.1.call-done), channel_id=1, source_target_pairs={{0,16},{1,17},{2,18},{3,19},{4,20},{5,21},{6,22},{7,23},{8,24},{9,... | collective-permute-start | bytes 5505032 | tf_op jit(solution)/shard_map/ppermute | solution.py:1059
  1138.2 51.5 %collective-permute-start.65 = (bf16[512,1792]{1,0:T(8,128)(2,1)}, bf16[512,1792]{1,0:T(8,128)(2,1)}, u32[]{:S(2)}, u32[]{:S(2)}) collective-permute-start(bf16[512,1792]{1,0:T(8,128)(2,1)} %reduce-scatter.6.cloned.1.call-done), channel_id=1, source_target_pairs={{16,0},{17,1},{18,2},{19,3},{20,4},{21,5},{22,6},{23,7},{24,8},{25... | collective-permute-start | bytes 5505032 | tf_op jit(solution)/shard_map/ppermute | solution.py:1056
  (111 other events, 1844.0 us)
Sparse Core Ops, SparseCore 0:
  39.9 64.8 all-gather.5
  107.0 116.7 all-gather.3
  305.5 144.7 all-gather.7
  507.7 162.0 reduce-scatter.13
  752.5 127.6 reduce-scatter.7
  927.6 127.7 reduce-scatter.5
  1057.6 77.2 reduce-scatter.11
  1137.2 27.7 reduce-scatter.9

commit v5 on v4

--- a/solution.py
+++ b/solution.py
@@ -1096,7 +1096,8 @@
     norms = jnp.where(low, *norm_parts) + swap(jnp.where(low, *norm_parts[::-1]), SECTION, 1)
     norms = take(sum_over(norms, COL), 1, c, deep // cols_axis)
     end_grad = take(end_grad, 0, r * cols_axis + c, deep // cols_axis)
-    fc_out_upper = to_first(after(fc_out_part0, ins_upper))
+    fc_out_part0 = after(fc_out_part0, ins_upper, norms)
+    fc_out_upper = to_first(fc_out_part0)
     fc_out_w_grad = jnp.concatenate(
         [
             jnp.where(low, fc_out_part0, outs_lower[:inner]),
@@ -1106,9 +1107,7 @@
     ).astype(F32)[None]
     qkv_w_grad = qkv_w_grad.reshape(qkv_w.shape)[None]
     fc_in_w_grad = fc_in_w_grad[None]
-    out_part0, fc_out_w_grad, norms = lax.optimization_barrier(
-        (out_part0, fc_out_w_grad, norms)
-    )
+    out_part0, norms = lax.optimization_barrier((out_part0, norms))
     out_upper = to_first(out_part0)
     out_w_grad = jnp.concatenate(
         [
@@ -1118,8 +1117,9 @@
         axis=0,
     ).astype(F32)
     last = to_second(ends[1])
+    first = to_first(grads)
+    last, first = (after(last, norms), after(first, norms))
     layer_outputs = jnp.stack([jnp.where(low, ends[0], last), jnp.where(low, middle, ends[1])])
-    first = to_first(grads)
     input_gradients = jnp.stack(
         [jnp.where(low, grads, middle_grads[0]), jnp.where(low, first, middle_grads[1])]
     )

time: 1250 us -> 1130 us (0.904)
  waiting for transfers between devices: 604 us -> 473 us
  starting transfers between devices: 88.9 us -> 104 us
    ppermute x6, waiting for transfers between devices: 57.8 us -> 0.02 us  [send(): return lax.ppermute(value, ROW, pairs)]
    ppermute x62, waiting for transfers between devices: 453 us -> 416 us  [swap(): lax.ppermute(value, axis, [(source, source ^ bit) for source in range(cou...]
    all_gather x3, waiting for transfers between devices: 29.1 us -> 0.01 us  [gathered(): return lax.all_gather(shard, ROW, axis=axis, tiled=True)]
    reduce_scatter x5, waiting for transfers between devices: 0.03 us -> 21.9 us  [reduced(): return lax.psum_scatter(value, ROW, scatter_dimension=axis, tiled=True)]
    ppermute x4, waiting for transfers between devices: 22.7 us -> 6.25 us  [to_first(): return lax.ppermute(value, SECTION, [(1, 0)])]
    ppermute x62, starting transfers between devices: 57.7 us -> 72.3 us  [swap(): lax.ppermute(value, axis, [(source, source ^ bit) for source in range(cou...]
    ppermute x3, waiting for transfers between devices: 41.3 us -> 28.8 us  [to_second(): return lax.ppermute(value, SECTION, [(0, 1)])]
    unnamed x151 -> x153, local copies, waits for them, and re-layouts: 41.9 us -> 40.1 us
  transfers between devices with their start and end apart: 83 -> 83, of which waited for: 45 -> 41; matrix products, arithmetic and copies ran while one was open for 17% -> 18% of each run, Pallas kernels for 19% -> 22%
where the time goes in v5:
time: 1130 us; the launch traced here: 1120 us
  waiting for transfers between devices  473 us (42%)
  Pallas kernels  287 us (25%)
  starting transfers between devices  104 us (9%)
  other arithmetic  87.8 us (8%)
  matrix products  81.1 us (7%)
  local copies, waits for them, and re-layouts  72.8 us (6%)
  between operations  15.5 us (1%)
    ppermute x62, waiting for transfers between devices, swap(): lax.ppermute(value, axis, [(source, source ^ bit) for source in range(cou...  416 us
    dot_general x5, matrix products, contract_rows(): lax.dot_general(first_operand, second_operand, (((0,), (0,)), ((), ())),...  80.4 us
    ppermute x62, starting transfers between devices, swap(): lax.ppermute(value, axis, [(source, source ^ bit) for source in range(cou...  72.3 us
    pallas_call x4, Pallas kernels, inward(): pl.pallas_call(inward_kernel, grid=(rows // ROW_BLOCK,), in_specs=[split_...  51.4 us
    pallas_call x8, Pallas kernels, column_call(): pl.pallas_call(kernel, grid=(width // tile,), in_specs=[spec(member.shape...  44.7 us
    pallas_call x4, Pallas kernels, outer(): pl.pallas_call(outer_kernel, grid=(rows // ROW_BLOCK,), in_specs=[pl.Bloc...  40.1 us
    unnamed x153, local copies, waits for them, and re-layouts  40.1 us
    pallas_call x2, Pallas kernels, outer_back(): pl.pallas_call(outer_back_kernel, grid=(rows // ROW_BLOCK,), in_specs=[pl...  38 us
  transfers between devices with their start and end apart: 83, of which 41 were waited for; matrix products, arithmetic and copies ran while one was open for 18% of the time, Pallas kernels for 22%

profile of v5, /device:TPU:0, one launch (start us, length us, event | category | flops | bytes accessed | tf_op | source)
XLA Modules:
  0.0 1121.6 jit_solution(8688288712463456250)
XLA Ops:
  22.0 14.0 %collective-permute-done.1 = bf16[512,768]{1,0:T(8,128)(2,1)} collective-permute-done((bf16[512,768]{1,0:T(8,128)(2,1)}, bf16[512,768]{1,0:T(8,128)(2,1)}, u32[]{:S(2)}, u32[]{:S(2)}) %collective-permute-start.1) | collective-permute-done | bytes 786464 | tf_op jit(solution)/shard_map/ppermute | solution.py:421
  44.7 15.2 %collective-permute-done.2 = bf16[512,1024]{1,0:T(8,128)(2,1)} collective-permute-done((bf16[512,1024]{1,0:T(8,128)(2,1)S(1)}, bf16[512,1024]{1,0:T(8,128)(2,1)}, u32[]{:S(2)}, u32[]{:S(2)}) %collective-permute-start.2) | collective-permute-done | bytes 1048608 | tf_op jit(solution)/shard_map/ppermute | solution.py:421
  60.7 28.1 %collective-permute-done.3 = bf16[1280,512]{1,0:T(8,128)(2,1)} collective-permute-done((bf16[1280,512]{1,0:T(8,128)(2,1)}, bf16[1280,512]{1,0:T(8,128)(2,1)}, u32[]{:S(2)}, u32[]{:S(2)}) %collective-permute-start.3) | collective-permute-done | bytes 1310752 | tf_op jit(solution)/shard_map/ppermute | solution.py:421
  101.5 12.0 %collective-permute-done.8 = bf16[256,2048]{1,0:T(8,128)(2,1)} collective-permute-done((bf16[256,2048]{1,0:T(8,128)(2,1)}, bf16[256,2048]{1,0:T(8,128)(2,1)}, u32[]{:S(2)}, u32[]{:S(2)}) %collective-permute-start.8) | collective-permute-done | bytes 1048608 | tf_op jit(solution)/shard_map/ppermute | solution.py:421
  172.7 15.6 %collective-permute-done.19 = bf16[256,2048]{1,0:T(8,128)(2,1)S(1)} collective-permute-done((bf16[256,2048]{1,0:T(8,128)(2,1)S(1)}, bf16[256,2048]{1,0:T(8,128)(2,1)S(1)}, u32[]{:S(2)}, u32[]{:S(2)}) %collective-permute-start.19) | collective-permute-done | bytes 1048608 | tf_op jit(solution)/shard_map/ppermute | solution.py:421
  194.8 12.8 %project.2 = (bf16[2048,256]{1,0:T(8,128)(2,1)}, bf16[2048,256]{1,0:T(8,128)(2,1)}, bf16[2048,256]{1,0:T(8,128)(2,1)}) custom-call(bf16[2048,2048]{1,0:T(8,128)(2,1)} %constant_dynamic-update-slice_fusion.x_ref, bf16[2048,768]{1,0:T(8,128)(2,1)} %all-gather.6.cloned.1.call-done.wq_ref.wk_ref.wv_ref, ...), custom_call_target="tpu_custom_call" | custom-call | flops 6442450944 | bytes 11534336 | tf_op jit(solution)/shard_map/project/pallas_call | solution.py:713
  207.6 35.7 %collective-permute-done.5.w2_ref = bf16[1280,512]{1,0:T(8,128)(2,1)} collective-permute-done((bf16[1280,512]{1,0:T(8,128)(2,1)}, bf16[1280,512]{1,0:T(8,128)(2,1)}, u32[]{:S(2)}, u32[]{:S(2)}) %collective-permute-start.5) | collective-permute-done | bytes 1310752 | tf_op jit(solution)/shard_map/ppermute | solution.py:421
  262.3 16.7 %inner.2 = (bf16[2048,1280]{1,0:T(8,128)(2,1)}, bf16[2048,1024]{1,0:T(8,128)(2,1)}) custom-call(bf16[2048,2048]{1,0:T(8,128)(2,1)} %constant_dynamic-update-slice_fusion.x_ref, bf16[2048,1024]{1,0:T(8,128)(2,1)} %all-gather.4.cloned.1.call-done.w_ref.wf_ref, f32[1,1024]{1,0:T(1,128)} %bitcast.170, ...), custom_call_target="tpu_custom_call", output_to_operand_aliasing={{0}: (3, {})} | custom-call | flops 8589934592 | bytes 16777216 | tf_op jit(solution)/shard_map/inner/pallas_call | solution.py:728
  323.4 22.5 %collective-permute-done.26.across_ref = bf16[256,2048]{1,0:T(8,128)(2,1)S(1)} collective-permute-done((bf16[256,2048]{1,0:T(8,128)(2,1)}, bf16[256,2048]{1,0:T(8,128)(2,1)S(1)}, u32[]{:S(2)}, u32[]{:S(2)}) %collective-permute-start.26) | collective-permute-done | bytes 1048608 | tf_op jit(solution)/shard_map/ppermute | solution.py:421
  374.3 21.2 %collective-permute-done.30 = bf16[256,2048]{1,0:T(8,128)(2,1)S(1)} collective-permute-done((bf16[256,2048]{1,0:T(8,128)(2,1)S(1)}, bf16[256,2048]{1,0:T(8,128)(2,1)S(1)}, u32[]{:S(2)}, u32[]{:S(2)}) %collective-permute-start.30) | collective-permute-done | bytes 1048608 | tf_op jit(solution)/shard_map/ppermute | solution.py:421
  398.5 14.9 %collective-permute-start.37 = (bf16[1280,512]{1,0:T(8,128)(2,1)S(1)}, bf16[1280,512]{1,0:T(8,128)(2,1)}, u32[]{:S(2)}, u32[]{:S(2)}) collective-permute-start(bf16[1280,512]{1,0:T(8,128)(2,1)S(1)} %copy-done.33), channel_id=1, source_target_pairs={{0,8},{4,12},{8,0},{12,4},{1,9},{5,13},{9,1},{13,5},{2,10},{6,14},... | collective-permute-start | bytes 3932168 | tf_op jit(solution)/shard_map/ppermute | solution.py:421
  422.6 83.4 %collective-permute-done.37.w2_ref = bf16[1280,512]{1,0:T(8,128)(2,1)} collective-permute-done((bf16[1280,512]{1,0:T(8,128)(2,1)S(1)}, bf16[1280,512]{1,0:T(8,128)(2,1)}, u32[]{:S(2)}, u32[]{:S(2)}) %collective-permute-start.37) | collective-permute-done | bytes 1310752 | tf_op jit(solution)/shard_map/ppermute | solution.py:421
  514.4 12.9 %project.3 = (bf16[2048,256]{1,0:T(8,128)(2,1)}, bf16[2048,256]{1,0:T(8,128)(2,1)}, bf16[2048,256]{1,0:T(8,128)(2,1)}) custom-call(bf16[2048,2048]{1,0:T(8,128)(2,1)} %constant_dynamic-update-slice_fusion.14.x_ref, bf16[2048,1792]{1,0:T(8,128)(2,1)} %all-gather.8.cloned.1.call-done.wq_ref.wk_ref.wv_ref.w_ref.wf_ref, ...), custom_call_target="tpu_custom_call" | custom-call | flops 6442450944 | bytes 11534336 | tf_op jit(solution)/shard_map/project/pallas_call | solution.py:713
  538.2 16.7 %inner.3 = (bf16[2048,1280]{1,0:T(8,128)(2,1)}, bf16[2048,1024]{1,0:T(8,128)(2,1)}) custom-call(bf16[2048,2048]{1,0:T(8,128)(2,1)} %constant_dynamic-update-slice_fusion.14.x_ref, bf16[2048,1792]{1,0:T(8,128)(2,1)} %all-gather.8.cloned.1.call-done.wq_ref.wk_ref.wv_ref.w_ref.wf_ref, f32[1,1024]{1,0:T(1,128)} %bitcast.171, ...), custom_call_target="tpu_custom_call", output_to_operand_aliasing={{0}: (3, {})} | custom-call | flops 8589934592 | bytes 16777216 | tf_op jit(solution)/shard_map/inner/pallas_call | solution.py:728
  554.9 16.7 %convolution_convert_fusion.2 = bf16[1280,2048]{1,0:T(8,128)(2,1)} fusion(bf16[2048,1280]{1,0:T(8,128)(2,1)} %get-tuple-element.119.act_ref, bf16[2048,2048]{1,0:T(8,128)(2,1)} %constant_dynamic-update-slice_fusion.7.dy_ref), kind=kOutput, calls=%fused_computation.2 | convolution fusion | flops 10740039680 | bytes 18874368 | tf_op jit(solution)/shard_map/dot_general | solution.py:60
  575.0 18.8 %outer_back.2 = (bf16[2048,1792]{1,0:T(8,128)(2,1)}, bf16[2048,256]{1,0:T(8,128)(2,1)}, f32[1,1024]{1,0:T(1,128)}, f32[1,2048]{1,0:T(1,128)}) custom-call(s32[1]{0:T(128)} %bitcast.6.row_ref, bf16[2048,2048]{1,0:T(8,128)(2,1)} %constant_dynamic-update-slice_fusion.7.dy_ref, bf16[1280,512]{1,0:T(8,128)(2,1)} %get-tuple-element.198.w0_ref, ...), custom_call_target="tpu_custom_call" | custom-call | flops 10737418240 | bytes 16777216 | tf_op jit(solution)/shard_map/outer_back/pallas_call | solution.py:789
  593.9 15.9 %attend_back.2 = (bf16[2048,1792]{1,0:T(8,128)(2,1)}, f32[1,768]{1,0:T(1,128)}) custom-call(bf16[2048,256]{1,0:T(8,128)(2,1)} %get-tuple-element.115.q_ref, bf16[2048,256]{1,0:T(8,128)(2,1)} %get-tuple-element.116.k_ref, bf16[2048,256]{1,0:T(8,128)(2,1)} %get-tuple-element.117.v_ref, s32[1024,1]{1,0:T(8,128)} %bitcast.119, ...), custom_call_target="tpu_custom_call", output_to_operand_aliasing={{0}: (9, {})} | custom-call | flops 5368709120 | bytes 4194304 | tf_op jit(solution)/shard_map/attend_back/pallas_call | solution.py:846
  609.7 21.4 %convolution_convert_fusion = bf16[2048,1792]{1,0:T(8,128)(2,1)} fusion(bf16[2048,2048]{1,0:T(8,128)(2,1)} %constant_dynamic-update-slice_fusion.14.x_ref, bf16[2048,1792]{1,0:T(8,128)(2,1)} %get-tuple-element.135.dz_ref), kind=kOutput, calls=%fused_computation | convolution fusion | flops 15036055552 | bytes 23068672 | tf_op jit(solution)/shard_map/dot_general | solution.py:60
  631.2 12.9 %inward.5 = bf16[1024,2048]{1,0:T(8,128)(2,1)} custom-call(bf16[2048,1792]{1,0:T(8,128)(2,1)} %get-tuple-element.135.dz_ref, bf16[2048,1792]{1,0:T(8,128)(2,1)} %all-gather.8.cloned.1.call-done.wq_ref.wk_ref.wv_ref.w_ref.wf_ref, bf16[2048,1792]{1,0:T(8,128)(2,1)} %all-gather.8.cloned.1.call-done.wq_ref.wk_ref.wv_ref.w_ref.wf_ref, ...), custom_call_target="tpu_custom_call" | custom-call | flops 7516192768 | bytes 11534336 | tf_op jit(solution)/shard_map/inward/pallas_call | solution.py:770
  644.2 12.8 %inward.4.keep_ref = bf16[1024,2048]{1,0:T(8,128)(2,1)} custom-call(bf16[2048,1792]{1,0:T(8,128)(2,1)} %get-tuple-element.135.dz_ref, bf16[2048,1792]{1,0:T(8,128)(2,1)} %all-gather.8.cloned.1.call-done.wq_ref.wk_ref.wv_ref.w_ref.wf_ref, bf16[2048,1792]{1,0:T(8,128)(2,1)} %all-gather.8.cloned.1.call-done.wq_ref.wk_ref.wv_ref.w_ref.wf_ref, ...), custom_call_target="tpu_custom_call" | custom-call | flops 7516192768 | bytes 11534336 | tf_op jit(solution)/shard_map/inward/pallas_call | solution.py:770
  665.1 22.7 %collective-permute-done.46.across_ref = bf16[256,2048]{1,0:T(8,128)(2,1)S(1)} collective-permute-done((bf16[256,2048]{1,0:T(8,128)(2,1)}, bf16[256,2048]{1,0:T(8,128)(2,1)S(1)}, u32[]{:S(2)}, u32[]{:S(2)}) %collective-permute-start.46) | collective-permute-done | bytes 1048608 | tf_op jit(solution)/shard_map/ppermute | solution.py:421
  717.3 21.4 %collective-permute-done.50 = bf16[256,2048]{1,0:T(8,128)(2,1)S(1)} collective-permute-done((bf16[256,2048]{1,0:T(8,128)(2,1)S(1)}, bf16[256,2048]{1,0:T(8,128)(2,1)S(1)}, u32[]{:S(2)}, u32[]{:S(2)}) %collective-permute-start.50) | collective-permute-done | bytes 1048608 | tf_op jit(solution)/shard_map/ppermute | solution.py:421
  741.7 13.2 %collective-permute-done.53 = bf16[128,2048]{1,0:T(8,128)(2,1)S(1)} collective-permute-done((bf16[128,2048]{1,0:T(8,128)(2,1)S(1)}, bf16[128,2048]{1,0:T(8,128)(2,1)S(1)}, u32[]{:S(2)}, u32[]{:S(2)}) %collective-permute-start.53) | collective-permute-done | bytes 524320 | tf_op jit(solution)/shard_map/ppermute | solution.py:421
  762.3 19.2 %outer_back.3 = (bf16[2048,1792]{1,0:T(8,128)(2,1)}, bf16[2048,256]{1,0:T(8,128)(2,1)}, f32[1,1024]{1,0:T(1,128)}, f32[1,2048]{1,0:T(1,128)}) custom-call(s32[1]{0:T(128)} %bitcast.6.row_ref, bf16[2048,2048]{1,0:T(8,128)(2,1)} %constant_dynamic-update-slice_fusion.21.dy_ref, bf16[1280,512]{1,0:T(8,128)(2,1)} %get-tuple-element.199.w0_ref, ...), custom_call_target="tpu_custom_call" | custom-call | flops 10737418240 | bytes 16777216 | tf_op jit(solution)/shard_map/outer_back/pallas_call | solution.py:789
  781.4 15.9 %attend_back.3 = (bf16[2048,1792]{1,0:T(8,128)(2,1)}, f32[1,768]{1,0:T(1,128)}) custom-call(bf16[2048,256]{1,0:T(8,128)(2,1)} %get-tuple-element.95.q_ref, bf16[2048,256]{1,0:T(8,128)(2,1)} %get-tuple-element.96.k_ref, bf16[2048,256]{1,0:T(8,128)(2,1)} %get-tuple-element.97.v_ref, s32[1024,1]{1,0:T(8,128)} %bitcast.120, ...), custom_call_target="tpu_custom_call", output_to_operand_aliasing={{0}: (9, {})} | custom-call | flops 5368709120 | bytes 4194304 | tf_op jit(solution)/shard_map/attend_back/pallas_call | solution.py:846
  797.4 21.2 %convolution_convert_fusion.1 = bf16[2048,1792]{1,0:T(8,128)(2,1)} fusion(bf16[2048,2048]{1,0:T(8,128)(2,1)} %constant_dynamic-update-slice_fusion.x_ref, bf16[2048,1792]{1,0:T(8,128)(2,1)} %get-tuple-element.148.dz_ref), kind=kOutput, calls=%fused_computation.1 | convolution fusion | flops 15036055552 | bytes 23068672 | tf_op jit(solution)/shard_map/dot_general | solution.py:60
  829.1 14.0 %fusion.2 = bf16[1024,2048]{1,0:T(8,128)(2,1)} fusion(bf16[2048,2048]{1,0:T(8,128)(2,1)} %constant_dynamic-update-slice_fusion.21.dy_ref, bf16[2048,1280]{1,0:T(8,128)(2,1)} %get-tuple-element.103.act_ref), kind=kOutput, calls=%fused_computation.6 | convolution fusion | flops 8592031744 | bytes 16777216 | tf_op jit(solution)/shard_map/dot_general | solution.py:60
  861.0 12.8 %inward.7 = bf16[1024,2048]{1,0:T(8,128)(2,1)} custom-call(bf16[2048,1792]{1,0:T(8,128)(2,1)} %get-tuple-element.148.dz_ref, bf16[2048,1024]{1,0:T(8,128)(2,1)} %all-gather.4.cloned.1.call-done.w_ref.wf_ref, bf16[2048,768]{1,0:T(8,128)(2,1)} %all-gather.6.cloned.1.call-done.wq_ref.wk_ref.wv_ref, ...), custom_call_target="tpu_custom_call" | custom-call | flops 7516192768 | bytes 11534336 | tf_op jit(solution)/shard_map/inward/pallas_call | solution.py:770
  922.1 12.8 %inward.6.keep_ref = bf16[1024,2048]{1,0:T(8,128)(2,1)} custom-call(bf16[2048,1792]{1,0:T(8,128)(2,1)} %get-tuple-element.148.dz_ref, bf16[2048,1024]{1,0:T(8,128)(2,1)} %all-gather.4.cloned.1.call-done.w_ref.wf_ref, bf16[2048,768]{1,0:T(8,128)(2,1)} %all-gather.6.cloned.1.call-done.wq_ref.wk_ref.wv_ref, ...), custom_call_target="tpu_custom_call" | custom-call | flops 7516192768 | bytes 11534336 | tf_op jit(solution)/shard_map/inward/pallas_call | solution.py:770
  950.5 14.8 %collective-permute-done.64.across_ref = bf16[256,2048]{1,0:T(8,128)(2,1)} collective-permute-done((bf16[256,2048]{1,0:T(8,128)(2,1)}, bf16[256,2048]{1,0:T(8,128)(2,1)}, u32[]{:S(2)}, u32[]{:S(2)}) %collective-permute-start.64) | collective-permute-done | bytes 1048608 | tf_op jit(solution)/shard_map/ppermute | solution.py:421
  1009.9 28.8 %collective-permute-done.69 = bf16[512,1792]{1,0:T(8,128)(2,1)} collective-permute-done((bf16[512,1792]{1,0:T(8,128)(2,1)}, bf16[512,1792]{1,0:T(8,128)(2,1)}, u32[]{:S(2)}, u32[]{:S(2)}) %collective-permute-start.69) | collective-permute-done | bytes 1835040 | tf_op jit(solution)/shard_map/ppermute | solution.py:1059
  1076.9 21.8 %reduce-scatter.6.cloned.1.call-done = bf16[256,512]{1,0:T(8,128)(2,1)} async-done(((bf16[256,2048]{1,0:T(8,128)(2,1)}), bf16[256,512]{1,0:T(8,128)(2,1)}) %reduce-scatter.6.cloned.1.call-update) | async-done | bytes 262160 | tf_op jit(solution)/shard_map/reduce_scatter | solution.py:1016
  (472 shorter events, 467.2 us)
Async XLA Ops:
  7.2 187.6 %all-gather.6.cloned.1.call-start = ((), (), s32[]{:S(2)}) async-start(), calls=%async_computation.6 | async-start | bytes 3932160 | tf_op jit(solution)/shard_map/all_gather | solution.py:918
  39.8 222.5 %all-gather.4.cloned.1.call-start = ((), (), s32[]{:S(2)}) async-start(), calls=%async_computation.5 | async-start | bytes 5242880 | tf_op jit(solution)/shard_map/all_gather | solution.py:918
  101.4 413.0 %all-gather.8.cloned.1.call-start = ((), (), s32[]{:S(2)}) async-start(), calls=%async_computation.7 | async-start | bytes 9175040 | tf_op jit(solution)/shard_map/all_gather | solution.py:918
  117.6 35.6 %collective-permute-start.10 = (bf16[512,2048]{1,0:T(8,128)(2,1)}, bf16[512,2048]{1,0:T(8,128)(2,1)}, u32[]{:S(2)}, u32[]{:S(2)}) collective-permute-start(bf16[512,2048]{1,0:T(8,128)(2,1)} %pad_maximum_fusion), channel_id=1, source_target_pairs={{0,1},{1,0},{2,3},{3,2},{4,5},{5,4},{6,7},{7,6},{8,9},{9,8},{10,11... | collective-permute-start | bytes 6291464 | tf_op jit(solution)/shard_map/ppermute | solution.py:421
  169.7 73.6 %collective-permute-start.5 = (bf16[1280,512]{1,0:T(8,128)(2,1)}, bf16[1280,512]{1,0:T(8,128)(2,1)}, u32[]{:S(2)}, u32[]{:S(2)}) collective-permute-start(bf16[1280,512]{1,0:T(8,128)(2,1)} %get-tuple-element.199.w0_ref), channel_id=1, source_target_pairs={{0,8},{4,12},{8,0},{12,4},{1,9},{5,13},{9,1},{13,5},{2,10},{6,14},... | collective-permute-start | bytes 3932168 | tf_op jit(solution)/shard_map/ppermute | solution.py:421
  170.4 119.8 %collective-permute-start.4 = (bf16[1280,512]{1,0:T(8,128)(2,1)}, bf16[1280,512]{1,0:T(8,128)(2,1)}, u32[]{:S(2)}, u32[]{:S(2)}) collective-permute-start(bf16[1280,512]{1,0:T(8,128)(2,1)} %get-tuple-element.199.w0_ref), channel_id=1, source_target_pairs={{12,8},{8,4},{4,0},{13,9},{9,5},{5,1},{14,10},{10,6},{6,2},{15,11}... | collective-permute-start | bytes 3932168 | tf_op jit(solution)/shard_map/ppermute | solution.py:461
  190.2 55.4 %collective-permute-start.22 = (bf16[128,2048]{1,0:T(8,128)(2,1)}, bf16[128,2048]{1,0:T(8,128)(2,1)}, u32[]{:S(2)}, u32[]{:S(2)}) collective-permute-start(bf16[128,2048]{1,0:T(8,128)(2,1)} %slice.184), channel_id=1, source_target_pairs={{0,16},{16,0},{1,17},{17,1},{2,18},{18,2},{3,19},{19,3},{4,20},{20... | collective-permute-start | bytes 1572872 | tf_op jit(solution)/shard_map/ppermute | solution.py:421
  191.8 55.6 %collective-permute-start.23 = (bf16[128,2048]{1,0:T(8,128)(2,1)}, bf16[128,2048]{1,0:T(8,128)(2,1)}, u32[]{:S(2)}, u32[]{:S(2)}) collective-permute-start(bf16[128,2048]{1,0:T(8,128)(2,1)} %slice.185), channel_id=1, source_target_pairs={{0,2},{1,3},{2,0},{3,1},{4,6},{5,7},{6,4},{7,5},{8,10},{9,11},{10,... | collective-permute-start | bytes 1572872 | tf_op jit(solution)/shard_map/ppermute | solution.py:421
  194.8 84.2 %collective-permute-start.21 = (bf16[512,2048]{1,0:T(8,128)(2,1)}, bf16[512,2048]{1,0:T(8,128)(2,1)}, u32[]{:S(2)}, u32[]{:S(2)}) collective-permute-start(bf16[512,2048]{1,0:T(8,128)(2,1)} %pad_maximum_fusion.2), channel_id=1, source_target_pairs={{0,1},{1,0},{2,3},{3,2},{4,5},{5,4},{6,7},{7,6},{8,9},{9,8},{10,11... | collective-permute-start | bytes 6291464 | tf_op jit(solution)/shard_map/ppermute | solution.py:421
  243.3 46.8 %collective-permute-start.6 = (bf16[1280,512]{1,0:T(8,128)(2,1)}, bf16[1280,512]{1,0:T(8,128)(2,1)}, u32[]{:S(2)}, u32[]{:S(2)}) collective-permute-start(bf16[1280,512]{1,0:T(8,128)(2,1)} %get-tuple-element.199.w0_ref), channel_id=1, source_target_pairs={{0,4},{4,8},{8,12},{1,5},{5,9},{9,13},{2,6},{6,10},{10,14},{3,7},{... | collective-permute-start | bytes 3932168 | tf_op jit(solution)/shard_map/ppermute | solution.py:461
  245.6 44.5 %collective-permute-start.7 = (bf16[1280,512]{1,0:T(8,128)(2,1)}, bf16[1280,512]{1,0:T(8,128)(2,1)}, u32[]{:S(2)}, u32[]{:S(2)}) collective-permute-start(bf16[1280,512]{1,0:T(8,128)(2,1)} %collective-permute-done.5.w2_ref), channel_id=1, source_target_pairs={{8,12},{4,0},{9,13},{5,1},{10,14},{6,2},{11,15},{7,3},{24,28},{20,... | collective-permute-start | bytes 3932168 | tf_op jit(solution)/shard_map/ppermute | solution.py:461
  250.2 36.8 %collective-permute-start.24 = (bf16[512,2048]{1,0:T(8,128)(2,1)}, bf16[512,2048]{1,0:T(8,128)(2,1)}, u32[]{:S(2)}, u32[]{:S(2)}) collective-permute-start(bf16[512,2048]{1,0:T(8,128)(2,1)} %pad_maximum_fusion.3), channel_id=1, source_target_pairs={{0,1},{1,0},{2,3},{3,2},{4,5},{5,4},{6,7},{7,6},{8,9},{9,8},{10,11... | collective-permute-start | bytes 6291464 | tf_op jit(solution)/shard_map/ppermute | solution.py:421
  305.4 669.9 %reduce-scatter.10.cloned.1.call-start = ((), (), s32[]{:S(2)}) async-start(), calls=%async_computation.10 | async-start | bytes 9175040 | tf_op jit(solution)/shard_map/reduce_scatter | solution.py:1016
  397.0 111.5 %collective-permute-start.32 = (bf16[512,2048]{1,0:T(8,128)(2,1)S(1)}, bf16[512,2048]{1,0:T(8,128)(2,1)S(1)}, u32[]{:S(2)}, u32[]{:S(2)}) collective-permute-start(bf16[512,2048]{1,0:T(8,128)(2,1)S(1)} %pad_maximum_fusion.4), channel_id=1, source_target_pairs={{0,1},{1,0},{2,3},{3,2},{4,5},{5,4},{6,7},{7,6},{8,9},{9,8},{10,11... | collective-permute-start | bytes 6291464 | tf_op jit(solution)/shard_map/ppermute | solution.py:421
  398.5 107.6 %collective-permute-start.37 = (bf16[1280,512]{1,0:T(8,128)(2,1)S(1)}, bf16[1280,512]{1,0:T(8,128)(2,1)}, u32[]{:S(2)}, u32[]{:S(2)}) collective-permute-start(bf16[1280,512]{1,0:T(8,128)(2,1)S(1)} %copy-done.33), channel_id=1, source_target_pairs={{0,8},{4,12},{8,0},{12,4},{1,9},{5,13},{9,1},{13,5},{2,10},{6,14},... | collective-permute-start | bytes 3932168 | tf_op jit(solution)/shard_map/ppermute | solution.py:421
  413.7 99.3 %collective-permute-start.35 = (bf16[512,2048]{1,0:T(8,128)(2,1)S(1)}, bf16[512,2048]{1,0:T(8,128)(2,1)S(1)}, u32[]{:S(2)}, u32[]{:S(2)}) collective-permute-start(bf16[512,2048]{1,0:T(8,128)(2,1)S(1)} %pad_maximum_fusion.5), channel_id=1, source_target_pairs={{0,1},{1,0},{2,3},{3,2},{4,5},{5,4},{6,7},{7,6},{8,9},{9,8},{10,11... | collective-permute-start | bytes 6291464 | tf_op jit(solution)/shard_map/ppermute | solution.py:421
  415.6 155.9 %collective-permute-start.36 = (bf16[1280,512]{1,0:T(8,128)(2,1)S(1)}, bf16[1280,512]{1,0:T(8,128)(2,1)}, u32[]{:S(2)}, u32[]{:S(2)}) collective-permute-start(bf16[1280,512]{1,0:T(8,128)(2,1)S(1)} %copy-done.33), channel_id=1, source_target_pairs={{12,8},{8,4},{4,0},{13,9},{9,5},{5,1},{14,10},{10,6},{6,2},{15,11}... | collective-permute-start | bytes 3932168 | tf_op jit(solution)/shard_map/ppermute | solution.py:461
  416.9 154.6 %collective-permute-start.38 = (bf16[1280,512]{1,0:T(8,128)(2,1)S(1)}, bf16[1280,512]{1,0:T(8,128)(2,1)}, u32[]{:S(2)}, u32[]{:S(2)}) collective-permute-start(bf16[1280,512]{1,0:T(8,128)(2,1)S(1)} %copy-done.33), channel_id=1, source_target_pairs={{0,4},{4,8},{8,12},{1,5},{5,9},{9,13},{2,6},{6,10},{10,14},{3,7},{... | collective-permute-start | bytes 3932168 | tf_op jit(solution)/shard_map/ppermute | solution.py:461
  506.1 65.5 %collective-permute-start.39 = (bf16[1280,512]{1,0:T(8,128)(2,1)}, bf16[1280,512]{1,0:T(8,128)(2,1)}, u32[]{:S(2)}, u32[]{:S(2)}) collective-permute-start(bf16[1280,512]{1,0:T(8,128)(2,1)} %collective-permute-done.37.w2_ref), channel_id=1, source_target_pairs={{8,12},{4,0},{9,13},{5,1},{10,14},{6,2},{11,15},{7,3},{24,28},{20,... | collective-permute-start | bytes 3932168 | tf_op jit(solution)/shard_map/ppermute | solution.py:461
  631.1 358.2 %reduce-scatter.12.cloned.1.call-start = ((), (), s32[]{:S(2)}) async-start(), calls=%async_computation.11 | async-start | bytes 6553600 | tf_op jit(solution)/shard_map/reduce_scatter | solution.py:1016
  698.7 303.2 %reduce-scatter.8.cloned.1.call-start = ((), (), s32[]{:S(2)}) async-start(), calls=%async_computation.9 | async-start | bytes 9175040 | tf_op jit(solution)/shard_map/reduce_scatter | solution.py:1016
  818.6 257.0 %reduce-scatter.14.cloned.1.call-start = ((), (), s32[]{:S(2)}) async-start(), calls=%async_computation.12 | async-start | bytes 5242880 | tf_op jit(solution)/shard_map/reduce_scatter | solution.py:1016
  843.2 255.6 %reduce-scatter.6.cloned.1.call-start = ((), (), s32[]{:S(2)}) async-start(), calls=%async_computation.8 | async-start | bytes 1310720 | tf_op jit(solution)/shard_map/reduce_scatter | solution.py:1016
  873.8 61.2 %collective-permute-start.63 = (bf16[1024,2048]{1,0:T(8,128)(2,1)}, bf16[1024,2048]{1,0:T(8,128)(2,1)}, u32[]{:S(2)}, u32[]{:S(2)}) collective-permute-start(bf16[1024,2048]{1,0:T(8,128)(2,1)} %inward.7), channel_id=1, source_target_pairs={{0,1},{1,0},{2,3},{3,2},{4,5},{5,4},{6,7},{7,6},{8,9},{9,8},{10,11... | collective-permute-start | bytes 12582920 | tf_op jit(solution)/shard_map/ppermute | solution.py:421
  893.2 49.7 %collective-permute-start.62 = (bf16[256,2048]{1,0:T(8,128)(2,1)S(1)}, bf16[256,2048]{1,0:T(8,128)(2,1)S(1)}, u32[]{:S(2)}, u32[]{:S(2)}) collective-permute-start(bf16[256,2048]{1,0:T(8,128)(2,1)S(1)} %get-tuple-element.189), channel_id=1, source_target_pairs={{0,16},{16,0},{1,17},{17,1},{2,18},{18,2},{3,19},{19,3},{4,20},{20... | collective-permute-start | bytes 3145736 | tf_op jit(solution)/shard_map/ppermute | solution.py:421
  946.4 153.9 %collective-permute-start.56 = (bf16[256,2048]{1,0:T(8,128)(2,1)}, bf16[256,2048]{1,0:T(8,128)(2,1)}, u32[]{:S(2)}, u32[]{:S(2)}) collective-permute-start(bf16[256,2048]{1,0:T(8,128)(2,1)} %get-tuple-element.179), channel_id=1, source_target_pairs={{0,16},{1,17},{2,18},{3,19},{4,20},{5,21},{6,22},{7,23},{8,24},{9,... | collective-permute-start | bytes 3145736 | tf_op jit(solution)/shard_map/ppermute | solution.py:1059
  950.3 37.7 %collective-permute-start.71 = (f32[3584]{0:T(1024)S(1)}, f32[3584]{0:T(1024)S(1)}, u32[]{:S(2)}, u32[]{:S(2)}) collective-permute-start(f32[3584]{0:T(1024)S(1)} %slice.246), channel_id=1, source_target_pairs={{0,16},{16,0},{1,17},{17,1},{2,18},{18,2},{3,19},{19,3},{4,20},{20... | collective-permute-start | bytes 43016 | tf_op jit(solution)/shard_map/ppermute | solution.py:421
  975.3 63.4 %collective-permute-start.69 = (bf16[512,1792]{1,0:T(8,128)(2,1)}, bf16[512,1792]{1,0:T(8,128)(2,1)}, u32[]{:S(2)}, u32[]{:S(2)}) collective-permute-start(bf16[512,1792]{1,0:T(8,128)(2,1)} %reduce-scatter.10.cloned.1.call-done), channel_id=1, source_target_pairs={{0,16},{1,17},{2,18},{3,19},{4,20},{5,21},{6,22},{7,23},{8,24},{9,... | collective-permute-start | bytes 5505032 | tf_op jit(solution)/shard_map/ppermute | solution.py:1059
  989.4 113.9 %collective-permute-start.72 = (bf16[1280,512]{1,0:T(8,128)(2,1)}, bf16[1280,512]{1,0:T(8,128)(2,1)}, u32[]{:S(2)}, u32[]{:S(2)}) collective-permute-start(bf16[1280,512]{1,0:T(8,128)(2,1)} %reduce-scatter.12.cloned.1.call-done), channel_id=1, source_target_pairs={{0,16},{1,17},{2,18},{3,19},{4,20},{5,21},{6,22},{7,23},{8,24},{9,... | collective-permute-start | bytes 3932168 | tf_op jit(solution)/shard_map/ppermute | solution.py:1059
  1001.8 45.1 %collective-permute-start.70 = (bf16[512,1792]{1,0:T(8,128)(2,1)}, bf16[512,1792]{1,0:T(8,128)(2,1)S(1)}, u32[]{:S(2)}, u32[]{:S(2)}) collective-permute-start(bf16[512,1792]{1,0:T(8,128)(2,1)} %reduce-scatter.8.cloned.1.call-done), channel_id=1, source_target_pairs={{16,0},{17,1},{18,2},{19,3},{20,4},{21,5},{22,6},{23,7},{24,8},{25... | collective-permute-start | bytes 5505032 | tf_op jit(solution)/shard_map/ppermute | solution.py:1056
  1008.4 91.8 %collective-permute-start.68 = (bf16[256,2048]{1,0:T(8,128)(2,1)}, bf16[256,2048]{1,0:T(8,128)(2,1)}, u32[]{:S(2)}, u32[]{:S(2)}) collective-permute-start(bf16[256,2048]{1,0:T(8,128)(2,1)} %get-tuple-element.177), channel_id=1, source_target_pairs={{16,0},{17,1},{18,2},{19,3},{20,4},{21,5},{22,6},{23,7},{24,8},{25... | collective-permute-start | bytes 3145736 | tf_op jit(solution)/shard_map/ppermute | solution.py:1056
  1075.6 34.3 %collective-permute-start.74 = (bf16[1024,512]{1,0:T(8,128)(2,1)}, bf16[1024,512]{1,0:T(8,128)(2,1)}, u32[]{:S(2)}, u32[]{:S(2)}) collective-permute-start(bf16[1024,512]{1,0:T(8,128)(2,1)} %reduce-scatter.14.cloned.1.call-done), channel_id=1, source_target_pairs={{16,0},{17,1},{18,2},{19,3},{20,4},{21,5},{22,6},{23,7},{24,8},{25... | collective-permute-start | bytes 3145736 | tf_op jit(solution)/shard_map/ppermute | solution.py:1056
  (112 other events, 1952.7 us)
Sparse Core Ops, SparseCore 0:
  39.9 64.8 all-gather.5
  107.0 116.7 all-gather.3
  305.5 192.1 all-gather.7
  631.3 129.4 reduce-scatter.9
  762.9 94.2 reduce-scatter.11
  859.4 129.6 reduce-scatter.7
  991.4 77.2 reduce-scatter.13
  1071.0 27.7 reduce-scatter.5

commit v6 on v5

--- a/solution.py
+++ b/solution.py
@@ -1,3 +1,4 @@
+import functools
 import math
 
 import jax
@@ -453,7 +454,7 @@
     near = jnp.concatenate([block, beside], axis=0)
     far = jnp.concatenate([across, corner], axis=0)
     near_other, far_other = (swap(near, COL, 1), swap(far, COL, 1))
-    return jnp.concatenate([near, near_other, far, far_other], axis=0), across
+    return (near, near_other, far, far_other), across
 
 
 def gather_pieces(shard):
@@ -585,15 +586,19 @@
         out_ref[:, columns] = mm(act, w_ref[...]).astype(BF16)
 
 
-def outer_back_kernel(
-    row_ref, dy_ref, w0_ref, w1_ref, w2_ref, w3_ref, slope_ref, dz_ref, do_ref, sum_ref, dy_sum_ref
-):
+def outer_back_kernel(count, row_ref, *refs):
+    dys, (w0_ref, w1_ref, w2_ref, w3_ref, slope_ref) = (refs[:count], refs[count : count + 5])
+    dz_ref, do_ref, sum_ref, dy_sum_ref, dy_ref = refs[-5:]
     inner = slope_ref.shape[1]
+    dy = dys[0][...]
+    for place, ref in enumerate(dys[1:], 1):
+        start = place * (pl.num_programs(0) // count)
+        dy = jnp.where(pl.program_id(0) >= start, ref[...], dy)
+    dy_ref[...] = dy
     total = None
     for w_ref, columns in piece_columns(row_ref, (w0_ref, w1_ref, w2_ref, w3_ref)):
         part = contract_cols(dy_ref[:, columns], w_ref[...])
         total = part if total is None else total + part
-    dy = dy_ref[...]
     dz = (total[:, :inner] * slope_ref[...].astype(F32)).astype(BF16)
     dz_ref[...] = dz
     do_ref[...] = total[:, inner:].astype(BF16)
@@ -627,7 +632,7 @@
 
 
 def attend_back_kernel(
-    q_ref, k_ref, v_ref, row_ref, col_ref, log_ref, do_ref, cos_ref, sin_ref, held_ref,
+    first, q_ref, k_ref, v_ref, row_ref, col_ref, log_ref, do_ref, cos_ref, sin_ref, held_ref,
     all_ref, sum_ref, out_ref, dk_ref, dv_ref, sem,
 ):
     step = pl.program_id(1)
@@ -670,7 +675,7 @@
         sum_ref[:, HD : 2 * HD] += column_sum(grad_keys)
         sum_ref[:, 2 * HD :] += column_sum(grad_values)
         length, width = out_ref.shape
-        micro = pl.ds(pl.multiple_of(pl.program_id(0) * length, length), length)
+        micro = pl.ds(pl.multiple_of((first + pl.program_id(0)) * length, length), length)
         copy = pltpu.make_async_copy(
             out_ref, all_ref.at[micro, pl.ds(all_ref.shape[1] - width, width)], sem
         )
@@ -782,29 +787,40 @@
     )(dz, w_in, w_qkv, w_qkv, w_qkv)
 
 
-def outer_back(dy, pieces, row, slopes):
-    rows, width = dy.shape
+def outer_back(dys, pieces, row, slopes, start=0, held=None):
+    rows, width = (sum(dy.shape[0] for dy in dys), dys[0].shape[1])
     inner = slopes.shape[1]
-    dz = jax.ShapeDtypeStruct((rows, inner + 3 * HD), BF16)
+    each, first = (dys[0].shape[0] // ROW_BLOCK, start // ROW_BLOCK)
+
+    def part(place):
+        return pl.BlockSpec(
+            (ROW_BLOCK, width), lambda i: (jnp.clip(i - place * each, 0, each - 1), 0)
+        )
+
+    below = pl.BlockSpec((ROW_BLOCK, inner), lambda i: (first + i, 0))
+    extra = () if held is None else (held,)
     return pl.pallas_call(
-        outer_back_kernel,
+        functools.partial(outer_back_kernel, len(dys)),
         grid=(rows // ROW_BLOCK,),
         in_specs=[
             pl.BlockSpec(memory_space=pltpu.SMEM),
-            by_rows(width),
+            *(part(place) for place in range(len(dys))),
             *(whole(piece.shape) for piece in pieces),
-            by_rows(inner),
+            below,
+            *(pl.BlockSpec(memory_space=pl.ANY) for member in extra),
         ],
-        out_specs=[by_rows(inner), by_rows(HD), whole((1, inner)), whole((1, width))],
+        out_specs=[below, by_rows(HD), whole((1, inner)), whole((1, width))],
         out_shape=[
-            dz,
+            jax.ShapeDtypeStruct((slopes.shape[0], inner + 3 * HD), BF16),
             jax.ShapeDtypeStruct((rows, HD), BF16),
             jax.ShapeDtypeStruct((1, inner), F32),
             jax.ShapeDtypeStruct((1, width), F32),
         ],
-        cost_estimate=cost(2 * rows * width * (inner + HD), dy, slopes, slopes),
+        scratch_shapes=[pltpu.VMEM((ROW_BLOCK, width), BF16)],
+        input_output_aliases={6 + len(dys): 0} if extra else {},
+        cost_estimate=cost(2 * rows * width * (inner + HD), *dys, slopes),
         name="outer_back",
-    )(row, dy, *pieces, slopes)
+    )(row, *dys, *pieces, slopes, *extra)
 
 
 def attend(queries, keys_all, values_all, places, inner):
@@ -836,15 +852,15 @@
     )(queries, keys_all, values_all, places[:, None], places[None, :])
 
 
-def attend_back(queries, keys_all, values_all, places, log_sums, grads, tables, held):
-    rows = queries.shape[0]
+def attend_back(queries, keys_all, values_all, places, log_sums, grads, tables, held, first=0):
+    rows = grads.shape[0]
     length = places.shape[0]
     steps = length // ROW_BLOCK
-    row = pl.BlockSpec((ROW_BLOCK, HD), lambda m, i: (m * steps + i, 0))
-    every = pl.BlockSpec((length, HD), lambda m, i: (m, 0))
+    row = pl.BlockSpec((ROW_BLOCK, HD), lambda m, i: ((first + m) * steps + i, 0))
+    every = pl.BlockSpec((length, HD), lambda m, i: (first + m, 0))
     anywhere = pl.BlockSpec(memory_space=pl.ANY)
     return pl.pallas_call(
-        attend_back_kernel,
+        functools.partial(attend_back_kernel, first),
         grid=(rows // length, steps),
         in_specs=[
             row,
@@ -852,8 +868,8 @@
             every,
             pl.BlockSpec((ROW_BLOCK, 1), lambda m, i: (i, 0)),
             pl.BlockSpec((1, length), lambda m, i: (0, 0)),
-            pl.BlockSpec((ROW_BLOCK, 1), lambda m, i: (m * steps + i, 0)),
-            row,
+            pl.BlockSpec((ROW_BLOCK, 1), lambda m, i: ((first + m) * steps + i, 0)),
+            pl.BlockSpec((ROW_BLOCK, HD), lambda m, i: (m * steps + i, 0)),
             whole(tables[0].shape),
             whole(tables[1].shape),
             anywhere,
@@ -990,8 +1006,10 @@
         hidden_list.append(hidden)
         scaled, unused = norm_rows(hidden.astype(F32))
         x, unused = gather_rows(scaled.astype(BF16))
+        x = jnp.concatenate(x, axis=0)
         if layer == 0:
             seed_rows, unused = gather_rows(after(seed, x))
+            seed_rows = jnp.concatenate(seed_rows, axis=0)
         w_fc_in, w_qkv, offset = w_ins[layer]
         queries, keys_all, values_all = project(x, w_qkv, offset, qkv_e[layer], tables)
         attended, log_sums = attend(queries, keys_all, values_all, places, inner)
@@ -1024,12 +1042,21 @@
         if layer == 1:
             dy = seed_rows
         else:
-            dy, across = gather_rows(grads)
+            dys, across = gather_rows(grads)
+            dy = jnp.concatenate(lax.optimization_barrier(dys), axis=0)
             middle_grads = (jnp.where(low, grads, across), jnp.where(low, across, grads))
-        dz, grad_attended, inner_sum, dy_sum = outer_back(dy, w_outs[layer], row, slopes)
-        dz, heads_sum = attend_back(
-            queries, keys_all, values_all, places, log_sums, grad_attended, tables, dz
-        )
+        halves = ((dy,),) if layer == 1 else (dys[:2], dys[2:])
+        dz, start, column_sums = (None, 0, [])
+        for half in halves:
+            dz, grad_attended, inner_sum, dy_sum = outer_back(
+                half, w_outs[layer], row, slopes, start, dz
+            )
+            dz, heads_sum = attend_back(
+                queries, keys_all, values_all, places, log_sums, grad_attended, tables, dz,
+                start // places.shape[0],
+            )
+            start += grad_attended.shape[0]
+            column_sums.append((heads_sum[0], inner_sum[0], dy_sum[0]))
         combined = scatter_rows(lambda other: inward(dz, w_fc_in, w_qkv, offset, other))
         ins_grad = contract_rows(x, dz).astype(BF16)
         ins_list[layer] = reduced(ins_grad, 0)
@@ -1040,7 +1067,7 @@
             - scaled * jnp.mean(combined * scaled, axis=-1, keepdims=True)
         )
         grads = (grads.astype(F32) + grad_norm).astype(BF16)
-        small_list[layer] = (heads_sum[0], inner_sum[0], dy_sum[0])
+        small_list[layer] = tuple(sum(members) for members in zip(*column_sums))
         if layer == 0:
             fc_out_part0 = reduced(contract_rows(act[:, :inner], dy).astype(BF16), 1)
             out_part0 = reduced(contract_rows(act[:, inner:], dy).astype(BF16), 1)
@@ -1107,7 +1134,7 @@
     ).astype(F32)[None]
     qkv_w_grad = qkv_w_grad.reshape(qkv_w.shape)[None]
     fc_in_w_grad = fc_in_w_grad[None]
-    out_part0, norms = lax.optimization_barrier((out_part0, norms))
+    out_part0, norms, unused = lax.optimization_barrier((out_part0, norms, fc_out_upper))
     out_upper = to_first(out_part0)
     out_w_grad = jnp.concatenate(
         [

time: 1130 us -> 1140 us (level)
    reduce_scatter x5, waiting for transfers between devices: 21.9 us -> 9.84 us  [reduced(): return lax.psum_scatter(value, ROW, scatter_dimension=axis, tiled=True)]
    unnamed x153 -> x175, local copies, waits for them, and re-layouts: 40.1 us -> 46.8 us
    pallas_call x4 -> x6, Pallas kernels: 69.8 us -> 76.1 us  [the longest x3 41.7 us: outer_back(): pl.pallas_call(functools.partial(outer_back_kernel, len(dys)), grid=(rows...]
  transfers between devices with their start and end apart: 83 -> 83, of which waited for: 41 -> 40; matrix products, arithmetic and copies ran while one was open for 18% -> 18% of each run, Pallas kernels for 22% -> 22%
where the time goes in v6:
time: 1140 us; the launch traced here: 1130 us
  waiting for transfers between devices  469 us (41%)
  Pallas kernels  295 us (26%)
  starting transfers between devices  104 us (9%)
  other arithmetic  87.1 us (8%)
  local copies, waits for them, and re-layouts  81.9 us (7%)
  matrix products  78.5 us (7%)
  between operations  15.6 us (1%)
    ppermute x62, waiting for transfers between devices, swap(): lax.ppermute(value, axis, [(source, source ^ bit) for source in range(cou...  413 us
    dot_general x5, matrix products, contract_rows(): lax.dot_general(first_operand, second_operand, (((0,), (0,)), ((), ())),...  77.8 us
    ppermute x62, starting transfers between devices, swap(): lax.ppermute(value, axis, [(source, source ^ bit) for source in range(cou...  72.5 us
    pallas_call x4, Pallas kernels, inward(): pl.pallas_call(inward_kernel, grid=(rows // ROW_BLOCK,), in_specs=[split_...  52.6 us
    unnamed x175, local copies, waits for them, and re-layouts  46.8 us
    pallas_call x8, Pallas kernels, column_call(): pl.pallas_call(kernel, grid=(width // tile,), in_specs=[spec(member.shape...  44.5 us
    pallas_call x3, Pallas kernels, outer_back(): pl.pallas_call(functools.partial(outer_back_kernel, len(dys)), grid=(rows...  41.7 us
    pallas_call x4, Pallas kernels, outer(): pl.pallas_call(outer_kernel, grid=(rows // ROW_BLOCK,), in_specs=[pl.Bloc...  40.4 us
  transfers between devices with their start and end apart: 83, of which 40 were waited for; matrix products, arithmetic and copies ran while one was open for 18% of the time, Pallas kernels for 22%

profile of v6, /device:TPU:0, one launch (start us, length us, event | category | flops | bytes accessed | tf_op | source)
XLA Modules:
  0.0 1130.5 jit_solution(16681054840388292039)
XLA Ops:
  22.0 14.0 %collective-permute-done.1 = bf16[512,768]{1,0:T(8,128)(2,1)} collective-permute-done((bf16[512,768]{1,0:T(8,128)(2,1)}, bf16[512,768]{1,0:T(8,128)(2,1)}, u32[]{:S(2)}, u32[]{:S(2)}) %collective-permute-start.1) | collective-permute-done | bytes 786464 | tf_op jit(solution)/shard_map/ppermute | solution.py:422
  44.8 15.1 %collective-permute-done.2 = bf16[512,1024]{1,0:T(8,128)(2,1)} collective-permute-done((bf16[512,1024]{1,0:T(8,128)(2,1)S(1)}, bf16[512,1024]{1,0:T(8,128)(2,1)}, u32[]{:S(2)}, u32[]{:S(2)}) %collective-permute-start.2) | collective-permute-done | bytes 1048608 | tf_op jit(solution)/shard_map/ppermute | solution.py:422
  60.7 28.1 %collective-permute-done.3 = bf16[1280,512]{1,0:T(8,128)(2,1)} collective-permute-done((bf16[1280,512]{1,0:T(8,128)(2,1)}, bf16[1280,512]{1,0:T(8,128)(2,1)}, u32[]{:S(2)}, u32[]{:S(2)}) %collective-permute-start.3) | collective-permute-done | bytes 1310752 | tf_op jit(solution)/shard_map/ppermute | solution.py:422
  101.5 12.0 %collective-permute-done.8 = bf16[256,2048]{1,0:T(8,128)(2,1)} collective-permute-done((bf16[256,2048]{1,0:T(8,128)(2,1)}, bf16[256,2048]{1,0:T(8,128)(2,1)}, u32[]{:S(2)}, u32[]{:S(2)}) %collective-permute-start.8) | collective-permute-done | bytes 1048608 | tf_op jit(solution)/shard_map/ppermute | solution.py:422
  172.6 15.6 %collective-permute-done.19 = bf16[256,2048]{1,0:T(8,128)(2,1)S(1)} collective-permute-done((bf16[256,2048]{1,0:T(8,128)(2,1)S(1)}, bf16[256,2048]{1,0:T(8,128)(2,1)S(1)}, u32[]{:S(2)}, u32[]{:S(2)}) %collective-permute-start.19) | collective-permute-done | bytes 1048608 | tf_op jit(solution)/shard_map/ppermute | solution.py:422
  194.9 12.7 %project.2 = (bf16[2048,256]{1,0:T(8,128)(2,1)}, bf16[2048,256]{1,0:T(8,128)(2,1)}, bf16[2048,256]{1,0:T(8,128)(2,1)}) custom-call(bf16[2048,2048]{1,0:T(8,128)(2,1)} %constant_dynamic-update-slice_fusion.x_ref, bf16[2048,768]{1,0:T(8,128)(2,1)} %all-gather.6.cloned.1.call-done.wq_ref.wk_ref.wv_ref, ...), custom_call_target="tpu_custom_call" | custom-call | flops 6442450944 | bytes 11534336 | tf_op jit(solution)/shard_map/project/pallas_call | solution.py:718
  207.6 35.8 %collective-permute-done.5.w2_ref.refs_4_ = bf16[1280,512]{1,0:T(8,128)(2,1)} collective-permute-done((bf16[1280,512]{1,0:T(8,128)(2,1)}, bf16[1280,512]{1,0:T(8,128)(2,1)}, u32[]{:S(2)}, u32[]{:S(2)}) %collective-permute-start.5) | collective-permute-done | bytes 1310752 | tf_op jit(solution)/shard_map/ppermute | solution.py:422
  250.1 10.9 attend.2
  262.1 16.7 %inner.2 = (bf16[2048,1280]{1,0:T(8,128)(2,1)}, bf16[2048,1024]{1,0:T(8,128)(2,1)}) custom-call(bf16[2048,2048]{1,0:T(8,128)(2,1)} %constant_dynamic-update-slice_fusion.x_ref, bf16[2048,1024]{1,0:T(8,128)(2,1)} %all-gather.4.cloned.1.call-done.w_ref.wf_ref, f32[1,1024]{1,0:T(1,128)} %bitcast.174, ...), custom_call_target="tpu_custom_call", output_to_operand_aliasing={{0}: (3, {})} | custom-call | flops 8589934592 | bytes 16777216 | tf_op jit(solution)/shard_map/inner/pallas_call | solution.py:733
  323.2 22.5 %collective-permute-done.26.across_ref = bf16[256,2048]{1,0:T(8,128)(2,1)S(1)} collective-permute-done((bf16[256,2048]{1,0:T(8,128)(2,1)}, bf16[256,2048]{1,0:T(8,128)(2,1)S(1)}, u32[]{:S(2)}, u32[]{:S(2)}) %collective-permute-start.26) | collective-permute-done | bytes 1048608 | tf_op jit(solution)/shard_map/ppermute | solution.py:422
  374.1 21.2 %collective-permute-done.30 = bf16[256,2048]{1,0:T(8,128)(2,1)S(1)} collective-permute-done((bf16[256,2048]{1,0:T(8,128)(2,1)S(1)}, bf16[256,2048]{1,0:T(8,128)(2,1)S(1)}, u32[]{:S(2)}, u32[]{:S(2)}) %collective-permute-start.30) | collective-permute-done | bytes 1048608 | tf_op jit(solution)/shard_map/ppermute | solution.py:422
  398.2 15.3 %collective-permute-start.37 = (bf16[1280,512]{1,0:T(8,128)(2,1)S(1)}, bf16[1280,512]{1,0:T(8,128)(2,1)}, u32[]{:S(2)}, u32[]{:S(2)}) collective-permute-start(bf16[1280,512]{1,0:T(8,128)(2,1)S(1)} %copy-done.39), channel_id=1, source_target_pairs={{0,8},{4,12},{8,0},{12,4},{1,9},{5,13},{9,1},{13,5},{2,10},{6,14},... | collective-permute-start | bytes 3932168 | tf_op jit(solution)/shard_map/ppermute | solution.py:422
  422.6 83.6 %collective-permute-done.37.w2_ref.refs_3_ = bf16[1280,512]{1,0:T(8,128)(2,1)} collective-permute-done((bf16[1280,512]{1,0:T(8,128)(2,1)S(1)}, bf16[1280,512]{1,0:T(8,128)(2,1)}, u32[]{:S(2)}, u32[]{:S(2)}) %collective-permute-start.37) | collective-permute-done | bytes 1310752 | tf_op jit(solution)/shard_map/ppermute | solution.py:422
  514.5 13.0 %project.3 = (bf16[2048,256]{1,0:T(8,128)(2,1)}, bf16[2048,256]{1,0:T(8,128)(2,1)}, bf16[2048,256]{1,0:T(8,128)(2,1)}) custom-call(bf16[2048,2048]{1,0:T(8,128)(2,1)} %constant_dynamic-update-slice_fusion.14.x_ref, bf16[2048,1792]{1,0:T(8,128)(2,1)} %all-gather.8.cloned.1.call-done.wq_ref.wk_ref.wv_ref.w_ref.wf_ref, ...), custom_call_target="tpu_custom_call" | custom-call | flops 6442450944 | bytes 11534336 | tf_op jit(solution)/shard_map/project/pallas_call | solution.py:718
  538.3 16.7 %inner.3 = (bf16[2048,1280]{1,0:T(8,128)(2,1)}, bf16[2048,1024]{1,0:T(8,128)(2,1)}) custom-call(bf16[2048,2048]{1,0:T(8,128)(2,1)} %constant_dynamic-update-slice_fusion.14.x_ref, bf16[2048,1792]{1,0:T(8,128)(2,1)} %all-gather.8.cloned.1.call-done.wq_ref.wk_ref.wv_ref.w_ref.wf_ref, f32[1,1024]{1,0:T(1,128)} %bitcast.175, ...), custom_call_target="tpu_custom_call", output_to_operand_aliasing={{0}: (3, {})} | custom-call | flops 8589934592 | bytes 16777216 | tf_op jit(solution)/shard_map/inner/pallas_call | solution.py:733
  555.0 16.6 %convolution_convert_fusion.2 = bf16[1280,2048]{1,0:T(8,128)(2,1)} fusion(bf16[2048,1280]{1,0:T(8,128)(2,1)} %get-tuple-element.129.act_ref, bf16[2048,2048]{1,0:T(8,128)(2,1)} %constant_dynamic-update-slice_fusion.7.refs_0_), kind=kOutput, calls=%fused_computation.2 | convolution fusion | flops 10740039680 | bytes 18874368 | tf_op jit(solution)/shard_map/dot_general | solution.py:61
  575.1 18.6 %outer_back.3 = (bf16[2048,1792]{1,0:T(8,128)(2,1)}, bf16[2048,256]{1,0:T(8,128)(2,1)}, f32[1,1024]{1,0:T(1,128)}, f32[1,2048]{1,0:T(1,128)}) custom-call(s32[1]{0:T(128)} %bitcast.6.row_ref, bf16[2048,2048]{1,0:T(8,128)(2,1)} %constant_dynamic-update-slice_fusion.7.refs_0_, bf16[1280,512]{1,0:T(8,128)(2,1)} %get-tuple-element.216.w0_ref.refs_1_, ...), custom_call_target="tpu_custom_call" | custom-call | flops 10737418240 | bytes 12582912 | tf_op jit(solution)/shard_map/outer_back/pallas_call | solution.py:802
  593.7 15.9 %attend_back.3 = (bf16[2048,1792]{1,0:T(8,128)(2,1)}, f32[1,768]{1,0:T(1,128)}) custom-call(bf16[2048,256]{1,0:T(8,128)(2,1)} %get-tuple-element.125.q_ref, bf16[2048,256]{1,0:T(8,128)(2,1)} %get-tuple-element.126.k_ref, bf16[2048,256]{1,0:T(8,128)(2,1)} %get-tuple-element.127.v_ref, s32[1024,1]{1,0:T(8,128)} %bitcast.118, ...), custom_call_target="tpu_custom_call", output_to_operand_aliasing={{0}: (9, {})} | custom-call | flops 5368709120 | bytes 4194304 | tf_op jit(solution)/shard_map/attend_back/pallas_call | solution.py:862
  609.6 21.6 %convolution_convert_fusion = bf16[2048,1792]{1,0:T(8,128)(2,1)} fusion(bf16[2048,2048]{1,0:T(8,128)(2,1)} %constant_dynamic-update-slice_fusion.14.x_ref, bf16[2048,1792]{1,0:T(8,128)(2,1)} %get-tuple-element.145.dz_ref), kind=kOutput, calls=%fused_computation | convolution fusion | flops 15036055552 | bytes 23068672 | tf_op jit(solution)/shard_map/dot_general | solution.py:61
  631.3 12.9 %inward.5 = bf16[1024,2048]{1,0:T(8,128)(2,1)} custom-call(bf16[2048,1792]{1,0:T(8,128)(2,1)} %get-tuple-element.145.dz_ref, bf16[2048,1792]{1,0:T(8,128)(2,1)} %all-gather.8.cloned.1.call-done.wq_ref.wk_ref.wv_ref.w_ref.wf_ref, bf16[2048,1792]{1,0:T(8,128)(2,1)} %all-gather.8.cloned.1.call-done.wq_ref.wk_ref.wv_ref.w_ref.wf_ref, ...), custom_call_target="tpu_custom_call" | custom-call | flops 7516192768 | bytes 11534336 | tf_op jit(solution)/shard_map/inward/pallas_call | solution.py:775
  644.3 12.8 %inward.4.keep_ref = bf16[1024,2048]{1,0:T(8,128)(2,1)} custom-call(bf16[2048,1792]{1,0:T(8,128)(2,1)} %get-tuple-element.145.dz_ref, bf16[2048,1792]{1,0:T(8,128)(2,1)} %all-gather.8.cloned.1.call-done.wq_ref.wk_ref.wv_ref.w_ref.wf_ref, bf16[2048,1792]{1,0:T(8,128)(2,1)} %all-gather.8.cloned.1.call-done.wq_ref.wk_ref.wv_ref.w_ref.wf_ref, ...), custom_call_target="tpu_custom_call" | custom-call | flops 7516192768 | bytes 11534336 | tf_op jit(solution)/shard_map/inward/pallas_call | solution.py:775
  665.3 22.7 %collective-permute-done.46.across_ref = bf16[256,2048]{1,0:T(8,128)(2,1)S(1)} collective-permute-done((bf16[256,2048]{1,0:T(8,128)(2,1)}, bf16[256,2048]{1,0:T(8,128)(2,1)S(1)}, u32[]{:S(2)}, u32[]{:S(2)}) %collective-permute-start.46) | collective-permute-done | bytes 1048608 | tf_op jit(solution)/shard_map/ppermute | solution.py:422
  716.8 21.4 %collective-permute-done.50 = bf16[256,2048]{1,0:T(8,128)(2,1)S(1)} collective-permute-done((bf16[256,2048]{1,0:T(8,128)(2,1)S(1)}, bf16[256,2048]{1,0:T(8,128)(2,1)S(1)}, u32[]{:S(2)}, u32[]{:S(2)}) %collective-permute-start.50) | collective-permute-done | bytes 1048608 | tf_op jit(solution)/shard_map/ppermute | solution.py:422
  754.2 11.5 %outer_back.4 = (bf16[2048,1792]{1,0:T(8,128)(2,1)}, bf16[1024,256]{1,0:T(8,128)(2,1)}, f32[1,1024]{1,0:T(1,128)}, f32[1,2048]{1,0:T(1,128)}) custom-call(s32[1]{0:T(128)} %bitcast.6.row_ref, bf16[512,2048]{1,0:T(8,128)(2,1)} %copy-done.10, bf16[512,2048]{1,0:T(8,128)(2,1)} %copy-done.30, bf16[1280,512]{1,0:T(8,128)(2,1)} %get-tuple-element.217.w0_ref.refs_2_, ...), custom_call_target="tpu_custom_call" | custom-call | flops 5368709120 | bytes 8388608 | tf_op jit(solution)/shard_map/outer_back/pallas_call | solution.py:802
  774.9 11.6 %outer_back.5 = (bf16[2048,1792]{1,0:T(8,128)(2,1)}, bf16[1024,256]{1,0:T(8,128)(2,1)}, f32[1,1024]{1,0:T(1,128)}, f32[1,2048]{1,0:T(1,128)}) custom-call(s32[1]{0:T(128)} %bitcast.6.row_ref, bf16[512,2048]{1,0:T(8,128)(2,1)} %constant_dynamic-update-slice_fusion.21.refs_0_, ...), custom_call_target="tpu_custom_call", output_to_operand_aliasing={{0}: (8, {})} | custom-call | flops 5368709120 | bytes 8388608 | tf_op jit(solution)/shard_map/outer_back/pallas_call | solution.py:802
  795.8 21.5 %convolution_convert_fusion.1 = bf16[2048,1792]{1,0:T(8,128)(2,1)} fusion(bf16[2048,2048]{1,0:T(8,128)(2,1)} %constant_dynamic-update-slice_fusion.x_ref, bf16[2048,1792]{1,0:T(8,128)(2,1)} %get-tuple-element.166.dz_ref), kind=kOutput, calls=%fused_computation.1 | convolution fusion | flops 15036055552 | bytes 23068672 | tf_op jit(solution)/shard_map/dot_general | solution.py:61
  837.2 10.9 fusion.2
  865.3 14.1 %inward.7 = bf16[1024,2048]{1,0:T(8,128)(2,1)} custom-call(bf16[2048,1792]{1,0:T(8,128)(2,1)} %get-tuple-element.166.dz_ref, bf16[2048,1024]{1,0:T(8,128)(2,1)} %all-gather.4.cloned.1.call-done.w_ref.wf_ref, bf16[2048,768]{1,0:T(8,128)(2,1)} %all-gather.6.cloned.1.call-done.wq_ref.wk_ref.wv_ref, ...), custom_call_target="tpu_custom_call" | custom-call | flops 7516192768 | bytes 11534336 | tf_op jit(solution)/shard_map/inward/pallas_call | solution.py:775
  927.2 12.8 %inward.6.keep_ref = bf16[1024,2048]{1,0:T(8,128)(2,1)} custom-call(bf16[2048,1792]{1,0:T(8,128)(2,1)} %get-tuple-element.166.dz_ref, bf16[2048,1024]{1,0:T(8,128)(2,1)} %all-gather.4.cloned.1.call-done.w_ref.wf_ref, bf16[2048,768]{1,0:T(8,128)(2,1)} %all-gather.6.cloned.1.call-done.wq_ref.wk_ref.wv_ref, ...), custom_call_target="tpu_custom_call" | custom-call | flops 7516192768 | bytes 11534336 | tf_op jit(solution)/shard_map/inward/pallas_call | solution.py:775
  956.0 14.2 %collective-permute-done.66.across_ref = bf16[256,2048]{1,0:T(8,128)(2,1)} collective-permute-done((bf16[256,2048]{1,0:T(8,128)(2,1)}, bf16[256,2048]{1,0:T(8,128)(2,1)}, u32[]{:S(2)}, u32[]{:S(2)}) %collective-permute-start.66) | collective-permute-done | bytes 1048608 | tf_op jit(solution)/shard_map/ppermute | solution.py:422
  1014.4 29.2 %collective-permute-done.71 = bf16[512,1792]{1,0:T(8,128)(2,1)} collective-permute-done((bf16[512,1792]{1,0:T(8,128)(2,1)}, bf16[512,1792]{1,0:T(8,128)(2,1)}, u32[]{:S(2)}, u32[]{:S(2)}) %collective-permute-start.71) | collective-permute-done | bytes 1835040 | tf_op jit(solution)/shard_map/ppermute | solution.py:1086
  1055.0 12.5 %collective-permute-done.59 = f32[4,512]{1,0:T(4,128)S(1)} collective-permute-done((f32[4,512]{1,0:T(4,128)S(1)}, f32[4,512]{1,0:T(4,128)S(1)}, u32[]{:S(2)}, u32[]{:S(2)}) %collective-permute-start.59) | collective-permute-done | bytes 8224 | tf_op jit(solution)/shard_map/ppermute | solution.py:422
  (499 shorter events, 500.8 us)
Async XLA Ops:
  7.2 187.7 %all-gather.6.cloned.1.call-start = ((), (), s32[]{:S(2)}) async-start(), calls=%async_computation.6 | async-start | bytes 3932160 | tf_op jit(solution)/shard_map/all_gather | solution.py:934
  39.9 222.2 %all-gather.4.cloned.1.call-start = ((), (), s32[]{:S(2)}) async-start(), calls=%async_computation.5 | async-start | bytes 5242880 | tf_op jit(solution)/shard_map/all_gather | solution.py:934
  101.4 413.1 %all-gather.8.cloned.1.call-start = ((), (), s32[]{:S(2)}) async-start(), calls=%async_computation.7 | async-start | bytes 9175040 | tf_op jit(solution)/shard_map/all_gather | solution.py:934
  117.6 35.6 %collective-permute-start.10 = (bf16[512,2048]{1,0:T(8,128)(2,1)}, bf16[512,2048]{1,0:T(8,128)(2,1)}, u32[]{:S(2)}, u32[]{:S(2)}) collective-permute-start(bf16[512,2048]{1,0:T(8,128)(2,1)} %pad_maximum_fusion), channel_id=1, source_target_pairs={{0,1},{1,0},{2,3},{3,2},{4,5},{5,4},{6,7},{7,6},{8,9},{9,8},{10,11... | collective-permute-start | bytes 6291464 | tf_op jit(solution)/shard_map/ppermute | solution.py:422
  169.7 73.7 %collective-permute-start.5 = (bf16[1280,512]{1,0:T(8,128)(2,1)}, bf16[1280,512]{1,0:T(8,128)(2,1)}, u32[]{:S(2)}, u32[]{:S(2)}) collective-permute-start(bf16[1280,512]{1,0:T(8,128)(2,1)} %get-tuple-element.217.w0_ref.refs_2_), channel_id=1, source_target_pairs={{0,8},{4,12},{8,0},{12,4},{1,9},{5,13},{9,1},{13,5},{2,10},{6,14},... | collective-permute-start | bytes 3932168 | tf_op jit(solution)/shard_map/ppermute | solution.py:422
  170.3 119.7 %collective-permute-start.4 = (bf16[1280,512]{1,0:T(8,128)(2,1)}, bf16[1280,512]{1,0:T(8,128)(2,1)}, u32[]{:S(2)}, u32[]{:S(2)}) collective-permute-start(bf16[1280,512]{1,0:T(8,128)(2,1)} %get-tuple-element.217.w0_ref.refs_2_), channel_id=1, source_target_pairs={{12,8},{8,4},{4,0},{13,9},{9,5},{5,1},{14,10},{10,6},{6,2},{15,11}... | collective-permute-start | bytes 3932168 | tf_op jit(solution)/shard_map/ppermute | solution.py:462
  190.2 55.5 %collective-permute-start.22 = (bf16[128,2048]{1,0:T(8,128)(2,1)}, bf16[128,2048]{1,0:T(8,128)(2,1)}, u32[]{:S(2)}, u32[]{:S(2)}) collective-permute-start(bf16[128,2048]{1,0:T(8,128)(2,1)} %slice.184), channel_id=1, source_target_pairs={{0,16},{16,0},{1,17},{17,1},{2,18},{18,2},{3,19},{19,3},{4,20},{20... | collective-permute-start | bytes 1572872 | tf_op jit(solution)/shard_map/ppermute | solution.py:422
  191.8 55.4 %collective-permute-start.23 = (bf16[128,2048]{1,0:T(8,128)(2,1)}, bf16[128,2048]{1,0:T(8,128)(2,1)}, u32[]{:S(2)}, u32[]{:S(2)}) collective-permute-start(bf16[128,2048]{1,0:T(8,128)(2,1)} %slice.185), channel_id=1, source_target_pairs={{0,2},{1,3},{2,0},{3,1},{4,6},{5,7},{6,4},{7,5},{8,10},{9,11},{10,... | collective-permute-start | bytes 1572872 | tf_op jit(solution)/shard_map/ppermute | solution.py:422
  194.9 83.9 %collective-permute-start.21 = (bf16[512,2048]{1,0:T(8,128)(2,1)}, bf16[512,2048]{1,0:T(8,128)(2,1)}, u32[]{:S(2)}, u32[]{:S(2)}) collective-permute-start(bf16[512,2048]{1,0:T(8,128)(2,1)} %pad_maximum_fusion.2), channel_id=1, source_target_pairs={{0,1},{1,0},{2,3},{3,2},{4,5},{5,4},{6,7},{7,6},{8,9},{9,8},{10,11... | collective-permute-start | bytes 6291464 | tf_op jit(solution)/shard_map/ppermute | solution.py:422
  243.4 46.6 %collective-permute-start.6 = (bf16[1280,512]{1,0:T(8,128)(2,1)}, bf16[1280,512]{1,0:T(8,128)(2,1)}, u32[]{:S(2)}, u32[]{:S(2)}) collective-permute-start(bf16[1280,512]{1,0:T(8,128)(2,1)} %get-tuple-element.217.w0_ref.refs_2_), channel_id=1, source_target_pairs={{0,4},{4,8},{8,12},{1,5},{5,9},{9,13},{2,6},{6,10},{10,14},{3,7},{... | collective-permute-start | bytes 3932168 | tf_op jit(solution)/shard_map/ppermute | solution.py:462
  245.7 44.2 %collective-permute-start.7 = (bf16[1280,512]{1,0:T(8,128)(2,1)}, bf16[1280,512]{1,0:T(8,128)(2,1)}, u32[]{:S(2)}, u32[]{:S(2)}) collective-permute-start(bf16[1280,512]{1,0:T(8,128)(2,1)} %collective-permute-done.5.w2_ref.refs_4_), channel_id=1, source_target_pairs={{8,12},{4,0},{9,13},{5,1},{10,14},{6,2},{11,15},{7,3},{24,28},{20,... | collective-permute-start | bytes 3932168 | tf_op jit(solution)/shard_map/ppermute | solution.py:462
  249.9 36.8 %collective-permute-start.24 = (bf16[512,2048]{1,0:T(8,128)(2,1)}, bf16[512,2048]{1,0:T(8,128)(2,1)}, u32[]{:S(2)}, u32[]{:S(2)}) collective-permute-start(bf16[512,2048]{1,0:T(8,128)(2,1)} %pad_maximum_fusion.3), channel_id=1, source_target_pairs={{0,1},{1,0},{2,3},{3,2},{4,5},{5,4},{6,7},{7,6},{8,9},{9,8},{10,11... | collective-permute-start | bytes 6291464 | tf_op jit(solution)/shard_map/ppermute | solution.py:422
  305.2 675.2 %reduce-scatter.10.cloned.1.call-start = ((), (), s32[]{:S(2)}) async-start(), calls=%async_computation.10 | async-start | bytes 9175040 | tf_op jit(solution)/shard_map/reduce_scatter | solution.py:1034
  396.8 111.8 %collective-permute-start.32 = (bf16[512,2048]{1,0:T(8,128)(2,1)S(1)}, bf16[512,2048]{1,0:T(8,128)(2,1)S(1)}, u32[]{:S(2)}, u32[]{:S(2)}) collective-permute-start(bf16[512,2048]{1,0:T(8,128)(2,1)S(1)} %pad_maximum_fusion.4), channel_id=1, source_target_pairs={{0,1},{1,0},{2,3},{3,2},{4,5},{5,4},{6,7},{7,6},{8,9},{9,8},{10,11... | collective-permute-start | bytes 6291464 | tf_op jit(solution)/shard_map/ppermute | solution.py:422
  398.2 107.9 %collective-permute-start.37 = (bf16[1280,512]{1,0:T(8,128)(2,1)S(1)}, bf16[1280,512]{1,0:T(8,128)(2,1)}, u32[]{:S(2)}, u32[]{:S(2)}) collective-permute-start(bf16[1280,512]{1,0:T(8,128)(2,1)S(1)} %copy-done.39), channel_id=1, source_target_pairs={{0,8},{4,12},{8,0},{12,4},{1,9},{5,13},{9,1},{13,5},{2,10},{6,14},... | collective-permute-start | bytes 3932168 | tf_op jit(solution)/shard_map/ppermute | solution.py:422
  413.7 99.2 %collective-permute-start.35 = (bf16[512,2048]{1,0:T(8,128)(2,1)S(1)}, bf16[512,2048]{1,0:T(8,128)(2,1)S(1)}, u32[]{:S(2)}, u32[]{:S(2)}) collective-permute-start(bf16[512,2048]{1,0:T(8,128)(2,1)S(1)} %pad_maximum_fusion.5), channel_id=1, source_target_pairs={{0,1},{1,0},{2,3},{3,2},{4,5},{5,4},{6,7},{7,6},{8,9},{9,8},{10,11... | collective-permute-start | bytes 6291464 | tf_op jit(solution)/shard_map/ppermute | solution.py:422
  415.7 156.0 %collective-permute-start.36 = (bf16[1280,512]{1,0:T(8,128)(2,1)S(1)}, bf16[1280,512]{1,0:T(8,128)(2,1)}, u32[]{:S(2)}, u32[]{:S(2)}) collective-permute-start(bf16[1280,512]{1,0:T(8,128)(2,1)S(1)} %copy-done.39), channel_id=1, source_target_pairs={{12,8},{8,4},{4,0},{13,9},{9,5},{5,1},{14,10},{10,6},{6,2},{15,11}... | collective-permute-start | bytes 3932168 | tf_op jit(solution)/shard_map/ppermute | solution.py:462
  417.0 154.7 %collective-permute-start.38 = (bf16[1280,512]{1,0:T(8,128)(2,1)S(1)}, bf16[1280,512]{1,0:T(8,128)(2,1)}, u32[]{:S(2)}, u32[]{:S(2)}) collective-permute-start(bf16[1280,512]{1,0:T(8,128)(2,1)S(1)} %copy-done.39), channel_id=1, source_target_pairs={{0,4},{4,8},{8,12},{1,5},{5,9},{9,13},{2,6},{6,10},{10,14},{3,7},{... | collective-permute-start | bytes 3932168 | tf_op jit(solution)/shard_map/ppermute | solution.py:462
  506.2 65.5 %collective-permute-start.39 = (bf16[1280,512]{1,0:T(8,128)(2,1)}, bf16[1280,512]{1,0:T(8,128)(2,1)}, u32[]{:S(2)}, u32[]{:S(2)}) collective-permute-start(bf16[1280,512]{1,0:T(8,128)(2,1)} %collective-permute-done.37.w2_ref.refs_3_), channel_id=1, source_target_pairs={{8,12},{4,0},{9,13},{5,1},{10,14},{6,2},{11,15},{7,3},{24,28},{20,... | collective-permute-start | bytes 3932168 | tf_op jit(solution)/shard_map/ppermute | solution.py:462
  631.3 363.1 %reduce-scatter.14.cloned.1.call-start = ((), (), s32[]{:S(2)}) async-start(), calls=%async_computation.12 | async-start | bytes 6553600 | tf_op jit(solution)/shard_map/reduce_scatter | solution.py:1034
  665.3 341.5 %reduce-scatter.8.cloned.1.call-start = ((), (), s32[]{:S(2)}) async-start(), calls=%async_computation.9 | async-start | bytes 9175040 | tf_op jit(solution)/shard_map/reduce_scatter | solution.py:1034
  817.3 264.1 %reduce-scatter.12.cloned.1.call-start = ((), (), s32[]{:S(2)}) async-start(), calls=%async_computation.11 | async-start | bytes 5242880 | tf_op jit(solution)/shard_map/reduce_scatter | solution.py:1034
  827.3 31.2 %collective-permute-start.40 = (bf16[1024,2048]{1,0:T(8,128)(2,1)}, bf16[1024,2048]{1,0:T(8,128)(2,1)}, u32[]{:S(2)}, u32[]{:S(2)}) collective-permute-start(bf16[1024,2048]{1,0:T(8,128)(2,1)} %outer.7), channel_id=1, source_target_pairs={{0,1},{1,0},{2,3},{3,2},{4,5},{5,4},{6,7},{7,6},{8,9},{9,8},{10,11... | collective-permute-start | bytes 12582920 | tf_op jit(solution)/shard_map/ppermute | solution.py:422
  848.1 250.8 %reduce-scatter.6.cloned.1.call-start = ((), (), s32[]{:S(2)}) async-start(), calls=%async_computation.8 | async-start | bytes 1310720 | tf_op jit(solution)/shard_map/reduce_scatter | solution.py:1034
  879.3 60.8 %collective-permute-start.65 = (bf16[1024,2048]{1,0:T(8,128)(2,1)}, bf16[1024,2048]{1,0:T(8,128)(2,1)}, u32[]{:S(2)}, u32[]{:S(2)}) collective-permute-start(bf16[1024,2048]{1,0:T(8,128)(2,1)} %inward.7), channel_id=1, source_target_pairs={{0,1},{1,0},{2,3},{3,2},{4,5},{5,4},{6,7},{7,6},{8,9},{9,8},{10,11... | collective-permute-start | bytes 12582920 | tf_op jit(solution)/shard_map/ppermute | solution.py:422
  897.9 50.2 %collective-permute-start.64 = (bf16[256,2048]{1,0:T(8,128)(2,1)S(1)}, bf16[256,2048]{1,0:T(8,128)(2,1)S(1)}, u32[]{:S(2)}, u32[]{:S(2)}) collective-permute-start(bf16[256,2048]{1,0:T(8,128)(2,1)S(1)} %get-tuple-element.207), channel_id=1, source_target_pairs={{0,16},{16,0},{1,17},{17,1},{2,18},{18,2},{3,19},{19,3},{4,20},{20... | collective-permute-start | bytes 3145736 | tf_op jit(solution)/shard_map/ppermute | solution.py:422
  951.6 160.7 %collective-permute-start.56 = (bf16[256,2048]{1,0:T(8,128)(2,1)}, bf16[256,2048]{1,0:T(8,128)(2,1)}, u32[]{:S(2)}, u32[]{:S(2)}) collective-permute-start(bf16[256,2048]{1,0:T(8,128)(2,1)} %get-tuple-element.199), channel_id=1, source_target_pairs={{0,16},{1,17},{2,18},{3,19},{4,20},{5,21},{6,22},{7,23},{8,24},{9,... | collective-permute-start | bytes 3145736 | tf_op jit(solution)/shard_map/ppermute | solution.py:1086
  955.8 37.2 %collective-permute-start.72 = (f32[3584]{0:T(1024)S(1)}, f32[3584]{0:T(1024)S(1)}, u32[]{:S(2)}, u32[]{:S(2)}) collective-permute-start(f32[3584]{0:T(1024)S(1)} %slice.246), channel_id=1, source_target_pairs={{0,16},{16,0},{1,17},{17,1},{2,18},{18,2},{3,19},{19,3},{4,20},{20... | collective-permute-start | bytes 43016 | tf_op jit(solution)/shard_map/ppermute | solution.py:422
  980.4 63.2 %collective-permute-start.71 = (bf16[512,1792]{1,0:T(8,128)(2,1)}, bf16[512,1792]{1,0:T(8,128)(2,1)}, u32[]{:S(2)}, u32[]{:S(2)}) collective-permute-start(bf16[512,1792]{1,0:T(8,128)(2,1)} %reduce-scatter.10.cloned.1.call-done), channel_id=1, source_target_pairs={{0,16},{1,17},{2,18},{3,19},{4,20},{5,21},{6,22},{7,23},{8,24},{9,... | collective-permute-start | bytes 5505032 | tf_op jit(solution)/shard_map/ppermute | solution.py:1086
  994.3 92.4 %collective-permute-start.73 = (bf16[1280,512]{1,0:T(8,128)(2,1)}, bf16[1280,512]{1,0:T(8,128)(2,1)}, u32[]{:S(2)}, u32[]{:S(2)}) collective-permute-start(bf16[1280,512]{1,0:T(8,128)(2,1)} %reduce-scatter.14.cloned.1.call-done), channel_id=1, source_target_pairs={{0,16},{1,17},{2,18},{3,19},{4,20},{5,21},{6,22},{7,23},{8,24},{9,... | collective-permute-start | bytes 3932168 | tf_op jit(solution)/shard_map/ppermute | solution.py:1086
  1006.8 45.0 %collective-permute-start.62 = (bf16[512,1792]{1,0:T(8,128)(2,1)}, bf16[512,1792]{1,0:T(8,128)(2,1)S(1)}, u32[]{:S(2)}, u32[]{:S(2)}) collective-permute-start(bf16[512,1792]{1,0:T(8,128)(2,1)} %reduce-scatter.8.cloned.1.call-done), channel_id=1, source_target_pairs={{16,0},{17,1},{18,2},{19,3},{20,4},{21,5},{22,6},{23,7},{24,8},{25... | collective-permute-start | bytes 5505032 | tf_op jit(solution)/shard_map/ppermute | solution.py:1083
  1012.8 97.6 %collective-permute-start.70 = (bf16[256,2048]{1,0:T(8,128)(2,1)}, bf16[256,2048]{1,0:T(8,128)(2,1)}, u32[]{:S(2)}, u32[]{:S(2)}) collective-permute-start(bf16[256,2048]{1,0:T(8,128)(2,1)} %get-tuple-element.197), channel_id=1, source_target_pairs={{16,0},{17,1},{18,2},{19,3},{20,4},{21,5},{22,6},{23,7},{24,8},{25... | collective-permute-start | bytes 3145736 | tf_op jit(solution)/shard_map/ppermute | solution.py:1083
  (123 other events, 2023.3 us)
Sparse Core Ops, SparseCore 0:
  40.0 64.8 all-gather.5
  107.1 116.7 all-gather.3
  305.3 192.3 all-gather.7
  631.4 129.4 reduce-scatter.9
  763.1 94.2 reduce-scatter.13
  859.5 129.6 reduce-scatter.7
  991.5 77.2 reduce-scatter.11
  1071.1 27.8 reduce-scatter.5

commit v7 on v6

--- a/solution.py
+++ b/solution.py
@@ -965,8 +965,9 @@
     outs_pair = both_layers(outs_kept, outs_came)
     w_qkv0 = gathered(qkv_pair[0], 0)
     w_fc_in0 = gathered(fc_in_pair[0], 0)
-    w_ins1 = gathered(jnp.concatenate([fc_in_pair[1], qkv_pair[1]], axis=1), 0)
-    w_ins = ((w_fc_in0, w_qkv0, 0), (w_ins1, w_ins1, inner))
+    w_qkv1 = gathered(qkv_pair[1], 0)
+    w_fc_in1 = gathered(fc_in_pair[1], 0)
+    w_ins = ((w_fc_in0, w_qkv0), (w_fc_in1, w_qkv1))
     w_outs = [gather_pieces(outs_pair[layer]) for layer in range(2)]
     row = r.astype(jnp.int32)[None]
 
@@ -1010,8 +1011,8 @@
         if layer == 0:
             seed_rows, unused = gather_rows(after(seed, x))
             seed_rows = jnp.concatenate(seed_rows, axis=0)
-        w_fc_in, w_qkv, offset = w_ins[layer]
-        queries, keys_all, values_all = project(x, w_qkv, offset, qkv_e[layer], tables)
+        w_fc_in, w_qkv = w_ins[layer]
+        queries, keys_all, values_all = project(x, w_qkv, 0, qkv_e[layer], tables)
         attended, log_sums = attend(queries, keys_all, values_all, places, inner)
         act, slopes = inner_layer(x, w_fc_in, fc_e[layer], attended)
         if layer == 0:
@@ -1038,7 +1039,7 @@
     ins_list, small_list = ([None, None], [None, None])
     for layer in (1, 0):
         x, queries, keys_all, values_all, log_sums, slopes, act = kept_list[layer]
-        w_fc_in, w_qkv, offset = w_ins[layer]
+        w_fc_in, w_qkv = w_ins[layer]
         if layer == 1:
             dy = seed_rows
         else:
@@ -1057,7 +1058,7 @@
             )
             start += grad_attended.shape[0]
             column_sums.append((heads_sum[0], inner_sum[0], dy_sum[0]))
-        combined = scatter_rows(lambda other: inward(dz, w_fc_in, w_qkv, offset, other))
+        combined = scatter_rows(lambda other: inward(dz, w_fc_in, w_qkv, 0, other))
         ins_grad = contract_rows(x, dz).astype(BF16)
         ins_list[layer] = reduced(ins_grad, 0)
         scaled, inverse_std = norm_rows(hidden_list[layer].astype(F32))
@@ -1134,7 +1135,9 @@
     ).astype(F32)[None]
     qkv_w_grad = qkv_w_grad.reshape(qkv_w.shape)[None]
     fc_in_w_grad = fc_in_w_grad[None]
-    out_part0, norms, unused = lax.optimization_barrier((out_part0, norms, fc_out_upper))
+    out_part0, fc_out_w_grad, norms = lax.optimization_barrier(
+        (out_part0, fc_out_w_grad, norms)
+    )
     out_upper = to_first(out_part0)
     out_w_grad = jnp.concatenate(
         [

time: 1140 us -> 1140 us (level)
    ppermute x62, waiting for transfers between devices: 413 us -> 427 us  [swap(): lax.ppermute(value, axis, [(source, source ^ bit) for source in range(cou...]
    unnamed x175 -> x167, local copies, waits for them, and re-layouts: 46.8 us -> 46.2 us
  transfers between devices with their start and end apart: 83 -> 84, of which waited for: 40 -> 41; matrix products, arithmetic and copies ran while one was open for 18% -> 18% of each run, Pallas kernels for 22% -> 22%
where the time goes in v7:
time: 1140 us; the launch traced here: 1130 us
  waiting for transfers between devices  474 us (42%)
  Pallas kernels  294 us (26%)
  starting transfers between devices  104 us (9%)
  other arithmetic  87.1 us (8%)
  local copies, waits for them, and re-layouts  81.1 us (7%)
  matrix products  78.5 us (7%)
  between operations  15.3 us (1%)
    ppermute x62, waiting for transfers between devices, swap(): lax.ppermute(value, axis, [(source, source ^ bit) for source in range(cou...  427 us
    dot_general x5, matrix products, contract_rows(): lax.dot_general(first_operand, second_operand, (((0,), (0,)), ((), ())),...  77.8 us
    ppermute x62, starting transfers between devices, swap(): lax.ppermute(value, axis, [(source, source ^ bit) for source in range(cou...  71.8 us
    pallas_call x4, Pallas kernels, inward(): pl.pallas_call(inward_kernel, grid=(rows // ROW_BLOCK,), in_specs=[split_...  52.7 us
    unnamed x167, local copies, waits for them, and re-layouts  46.2 us
    pallas_call x8, Pallas kernels, column_call(): pl.pallas_call(kernel, grid=(width // tile,), in_specs=[spec(member.shape...  44.5 us
    pallas_call x3, Pallas kernels, outer_back(): pl.pallas_call(functools.partial(outer_back_kernel, len(dys)), grid=(rows...  41.7 us
    pallas_call x4, Pallas kernels, outer(): pl.pallas_call(outer_kernel, grid=(rows // ROW_BLOCK,), in_specs=[pl.Bloc...  40.3 us
  transfers between devices with their start and end apart: 84, of which 41 were waited for; matrix products, arithmetic and copies ran while one was open for 18% of the time, Pallas kernels for 22%

profile of v7, /device:TPU:0, one launch (start us, length us, event | category | flops | bytes accessed | tf_op | source)
XLA Modules:
  0.0 1134.6 jit_solution(6160590998351198717)
XLA Ops:
  22.0 14.0 %collective-permute-done.1 = bf16[512,768]{1,0:T(8,128)(2,1)} collective-permute-done((bf16[512,768]{1,0:T(8,128)(2,1)}, bf16[512,768]{1,0:T(8,128)(2,1)}, u32[]{:S(2)}, u32[]{:S(2)}) %collective-permute-start.1) | collective-permute-done | bytes 786464 | tf_op jit(solution)/shard_map/ppermute | solution.py:422
  44.7 15.2 %collective-permute-done.2 = bf16[512,1024]{1,0:T(8,128)(2,1)} collective-permute-done((bf16[512,1024]{1,0:T(8,128)(2,1)S(1)}, bf16[512,1024]{1,0:T(8,128)(2,1)}, u32[]{:S(2)}, u32[]{:S(2)}) %collective-permute-start.2) | collective-permute-done | bytes 1048608 | tf_op jit(solution)/shard_map/ppermute | solution.py:422
  60.7 28.1 %collective-permute-done.3 = bf16[1280,512]{1,0:T(8,128)(2,1)} collective-permute-done((bf16[1280,512]{1,0:T(8,128)(2,1)}, bf16[1280,512]{1,0:T(8,128)(2,1)}, u32[]{:S(2)}, u32[]{:S(2)}) %collective-permute-start.3) | collective-permute-done | bytes 1310752 | tf_op jit(solution)/shard_map/ppermute | solution.py:422
  101.5 12.0 %collective-permute-done.8 = bf16[256,2048]{1,0:T(8,128)(2,1)} collective-permute-done((bf16[256,2048]{1,0:T(8,128)(2,1)}, bf16[256,2048]{1,0:T(8,128)(2,1)}, u32[]{:S(2)}, u32[]{:S(2)}) %collective-permute-start.8) | collective-permute-done | bytes 1048608 | tf_op jit(solution)/shard_map/ppermute | solution.py:422
  172.8 15.6 %collective-permute-done.19 = bf16[256,2048]{1,0:T(8,128)(2,1)S(1)} collective-permute-done((bf16[256,2048]{1,0:T(8,128)(2,1)S(1)}, bf16[256,2048]{1,0:T(8,128)(2,1)S(1)}, u32[]{:S(2)}, u32[]{:S(2)}) %collective-permute-start.19) | collective-permute-done | bytes 1048608 | tf_op jit(solution)/shard_map/ppermute | solution.py:422
  194.9 12.8 %project.2 = (bf16[2048,256]{1,0:T(8,128)(2,1)}, bf16[2048,256]{1,0:T(8,128)(2,1)}, bf16[2048,256]{1,0:T(8,128)(2,1)}) custom-call(bf16[2048,2048]{1,0:T(8,128)(2,1)} %constant_dynamic-update-slice_fusion.x_ref, bf16[2048,768]{1,0:T(8,128)(2,1)} %all-gather.7.cloned.1.call-done.wq_ref.wk_ref.wv_ref, ...), custom_call_target="tpu_custom_call" | custom-call | flops 6442450944 | bytes 11534336 | tf_op jit(solution)/shard_map/project/pallas_call | solution.py:718
  207.7 35.6 %collective-permute-done.5.w2_ref.refs_4_ = bf16[1280,512]{1,0:T(8,128)(2,1)} collective-permute-done((bf16[1280,512]{1,0:T(8,128)(2,1)}, bf16[1280,512]{1,0:T(8,128)(2,1)}, u32[]{:S(2)}, u32[]{:S(2)}) %collective-permute-start.5) | collective-permute-done | bytes 1310752 | tf_op jit(solution)/shard_map/ppermute | solution.py:422
  250.0 10.9 attend.2
  262.0 16.7 %inner.2 = (bf16[2048,1280]{1,0:T(8,128)(2,1)}, bf16[2048,1024]{1,0:T(8,128)(2,1)}) custom-call(bf16[2048,2048]{1,0:T(8,128)(2,1)} %constant_dynamic-update-slice_fusion.x_ref, bf16[2048,1024]{1,0:T(8,128)(2,1)} %all-gather.5.cloned.1.call-done.w_ref.wf_ref, f32[1,1024]{1,0:T(1,128)} %bitcast.174, ...), custom_call_target="tpu_custom_call", output_to_operand_aliasing={{0}: (3, {})} | custom-call | flops 8589934592 | bytes 16777216 | tf_op jit(solution)/shard_map/inner/pallas_call | solution.py:733
  321.8 22.5 %collective-permute-done.26.across_ref = bf16[256,2048]{1,0:T(8,128)(2,1)S(1)} collective-permute-done((bf16[256,2048]{1,0:T(8,128)(2,1)}, bf16[256,2048]{1,0:T(8,128)(2,1)S(1)}, u32[]{:S(2)}, u32[]{:S(2)}) %collective-permute-start.26) | collective-permute-done | bytes 1048608 | tf_op jit(solution)/shard_map/ppermute | solution.py:422
  372.8 21.2 %collective-permute-done.30 = bf16[256,2048]{1,0:T(8,128)(2,1)S(1)} collective-permute-done((bf16[256,2048]{1,0:T(8,128)(2,1)S(1)}, bf16[256,2048]{1,0:T(8,128)(2,1)S(1)}, u32[]{:S(2)}, u32[]{:S(2)}) %collective-permute-start.30) | collective-permute-done | bytes 1048608 | tf_op jit(solution)/shard_map/ppermute | solution.py:422
  396.9 14.6 %collective-permute-start.37 = (bf16[1280,512]{1,0:T(8,128)(2,1)S(1)}, bf16[1280,512]{1,0:T(8,128)(2,1)}, u32[]{:S(2)}, u32[]{:S(2)}) collective-permute-start(bf16[1280,512]{1,0:T(8,128)(2,1)S(1)} %copy-done.35), channel_id=1, source_target_pairs={{0,8},{4,12},{8,0},{12,4},{1,9},{5,13},{9,1},{13,5},{2,10},{6,14},... | collective-permute-start | bytes 3932168 | tf_op jit(solution)/shard_map/ppermute | solution.py:422
  421.2 95.6 %collective-permute-done.37.w2_ref.refs_3_ = bf16[1280,512]{1,0:T(8,128)(2,1)} collective-permute-done((bf16[1280,512]{1,0:T(8,128)(2,1)S(1)}, bf16[1280,512]{1,0:T(8,128)(2,1)}, u32[]{:S(2)}, u32[]{:S(2)}) %collective-permute-start.37) | collective-permute-done | bytes 1310752 | tf_op jit(solution)/shard_map/ppermute | solution.py:422
  525.1 13.0 %project.3 = (bf16[2048,256]{1,0:T(8,128)(2,1)}, bf16[2048,256]{1,0:T(8,128)(2,1)}, bf16[2048,256]{1,0:T(8,128)(2,1)}) custom-call(bf16[2048,2048]{1,0:T(8,128)(2,1)} %constant_dynamic-update-slice_fusion.14.x_ref, bf16[2048,768]{1,0:T(8,128)(2,1)} %all-gather.11.cloned.1.call-done.wq_ref.wk_ref.wv_ref, ...), custom_call_target="tpu_custom_call" | custom-call | flops 6442450944 | bytes 11534336 | tf_op jit(solution)/shard_map/project/pallas_call | solution.py:718
  548.9 16.8 %inner.3 = (bf16[2048,1280]{1,0:T(8,128)(2,1)}, bf16[2048,1024]{1,0:T(8,128)(2,1)}) custom-call(bf16[2048,2048]{1,0:T(8,128)(2,1)} %constant_dynamic-update-slice_fusion.14.x_ref, bf16[2048,1024]{1,0:T(8,128)(2,1)} %all-gather.9.cloned.1.call-done.w_ref.wf_ref, f32[1,1024]{1,0:T(1,128)} %bitcast.175, ...), custom_call_target="tpu_custom_call", output_to_operand_aliasing={{0}: (3, {})} | custom-call | flops 8589934592 | bytes 16777216 | tf_op jit(solution)/shard_map/inner/pallas_call | solution.py:733
  565.7 16.6 %convolution_convert_fusion.2 = bf16[1280,2048]{1,0:T(8,128)(2,1)} fusion(bf16[2048,1280]{1,0:T(8,128)(2,1)} %get-tuple-element.130.act_ref, bf16[2048,2048]{1,0:T(8,128)(2,1)} %constant_dynamic-update-slice_fusion.7.refs_0_), kind=kOutput, calls=%fused_computation.2 | convolution fusion | flops 10740039680 | bytes 18874368 | tf_op jit(solution)/shard_map/dot_general | solution.py:61
  585.9 18.6 %outer_back.3 = (bf16[2048,1792]{1,0:T(8,128)(2,1)}, bf16[2048,256]{1,0:T(8,128)(2,1)}, f32[1,1024]{1,0:T(1,128)}, f32[1,2048]{1,0:T(1,128)}) custom-call(s32[1]{0:T(128)} %bitcast.6.row_ref, bf16[2048,2048]{1,0:T(8,128)(2,1)} %constant_dynamic-update-slice_fusion.7.refs_0_, bf16[1280,512]{1,0:T(8,128)(2,1)} %get-tuple-element.218.w0_ref.refs_1_, ...), custom_call_target="tpu_custom_call" | custom-call | flops 10737418240 | bytes 12582912 | tf_op jit(solution)/shard_map/outer_back/pallas_call | solution.py:802
  604.5 15.8 %attend_back.3 = (bf16[2048,1792]{1,0:T(8,128)(2,1)}, f32[1,768]{1,0:T(1,128)}) custom-call(bf16[2048,256]{1,0:T(8,128)(2,1)} %get-tuple-element.126.q_ref, bf16[2048,256]{1,0:T(8,128)(2,1)} %get-tuple-element.127.k_ref, bf16[2048,256]{1,0:T(8,128)(2,1)} %get-tuple-element.128.v_ref, s32[1024,1]{1,0:T(8,128)} %bitcast.118, ...), custom_call_target="tpu_custom_call", output_to_operand_aliasing={{0}: (9, {})} | custom-call | flops 5368709120 | bytes 4194304 | tf_op jit(solution)/shard_map/attend_back/pallas_call | solution.py:862
  620.3 21.6 %convolution_convert_fusion = bf16[2048,1792]{1,0:T(8,128)(2,1)} fusion(bf16[2048,2048]{1,0:T(8,128)(2,1)} %constant_dynamic-update-slice_fusion.14.x_ref, bf16[2048,1792]{1,0:T(8,128)(2,1)} %get-tuple-element.146.dz_ref), kind=kOutput, calls=%fused_computation | convolution fusion | flops 15036055552 | bytes 23068672 | tf_op jit(solution)/shard_map/dot_general | solution.py:61
  642.0 13.0 %inward.5 = bf16[1024,2048]{1,0:T(8,128)(2,1)} custom-call(bf16[2048,1792]{1,0:T(8,128)(2,1)} %get-tuple-element.146.dz_ref, bf16[2048,1024]{1,0:T(8,128)(2,1)} %all-gather.9.cloned.1.call-done.w_ref.wf_ref, bf16[2048,768]{1,0:T(8,128)(2,1)} %all-gather.11.cloned.1.call-done.wq_ref.wk_ref.wv_ref, ...), custom_call_target="tpu_custom_call" | custom-call | flops 7516192768 | bytes 11534336 | tf_op jit(solution)/shard_map/inward/pallas_call | solution.py:775
  655.1 12.8 %inward.4.keep_ref = bf16[1024,2048]{1,0:T(8,128)(2,1)} custom-call(bf16[2048,1792]{1,0:T(8,128)(2,1)} %get-tuple-element.146.dz_ref, bf16[2048,1024]{1,0:T(8,128)(2,1)} %all-gather.9.cloned.1.call-done.w_ref.wf_ref, bf16[2048,768]{1,0:T(8,128)(2,1)} %all-gather.11.cloned.1.call-done.wq_ref.wk_ref.wv_ref, ...), custom_call_target="tpu_custom_call" | custom-call | flops 7516192768 | bytes 11534336 | tf_op jit(solution)/shard_map/inward/pallas_call | solution.py:775
  676.1 22.6 %collective-permute-done.46.across_ref = bf16[256,2048]{1,0:T(8,128)(2,1)S(1)} collective-permute-done((bf16[256,2048]{1,0:T(8,128)(2,1)}, bf16[256,2048]{1,0:T(8,128)(2,1)S(1)}, u32[]{:S(2)}, u32[]{:S(2)}) %collective-permute-start.46) | collective-permute-done | bytes 1048608 | tf_op jit(solution)/shard_map/ppermute | solution.py:422
  727.5 21.4 %collective-permute-done.50 = bf16[256,2048]{1,0:T(8,128)(2,1)S(1)} collective-permute-done((bf16[256,2048]{1,0:T(8,128)(2,1)S(1)}, bf16[256,2048]{1,0:T(8,128)(2,1)S(1)}, u32[]{:S(2)}, u32[]{:S(2)}) %collective-permute-start.50) | collective-permute-done | bytes 1048608 | tf_op jit(solution)/shard_map/ppermute | solution.py:422
  764.9 11.5 %outer_back.4 = (bf16[2048,1792]{1,0:T(8,128)(2,1)}, bf16[1024,256]{1,0:T(8,128)(2,1)}, f32[1,1024]{1,0:T(1,128)}, f32[1,2048]{1,0:T(1,128)}) custom-call(s32[1]{0:T(128)} %bitcast.6.row_ref, bf16[512,2048]{1,0:T(8,128)(2,1)} %copy-done.10, bf16[512,2048]{1,0:T(8,128)(2,1)} %copy-done.26, bf16[1280,512]{1,0:T(8,128)(2,1)} %get-tuple-element.219.w0_ref.refs_2_, ...), custom_call_target="tpu_custom_call" | custom-call | flops 5368709120 | bytes 8388608 | tf_op jit(solution)/shard_map/outer_back/pallas_call | solution.py:802
  785.7 11.6 %outer_back.5 = (bf16[2048,1792]{1,0:T(8,128)(2,1)}, bf16[1024,256]{1,0:T(8,128)(2,1)}, f32[1,1024]{1,0:T(1,128)}, f32[1,2048]{1,0:T(1,128)}) custom-call(s32[1]{0:T(128)} %bitcast.6.row_ref, bf16[512,2048]{1,0:T(8,128)(2,1)} %constant_dynamic-update-slice_fusion.21.refs_0_, ...), custom_call_target="tpu_custom_call", output_to_operand_aliasing={{0}: (8, {})} | custom-call | flops 5368709120 | bytes 8388608 | tf_op jit(solution)/shard_map/outer_back/pallas_call | solution.py:802
  806.6 21.5 %convolution_convert_fusion.1 = bf16[2048,1792]{1,0:T(8,128)(2,1)} fusion(bf16[2048,2048]{1,0:T(8,128)(2,1)} %constant_dynamic-update-slice_fusion.x_ref, bf16[2048,1792]{1,0:T(8,128)(2,1)} %get-tuple-element.167.dz_ref), kind=kOutput, calls=%fused_computation.1 | convolution fusion | flops 15036055552 | bytes 23068672 | tf_op jit(solution)/shard_map/dot_general | solution.py:61
  848.1 10.9 fusion.2
  876.2 14.0 %inward.7 = bf16[1024,2048]{1,0:T(8,128)(2,1)} custom-call(bf16[2048,1792]{1,0:T(8,128)(2,1)} %get-tuple-element.167.dz_ref, bf16[2048,1024]{1,0:T(8,128)(2,1)} %all-gather.5.cloned.1.call-done.w_ref.wf_ref, bf16[2048,768]{1,0:T(8,128)(2,1)} %all-gather.7.cloned.1.call-done.wq_ref.wk_ref.wv_ref, ...), custom_call_target="tpu_custom_call" | custom-call | flops 7516192768 | bytes 11534336 | tf_op jit(solution)/shard_map/inward/pallas_call | solution.py:775
  938.0 12.9 %inward.6.keep_ref = bf16[1024,2048]{1,0:T(8,128)(2,1)} custom-call(bf16[2048,1792]{1,0:T(8,128)(2,1)} %get-tuple-element.167.dz_ref, bf16[2048,1024]{1,0:T(8,128)(2,1)} %all-gather.5.cloned.1.call-done.w_ref.wf_ref, bf16[2048,768]{1,0:T(8,128)(2,1)} %all-gather.7.cloned.1.call-done.wq_ref.wk_ref.wv_ref, ...), custom_call_target="tpu_custom_call" | custom-call | flops 7516192768 | bytes 11534336 | tf_op jit(solution)/shard_map/inward/pallas_call | solution.py:775
  966.9 14.2 %collective-permute-done.67.across_ref = bf16[256,2048]{1,0:T(8,128)(2,1)} collective-permute-done((bf16[256,2048]{1,0:T(8,128)(2,1)}, bf16[256,2048]{1,0:T(8,128)(2,1)}, u32[]{:S(2)}, u32[]{:S(2)}) %collective-permute-start.67) | collective-permute-done | bytes 1048608 | tf_op jit(solution)/shard_map/ppermute | solution.py:422
  1025.2 29.3 %collective-permute-done.72 = bf16[512,1792]{1,0:T(8,128)(2,1)} collective-permute-done((bf16[512,1792]{1,0:T(8,128)(2,1)}, bf16[512,1792]{1,0:T(8,128)(2,1)}, u32[]{:S(2)}, u32[]{:S(2)}) %collective-permute-start.72) | collective-permute-done | bytes 1835040 | tf_op jit(solution)/shard_map/ppermute | solution.py:1087
  1065.2 13.2 %collective-permute-done.60 = f32[4,512]{1,0:T(4,128)S(1)} collective-permute-done((f32[4,512]{1,0:T(4,128)S(1)}, f32[4,512]{1,0:T(4,128)S(1)}, u32[]{:S(2)}, u32[]{:S(2)}) %collective-permute-start.60) | collective-permute-done | bytes 8224 | tf_op jit(solution)/shard_map/ppermute | solution.py:422
  (493 shorter events, 493.2 us)
Async XLA Ops:
  7.2 187.7 %all-gather.7.cloned.1.call-start = ((), (), s32[]{:S(2)}) async-start(), calls=%async_computation.6 | async-start | bytes 3932160 | tf_op jit(solution)/shard_map/all_gather | solution.py:934
  39.8 222.2 %all-gather.5.cloned.1.call-start = ((), (), s32[]{:S(2)}) async-start(), calls=%async_computation.5 | async-start | bytes 5242880 | tf_op jit(solution)/shard_map/all_gather | solution.py:934
  101.4 423.7 %all-gather.11.cloned.1.call-start = ((), (), s32[]{:S(2)}) async-start(), calls=%async_computation.8 | async-start | bytes 3932160 | tf_op jit(solution)/shard_map/all_gather | solution.py:934
  117.6 35.5 %collective-permute-start.10 = (bf16[512,2048]{1,0:T(8,128)(2,1)}, bf16[512,2048]{1,0:T(8,128)(2,1)}, u32[]{:S(2)}, u32[]{:S(2)}) collective-permute-start(bf16[512,2048]{1,0:T(8,128)(2,1)} %pad_maximum_fusion), channel_id=1, source_target_pairs={{0,1},{1,0},{2,3},{3,2},{4,5},{5,4},{6,7},{7,6},{8,9},{9,8},{10,11... | collective-permute-start | bytes 6291464 | tf_op jit(solution)/shard_map/ppermute | solution.py:422
  169.8 73.5 %collective-permute-start.5 = (bf16[1280,512]{1,0:T(8,128)(2,1)}, bf16[1280,512]{1,0:T(8,128)(2,1)}, u32[]{:S(2)}, u32[]{:S(2)}) collective-permute-start(bf16[1280,512]{1,0:T(8,128)(2,1)} %get-tuple-element.219.w0_ref.refs_2_), channel_id=1, source_target_pairs={{0,8},{4,12},{8,0},{12,4},{1,9},{5,13},{9,1},{13,5},{2,10},{6,14},... | collective-permute-start | bytes 3932168 | tf_op jit(solution)/shard_map/ppermute | solution.py:422
  170.4 119.6 %collective-permute-start.4 = (bf16[1280,512]{1,0:T(8,128)(2,1)}, bf16[1280,512]{1,0:T(8,128)(2,1)}, u32[]{:S(2)}, u32[]{:S(2)}) collective-permute-start(bf16[1280,512]{1,0:T(8,128)(2,1)} %get-tuple-element.219.w0_ref.refs_2_), channel_id=1, source_target_pairs={{12,8},{8,4},{4,0},{13,9},{9,5},{5,1},{14,10},{10,6},{6,2},{15,11}... | collective-permute-start | bytes 3932168 | tf_op jit(solution)/shard_map/ppermute | solution.py:462
  190.3 55.3 %collective-permute-start.22 = (bf16[128,2048]{1,0:T(8,128)(2,1)}, bf16[128,2048]{1,0:T(8,128)(2,1)}, u32[]{:S(2)}, u32[]{:S(2)}) collective-permute-start(bf16[128,2048]{1,0:T(8,128)(2,1)} %slice.184), channel_id=1, source_target_pairs={{0,16},{16,0},{1,17},{17,1},{2,18},{18,2},{3,19},{19,3},{4,20},{20... | collective-permute-start | bytes 1572872 | tf_op jit(solution)/shard_map/ppermute | solution.py:422
  191.9 55.2 %collective-permute-start.23 = (bf16[128,2048]{1,0:T(8,128)(2,1)}, bf16[128,2048]{1,0:T(8,128)(2,1)}, u32[]{:S(2)}, u32[]{:S(2)}) collective-permute-start(bf16[128,2048]{1,0:T(8,128)(2,1)} %slice.185), channel_id=1, source_target_pairs={{0,2},{1,3},{2,0},{3,1},{4,6},{5,7},{6,4},{7,5},{8,10},{9,11},{10,... | collective-permute-start | bytes 1572872 | tf_op jit(solution)/shard_map/ppermute | solution.py:422
  194.9 83.9 %collective-permute-start.21 = (bf16[512,2048]{1,0:T(8,128)(2,1)}, bf16[512,2048]{1,0:T(8,128)(2,1)}, u32[]{:S(2)}, u32[]{:S(2)}) collective-permute-start(bf16[512,2048]{1,0:T(8,128)(2,1)} %pad_maximum_fusion.2), channel_id=1, source_target_pairs={{0,1},{1,0},{2,3},{3,2},{4,5},{5,4},{6,7},{7,6},{8,9},{9,8},{10,11... | collective-permute-start | bytes 6291464 | tf_op jit(solution)/shard_map/ppermute | solution.py:422
  243.3 46.7 %collective-permute-start.6 = (bf16[1280,512]{1,0:T(8,128)(2,1)}, bf16[1280,512]{1,0:T(8,128)(2,1)}, u32[]{:S(2)}, u32[]{:S(2)}) collective-permute-start(bf16[1280,512]{1,0:T(8,128)(2,1)} %get-tuple-element.219.w0_ref.refs_2_), channel_id=1, source_target_pairs={{0,4},{4,8},{8,12},{1,5},{5,9},{9,13},{2,6},{6,10},{10,14},{3,7},{... | collective-permute-start | bytes 3932168 | tf_op jit(solution)/shard_map/ppermute | solution.py:462
  245.6 44.4 %collective-permute-start.7 = (bf16[1280,512]{1,0:T(8,128)(2,1)}, bf16[1280,512]{1,0:T(8,128)(2,1)}, u32[]{:S(2)}, u32[]{:S(2)}) collective-permute-start(bf16[1280,512]{1,0:T(8,128)(2,1)} %collective-permute-done.5.w2_ref.refs_4_), channel_id=1, source_target_pairs={{8,12},{4,0},{9,13},{5,1},{10,14},{6,2},{11,15},{7,3},{24,28},{20,... | collective-permute-start | bytes 3932168 | tf_op jit(solution)/shard_map/ppermute | solution.py:462
  249.9 37.0 %collective-permute-start.24 = (bf16[512,2048]{1,0:T(8,128)(2,1)}, bf16[512,2048]{1,0:T(8,128)(2,1)}, u32[]{:S(2)}, u32[]{:S(2)}) collective-permute-start(bf16[512,2048]{1,0:T(8,128)(2,1)} %pad_maximum_fusion.3), channel_id=1, source_target_pairs={{0,1},{1,0},{2,3},{3,2},{4,5},{5,4},{6,7},{7,6},{8,9},{9,8},{10,11... | collective-permute-start | bytes 6291464 | tf_op jit(solution)/shard_map/ppermute | solution.py:422
  303.8 245.1 %all-gather.9.cloned.1.call-start = ((), (), s32[]{:S(2)}) async-start(), calls=%async_computation.7 | async-start | bytes 5242880 | tf_op jit(solution)/shard_map/all_gather | solution.py:934
  355.2 636.2 %reduce-scatter.12.cloned.1.call-start = ((), (), s32[]{:S(2)}) async-start(), calls=%async_computation.12 | async-start | bytes 9175040 | tf_op jit(solution)/shard_map/reduce_scatter | solution.py:1035
  395.5 123.6 %collective-permute-start.32 = (bf16[512,2048]{1,0:T(8,128)(2,1)S(1)}, bf16[512,2048]{1,0:T(8,128)(2,1)S(1)}, u32[]{:S(2)}, u32[]{:S(2)}) collective-permute-start(bf16[512,2048]{1,0:T(8,128)(2,1)S(1)} %pad_maximum_fusion.4), channel_id=1, source_target_pairs={{0,1},{1,0},{2,3},{3,2},{4,5},{5,4},{6,7},{7,6},{8,9},{9,8},{10,11... | collective-permute-start | bytes 6291464 | tf_op jit(solution)/shard_map/ppermute | solution.py:422
  396.9 119.9 %collective-permute-start.37 = (bf16[1280,512]{1,0:T(8,128)(2,1)S(1)}, bf16[1280,512]{1,0:T(8,128)(2,1)}, u32[]{:S(2)}, u32[]{:S(2)}) collective-permute-start(bf16[1280,512]{1,0:T(8,128)(2,1)S(1)} %copy-done.35), channel_id=1, source_target_pairs={{0,8},{4,12},{8,0},{12,4},{1,9},{5,13},{9,1},{13,5},{2,10},{6,14},... | collective-permute-start | bytes 3932168 | tf_op jit(solution)/shard_map/ppermute | solution.py:422
  411.7 111.9 %collective-permute-start.35 = (bf16[512,2048]{1,0:T(8,128)(2,1)S(1)}, bf16[512,2048]{1,0:T(8,128)(2,1)S(1)}, u32[]{:S(2)}, u32[]{:S(2)}) collective-permute-start(bf16[512,2048]{1,0:T(8,128)(2,1)S(1)} %pad_maximum_fusion.5), channel_id=1, source_target_pairs={{0,1},{1,0},{2,3},{3,2},{4,5},{5,4},{6,7},{7,6},{8,9},{9,8},{10,11... | collective-permute-start | bytes 6291464 | tf_op jit(solution)/shard_map/ppermute | solution.py:422
  413.7 168.6 %collective-permute-start.36 = (bf16[1280,512]{1,0:T(8,128)(2,1)S(1)}, bf16[1280,512]{1,0:T(8,128)(2,1)}, u32[]{:S(2)}, u32[]{:S(2)}) collective-permute-start(bf16[1280,512]{1,0:T(8,128)(2,1)S(1)} %copy-done.35), channel_id=1, source_target_pairs={{12,8},{8,4},{4,0},{13,9},{9,5},{5,1},{14,10},{10,6},{6,2},{15,11}... | collective-permute-start | bytes 3932168 | tf_op jit(solution)/shard_map/ppermute | solution.py:462
  415.0 167.4 %collective-permute-start.38 = (bf16[1280,512]{1,0:T(8,128)(2,1)S(1)}, bf16[1280,512]{1,0:T(8,128)(2,1)}, u32[]{:S(2)}, u32[]{:S(2)}) collective-permute-start(bf16[1280,512]{1,0:T(8,128)(2,1)S(1)} %copy-done.35), channel_id=1, source_target_pairs={{0,4},{4,8},{8,12},{1,5},{5,9},{9,13},{2,6},{6,10},{10,14},{3,7},{... | collective-permute-start | bytes 3932168 | tf_op jit(solution)/shard_map/ppermute | solution.py:462
  516.8 65.6 %collective-permute-start.39 = (bf16[1280,512]{1,0:T(8,128)(2,1)}, bf16[1280,512]{1,0:T(8,128)(2,1)}, u32[]{:S(2)}, u32[]{:S(2)}) collective-permute-start(bf16[1280,512]{1,0:T(8,128)(2,1)} %collective-permute-done.37.w2_ref.refs_3_), channel_id=1, source_target_pairs={{8,12},{4,0},{9,13},{5,1},{10,14},{6,2},{11,15},{7,3},{24,28},{20,... | collective-permute-start | bytes 3932168 | tf_op jit(solution)/shard_map/ppermute | solution.py:462
  642.0 363.3 %reduce-scatter.14.cloned.1.call-start = ((), (), s32[]{:S(2)}) async-start(), calls=%async_computation.13 | async-start | bytes 6553600 | tf_op jit(solution)/shard_map/reduce_scatter | solution.py:1035
  676.1 341.6 %reduce-scatter.10.cloned.1.call-start = ((), (), s32[]{:S(2)}) async-start(), calls=%async_computation.11 | async-start | bytes 9175040 | tf_op jit(solution)/shard_map/reduce_scatter | solution.py:1035
  828.1 256.5 %reduce-scatter.8.cloned.1.call-start = ((), (), s32[]{:S(2)}) async-start(), calls=%async_computation.10 | async-start | bytes 5242880 | tf_op jit(solution)/shard_map/reduce_scatter | solution.py:1035
  859.1 256.8 %reduce-scatter.6.cloned.1.call-start = ((), (), s32[]{:S(2)}) async-start(), calls=%async_computation.9 | async-start | bytes 1310720 | tf_op jit(solution)/shard_map/reduce_scatter | solution.py:1035
  890.2 60.8 %collective-permute-start.66 = (bf16[1024,2048]{1,0:T(8,128)(2,1)}, bf16[1024,2048]{1,0:T(8,128)(2,1)}, u32[]{:S(2)}, u32[]{:S(2)}) collective-permute-start(bf16[1024,2048]{1,0:T(8,128)(2,1)} %inward.7), channel_id=1, source_target_pairs={{0,1},{1,0},{2,3},{3,2},{4,5},{5,4},{6,7},{7,6},{8,9},{9,8},{10,11... | collective-permute-start | bytes 12582920 | tf_op jit(solution)/shard_map/ppermute | solution.py:422
  908.9 50.1 %collective-permute-start.65 = (bf16[256,2048]{1,0:T(8,128)(2,1)S(1)}, bf16[256,2048]{1,0:T(8,128)(2,1)S(1)}, u32[]{:S(2)}, u32[]{:S(2)}) collective-permute-start(bf16[256,2048]{1,0:T(8,128)(2,1)S(1)} %get-tuple-element.209), channel_id=1, source_target_pairs={{0,16},{16,0},{1,17},{17,1},{2,18},{18,2},{3,19},{19,3},{4,20},{20... | collective-permute-start | bytes 3145736 | tf_op jit(solution)/shard_map/ppermute | solution.py:422
  962.5 156.6 %collective-permute-start.56 = (bf16[256,2048]{1,0:T(8,128)(2,1)}, bf16[256,2048]{1,0:T(8,128)(2,1)}, u32[]{:S(2)}, u32[]{:S(2)}) collective-permute-start(bf16[256,2048]{1,0:T(8,128)(2,1)} %get-tuple-element.201), channel_id=1, source_target_pairs={{0,16},{1,17},{2,18},{3,19},{4,20},{5,21},{6,22},{7,23},{8,24},{9,... | collective-permute-start | bytes 3145736 | tf_op jit(solution)/shard_map/ppermute | solution.py:1087
  966.7 37.2 %collective-permute-start.73 = (f32[3584]{0:T(1024)S(1)}, f32[3584]{0:T(1024)S(1)}, u32[]{:S(2)}, u32[]{:S(2)}) collective-permute-start(f32[3584]{0:T(1024)S(1)} %slice.248), channel_id=1, source_target_pairs={{0,16},{16,0},{1,17},{17,1},{2,18},{18,2},{3,19},{19,3},{4,20},{20... | collective-permute-start | bytes 43016 | tf_op jit(solution)/shard_map/ppermute | solution.py:422
  991.3 63.2 %collective-permute-start.72 = (bf16[512,1792]{1,0:T(8,128)(2,1)}, bf16[512,1792]{1,0:T(8,128)(2,1)}, u32[]{:S(2)}, u32[]{:S(2)}) collective-permute-start(bf16[512,1792]{1,0:T(8,128)(2,1)} %reduce-scatter.12.cloned.1.call-done), channel_id=1, source_target_pairs={{0,16},{1,17},{2,18},{3,19},{4,20},{5,21},{6,22},{7,23},{8,24},{9,... | collective-permute-start | bytes 5505032 | tf_op jit(solution)/shard_map/ppermute | solution.py:1087
  1005.2 94.3 %collective-permute-start.63 = (bf16[1280,512]{1,0:T(8,128)(2,1)}, bf16[1280,512]{1,0:T(8,128)(2,1)}, u32[]{:S(2)}, u32[]{:S(2)}) collective-permute-start(bf16[1280,512]{1,0:T(8,128)(2,1)} %reduce-scatter.14.cloned.1.call-done), channel_id=1, source_target_pairs={{0,16},{1,17},{2,18},{3,19},{4,20},{5,21},{6,22},{7,23},{8,24},{9,... | collective-permute-start | bytes 3932168 | tf_op jit(solution)/shard_map/ppermute | solution.py:1087
  1017.7 45.0 %collective-permute-start.57 = (bf16[512,1792]{1,0:T(8,128)(2,1)}, bf16[512,1792]{1,0:T(8,128)(2,1)S(1)}, u32[]{:S(2)}, u32[]{:S(2)}) collective-permute-start(bf16[512,1792]{1,0:T(8,128)(2,1)} %reduce-scatter.10.cloned.1.call-done), channel_id=1, source_target_pairs={{16,0},{17,1},{18,2},{19,3},{20,4},{21,5},{22,6},{23,7},{24,8},{25... | collective-permute-start | bytes 5505032 | tf_op jit(solution)/shard_map/ppermute | solution.py:1084
  1023.6 93.6 %collective-permute-start.71 = (bf16[256,2048]{1,0:T(8,128)(2,1)}, bf16[256,2048]{1,0:T(8,128)(2,1)}, u32[]{:S(2)}, u32[]{:S(2)}) collective-permute-start(bf16[256,2048]{1,0:T(8,128)(2,1)} %get-tuple-element.199), channel_id=1, source_target_pairs={{16,0},{17,1},{18,2},{19,3},{20,4},{21,5},{22,6},{23,7},{24,8},{25... | collective-permute-start | bytes 3145736 | tf_op jit(solution)/shard_map/ppermute | solution.py:1084
  (120 other events, 2026.1 us)
Sparse Core Ops, SparseCore 0:
  39.9 64.8 all-gather.6
  107.0 116.6 all-gather.4
  303.9 75.8 all-gather.10
  381.8 132.1 all-gather.8
  642.1 129.4 reduce-scatter.11
  773.7 94.2 reduce-scatter.13
  870.3 129.6 reduce-scatter.9
  1002.4 77.2 reduce-scatter.7
  1081.9 27.7 reduce-scatter.5

commit v8 on v6

--- a/solution.py
+++ b/solution.py
@@ -1013,13 +1013,16 @@
         w_fc_in, w_qkv, offset = w_ins[layer]
         queries, keys_all, values_all = project(x, w_qkv, offset, qkv_e[layer], tables)
         attended, log_sums = attend(queries, keys_all, values_all, places, inner)
+        if layer == 1:
+            out_grad1 = contract_rows(attended[:, inner:], seed_rows).astype(BF16)
+            attended = after(attended, out_grad1)
         act, slopes = inner_layer(x, w_fc_in, fc_e[layer], attended)
         if layer == 0:
             *pieces, act, unused = lax.optimization_barrier((*w_outs[0][1:], act, seed_rows))
             w_outs[0] = in_turn((w_outs[0][0], *pieces), r)
         kept = (x, queries, keys_all, values_all, log_sums, slopes, act)
         if layer == 1:
-            outs_grad1 = contract_rows(act, seed_rows).astype(BF16)
+            outs_grad1 = contract_rows(act[:, :inner], seed_rows).astype(BF16)
             seed_rows = after(seed_rows, outs_grad1)
             *pieces, unused = lax.optimization_barrier((*w_outs[1][1:], outs_grad1))
             w_outs[1] = in_turn((w_outs[1][0], *pieces), r)
@@ -1033,7 +1036,8 @@
     def reduced(value, axis):
         return lax.psum_scatter(value, ROW, scatter_dimension=axis, tiled=True)
 
-    outs_part1 = reduced(outs_grad1, 1)
+    out_part1 = reduced(out_grad1, 1)
+    outs_part1 = jnp.concatenate([reduced(outs_grad1, 1), out_part1], axis=0)
     grads = seed
     ins_list, small_list = ([None, None], [None, None])
     for layer in (1, 0):
@@ -1134,7 +1138,9 @@
     ).astype(F32)[None]
     qkv_w_grad = qkv_w_grad.reshape(qkv_w.shape)[None]
     fc_in_w_grad = fc_in_w_grad[None]
-    out_part0, norms, unused = lax.optimization_barrier((out_part0, norms, fc_out_upper))
+    out_part0, fc_out_w_grad, norms = lax.optimization_barrier(
+        (out_part0, fc_out_w_grad, norms)
+    )
     out_upper = to_first(out_part0)
     out_w_grad = jnp.concatenate(
         [

time: 1140 us -> 1260 us (1.11)
  waiting for transfers between devices: 469 us -> 601 us
  starting transfers between devices: 104 us -> 86.4 us
    ppermute x6, waiting for transfers between devices: 0.02 us -> 140 us  [send(): return lax.ppermute(value, ROW, pairs)]
    ppermute x62, waiting for transfers between devices: 413 us -> 359 us  [swap(): lax.ppermute(value, axis, [(source, source ^ bit) for source in range(cou...]
    all_gather x3, waiting for transfers between devices: 0.01 us -> 51.5 us  [gathered(): return lax.all_gather(shard, ROW, axis=axis, tiled=True)]
    ppermute x62, starting transfers between devices: 72.5 us -> 54.3 us  [swap(): lax.ppermute(value, axis, [(source, source ^ bit) for source in range(cou...]
    dot_general x5 -> x6, matrix products: 77.8 us -> 81.9 us  [contract_rows(): lax.dot_general(first_operand, second_operand, (((0,), (0,)), ((), ())),...]
  transfers between devices with their start and end apart: 83 -> 84, of which waited for: 40 -> 47; matrix products, arithmetic and copies ran while one was open for 18% -> 19% of each run, Pallas kernels for 22% -> 23%
where the time goes in v8:
time: 1260 us; the launch traced here: 1250 us
  waiting for transfers between devices  601 us (48%)
  Pallas kernels  293 us (23%)
  other arithmetic  88.3 us (7%)
  starting transfers between devices  86.4 us (7%)
  matrix products  82.6 us (7%)
  local copies, waits for them, and re-layouts  81.1 us (6%)
  between operations  15.4 us (1%)
    ppermute x62, waiting for transfers between devices, swap(): lax.ppermute(value, axis, [(source, source ^ bit) for source in range(cou...  359 us
    ppermute x6, waiting for transfers between devices, send(): return lax.ppermute(value, ROW, pairs)  140 us
    dot_general x6, matrix products, contract_rows(): lax.dot_general(first_operand, second_operand, (((0,), (0,)), ((), ())),...  81.9 us
    ppermute x62, starting transfers between devices, swap(): lax.ppermute(value, axis, [(source, source ^ bit) for source in range(cou...  54.3 us
    pallas_call x4, Pallas kernels, inward(): pl.pallas_call(inward_kernel, grid=(rows // ROW_BLOCK,), in_specs=[split_...  51.7 us
    all_gather x3, waiting for transfers between devices, gathered(): return lax.all_gather(shard, ROW, axis=axis, tiled=True)  51.5 us
    unnamed x175, local copies, waits for them, and re-layouts  45.5 us
    pallas_call x8, Pallas kernels, column_call(): pl.pallas_call(kernel, grid=(width // tile,), in_specs=[spec(member.shape...  44.7 us
  transfers between devices with their start and end apart: 84, of which 47 were waited for; matrix products, arithmetic and copies ran while one was open for 19% of the time, Pallas kernels for 23%

profile of v8, /device:TPU:0, one launch (start us, length us, event | category | flops | bytes accessed | tf_op | source)
XLA Modules:
  0.0 1247.8 jit_solution(12909261957882192626)
XLA Ops:
  22.0 14.0 %collective-permute-done.1 = bf16[512,768]{1,0:T(8,128)(2,1)} collective-permute-done((bf16[512,768]{1,0:T(8,128)(2,1)}, bf16[512,768]{1,0:T(8,128)(2,1)}, u32[]{:S(2)}, u32[]{:S(2)}) %collective-permute-start.1) | collective-permute-done | bytes 786464 | tf_op jit(solution)/shard_map/ppermute | solution.py:422
  44.7 15.2 %collective-permute-done.2 = bf16[512,1024]{1,0:T(8,128)(2,1)} collective-permute-done((bf16[512,1024]{1,0:T(8,128)(2,1)S(1)}, bf16[512,1024]{1,0:T(8,128)(2,1)}, u32[]{:S(2)}, u32[]{:S(2)}) %collective-permute-start.2) | collective-permute-done | bytes 1048608 | tf_op jit(solution)/shard_map/ppermute | solution.py:422
  60.7 28.1 %collective-permute-done.3 = bf16[1280,512]{1,0:T(8,128)(2,1)} collective-permute-done((bf16[1280,512]{1,0:T(8,128)(2,1)}, bf16[1280,512]{1,0:T(8,128)(2,1)}, u32[]{:S(2)}, u32[]{:S(2)}) %collective-permute-start.3) | collective-permute-done | bytes 1310752 | tf_op jit(solution)/shard_map/ppermute | solution.py:422
  101.5 12.0 collective-permute-done.9
  175.8 12.5 collective-permute-done.20
  194.6 12.7 %project.2 = (bf16[2048,256]{1,0:T(8,128)(2,1)}, bf16[2048,256]{1,0:T(8,128)(2,1)}, bf16[2048,256]{1,0:T(8,128)(2,1)}) custom-call(bf16[2048,2048]{1,0:T(8,128)(2,1)} %constant_dynamic-update-slice_fusion.x_ref, bf16[2048,768]{1,0:T(8,128)(2,1)} %all-gather.6.cloned.1.call-done.wq_ref.wk_ref.wv_ref, ...), custom_call_target="tpu_custom_call" | custom-call | flops 6442450944 | bytes 11534336 | tf_op jit(solution)/shard_map/project/pallas_call | solution.py:718
  207.3 35.9 %collective-permute-done.5.w2_ref.refs_4_ = bf16[1280,512]{1,0:T(8,128)(2,1)} collective-permute-done((bf16[1280,512]{1,0:T(8,128)(2,1)}, bf16[1280,512]{1,0:T(8,128)(2,1)}, u32[]{:S(2)}, u32[]{:S(2)}) %collective-permute-start.5) | collective-permute-done | bytes 1310752 | tf_op jit(solution)/shard_map/ppermute | solution.py:422
  260.9 16.7 %inner.2 = (bf16[2048,1280]{1,0:T(8,128)(2,1)}, bf16[2048,1024]{1,0:T(8,128)(2,1)}) custom-call(bf16[2048,2048]{1,0:T(8,128)(2,1)} %constant_dynamic-update-slice_fusion.x_ref, bf16[2048,1024]{1,0:T(8,128)(2,1)} %all-gather.4.cloned.1.call-done.w_ref.wf_ref, f32[1,1024]{1,0:T(1,128)} %bitcast.174, ...), custom_call_target="tpu_custom_call", output_to_operand_aliasing={{0}: (3, {})} | custom-call | flops 8589934592 | bytes 16777216 | tf_op jit(solution)/shard_map/inner/pallas_call | solution.py:733
  288.9 15.4 %collective-permute-done.7 = bf16[1280,512]{1,0:T(8,128)(2,1)} collective-permute-done((bf16[1280,512]{1,0:T(8,128)(2,1)}, bf16[1280,512]{1,0:T(8,128)(2,1)}, u32[]{:S(2)}, u32[]{:S(2)}) %collective-permute-start.7) | collective-permute-done | bytes 1310752 | tf_op jit(solution)/shard_map/ppermute | solution.py:462
  337.5 22.8 %collective-permute-done.26.across_ref = bf16[256,2048]{1,0:T(8,128)(2,1)S(1)} collective-permute-done((bf16[256,2048]{1,0:T(8,128)(2,1)}, bf16[256,2048]{1,0:T(8,128)(2,1)S(1)}, u32[]{:S(2)}, u32[]{:S(2)}) %collective-permute-start.26) | collective-permute-done | bytes 1048608 | tf_op jit(solution)/shard_map/ppermute | solution.py:422
  389.3 21.5 %collective-permute-done.31 = bf16[256,2048]{1,0:T(8,128)(2,1)S(1)} collective-permute-done((bf16[256,2048]{1,0:T(8,128)(2,1)S(1)}, bf16[256,2048]{1,0:T(8,128)(2,1)S(1)}, u32[]{:S(2)}, u32[]{:S(2)}) %collective-permute-start.31) | collective-permute-done | bytes 1048608 | tf_op jit(solution)/shard_map/ppermute | solution.py:422
  436.3 51.5 %all-gather.8.cloned.1.call-done.wq_ref.wk_ref.wv_ref.w_ref.wf_ref = bf16[2048,1792]{1,0:T(8,128)(2,1)} async-done(((bf16[512,1792]{1,0:T(8,128)(2,1)}), bf16[2048,1792]{1,0:T(8,128)(2,1)}) %all-gather.8.cloned.1.call-update) | async-done | bytes 7340048 | tf_op jit(solution)/shard_map/all_gather | solution.py:934
  487.8 12.7 %project.3 = (bf16[2048,256]{1,0:T(8,128)(2,1)}, bf16[2048,256]{1,0:T(8,128)(2,1)}, bf16[2048,256]{1,0:T(8,128)(2,1)}) custom-call(bf16[2048,2048]{1,0:T(8,128)(2,1)} %constant_dynamic-update-slice_fusion.14.x_ref, bf16[2048,1792]{1,0:T(8,128)(2,1)} %all-gather.8.cloned.1.call-done.wq_ref.wk_ref.wv_ref.w_ref.wf_ref, ...), custom_call_target="tpu_custom_call" | custom-call | flops 6442450944 | bytes 11534336 | tf_op jit(solution)/shard_map/project/pallas_call | solution.py:718
  518.8 16.7 %inner.3 = (bf16[2048,1280]{1,0:T(8,128)(2,1)}, bf16[2048,1024]{1,0:T(8,128)(2,1)}) custom-call(bf16[2048,2048]{1,0:T(8,128)(2,1)} %constant_dynamic-update-slice_fusion.14.x_ref, bf16[2048,1792]{1,0:T(8,128)(2,1)} %all-gather.8.cloned.1.call-done.wq_ref.wk_ref.wv_ref.w_ref.wf_ref, f32[1,1024]{1,0:T(1,128)} %bitcast.175, ...), custom_call_target="tpu_custom_call", output_to_operand_aliasing={{0}: (3, {})} | custom-call | flops 8589934592 | bytes 16777216 | tf_op jit(solution)/shard_map/inner/pallas_call | solution.py:733
  535.5 14.1 %fusion.4 = bf16[1024,2048]{1,0:T(8,128)(2,1)} fusion(bf16[2048,2048]{1,0:T(8,128)(2,1)} %constant_dynamic-update-slice_fusion.7.refs_0_, bf16[2048,1280]{1,0:T(8,128)(2,1)} %get-tuple-element.132.act_ref), kind=kOutput, calls=%fused_computation.7 | convolution fusion | flops 8592031744 | bytes 16777216 | tf_op jit(solution)/shard_map/dot_general | solution.py:61
  554.1 51.8 %collective-permute-done.38 = bf16[1280,512]{1,0:T(8,128)(2,1)S(1)} collective-permute-done((bf16[1280,512]{1,0:T(8,128)(2,1)S(1)}, bf16[1280,512]{1,0:T(8,128)(2,1)S(1)}, u32[]{:S(2)}, u32[]{:S(2)}) %collective-permute-start.38) | collective-permute-done | bytes 1310752 | tf_op jit(solution)/shard_map/ppermute | solution.py:462
  605.9 34.6 %collective-permute-done.36 = bf16[1280,512]{1,0:T(8,128)(2,1)S(1)} collective-permute-done((bf16[1280,512]{1,0:T(8,128)(2,1)S(1)}, bf16[1280,512]{1,0:T(8,128)(2,1)S(1)}, u32[]{:S(2)}, u32[]{:S(2)}) %collective-permute-start.36) | collective-permute-done | bytes 1310752 | tf_op jit(solution)/shard_map/ppermute | solution.py:462
  640.5 38.7 %collective-permute-done.39 = bf16[1280,512]{1,0:T(8,128)(2,1)S(1)} collective-permute-done((bf16[1280,512]{1,0:T(8,128)(2,1)}, bf16[1280,512]{1,0:T(8,128)(2,1)S(1)}, u32[]{:S(2)}, u32[]{:S(2)}) %collective-permute-start.39) | collective-permute-done | bytes 1310752 | tf_op jit(solution)/shard_map/ppermute | solution.py:462
  680.9 18.6 %outer_back.3 = (bf16[2048,1792]{1,0:T(8,128)(2,1)}, bf16[2048,256]{1,0:T(8,128)(2,1)}, f32[1,1024]{1,0:T(1,128)}, f32[1,2048]{1,0:T(1,128)}) custom-call(s32[1]{0:T(128)} %bitcast.6.row_ref, bf16[2048,2048]{1,0:T(8,128)(2,1)} %constant_dynamic-update-slice_fusion.7.refs_0_, bf16[1280,512]{1,0:T(8,128)(2,1)} %get-tuple-element.220.w0_ref.refs_1_, ...), custom_call_target="tpu_custom_call" | custom-call | flops 10737418240 | bytes 12582912 | tf_op jit(solution)/shard_map/outer_back/pallas_call | solution.py:802
  699.5 16.0 %attend_back.3 = (bf16[2048,1792]{1,0:T(8,128)(2,1)}, f32[1,768]{1,0:T(1,128)}) custom-call(bf16[2048,256]{1,0:T(8,128)(2,1)} %get-tuple-element.127.q_ref, bf16[2048,256]{1,0:T(8,128)(2,1)} %get-tuple-element.128.k_ref, bf16[2048,256]{1,0:T(8,128)(2,1)} %get-tuple-element.129.v_ref, s32[1024,1]{1,0:T(8,128)} %bitcast.118, ...), custom_call_target="tpu_custom_call", output_to_operand_aliasing={{0}: (9, {})} | custom-call | flops 5368709120 | bytes 4194304 | tf_op jit(solution)/shard_map/attend_back/pallas_call | solution.py:862
  715.4 12.9 %inward.5 = bf16[1024,2048]{1,0:T(8,128)(2,1)} custom-call(bf16[2048,1792]{1,0:T(8,128)(2,1)} %get-tuple-element.148.dz_ref, bf16[2048,1792]{1,0:T(8,128)(2,1)} %all-gather.8.cloned.1.call-done.wq_ref.wk_ref.wv_ref.w_ref.wf_ref, bf16[2048,1792]{1,0:T(8,128)(2,1)} %all-gather.8.cloned.1.call-done.wq_ref.wk_ref.wv_ref.w_ref.wf_ref, ...), custom_call_target="tpu_custom_call" | custom-call | flops 7516192768 | bytes 11534336 | tf_op jit(solution)/shard_map/inward/pallas_call | solution.py:775
  728.3 21.2 %convolution_convert_fusion = bf16[2048,1792]{1,0:T(8,128)(2,1)} fusion(bf16[2048,2048]{1,0:T(8,128)(2,1)} %constant_dynamic-update-slice_fusion.14.x_ref, bf16[2048,1792]{1,0:T(8,128)(2,1)} %get-tuple-element.148.dz_ref), kind=kOutput, calls=%fused_computation | convolution fusion | flops 15036055552 | bytes 23068672 | tf_op jit(solution)/shard_map/dot_general | solution.py:61
  749.6 13.0 %inward.4.keep_ref = bf16[1024,2048]{1,0:T(8,128)(2,1)} custom-call(bf16[2048,1792]{1,0:T(8,128)(2,1)} %get-tuple-element.148.dz_ref, bf16[2048,1792]{1,0:T(8,128)(2,1)} %all-gather.8.cloned.1.call-done.wq_ref.wk_ref.wv_ref.w_ref.wf_ref, bf16[2048,1792]{1,0:T(8,128)(2,1)} %all-gather.8.cloned.1.call-done.wq_ref.wk_ref.wv_ref.w_ref.wf_ref, ...), custom_call_target="tpu_custom_call" | custom-call | flops 7516192768 | bytes 11534336 | tf_op jit(solution)/shard_map/inward/pallas_call | solution.py:775
  770.7 22.9 %collective-permute-done.46.across_ref = bf16[256,2048]{1,0:T(8,128)(2,1)S(1)} collective-permute-done((bf16[256,2048]{1,0:T(8,128)(2,1)}, bf16[256,2048]{1,0:T(8,128)(2,1)S(1)}, u32[]{:S(2)}, u32[]{:S(2)}) %collective-permute-start.46) | collective-permute-done | bytes 1048608 | tf_op jit(solution)/shard_map/ppermute | solution.py:422
  822.3 21.6 %collective-permute-done.51 = bf16[256,2048]{1,0:T(8,128)(2,1)S(1)} collective-permute-done((bf16[256,2048]{1,0:T(8,128)(2,1)S(1)}, bf16[256,2048]{1,0:T(8,128)(2,1)S(1)}, u32[]{:S(2)}, u32[]{:S(2)}) %collective-permute-start.51) | collective-permute-done | bytes 1048608 | tf_op jit(solution)/shard_map/ppermute | solution.py:422
  901.5 21.5 %convolution_convert_fusion.1 = bf16[2048,1792]{1,0:T(8,128)(2,1)} fusion(bf16[2048,2048]{1,0:T(8,128)(2,1)} %constant_dynamic-update-slice_fusion.x_ref, bf16[2048,1792]{1,0:T(8,128)(2,1)} %get-tuple-element.169.dz_ref), kind=kOutput, calls=%fused_computation.1 | convolution fusion | flops 15036055552 | bytes 23068672 | tf_op jit(solution)/shard_map/dot_general | solution.py:61
  971.7 12.9 %inward.7 = bf16[1024,2048]{1,0:T(8,128)(2,1)} custom-call(bf16[2048,1792]{1,0:T(8,128)(2,1)} %get-tuple-element.169.dz_ref, bf16[2048,1024]{1,0:T(8,128)(2,1)} %all-gather.4.cloned.1.call-done.w_ref.wf_ref, bf16[2048,768]{1,0:T(8,128)(2,1)} %all-gather.6.cloned.1.call-done.wq_ref.wk_ref.wv_ref, ...), custom_call_target="tpu_custom_call" | custom-call | flops 7516192768 | bytes 11534336 | tf_op jit(solution)/shard_map/inward/pallas_call | solution.py:775
  1035.8 12.9 %inward.6.keep_ref = bf16[1024,2048]{1,0:T(8,128)(2,1)} custom-call(bf16[2048,1792]{1,0:T(8,128)(2,1)} %get-tuple-element.169.dz_ref, bf16[2048,1024]{1,0:T(8,128)(2,1)} %all-gather.4.cloned.1.call-done.w_ref.wf_ref, bf16[2048,768]{1,0:T(8,128)(2,1)} %all-gather.6.cloned.1.call-done.wq_ref.wk_ref.wv_ref, ...), custom_call_target="tpu_custom_call" | custom-call | flops 7516192768 | bytes 11534336 | tf_op jit(solution)/shard_map/inward/pallas_call | solution.py:775
  1064.3 25.6 %collective-permute-done.67.across_ref = bf16[256,2048]{1,0:T(8,128)(2,1)} collective-permute-done((bf16[256,2048]{1,0:T(8,128)(2,1)}, bf16[256,2048]{1,0:T(8,128)(2,1)}, u32[]{:S(2)}, u32[]{:S(2)}) %collective-permute-start.67) | collective-permute-done | bytes 1048608 | tf_op jit(solution)/shard_map/ppermute | solution.py:422
  1099.8 12.7 %collective-permute-done.73 = f32[3584]{0:T(1024)S(1)} collective-permute-done((f32[3584]{0:T(1024)S(1)}, f32[3584]{0:T(1024)S(1)}, u32[]{:S(2)}, u32[]{:S(2)}) %collective-permute-start.73) | collective-permute-done | bytes 14368 | tf_op jit(solution)/shard_map/ppermute | solution.py:422
  1134.0 27.5 %collective-permute-done.72 = bf16[512,1792]{1,0:T(8,128)(2,1)} collective-permute-done((bf16[512,1792]{1,0:T(8,128)(2,1)}, bf16[512,1792]{1,0:T(8,128)(2,1)}, u32[]{:S(2)}, u32[]{:S(2)}) %collective-permute-start.72) | collective-permute-done | bytes 1835040 | tf_op jit(solution)/shard_map/ppermute | solution.py:1090
  1174.6 15.3 %collective-permute-done.60 = f32[4,512]{1,0:T(4,128)S(1)} collective-permute-done((f32[4,512]{1,0:T(4,128)S(1)}, f32[4,512]{1,0:T(4,128)S(1)}, u32[]{:S(2)}, u32[]{:S(2)}) %collective-permute-start.60) | collective-permute-done | bytes 8224 | tf_op jit(solution)/shard_map/ppermute | solution.py:422
  (504 shorter events, 551.0 us)
Async XLA Ops:
  7.2 187.4 %all-gather.6.cloned.1.call-start = ((), (), s32[]{:S(2)}) async-start(), calls=%async_computation.7 | async-start | bytes 3932160 | tf_op jit(solution)/shard_map/all_gather | solution.py:934
  39.8 221.2 %all-gather.4.cloned.1.call-start = ((), (), s32[]{:S(2)}) async-start(), calls=%async_computation.6 | async-start | bytes 5242880 | tf_op jit(solution)/shard_map/all_gather | solution.py:934
  101.4 386.4 %all-gather.8.cloned.1.call-start = ((), (), s32[]{:S(2)}) async-start(), calls=%async_computation.8 | async-start | bytes 9175040 | tf_op jit(solution)/shard_map/all_gather | solution.py:934
  118.0 35.1 %collective-permute-start.10 = (bf16[512,2048]{1,0:T(8,128)(2,1)}, bf16[512,2048]{1,0:T(8,128)(2,1)}, u32[]{:S(2)}, u32[]{:S(2)}) collective-permute-start(bf16[512,2048]{1,0:T(8,128)(2,1)} %pad_maximum_fusion), channel_id=1, source_target_pairs={{0,1},{1,0},{2,3},{3,2},{4,5},{5,4},{6,7},{7,6},{8,9},{9,8},{10,11... | collective-permute-start | bytes 6291464 | tf_op jit(solution)/shard_map/ppermute | solution.py:422
  169.7 73.5 %collective-permute-start.5 = (bf16[1280,512]{1,0:T(8,128)(2,1)}, bf16[1280,512]{1,0:T(8,128)(2,1)}, u32[]{:S(2)}, u32[]{:S(2)}) collective-permute-start(bf16[1280,512]{1,0:T(8,128)(2,1)} %get-tuple-element.221.w0_ref.refs_2_), channel_id=1, source_target_pairs={{0,8},{4,12},{8,0},{12,4},{1,9},{5,13},{9,1},{13,5},{2,10},{6,14},... | collective-permute-start | bytes 3932168 | tf_op jit(solution)/shard_map/ppermute | solution.py:422
  170.3 118.6 %collective-permute-start.6 = (bf16[1280,512]{1,0:T(8,128)(2,1)}, bf16[1280,512]{1,0:T(8,128)(2,1)}, u32[]{:S(2)}, u32[]{:S(2)}) collective-permute-start(bf16[1280,512]{1,0:T(8,128)(2,1)} %get-tuple-element.221.w0_ref.refs_2_), channel_id=1, source_target_pairs={{0,4},{4,8},{8,12},{1,5},{5,9},{9,13},{2,6},{6,10},{10,14},{3,7},{... | collective-permute-start | bytes 3932168 | tf_op jit(solution)/shard_map/ppermute | solution.py:462
  191.1 53.4 %collective-permute-start.23 = (bf16[128,2048]{1,0:T(8,128)(2,1)}, bf16[128,2048]{1,0:T(8,128)(2,1)}, u32[]{:S(2)}, u32[]{:S(2)}) collective-permute-start(bf16[128,2048]{1,0:T(8,128)(2,1)} %slice.185), channel_id=1, source_target_pairs={{0,2},{1,3},{2,0},{3,1},{4,6},{5,7},{6,4},{7,5},{8,10},{9,11},{10,... | collective-permute-start | bytes 1572872 | tf_op jit(solution)/shard_map/ppermute | solution.py:422
  191.7 54.3 %collective-permute-start.22 = (bf16[128,2048]{1,0:T(8,128)(2,1)}, bf16[128,2048]{1,0:T(8,128)(2,1)}, u32[]{:S(2)}, u32[]{:S(2)}) collective-permute-start(bf16[128,2048]{1,0:T(8,128)(2,1)} %slice.184), channel_id=1, source_target_pairs={{0,16},{16,0},{1,17},{17,1},{2,18},{18,2},{3,19},{19,3},{4,20},{20... | collective-permute-start | bytes 1572872 | tf_op jit(solution)/shard_map/ppermute | solution.py:422
  194.6 83.1 %collective-permute-start.21 = (bf16[512,2048]{1,0:T(8,128)(2,1)}, bf16[512,2048]{1,0:T(8,128)(2,1)}, u32[]{:S(2)}, u32[]{:S(2)}) collective-permute-start(bf16[512,2048]{1,0:T(8,128)(2,1)} %pad_maximum_fusion.2), channel_id=1, source_target_pairs={{0,1},{1,0},{2,3},{3,2},{4,5},{5,4},{6,7},{7,6},{8,9},{9,8},{10,11... | collective-permute-start | bytes 6291464 | tf_op jit(solution)/shard_map/ppermute | solution.py:422
  243.2 45.7 %collective-permute-start.4 = (bf16[1280,512]{1,0:T(8,128)(2,1)}, bf16[1280,512]{1,0:T(8,128)(2,1)}, u32[]{:S(2)}, u32[]{:S(2)}) collective-permute-start(bf16[1280,512]{1,0:T(8,128)(2,1)} %get-tuple-element.221.w0_ref.refs_2_), channel_id=1, source_target_pairs={{12,8},{8,4},{4,0},{13,9},{9,5},{5,1},{14,10},{10,6},{6,2},{15,11}... | collective-permute-start | bytes 3932168 | tf_op jit(solution)/shard_map/ppermute | solution.py:462
  244.5 59.8 %collective-permute-start.7 = (bf16[1280,512]{1,0:T(8,128)(2,1)}, bf16[1280,512]{1,0:T(8,128)(2,1)}, u32[]{:S(2)}, u32[]{:S(2)}) collective-permute-start(bf16[1280,512]{1,0:T(8,128)(2,1)} %collective-permute-done.5.w2_ref.refs_4_), channel_id=1, source_target_pairs={{8,12},{4,0},{9,13},{5,1},{10,14},{6,2},{11,15},{7,3},{24,28},{20,... | collective-permute-start | bytes 3932168 | tf_op jit(solution)/shard_map/ppermute | solution.py:462
  248.8 36.9 %collective-permute-start.24 = (bf16[512,2048]{1,0:T(8,128)(2,1)}, bf16[512,2048]{1,0:T(8,128)(2,1)}, u32[]{:S(2)}, u32[]{:S(2)}) collective-permute-start(bf16[512,2048]{1,0:T(8,128)(2,1)} %pad_maximum_fusion.3), channel_id=1, source_target_pairs={{0,1},{1,0},{2,3},{3,2},{4,5},{5,4},{6,7},{7,6},{8,9},{9,8},{10,11... | collective-permute-start | bytes 6291464 | tf_op jit(solution)/shard_map/ppermute | solution.py:422
  319.3 702.6 %reduce-scatter.17.cloned.1.call-start = ((), (), s32[]{:S(2)}) async-start(), calls=%async_computation.14 | async-start | bytes 1310720 | tf_op jit(solution)/shard_map/reduce_scatter | solution.py:1037
  429.3 123.1 %collective-permute-start.37 = (bf16[1280,512]{1,0:T(8,128)(2,1)S(1)}, bf16[1280,512]{1,0:T(8,128)(2,1)}, u32[]{:S(2)}, u32[]{:S(2)}) collective-permute-start(bf16[1280,512]{1,0:T(8,128)(2,1)S(1)} %copy-done.38), channel_id=1, source_target_pairs={{0,8},{4,12},{8,0},{12,4},{1,9},{5,13},{9,1},{13,5},{2,10},{6,14},... | collective-permute-start | bytes 3932168 | tf_op jit(solution)/shard_map/ppermute | solution.py:422
  518.6 503.4 %reduce-scatter.15.cloned.1.call-start = ((), (), s32[]{:S(2)}) async-start(), calls=%async_computation.13 | async-start | bytes 5242880 | tf_op jit(solution)/shard_map/reduce_scatter | solution.py:1037
  549.7 562.9 %reduce-scatter.13.cloned.1.call-start = ((), (), s32[]{:S(2)}) async-start(), calls=%async_computation.12 | async-start | bytes 9175040 | tf_op jit(solution)/shard_map/reduce_scatter | solution.py:1037
  549.7 56.2 %collective-permute-start.38 = (bf16[1280,512]{1,0:T(8,128)(2,1)S(1)}, bf16[1280,512]{1,0:T(8,128)(2,1)S(1)}, u32[]{:S(2)}, u32[]{:S(2)}) collective-permute-start(bf16[1280,512]{1,0:T(8,128)(2,1)S(1)} %copy-done.38), channel_id=1, source_target_pairs={{0,4},{4,8},{8,12},{1,5},{5,9},{9,13},{2,6},{6,10},{10,14},{3,7},{... | collective-permute-start | bytes 3932168 | tf_op jit(solution)/shard_map/ppermute | solution.py:462
  551.1 89.4 %collective-permute-start.36 = (bf16[1280,512]{1,0:T(8,128)(2,1)S(1)}, bf16[1280,512]{1,0:T(8,128)(2,1)S(1)}, u32[]{:S(2)}, u32[]{:S(2)}) collective-permute-start(bf16[1280,512]{1,0:T(8,128)(2,1)S(1)} %copy-done.38), channel_id=1, source_target_pairs={{12,8},{8,4},{4,0},{13,9},{9,5},{5,1},{14,10},{10,6},{6,2},{15,11}... | collective-permute-start | bytes 3932168 | tf_op jit(solution)/shard_map/ppermute | solution.py:462
  552.4 126.8 %collective-permute-start.39 = (bf16[1280,512]{1,0:T(8,128)(2,1)}, bf16[1280,512]{1,0:T(8,128)(2,1)S(1)}, u32[]{:S(2)}, u32[]{:S(2)}) collective-permute-start(bf16[1280,512]{1,0:T(8,128)(2,1)} %collective-permute-done.37.w2_ref.refs_3_), channel_id=1, source_target_pairs={{8,12},{4,0},{9,13},{5,1},{10,14},{6,2},{11,15},{7,3},{24,28},{20,... | collective-permute-start | bytes 3932168 | tf_op jit(solution)/shard_map/ppermute | solution.py:462
  749.6 376.9 %reduce-scatter.11.cloned.1.call-start = ((), (), s32[]{:S(2)}) async-start(), calls=%async_computation.11 | async-start | bytes 9175040 | tf_op jit(solution)/shard_map/reduce_scatter | solution.py:1037
  923.0 273.3 %reduce-scatter.9.cloned.1.call-start = ((), (), s32[]{:S(2)}) async-start(), calls=%async_computation.10 | async-start | bytes 5242880 | tf_op jit(solution)/shard_map/reduce_scatter | solution.py:1037
  953.9 273.6 %reduce-scatter.7.cloned.1.call-start = ((), (), s32[]{:S(2)}) async-start(), calls=%async_computation.9 | async-start | bytes 1310720 | tf_op jit(solution)/shard_map/reduce_scatter | solution.py:1037
  984.6 64.2 %collective-permute-start.66 = (bf16[1024,2048]{1,0:T(8,128)(2,1)}, bf16[1024,2048]{1,0:T(8,128)(2,1)}, u32[]{:S(2)}, u32[]{:S(2)}) collective-permute-start(bf16[1024,2048]{1,0:T(8,128)(2,1)} %inward.7), channel_id=1, source_target_pairs={{0,1},{1,0},{2,3},{3,2},{4,5},{5,4},{6,7},{7,6},{8,9},{9,8},{10,11... | collective-permute-start | bytes 12582920 | tf_op jit(solution)/shard_map/ppermute | solution.py:422
  1004.2 51.4 %collective-permute-start.65 = (bf16[256,2048]{1,0:T(8,128)(2,1)S(1)}, bf16[256,2048]{1,0:T(8,128)(2,1)S(1)}, u32[]{:S(2)}, u32[]{:S(2)}) collective-permute-start(bf16[256,2048]{1,0:T(8,128)(2,1)S(1)} %get-tuple-element.211), channel_id=1, source_target_pairs={{0,16},{16,0},{1,17},{17,1},{2,18},{18,2},{3,19},{19,3},{4,20},{20... | collective-permute-start | bytes 3145736 | tf_op jit(solution)/shard_map/ppermute | solution.py:422
  1024.4 186.9 %collective-permute-start.63 = (bf16[1280,512]{1,0:T(8,128)(2,1)}, bf16[1280,512]{1,0:T(8,128)(2,1)}, u32[]{:S(2)}, u32[]{:S(2)}) collective-permute-start(bf16[1280,512]{1,0:T(8,128)(2,1)} %pad_maximum_fusion.10), channel_id=1, source_target_pairs={{0,16},{1,17},{2,18},{3,19},{4,20},{5,21},{6,22},{7,23},{8,24},{9,... | collective-permute-start | bytes 3932168 | tf_op jit(solution)/shard_map/ppermute | solution.py:1090
  1054.0 35.8 %collective-permute-start.67 = (bf16[256,2048]{1,0:T(8,128)(2,1)}, bf16[256,2048]{1,0:T(8,128)(2,1)}, u32[]{:S(2)}, u32[]{:S(2)}) collective-permute-start(bf16[256,2048]{1,0:T(8,128)(2,1)} %get-tuple-element.180), channel_id=1, source_target_pairs={{0,16},{16,0},{1,17},{17,1},{2,18},{18,2},{3,19},{19,3},{4,20},{20... | collective-permute-start | bytes 3145736 | tf_op jit(solution)/shard_map/ppermute | solution.py:422
  1054.0 35.8 %collective-permute-start.68 = (bf16[256,2048]{1,0:T(8,128)(2,1)}, bf16[256,2048]{1,0:T(8,128)(2,1)}, u32[]{:S(2)}, u32[]{:S(2)}) collective-permute-start(bf16[256,2048]{1,0:T(8,128)(2,1)} %get-tuple-element.181), channel_id=1, source_target_pairs={{0,2},{1,3},{2,0},{3,1},{4,6},{5,7},{6,4},{7,5},{8,10},{9,11},{10,... | collective-permute-start | bytes 3145736 | tf_op jit(solution)/shard_map/ppermute | solution.py:422
  1059.1 170.3 %collective-permute-start.56 = (bf16[256,2048]{1,0:T(8,128)(2,1)}, bf16[256,2048]{1,0:T(8,128)(2,1)}, u32[]{:S(2)}, u32[]{:S(2)}) collective-permute-start(bf16[256,2048]{1,0:T(8,128)(2,1)} %get-tuple-element.203), channel_id=1, source_target_pairs={{0,16},{1,17},{2,18},{3,19},{4,20},{5,21},{6,22},{7,23},{8,24},{9,... | collective-permute-start | bytes 3145736 | tf_op jit(solution)/shard_map/ppermute | solution.py:1090
  1064.0 48.5 %collective-permute-start.73 = (f32[3584]{0:T(1024)S(1)}, f32[3584]{0:T(1024)S(1)}, u32[]{:S(2)}, u32[]{:S(2)}) collective-permute-start(f32[3584]{0:T(1024)S(1)} %slice.247), channel_id=1, source_target_pairs={{0,16},{16,0},{1,17},{17,1},{2,18},{18,2},{3,19},{19,3},{4,20},{20... | collective-permute-start | bytes 43016 | tf_op jit(solution)/shard_map/ppermute | solution.py:422
  1112.6 48.9 %collective-permute-start.72 = (bf16[512,1792]{1,0:T(8,128)(2,1)}, bf16[512,1792]{1,0:T(8,128)(2,1)}, u32[]{:S(2)}, u32[]{:S(2)}) collective-permute-start(bf16[512,1792]{1,0:T(8,128)(2,1)} %reduce-scatter.13.cloned.1.call-done), channel_id=1, source_target_pairs={{0,16},{1,17},{2,18},{3,19},{4,20},{5,21},{6,22},{7,23},{8,24},{9,... | collective-permute-start | bytes 5505032 | tf_op jit(solution)/shard_map/ppermute | solution.py:1090
  1126.4 45.0 %collective-permute-start.57 = (bf16[512,1792]{1,0:T(8,128)(2,1)}, bf16[512,1792]{1,0:T(8,128)(2,1)S(1)}, u32[]{:S(2)}, u32[]{:S(2)}) collective-permute-start(bf16[512,1792]{1,0:T(8,128)(2,1)} %reduce-scatter.11.cloned.1.call-done), channel_id=1, source_target_pairs={{16,0},{17,1},{18,2},{19,3},{20,4},{21,5},{22,6},{23,7},{24,8},{25... | collective-permute-start | bytes 5505032 | tf_op jit(solution)/shard_map/ppermute | solution.py:1087
  1132.5 95.0 %collective-permute-start.71 = (bf16[256,2048]{1,0:T(8,128)(2,1)}, bf16[256,2048]{1,0:T(8,128)(2,1)}, u32[]{:S(2)}, u32[]{:S(2)}) collective-permute-start(bf16[256,2048]{1,0:T(8,128)(2,1)} %get-tuple-element.201), channel_id=1, source_target_pairs={{16,0},{17,1},{18,2},{19,3},{20,4},{21,5},{22,6},{23,7},{24,8},{25... | collective-permute-start | bytes 3145736 | tf_op jit(solution)/shard_map/ppermute | solution.py:1087
  (124 other events, 2154.0 us)
Sparse Core Ops, SparseCore 0:
  39.9 64.8 all-gather.5
  107.0 116.6 all-gather.3
  319.4 168.3 all-gather.7
  518.7 25.4 reduce-scatter.16
  549.8 108.7 reduce-scatter.14
  749.7 126.0 reduce-scatter.12
  923.1 126.1 reduce-scatter.10
  1051.6 77.6 reduce-scatter.8
  1131.6 27.7 reduce-scatter.6
